TPU v7x, 32 devices: a whole 2x2x4 slice. The times are simulated.
32 devices in a mesh: dp: 16 (over z, x, core), fsdp: 2 (over y).
Axes of the slice: x: 2, y: 2, z: 4, core: 2. Of those that a mesh axis runs over, the one named last changes fastest.
Arguments:
- hidden_in: bfloat16 [32, 1024, 1024], P(('dp', 'fsdp')), may hold values from -6 to 6
- segment_ids: int32 [32, 1024], P(('dp', 'fsdp')), may hold values from 0 to 7, as said below
- out_grad: bfloat16 [32, 1024, 1024], P(('dp', 'fsdp')), may hold values from -6 to 6
- norm1_gain: bfloat16 [1024], P(('dp', 'fsdp')), may hold values from 0.099609375 to 1.8984375
- norm1_bias: bfloat16 [1024], P(('dp', 'fsdp')), may hold values from -1.75 to 1.75
- norm2_gain: bfloat16 [1024], P(('dp', 'fsdp')), may hold values from 0.099609375 to 1.8984375
- norm2_bias: bfloat16 [1024], P(('dp', 'fsdp')), may hold values from -1.75 to 1.75
- qkv_weight: bfloat16 [1024, 3072], P(('dp', 'fsdp')), may hold values from -0.25 to 0.25
- qkv_bias: bfloat16 [3072], P(('dp', 'fsdp')), may hold values from -1.75 to 1.75
- proj_weight: bfloat16 [1024, 1024], P(('dp', 'fsdp')), may hold values from -0.75 to 0.75
- proj_bias: bfloat16 [1024], P(('dp', 'fsdp')), may hold values from -1.75 to 1.75
- up_weight: bfloat16 [1024, 4096], P(('dp', 'fsdp')), may hold values from -0.1875 to 0.1875
- up_bias: bfloat16 [4096], P(('dp', 'fsdp')), may hold values from -1.75 to 1.75
- down_weight: bfloat16 [4096, 1024], P(('dp', 'fsdp')), may hold values from -0.09375 to 0.09375
- down_bias: bfloat16 [1024], P(('dp', 'fsdp')), may hold values from -1.75 to 1.75
Outputs:
- layer_out: bfloat16 [32, 1024, 1024], P(('dp', 'fsdp'))
- input_grad: bfloat16 [32, 1024, 1024], P(('dp', 'fsdp'))
- norm1_gain_grad: float32 [1024], P(('dp', 'fsdp'))
- norm1_bias_grad: float32 [1024], P(('dp', 'fsdp'))
- norm2_gain_grad: float32 [1024], P(('dp', 'fsdp'))
- norm2_bias_grad: float32 [1024], P(('dp', 'fsdp'))
- qkv_weight_grad: float32 [1024, 3072], P(('dp', 'fsdp'))
- qkv_bias_grad: float32 [3072], P(('dp', 'fsdp'))
- proj_weight_grad: float32 [1024, 1024], P(('dp', 'fsdp'))
- proj_bias_grad: float32 [1024], P(('dp', 'fsdp'))
- up_weight_grad: float32 [1024, 4096], P(('dp', 'fsdp'))
- up_bias_grad: float32 [4096], P(('dp', 'fsdp'))
- down_weight_grad: float32 [4096, 1024], P(('dp', 'fsdp'))
- down_bias_grad: float32 [1024], P(('dp', 'fsdp'))
Inputs may be any that keep to these rules, and one draw needn't show every extreme that they name: `segment_ids`: within a sequence the ids never fall. A sequence holds 3 to 7 documents with ids 0, 1, 2 and so on, each of 60 to 800 tokens, followed by 0 to 64 padding tokens with id 8 - 1; ids between the last document's and 7 are unused. In every draw some document has exactly 800 tokens and some sequence exactly 64 padding tokens.
All inputs are finite; a program needn't handle non-finite values.
Results may differ from a plain program's by a relative error of at most 0.012.
The roundings to bfloat16 on the way count: a program that leaves them out, or rounds other values in their place, can miss the bound.
Values may be sent and summed in bfloat16 or wider, within the bound.
No kernel may reach another device: no remote copies, remote signals or barrier semaphores. Data moves between devices by JAX's collectives and lax.ppermute only.
A program may use at most 384 MiB of HBM per device.

v0:
```python
from functools import partial

import jax
import jax.numpy as jnp
from jax import lax
from jax.sharding import PartitionSpec as P

HEADS = 16
HEAD = 64
ROT = 16
DOCS = 8


norm_eps = 1e-05
masked_score = -1e30


def normed(values, gain):
    center = values - jnp.mean(values, axis=-1, keepdims=True)
    spread = jnp.mean(center * center, axis=-1, keepdims=True)
    return center * lax.rsqrt(spread + norm_eps) * gain


def rotate(part, cosine, sine):
    half_rot = ROT // 2
    first = part[..., :half_rot]
    second = part[..., half_rot:ROT]
    cos_wide = cosine[..., None, :]
    sin_wide = sine[..., None, :]
    return jnp.concatenate(
        [
            first * cos_wide - second * sin_wide,
            second * cos_wide + first * sin_wide,
            part[..., ROT:],
        ],
        axis=-1,
    )


def angles(segments):
    last_axis = segments.ndim - 1
    position = lax.broadcasted_iota(jnp.int32, segments.shape, last_axis)
    change = jnp.concatenate(
        [jnp.ones(segments.shape[:-1] + (1,), jnp.bool_), segments[..., 1:] != segments[..., :-1]],
        axis=-1,
    )
    first_index = lax.cummax(jnp.where(change, position, jnp.zeros_like(position)), axis=last_axis)
    place = (position - first_index).astype(jnp.float32)
    freqs = 10000.0 ** (-(jnp.arange(ROT // 2) * 2).astype(jnp.float32) / ROT)
    theta = place[..., None] * freqs
    return (jnp.cos(theta), jnp.sin(theta))


def block_mask(segments, block_start, block_rows):
    length = segments.shape[0]
    query_pos = block_start + lax.broadcasted_iota(jnp.int32, (block_rows, length), 0)
    key_pos = lax.broadcasted_iota(jnp.int32, (block_rows, length), 1)
    same = segments[block_start : block_start + block_rows][:, None] == segments[None, :]
    return ((key_pos <= query_pos) & same)[None]


def attend_forward(pieces):
    query, keys, values, segments = pieces
    length = segments.shape[0]
    block_rows = min(512, length)
    outputs = []
    log_sums = []
    for block_start in range(0, length, block_rows):
        allowed = block_mask(segments, block_start, block_rows)
        scores = jnp.einsum(
            "qhe,khe->hqk",
            query[block_start : block_start + block_rows],
            keys,
            preferred_element_type=jnp.float32,
        )
        scores = jnp.where(allowed, scores, masked_score)
        row_max = jnp.max(scores, axis=-1, keepdims=True)
        exponent = jnp.exp(scores - row_max)
        total = jnp.sum(exponent, axis=-1, keepdims=True)
        weights = (exponent / total).astype(jnp.bfloat16)
        outputs.append(
            jnp.einsum("hqk,khe->qhe", weights, values, preferred_element_type=jnp.float32)
        )
        log_sums.append(row_max + jnp.log(total))
    return (jnp.concatenate(outputs, axis=0), jnp.concatenate(log_sums, axis=1))


def attend_backward(pieces):
    query, keys, values, segments, log_sums, d_out = pieces
    length = segments.shape[0]
    block_rows = min(512, length)
    query_parts = []
    d_keys = jnp.zeros(keys.shape, jnp.float32)
    d_values = jnp.zeros(values.shape, jnp.float32)
    for block_start in range(0, length, block_rows):
        block_end = block_start + block_rows
        allowed = block_mask(segments, block_start, block_rows)
        scores = jnp.einsum(
            "qhe,khe->hqk", query[block_start:block_end], keys, preferred_element_type=jnp.float32
        )
        scores = jnp.where(allowed, scores, masked_score)
        probs = jnp.exp(scores - log_sums[:, block_start:block_end])
        d_probs = jnp.einsum(
            "qhe,khe->hqk", d_out[block_start:block_end], values, preferred_element_type=jnp.float32
        )
        inner = jnp.sum(d_probs * probs, axis=-1, keepdims=True)
        d_scores = (probs * (d_probs - inner)).astype(jnp.bfloat16)
        d_values = d_values + jnp.einsum(
            "hqk,qhe->khe",
            probs.astype(jnp.bfloat16),
            d_out[block_start:block_end],
            preferred_element_type=jnp.float32,
        )
        query_parts.append(
            jnp.einsum("hqk,khe->qhe", d_scores, keys, preferred_element_type=jnp.float32)
        )
        d_keys = d_keys + jnp.einsum(
            "hqk,qhe->khe",
            d_scores,
            query[block_start:block_end],
            preferred_element_type=jnp.float32,
        )
    return (jnp.concatenate(query_parts, axis=0), d_keys, d_values)


def body(
    hidden_in,
    segment_ids,
    out_grad,
    norm1_gain,
    norm1_bias,
    norm2_gain,
    norm2_bias,
    qkv_weight,
    qkv_bias,
    proj_weight,
    proj_bias,
    up_weight,
    up_bias,
    down_weight,
    down_bias,
):
    gathered = (
        lax.all_gather(norm1_gain, ("dp", "fsdp"), axis=0, tiled=True),
        lax.all_gather(norm1_bias, ("dp", "fsdp"), axis=0, tiled=True),
        lax.all_gather(norm2_gain, ("dp", "fsdp"), axis=0, tiled=True),
        lax.all_gather(norm2_bias, ("dp", "fsdp"), axis=0, tiled=True),
        lax.all_gather(qkv_weight, ("dp", "fsdp"), axis=0, tiled=True),
        lax.all_gather(qkv_bias, ("dp", "fsdp"), axis=0, tiled=True),
        lax.all_gather(proj_weight, ("dp", "fsdp"), axis=0, tiled=True),
        lax.all_gather(proj_bias, ("dp", "fsdp"), axis=0, tiled=True),
        lax.all_gather(up_weight, ("dp", "fsdp"), axis=0, tiled=True),
        lax.all_gather(up_bias, ("dp", "fsdp"), axis=0, tiled=True),
        lax.all_gather(down_weight, ("dp", "fsdp"), axis=0, tiled=True),
        lax.all_gather(down_bias, ("dp", "fsdp"), axis=0, tiled=True),
    )
    (
        gain_one,
        shift_one,
        gain_two,
        shift_two,
        w_qkv,
        b_qkv,
        w_proj,
        b_proj,
        w_up,
        b_up,
        w_down,
        b_down,
    ) = gathered
    seq_count, length, model_width = hidden_in.shape
    row_count = seq_count * length
    scale = HEAD ** (-0.5)
    flat = hidden_in.reshape(row_count, model_width).astype(jnp.float32)
    grad_rows = out_grad.reshape(row_count, model_width)
    valid = (segment_ids != DOCS - 1).astype(jnp.float32).reshape(row_count, 1)
    cosine, sine = angles(segment_ids)
    normed_one = (
        normed(flat, gain_one.astype(jnp.float32)) + shift_one.astype(jnp.float32)
    ).astype(jnp.bfloat16)
    mixed = jnp.dot(normed_one, w_qkv, preferred_element_type=jnp.float32) + b_qkv.astype(
        jnp.float32
    )
    raw = mixed.reshape(seq_count, length, 3, HEADS, HEAD)
    raw_query = raw[:, :, 0]
    raw_keys = raw[:, :, 1]

    def rope_pair(first_part, second_part):
        return (rotate(first_part, cosine, sine), rotate(second_part, cosine, sine))

    (turned_query, turned_keys), rope_pull = jax.vjp(rope_pair, raw_query, raw_keys)
    query = (turned_query * scale).astype(jnp.bfloat16)
    keys = turned_keys.astype(jnp.bfloat16)
    values = raw[:, :, 2].astype(jnp.bfloat16)
    heads_out, log_sums = lax.map(attend_forward, (query, keys, values, segment_ids))
    attended = (heads_out.reshape(row_count, model_width) * valid).astype(jnp.bfloat16)
    projected = jnp.dot(attended, w_proj, preferred_element_type=jnp.float32) + b_proj.astype(
        jnp.float32
    )
    normed_two = (
        normed(flat, gain_two.astype(jnp.float32)) + shift_two.astype(jnp.float32)
    ).astype(jnp.bfloat16)
    before = jnp.dot(normed_two, w_up, preferred_element_type=jnp.float32) + b_up.astype(
        jnp.float32
    )
    after = jax.nn.gelu(before, approximate=False).astype(jnp.bfloat16)
    branch = jnp.dot(after, w_down, preferred_element_type=jnp.float32) + b_down.astype(jnp.float32)
    layer_out = (
        (flat + projected + branch).astype(jnp.bfloat16).reshape(seq_count, length, model_width)
    )
    back_gain_one, back_gain_two, back_qkv, back_proj, back_up, back_down = (
        lax.all_gather(norm1_gain, ("dp", "fsdp"), axis=0, tiled=True),
        lax.all_gather(norm2_gain, ("dp", "fsdp"), axis=0, tiled=True),
        lax.all_gather(qkv_weight, ("dp", "fsdp"), axis=0, tiled=True),
        lax.all_gather(proj_weight, ("dp", "fsdp"), axis=0, tiled=True),
        lax.all_gather(up_weight, ("dp", "fsdp"), axis=0, tiled=True),
        lax.all_gather(down_weight, ("dp", "fsdp"), axis=0, tiled=True),
    )
    grad_wide = grad_rows.astype(jnp.float32)
    bias_grad = jnp.sum(grad_wide, axis=0)
    grad_down = jnp.einsum("rf,rd->fd", after, grad_rows, preferred_element_type=jnp.float32)
    d_after = jnp.einsum("rd,fd->rf", grad_rows, back_down, preferred_element_type=jnp.float32)
    gelu_value, gelu_pull = jax.vjp(partial(jax.nn.gelu, approximate=False), before)
    d_before = gelu_pull(d_after)[0].astype(jnp.bfloat16)
    grad_up_bias = jnp.sum(d_before.astype(jnp.float32), axis=0)
    grad_up = jnp.einsum("rd,rf->df", normed_two, d_before, preferred_element_type=jnp.float32)
    d_normed_two = jnp.einsum("rf,df->rd", d_before, back_up, preferred_element_type=jnp.float32)
    norm_value_two, pull_two = jax.vjp(normed, flat, back_gain_two.astype(jnp.float32))
    dx_two, grad_gain_two = pull_two(d_normed_two)
    grad_shift_two = jnp.sum(d_normed_two, axis=0)
    grad_proj = jnp.einsum("rd,re->de", attended, grad_rows, preferred_element_type=jnp.float32)
    d_attended = (
        jnp.einsum("re,de->rd", grad_rows, back_proj, preferred_element_type=jnp.float32) * valid
    ).astype(jnp.bfloat16)
    d_attended = d_attended.reshape(seq_count, length, HEADS, HEAD)
    d_query, d_keys, d_values = lax.map(
        attend_backward, (query, keys, values, segment_ids, log_sums, d_attended)
    )
    d_raw_query, d_raw_keys = rope_pull((d_query * scale, d_keys))
    d_mixed = (
        jnp.stack([d_raw_query, d_raw_keys, d_values], axis=2)
        .reshape(row_count, 3 * model_width)
        .astype(jnp.bfloat16)
    )
    grad_qkv_bias = jnp.sum(d_mixed.astype(jnp.float32), axis=0)
    grad_qkv = jnp.einsum("rd,rc->dc", normed_one, d_mixed, preferred_element_type=jnp.float32)
    d_normed_one = jnp.einsum("rc,dc->rd", d_mixed, back_qkv, preferred_element_type=jnp.float32)
    norm_value_one, pull_one = jax.vjp(normed, flat, back_gain_one.astype(jnp.float32))
    dx_one, grad_gain_one = pull_one(d_normed_one)
    grad_shift_one = jnp.sum(d_normed_one, axis=0)
    input_grad = (
        (grad_wide + dx_one + dx_two).astype(jnp.bfloat16).reshape(seq_count, length, model_width)
    )
    shards = (
        lax.psum_scatter(grad_gain_one, ("dp", "fsdp"), scatter_dimension=0, tiled=True),
        lax.psum_scatter(grad_shift_one, ("dp", "fsdp"), scatter_dimension=0, tiled=True),
        lax.psum_scatter(grad_gain_two, ("dp", "fsdp"), scatter_dimension=0, tiled=True),
        lax.psum_scatter(grad_shift_two, ("dp", "fsdp"), scatter_dimension=0, tiled=True),
        lax.psum_scatter(grad_qkv, ("dp", "fsdp"), scatter_dimension=0, tiled=True),
        lax.psum_scatter(grad_qkv_bias, ("dp", "fsdp"), scatter_dimension=0, tiled=True),
        lax.psum_scatter(grad_proj, ("dp", "fsdp"), scatter_dimension=0, tiled=True),
        lax.psum_scatter(bias_grad, ("dp", "fsdp"), scatter_dimension=0, tiled=True),
        lax.psum_scatter(grad_up, ("dp", "fsdp"), scatter_dimension=0, tiled=True),
        lax.psum_scatter(grad_up_bias, ("dp", "fsdp"), scatter_dimension=0, tiled=True),
        lax.psum_scatter(grad_down, ("dp", "fsdp"), scatter_dimension=0, tiled=True),
        lax.psum_scatter(bias_grad, ("dp", "fsdp"), scatter_dimension=0, tiled=True),
    )
    return (
        layer_out,
        input_grad,
        shards[0],
        shards[1],
        shards[2],
        shards[3],
        shards[4],
        shards[5],
        shards[6],
        shards[7],
        shards[8],
        shards[9],
        shards[10],
        shards[11],
    )


def solution(mesh):
    in_specs = (
        P(("dp", "fsdp"), None, None),
        P(("dp", "fsdp"), None),
        P(("dp", "fsdp"), None, None),
        P(("dp", "fsdp")),
        P(("dp", "fsdp")),
        P(("dp", "fsdp")),
        P(("dp", "fsdp")),
        P(("dp", "fsdp"), None),
        P(("dp", "fsdp")),
        P(("dp", "fsdp"), None),
        P(("dp", "fsdp")),
        P(("dp", "fsdp"), None),
        P(("dp", "fsdp")),
        P(("dp", "fsdp"), None),
        P(("dp", "fsdp")),
    )
    out_specs = (
        P(("dp", "fsdp"), None, None),
        P(("dp", "fsdp"), None, None),
        P(("dp", "fsdp")),
        P(("dp", "fsdp")),
        P(("dp", "fsdp")),
        P(("dp", "fsdp")),
        P(("dp", "fsdp"), None),
        P(("dp", "fsdp")),
        P(("dp", "fsdp"), None),
        P(("dp", "fsdp")),
        P(("dp", "fsdp"), None),
        P(("dp", "fsdp")),
        P(("dp", "fsdp"), None),
        P(("dp", "fsdp")),
    )
    return jax.shard_map(body, mesh=mesh, in_specs=in_specs, out_specs=out_specs, check_vma=False)
```

profile of v0, /device:TPU:1, one launch (start us, length us, event | category | flops | bytes accessed | tf_op | source)
XLA Modules:
  0.0 1435.2 jit_solution(9966620385994780129)
XLA Ops:
  18.2 42.5 %all-reduce.21 = (bf16[3072]{0:T(1024)(128)(2,1)S(1)}, bf16[1024]{0:T(1024)(128)(2,1)S(1)}, bf16[1024]{0:T(1024)(128)(2,1)S(1)}, bf16[1024]{0:T(1024)(128)(2,1)}...) all-reduce(bf16[3072]{0:T(1024)(128)(2,1)S(1)} %dynamic-update-slic, ...), channel_id=1, replica_groups=mesh['dp'=16,'fsdp'=2] {'dp','fsdp'}, use_global_device_ids=true, to_apply=%add.8 | all-reduce | flops 9216 | bytes 36864
  60.7 1.9 convert_reduce_fusion.2
  65.4 63.3 %all-gather = bf16[32,1,128]{2,1,0:T(2,128)(2,1)S(1)} all-gather(bf16[1,1,128]{2,1,0:T(2,128)(2,1)S(1)} %bitcast.224), channel_id=1, replica_groups=mesh['dp'=16,'fsdp'=2] {'dp','fsdp'}, dimensions={0}, use_global_device_ids=true | all-gather | bytes 8448 | tf_op jit(solution)/shard_map/all_gather | solution.py:153
  131.0 5.0 multiply_convert_fusion.3
  136.1 1.5 fusion.107
  137.6 4.3 all-gather.6.cloned.1.call-done
  141.9 13.0 broadcast_add_fusion
  154.9 12.6 copy.33
  167.5 4.5 slice_bitcast_fusion
  172.3 1.4 fusion.84
  174.7 1.9 fusion.51
  176.7 16.0 %select_reduce_fusion.1 = (f32[16,512]{1,0:T(8,128)S(1)}, f32[16,512,1024]{2,1,0:T(8,128)}) fusion(pred[512,1024]{1,0:T(8,128)(4,1)S(1)} %get-tuple-element.117, bf16[1024,16,48]{0,2,1:T(8,128)(2,1)} %fusion.84, bf16[1024,16,8]{0,2,1:T(8,128)(2,1)} %get-tuple-element.100, bf16[1024,16,8]{0,2,1:T(8,128)(2,1)S(1)} %get-tuple-element.99, ...), kind=kOutput, calls=%fused_computation.13 | convolution fusion | flops 1096802304 | bytes 37257216 | tf_op jit(solution)/shard_map/while/body/eval_jaxpr/qhe,khe->hqk/dot_general | solution.py:70
  192.7 15.2 %fusion = f32[16,512]{1,0:T(8,128)S(1)} fusion(f32[16,512,1024]{2,1,0:T(8,128)} %get-tuple-element.124, f32[16,512]{1,0:T(8,128)S(1)} %get-tuple-element.123, pred[512,1024]{1,0:T(8,128)(4,1)S(1)} %get-tuple-element.117), kind=kLoop, calls=%fused_computation.10 | loop fusion | flops 25157632 | bytes 34144256 | tf_op jit(solution)/shard_map/while/body/eval_jaxpr/reduce_sum | solution.py:79
  208.6 15.4 %fusion.20 = f32[16,64,512]{2,1,0:T(8,128)} fusion(f32[16,512,1024]{2,1,0:T(8,128)} %get-tuple-element.124, f32[16,512]{1,0:T(8,128)S(1)} %fusion, f32[16,512]{1,0:T(8,128)S(1)} %get-tuple-element.123, pred[512,1024]{1,0:T(8,128)(4,1)S(1)} %get-tuple-element.117, f32[1,1024,3,16,64]{1,4,3,2,0:T(8,128)S(1)} %bitcast.196), kind=kOutput, calls=%fused_computation.42 | convolution fusion | flops 1107296256 | bytes 38338560 | tf_op jit(solution)/shard_map/while/body/eval_jaxpr/hqk,khe->qhe/dot_general | solution.py:82
  224.0 15.3 %select_reduce_fusion = (f32[16,512]{1,0:T(8,128)S(1)}, f32[16,512,1024]{2,1,0:T(8,128)}) fusion(pred[512,1024]{1,0:T(8,128)(4,1)S(1)} %get-tuple-element.118, bf16[1024,16,48]{0,2,1:T(8,128)(2,1)} %fusion.84, bf16[1024,16,8]{0,2,1:T(8,128)(2,1)} %get-tuple-element.100, bf16[1024,16,8]{0,2,1:T(8,128)(2,1)S(1)} %get-tuple-element.99, ...), kind=kOutput, calls=%fused_computation.12 | convolution fusion | flops 1096802304 | bytes 37257216 | tf_op jit(solution)/shard_map/while/body/eval_jaxpr/qhe,khe->hqk/dot_general | solution.py:70
  239.3 15.0 %fusion.1 = f32[16,512]{1,0:T(8,128)S(1)} fusion(f32[16,512,1024]{2,1,0:T(8,128)} %get-tuple-element.122, f32[16,512]{1,0:T(8,128)S(1)} %get-tuple-element.121, pred[512,1024]{1,0:T(8,128)(4,1)S(1)} %get-tuple-element.118), kind=kLoop, calls=%fused_computation.11 | loop fusion | flops 25157632 | bytes 34144256 | tf_op jit(solution)/shard_map/while/body/eval_jaxpr/reduce_sum | solution.py:79
  254.4 15.1 %fusion.21 = f32[16,64,512]{2,1,0:T(8,128)} fusion(f32[16,512,1024]{2,1,0:T(8,128)} %get-tuple-element.122, f32[16,512]{1,0:T(8,128)S(1)} %fusion.1, f32[16,512]{1,0:T(8,128)S(1)} %get-tuple-element.121, pred[512,1024]{1,0:T(8,128)(4,1)S(1)} %get-tuple-element.118, f32[1,1024,3,16,64]{1,4,3,2,0:T(8,128)S(1)} %bitcast.199), kind=kOutput, calls=%fused_computation.43 | convolution fusion | flops 1107296256 | bytes 38338560 | tf_op jit(solution)/shard_map/while/body/eval_jaxpr/hqk,khe->qhe/dot_general | solution.py:82
  269.5 7.6 fusion.54
  277.1 28.4 %multiply_reduce_fusion.1 = (f32[16,512]{1,0:T(8,128)S(1)}, f32[16,512,1024]{2,1,0:T(8,128)}) fusion(f32[16,512,1024]{2,1,0:T(8,128)} %get-tuple-element.124, f32[16,512]{1,0:T(8,128)S(1)} %copy-done.18, pred[512,1024]{1,0:T(8,128)(4,1)} %copy-done.2, bf16[512,16,64]{0,2,1:T(8,128)(2,1)} %bitcast.203, f32[1,1024,3,16,64]{1,4,3,2,0:T(8,128)} %bitcast.193), kind=kOutput, calls=%fused_computation.4 | convolution fusion | flops 1107288064 | bytes 70844416 | tf_op jit(solution)/shard_map/while/body/eval_jaxpr/qhe,khe->hqk/dot_general | solution.py:103
  305.6 24.7 %multiply_reduce_fusion = (f32[16,512]{1,0:T(8,128)S(1)}, f32[16,512,1024]{2,1,0:T(8,128)}) fusion(f32[16,512,1024]{2,1,0:T(8,128)} %get-tuple-element.122, f32[16,512]{1,0:T(8,128)S(1)} %log_add_fusion, pred[512,1024]{1,0:T(8,128)(4,1)} %copy-done.4, bf16[512,16,64]{0,2,1:T(8,128)(2,1)} %bitcast.205, f32[1,1024,3,16,64]{1,4,3,2,0:T(8,128)S(1)} %bitcast.202), kind=kOutput, calls=%fused_computation.1 | convolution fusion | flops 1107288064 | bytes 70844416 | tf_op jit(solution)/shard_map/while/body/eval_jaxpr/qhe,khe->hqk/dot_general | solution.py:103
  330.3 54.5 %multiply_convert_fusion = (bf16[16,512,1024]{2,1,0:T(8,128)(2,1)}, bf16[16,512,1024]{2,1,0:T(8,128)(2,1)}) fusion(f32[16,512,1024]{2,1,0:T(8,128)} %get-tuple-element.127, f32[16,512,1024]{2,1,0:T(8,128)} %get-tuple-element.122, f32[16,512]{1,0:T(8,128)S(1)} %get-tuple-element.126, f32[16,512]{1,0:T(8,128)S(1)} %log_add_fusion, ...), kind=kLoop, calls=%fused_computation | loop fusion | flops 83886080 | bytes 168951808 | tf_op jit(solution)/shard_map/while/body/eval_jaxpr/convert_element_type | solution.py:107
  384.8 12.3 convolution_bitcast_fusion.1
  397.1 11.1 fusion.85
  408.5 12.4 convolution_bitcast_fusion
  420.9 2.7 maximum_multiply_fusion.1
  426.5 9.1 add_bitcast_fusion.2
  437.5 1.7 add_bitcast_fusion.3
  440.2 1.7 add_bitcast_fusion.1
  441.9 16.4 %fusion.4 = f32[16,64,1024]{2,1,0:T(8,128)} fusion(bf16[512,16,64]{0,2,1:T(8,128)(2,1)S(1)} %bitcast.206, f32[16,512,1024]{2,1,0:T(8,128)} %get-tuple-element.122, f32[16,512]{1,0:T(8,128)S(1)} %log_add_fusion, pred[512,1024]{1,0:T(8,128)(4,1)S(1)} %copy-done.5), kind=kOutput, calls=%fused_computation.17 | convolution fusion | flops 1098907648 | bytes 39354368 | tf_op jit(solution)/shard_map/while/body/eval_jaxpr/hqk,qhe->khe/dot_general | solution.py:108
  458.3 16.9 %add_bitcast_fusion = bf16[1,1024,1,16,64]{1,4,3,2,0:T(8,128)(2,1)} fusion(f32[16,64,1024]{2,1,0:T(8,128)} %fusion.4, bf16[512,16,64]{0,2,1:T(8,128)(2,1)S(1)} %bitcast.204, f32[16,512,1024]{2,1,0:T(8,128)} %get-tuple-element.124, f32[16,512]{1,0:T(8,128)S(1)} %copy-done.18, pred[512,1024]{1,0:T(8,128)(4,1)S(1)} %copy-done.3), kind=kOutput, calls=%fused_computation.94 | convolution fusion | flops 1101004800 | bytes 41451520 | tf_op jit(solution)/shard_map/while/body/eval_jaxpr/hqk,qhe->khe/dot_general | solution.py:108
  475.3 4.6 convert_reduce_fusion.1
  479.9 2.6 copy-done.15
  482.6 10.1 fusion.58
  493.4 51.4 %multiply_convert_fusion.2 = (bf16[1024,4096]{1,0:T(8,128)(2,1)}, f32[1024,4096]{1,0:T(8,128)}, f32[1024,4096]{1,0:T(8,128)}) fusion(f32[4096]{0:T(1024)S(1)} %bitcast.217, bf16[1024,4096]{1,0:T(8,128)(2,1)} %all-gather.10.cloned.1.call-done, bf16[1,1024,1024]{2,1,0:T(8,128)(2,1)S(1)} %copy-done.7, f32[1024]{0:T(1024)S(1)} %copy-done.41, ...), kind=kOutput, calls=%fused_computation.24 | convolution fusion | flops 8873050112 | bytes 52461568 | tf_op jit(solution)/shard_map/dot_general | solution.py:203
  544.8 24.6 %convert_reduce_fusion = (f32[4096]{0:T(1024)S(1)}, bf16[1024,4096]{1,0:T(8,128)(2,1)}) fusion(f32[1024,4096]{1,0:T(8,128)} %get-tuple-element.92, bf16[4096,1024]{1,0:T(8,128)(2,1)} %all-gather.12.cloned.1.call-done, bf16[1,1024,1024]{2,1,0:T(8,128)(2,1)} %param.17, f32[1024,4096]{1,0:T(8,128)} %get-tuple-element.125, f32[4096]{0:T(1024)S(1)} %bitcast.218), kind=kOutput, calls=%fused_computation.20 | convolution fusion | flops 8661233664 | bytes 52461568 | tf_op jit(solution)/shard_map/rd,fd->rf/dot_general | solution.py:222
  569.5 15.4 %fusion.98 = f32[1024,4096]{1,0:T(8,128)} fusion(bf16[1024,4096]{1,0:T(8,128)(2,1)} %get-tuple-element.132, bf16[1,1024,1024]{2,1,0:T(8,128)(2,1)S(1)} %copy-done.7, f32[1024]{0:T(1024)S(1)} %copy-done.41, f32[1024]{0:T(1024)S(1)} %copy-done.34, f32[1024]{0:T(1024)S(1)} %copy-done.33, f32[1024]{0:T(1024)S(1)} %copy-done.26), kind=kOutput, calls=%fused_computation.172 | convolution fusion | flops 8596226048 | bytes 27279360 | tf_op jit(solution)/shard_map/rd,rf->df/dot_general | solution.py:226
  585.0 16.9 %fusion.63 = f32[4096,1024]{1,0:T(8,128)} fusion(bf16[1024,4096]{1,0:T(8,128)(2,1)} %get-tuple-element.91, bf16[1,1024,1024]{2,1,0:T(8,128)(2,1)} %param.17), kind=kOutput, calls=%fused_computation.107 | convolution fusion | flops 8589934592 | bytes 27262976 | tf_op jit(solution)/shard_map/rf,rd->fd/dot_general | solution.py:221
  602.7 2.7 pad_maximum_fusion
  606.9 4.4 fusion.113
  611.4 12.8 fusion.114
  624.3 11.1 fusion.105
  635.4 3.9 fusion.41
  639.4 4.2 convert_reduce_fusion.3
  643.6 40.0 %all-reduce.20 = (f32[1024]{0:T(1024)S(1)}, f32[1024]{0:T(1024)S(1)}, f32[1024]{0:T(1024)S(1)}, f32[1024]{0:T(1024)S(1)}, f32[3072]{0:T(1024)S(1)}, /*index=5*/f32[1024]{0:T(1024)S(1)}, f32[4096]{0:T(1024)S(1)}) all-reduce(f32[1024]{0:T(1024)S(1)} %get-tuple-element.74, ...), channel_id=2, replica_groups=mesh['dp'=16,'fsdp'=2] {'dp','fsdp'}, use_global_device_ids=true, to_apply=%region_15.16.clone | all-reduce | flops 12288 | bytes 98304
  687.2 15.4 %fusion.60 = bf16[1,1024,1024]{2,1,0:T(8,128)(2,1)} fusion(f32[1024,1024]{1,0:T(8,128)} %fusion.113, bf16[1,1024,1024]{2,1,0:T(8,128)(2,1)S(1)} %copy-done.7, f32[1024]{0:T(1024)S(1)} %convert_element_type.187, f32[1024]{0:T(1024)S(1)} %convert_element_type.181, bf16[1024,4096]{1,0:T(8,128)(2,1)} %get-tuple-element.91, ...), kind=kOutput, calls=%fused_computation.104 | convolution fusion | flops 8596226048 | bytes 25174016 | tf_op jit(solution)/shard_map/dot_general | solution.py:207
  702.6 3.3 reduce-scatter.5.cloned.1.call-done
  705.9 360.0 %reduce-scatter.9.cloned.1.call-done = f32[32,4096]{1,0:T(8,128)} async-done(((f32[1024,4096]{1,0:T(8,128)}), f32[32,4096]{1,0:T(8,128)}) %reduce-scatter.9.cloned.1.call-update) | async-done | bytes 524304 | tf_op jit(solution)/shard_map/reduce_scatter | solution.py:263
  1065.9 361.5 %reduce-scatter.11.cloned.1.call-done = f32[128,1024]{1,0:T(8,128)} async-done(((f32[4096,1024]{1,0:T(8,128)}), f32[128,1024]{1,0:T(8,128)}) %reduce-scatter.11.cloned.1.call-update) | async-done | bytes 524304 | tf_op jit(solution)/shard_map/reduce_scatter | solution.py:265
  (200 shorter events, 31.2 us)
Async XLA Ops:
  7.2 122.4 %copy-start.23 = (s32[1,1024]{1,0:T(1,128)S(1)}, s32[1,1024]{1,0:T(1,128)}, u32[]{:S(2)}) copy-start(s32[1,1024]{1,0:T(1,128)} %param.16) | copy-start | bytes 12292
  7.2 55.5 %copy-start.6 = (bf16[1,1024,1024]{2,1,0:T(8,128)(2,1)S(1)}, bf16[1,1024,1024]{2,1,0:T(8,128)(2,1)}, u32[]{:S(2)}) copy-start(bf16[1,1024,1024]{2,1,0:T(8,128)(2,1)} %param.15) | copy-start | bytes 6291460
  7.2 58.2 %copy-start.44 = (bf16[128]{0:T(256)(128)(2,1)S(1)}, bf16[128]{0:T(256)(128)(2,1)}, u32[]{:S(2)}) copy-start(bf16[128]{0:T(256)(128)(2,1)} %param.27) | copy-start | bytes 772
  7.2 123.8 %all-gather.8.cloned.1.call-start = ((), (), s32[]{:S(2)}) async-start(), calls=%async_computation.5 | async-start | bytes 2162688 | tf_op jit(solution)/shard_map/all_gather | solution.py:150
  7.9 133.9 %all-gather.6.cloned.1.call-start = ((), (), s32[]{:S(2)}) async-start(), calls=%async_computation.4 | async-start | bytes 6488064 | tf_op jit(solution)/shard_map/all_gather | solution.py:148
  8.7 484.1 %all-gather.10.cloned.1.call-start = ((), (), s32[]{:S(2)}) async-start(), calls=%async_computation.6 | async-start | bytes 8650752 | tf_op jit(solution)/shard_map/all_gather | solution.py:152
  9.4 535.4 %all-gather.12.cloned.1.call-start = ((), (), s32[]{:S(2)}) async-start(), calls=%async_computation.7 | async-start | bytes 8650752 | tf_op jit(solution)/shard_map/all_gather | solution.py:154
  10.0 692.6 %reduce-scatter.7.cloned.1.call-start = ((), (), s32[]{:S(2)}) async-start(), calls=%async_computation.9 | async-start | bytes 4325376 | tf_op jit(solution)/shard_map/reduce_scatter | solution.py:261
  12.3 123.8 %copy-start.36 = (f32[1,1024]{1,0:T(1,128)}, f32[1,1024]{1,0:T(1,128)S(1)}, u32[]{:S(2)}) copy-start(f32[1,1024]{1,0:T(1,128)S(1)} %compare_convert_fusion) | copy-start | bytes 12292
  60.7 81.2 %copy-start.29 = (f32[1024]{0:T(1024)}, f32[1024]{0:T(1024)S(1)}, u32[]{:S(2)}) copy-start(f32[1024]{0:T(1024)S(1)} %convert_element_type.170) | copy-start | bytes 12292
  60.7 81.2 %copy-start.39 = (f32[1024]{0:T(1024)}, f32[1024]{0:T(1024)S(1)}, u32[]{:S(2)}) copy-start(f32[1024]{0:T(1024)S(1)} %convert_element_type.171) | copy-start | bytes 12292
  62.7 79.2 %copy-start.25 = (f32[1024]{0:T(1024)}, f32[1024]{0:T(1024)S(1)}, u32[]{:S(2)}) copy-start(f32[1024]{0:T(1024)S(1)} %broadcast_multiply_fusion) | copy-start | bytes 12292
  63.4 66.3 %copy-start.27 = (f32[1024]{0:T(1024)}, f32[1024]{0:T(1024)S(1)}, u32[]{:S(2)}) copy-start(f32[1024]{0:T(1024)S(1)} %fusion.42) | copy-start | bytes 12292
  63.4 78.5 %copy-start.32 = (f32[1024]{0:T(1024)}, f32[1024]{0:T(1024)S(1)}, u32[]{:S(2)}) copy-start(f32[1024]{0:T(1024)S(1)} %fusion.92) | copy-start | bytes 12292
  129.6 44.1 %copy-start.19 = (f32[1024,8]{0,1:T(8,128)}, f32[1024,8]{0,1:T(8,128)S(1)}, u32[]{:S(2)}) copy-start(f32[1024,8]{0,1:T(8,128)S(1)} %get-tuple-element.113) | copy-start | bytes 98308
  129.6 44.1 %copy-start.21 = (f32[1024,8]{0,1:T(8,128)}, f32[1024,8]{0,1:T(8,128)S(1)}, u32[]{:S(2)}) copy-start(f32[1024,8]{0,1:T(8,128)S(1)} %get-tuple-element.114) | copy-start | bytes 98308
  131.0 77.6 %copy-start.2 = (pred[512,1024]{1,0:T(8,128)(4,1)}, pred[512,1024]{1,0:T(8,128)(4,1)S(1)}, u32[]{:S(2)}) copy-start(pred[512,1024]{1,0:T(8,128)(4,1)S(1)} %get-tuple-element.117) | copy-start | bytes 1572868
  131.0 123.3 %copy-start.4 = (pred[512,1024]{1,0:T(8,128)(4,1)}, pred[512,1024]{1,0:T(8,128)(4,1)S(1)}, u32[]{:S(2)}) copy-start(pred[512,1024]{1,0:T(8,128)(4,1)S(1)} %get-tuple-element.118) | copy-start | bytes 1572868
  174.7 49.3 %copy-start.12 = (bf16[1024,16,8]{0,2,1:T(8,128)(2,1)}, bf16[1024,16,8]{0,2,1:T(8,128)(2,1)S(1)}, u32[]{:S(2)}) copy-start(bf16[1024,16,8]{0,2,1:T(8,128)(2,1)S(1)} %get-tuple-element.99) | copy-start | bytes 786436
  176.7 31.9 %slice-start = ((s8[12582912]{0:T(1024)(128)(4,1)}), s8[4194304]{0:T(1024)(128)(4,1)S(1)}, s32[]{:S(2)}) async-start(s8[12582912]{0:T(1024)(128)(4,1)} %bitcast.194), calls=%async_computation.12 | async-start | bytes 8388608
  176.7 31.9 %slice-start.1 = ((s8[12582912]{0:T(1024)(128)(4,1)}), s8[4194304]{0:T(1024)(128)(4,1)S(1)}, s32[]{:S(2)}) async-start(s8[12582912]{0:T(1024)(128)(4,1)} %bitcast.194), calls=%async_computation.13 | async-start | bytes 8388608
  192.7 15.9 %slice-start.2 = ((s8[12582912]{0:T(1024)(128)(4,1)}), s8[4194304]{0:T(1024)(128)(4,1)S(1)}, s32[]{:S(2)}) async-start(s8[12582912]{0:T(1024)(128)(4,1)} %bitcast.194), calls=%async_computation.14 | async-start | bytes 8388608
  224.0 30.4 %slice-start.3 = ((s8[12582912]{0:T(1024)(128)(4,1)}), s8[4194304]{0:T(1024)(128)(4,1)S(1)}, s32[]{:S(2)}) async-start(s8[12582912]{0:T(1024)(128)(4,1)} %bitcast.197), calls=%async_computation.15 | async-start | bytes 8388608
  224.0 30.4 %slice-start.4 = ((s8[12582912]{0:T(1024)(128)(4,1)}), s8[4194304]{0:T(1024)(128)(4,1)S(1)}, s32[]{:S(2)}) async-start(s8[12582912]{0:T(1024)(128)(4,1)} %bitcast.197), calls=%async_computation.16 | async-start | bytes 8388608
  239.3 15.1 %slice-start.5 = ((s8[12582912]{0:T(1024)(128)(4,1)}), s8[4194304]{0:T(1024)(128)(4,1)S(1)}, s32[]{:S(2)}) async-start(s8[12582912]{0:T(1024)(128)(4,1)} %bitcast.197), calls=%async_computation.17 | async-start | bytes 8388608
  254.4 15.1 %copy-start.16 = (bf16[1,1024,1024]{2,1,0:T(8,128)(2,1)S(1)}, bf16[1,1024,1024]{2,1,0:T(8,128)(2,1)}, u32[]{:S(2)}) copy-start(bf16[1,1024,1024]{2,1,0:T(8,128)(2,1)} %param.17) | copy-start | bytes 6291460
  254.4 15.1 %copy-start.37 = (f32[1,1024]{1,0:T(1,128)S(1)}, f32[1,1024]{1,0:T(1,128)}, u32[]{:S(2)}) copy-start(f32[1,1024]{1,0:T(1,128)} %copy-done.36) | copy-start | bytes 12292
  269.5 7.7 copy-start.18
  277.1 28.4 %slice-start.6 = ((s8[12582912]{0:T(1024)(128)(4,1)}), s8[4194304]{0:T(1024)(128)(4,1)S(1)}, s32[]{:S(2)}) async-start(s8[12582912]{0:T(1024)(128)(4,1)} %bitcast.200), calls=%async_computation.18 | async-start | bytes 8388608
  277.1 28.4 %slice-start.7 = ((s8[12582912]{0:T(1024)(128)(4,1)}), s8[4194304]{0:T(1024)(128)(4,1)S(1)}, s32[]{:S(2)}) async-start(s8[12582912]{0:T(1024)(128)(4,1)} %bitcast.200), calls=%async_computation.19 | async-start | bytes 8388608
  277.1 28.4 %slice-start.8 = ((s8[12582912]{0:T(1024)(128)(4,1)}), s8[4194304]{0:T(1024)(128)(4,1)S(1)}, s32[]{:S(2)}) async-start(s8[12582912]{0:T(1024)(128)(4,1)} %bitcast.200), calls=%async_computation.20 | async-start | bytes 8388608
  330.3 54.5 %copy-start = (bf16[1024,16,48]{0,2,1:T(8,128)(2,1)S(1)}, bf16[1024,16,48]{0,2,1:T(8,128)(2,1)}, u32[]{:S(2)}) copy-start(bf16[1024,16,48]{0,2,1:T(8,128)(2,1)} %fusion.84) | copy-start | bytes 4718596
  330.3 54.5 %copy-start.13 = (bf16[1024,16,8]{0,2,1:T(8,128)(2,1)S(1)}, bf16[1024,16,8]{0,2,1:T(8,128)(2,1)}, u32[]{:S(2)}) copy-start(bf16[1024,16,8]{0,2,1:T(8,128)(2,1)} %copy-done.12) | copy-start | bytes 786436
  330.3 54.5 %copy-start.14 = (bf16[1024,16,8]{0,2,1:T(8,128)(2,1)S(1)}, bf16[1024,16,8]{0,2,1:T(8,128)(2,1)}, u32[]{:S(2)}) copy-start(bf16[1024,16,8]{0,2,1:T(8,128)(2,1)} %get-tuple-element.100) | copy-start | bytes 786436
  408.2 297.6 %reduce-scatter.5.cloned.1.call-start = ((), (), s32[]{:S(2)}) async-start(), calls=%async_computation.8 | async-start | bytes 12976128 | tf_op jit(solution)/shard_map/reduce_scatter | solution.py:259
  441.9 16.4 %copy-start.3 = (pred[512,1024]{1,0:T(8,128)(4,1)S(1)}, pred[512,1024]{1,0:T(8,128)(4,1)}, u32[]{:S(2)}) copy-start(pred[512,1024]{1,0:T(8,128)(4,1)} %copy-done.2) | copy-start | bytes 1572868
  441.9 16.4 %copy-start.10 = (bf16[512,1024]{0,1:T(8,128)(2,1)S(1)}, bf16[512,1024]{0,1:T(8,128)(2,1)}, u32[]{:S(2)}) copy-start(bf16[512,1024]{0,1:T(8,128)(2,1)} %get-tuple-element.107) | copy-start | bytes 3145732
  475.3 7.3 copy-start.26
  475.3 7.3 copy-start.30
  475.3 7.3 copy-start.33
  475.3 7.3 copy-start.40
  492.7 573.2 %reduce-scatter.9.cloned.1.call-start = ((), (), s32[]{:S(2)}) async-start(), calls=%async_computation.10 | async-start | bytes 17301504 | tf_op jit(solution)/shard_map/reduce_scatter | solution.py:263
  584.9 842.5 %reduce-scatter.11.cloned.1.call-start = ((), (), s32[]{:S(2)}) async-start(), calls=%async_computation.11 | async-start | bytes 17301504 | tf_op jit(solution)/shard_map/reduce_scatter | solution.py:265
  606.9 17.3 %slice-start.10 = ((s8[6291456]{0:T(1024)(128)(4,1)}), s8[4194304]{0:T(1024)(128)(4,1)S(1)}, s32[]{:S(2)}) async-start(s8[6291456]{0:T(1024)(128)(4,1)} %bitcast.208), calls=%async_computation.22 | async-start | bytes 8388608
  611.4 12.9 slice-start.11
  611.4 12.9 copy-start.31
  624.3 11.1 copy-start.28
  683.7 743.7 %copy-start.46 = (f32[32]{0:T(128)}, f32[32]{0:T(128)S(1)}, u32[]{:S(2)}) copy-start(f32[32]{0:T(128)S(1)} %dynamic-slice.6) | copy-start | bytes 388
  (19 other events, 38.4 us)
Sparse Core Ops, SparseCore 0:
  11.1 59.3 all-gather.7
  73.5 68.3 all-gather.5
  145.0 75.8 all-gather.9
  223.9 76.0 all-gather.11
  408.4 137.4 reduce-scatter.6
  552.3 153.5 reduce-scatter.4
  708.8 357.0 reduce-scatter.8
  1068.9 358.4 reduce-scatter.10
where the time goes:
time: 1440 us
  waiting for transfers between devices  732 us (51%)
  matrix products  381 us (26%)
  blocking collectives  146 us (10%)
  other arithmetic  119 us (8%)
  local copies, waits for them, and re-layouts  41.8 us (3%)
  between operations  15.2 us (1%)
    reduce_scatter x1, waiting for transfers between devices, body(): lax.psum_scatter(grad_down, ('dp', 'fsdp'), scatter_dimension=0, tiled=True)  361 us
    reduce_scatter x1, waiting for transfers between devices, body(): lax.psum_scatter(grad_up, ('dp', 'fsdp'), scatter_dimension=0, tiled=True)  360 us
    unnamed x2, blocking collectives  82.5 us
    all_gather x1, blocking collectives, body(): lax.all_gather(up_bias, ('dp', 'fsdp'), axis=0, tiled=True)  63.3 us
    convert_element_type x1, other arithmetic, attend_backward(): d_scores = (probs * (d_probs - inner)).astype(jnp.bfloat16)  54.5 us
    dot_general x2, matrix products, attend_backward(): jnp.einsum('qhe,khe->hqk', d_out[block_start:block_end], values, preferre...  53.1 us
    dot_general x1, matrix products, body(): jnp.dot(normed_two, w_up, preferred_element_type=jnp.float32)  51.4 us
    dot_general x2, matrix products, attend_backward(): jnp.einsum('hqk,qhe->khe', probs.astype(jnp.bfloat16), d_out[block_start:...  33.3 us
  transfers between devices with their start and end apart: 8, of which 4 were waited for; matrix products, arithmetic and copies ran while one was open for 37% of the time, Pallas kernels for 0%

commit v1 on v0

--- a/solution.py
+++ b/solution.py
@@ -3,7 +3,11 @@
 import jax
 import jax.numpy as jnp
 from jax import lax
+from jax.experimental import pallas as pl
+from jax.experimental.pallas import tpu as pltpu
 from jax.sharding import PartitionSpec as P
+
+AXES = ("dp", "fsdp")
 
 HEADS = 16
 HEAD = 64
@@ -123,7 +127,128 @@
     return (jnp.concatenate(query_parts, axis=0), d_keys, d_values)
 
 
+class Grid:
+    def __init__(self, sizes):
+        dp, fsdp = sizes
+        self.total = dp * fsdp
+        self.low = fsdp.bit_length() - 1
+        self.bits = self.total.bit_length() - 1
+        self.core = self.low
+        self.x = self.low + 1
+        self.y = self.low - 1
+        stages = [(self.core, self.core), (self.x, self.y), (self.y, self.x)]
+        stages += [(b, b) for b in range(self.low - 2, -1, -1)]
+        stages += [(b, b) for b in range(self.x + 1, self.bits)]
+        self.stages = stages
+
+    def here(self):
+        return lax.axis_index("dp") * (1 << self.low) + lax.axis_index("fsdp")
+
+    def pairs(self, stage):
+        found = []
+        for device in range(self.total):
+            bit = stage[(device >> self.core) & 1]
+            found.append((device, device ^ (1 << bit)))
+        return found
+
+    def swap(self, value, stage):
+        return lax.ppermute(value, AXES, self.pairs(stage))
+
+    def plan(self, step):
+        here = self.here()
+        core = (here >> self.core) & 1
+        chosen = []
+        for which in (0, 1):
+            bit = self.stages[step][which]
+            gone = [s[which] for s in self.stages[:step]]
+            chosen.append((bit - sum(1 for g in gone if g < bit), (here >> bit) & 1))
+        place = jnp.where(core == 0, chosen[0][0], chosen[1][0])
+        value = jnp.where(core == 0, chosen[0][1], chosen[1][1])
+        return jnp.stack([place, value]).astype(jnp.int32)
+
+
+def insert_bit(index, place, value):
+    low = index & ((1 << place) - 1)
+    return ((index >> place) << (place + 1)) | (value << place) | low
+
+
+def split_kernel(plan, own_keep, own_send, keep, send):
+    keep[...] = own_keep[...]
+    send[...] = own_send[...]
+
+
+def join_kernel(plan, own_keep, own_send, come_keep, come_send, keep, send):
+    keep[...] = (own_keep[...].astype(jnp.float32) + come_keep[...].astype(jnp.float32)).astype(keep.dtype)
+    send[...] = (own_send[...].astype(jnp.float32) + come_send[...].astype(jnp.float32)).astype(send.dtype)
+
+
+def last_kernel(own, come, out):
+    out[...] = own[...].astype(jnp.float32) + come[...].astype(jnp.float32)
+
+
+def halves(plan, own, come):
+    blocks, rows, columns = own.shape
+    shape = jax.ShapeDtypeStruct((blocks // 2, rows, columns), own.dtype)
+    keep_map = lambda i, plan: (insert_bit(i, plan[0], plan[1]), 0, 0)
+    send_map = lambda i, plan: (insert_bit(i, plan[0], 1 - plan[1]), 0, 0)
+    block = (1, rows, columns)
+    taken = [own, own] if come is None else [own, own, come, come]
+    maps = [keep_map, send_map] * (len(taken) // 2)
+    cost = pl.CostEstimate(flops=own.size, transcendentals=0, bytes_accessed=len(taken) * own.size * 2)
+    return pl.pallas_call(
+        split_kernel if come is None else join_kernel,
+        grid_spec=pltpu.PrefetchScalarGridSpec(
+            num_scalar_prefetch=1,
+            grid=(blocks // 2,),
+            in_specs=[pl.BlockSpec(block, m) for m in maps],
+            out_specs=[pl.BlockSpec(block, lambda i, plan: (i, 0, 0))] * 2,
+        ),
+        out_shape=(shape, shape),
+        cost_estimate=cost,
+    )(plan, *taken)
+
+
+def scatter_sum(grid, value):
+    rows = value.shape[0] // grid.total
+    held = value.reshape(grid.total, rows, value.shape[1])
+    come = None
+    for step, stage in enumerate(grid.stages):
+        keep, send = halves(grid.plan(step), held, come)
+        come = grid.swap(send, stage)
+        held = keep
+    out = pl.pallas_call(
+        last_kernel,
+        out_shape=jax.ShapeDtypeStruct(held.shape, jnp.float32),
+        cost_estimate=pl.CostEstimate(flops=held.size, transcendentals=0, bytes_accessed=8 * held.size),
+    )(held, come)
+    return out.reshape(rows, value.shape[1])
+
+
+def gather_small(grid, value):
+    here = grid.here()
+    held = value[None]
+    for bit in range(grid.bits):
+        come = grid.swap(held, (bit, bit))
+        mine = (here >> bit) & 1
+        held = jnp.where(mine == 0, jnp.concatenate([held, come]), jnp.concatenate([come, held]))
+    return held
+
+
+def scatter_small(grid, value):
+    here = grid.here()
+    held = value
+    for bit in range(grid.bits - 1, -1, -1):
+        mine = (here >> bit) & 1
+        half = held.shape[0] // 2
+        upper = mine == 1
+        send = jnp.where(upper, held[:half], held[half:])
+        keep = jnp.where(upper, held[half:], held[:half])
+        held = keep + grid.swap(send, (bit, bit))
+    return held
+
+
 def body(
+    grid,
     hidden_in,
     segment_ids,
     out_grad,
@@ -140,34 +265,19 @@
     down_weight,
     down_bias,
 ):
-    gathered = (
-        lax.all_gather(norm1_gain, ("dp", "fsdp"), axis=0, tiled=True),
-        lax.all_gather(norm1_bias, ("dp", "fsdp"), axis=0, tiled=True),
-        lax.all_gather(norm2_gain, ("dp", "fsdp"), axis=0, tiled=True),
-        lax.all_gather(norm2_bias, ("dp", "fsdp"), axis=0, tiled=True),
-        lax.all_gather(qkv_weight, ("dp", "fsdp"), axis=0, tiled=True),
-        lax.all_gather(qkv_bias, ("dp", "fsdp"), axis=0, tiled=True),
-        lax.all_gather(proj_weight, ("dp", "fsdp"), axis=0, tiled=True),
-        lax.all_gather(proj_bias, ("dp", "fsdp"), axis=0, tiled=True),
-        lax.all_gather(up_weight, ("dp", "fsdp"), axis=0, tiled=True),
-        lax.all_gather(up_bias, ("dp", "fsdp"), axis=0, tiled=True),
-        lax.all_gather(down_weight, ("dp", "fsdp"), axis=0, tiled=True),
-        lax.all_gather(down_bias, ("dp", "fsdp"), axis=0, tiled=True),
-    )
-    (
-        gain_one,
-        shift_one,
-        gain_two,
-        shift_two,
-        w_qkv,
-        b_qkv,
-        w_proj,
-        b_proj,
-        w_up,
-        b_up,
-        w_down,
-        b_down,
-    ) = gathered
+    small = (norm1_gain, norm1_bias, norm2_gain, norm2_bias, qkv_bias, proj_bias, up_bias, down_bias)
+    widths = [entry.shape[0] for entry in small]
+    packed = jnp.concatenate(small)
+    packed = jnp.pad(packed, (0, -packed.shape[0] % 128))
+    spread = gather_small(grid, packed)
+    pieces, at = [], 0
+    for width in widths:
+        pieces.append(spread[:, at : at + width].reshape(-1))
+        at += width
+    gain_one, shift_one, gain_two, shift_two, b_qkv, b_proj, b_up, b_down = pieces
+    w_qkv, w_proj, w_up, w_down = (
+        lax.all_gather(entry, AXES, axis=0, tiled=True) for entry in (qkv_weight, proj_weight, up_weight, down_weight)
+    )
     seq_count, length, model_width = hidden_in.shape
     row_count = seq_count * length
     scale = HEAD ** (-0.5)
@@ -209,12 +319,7 @@
         (flat + projected + branch).astype(jnp.bfloat16).reshape(seq_count, length, model_width)
     )
     back_gain_one, back_gain_two, back_qkv, back_proj, back_up, back_down = (
-        lax.all_gather(norm1_gain, ("dp", "fsdp"), axis=0, tiled=True),
-        lax.all_gather(norm2_gain, ("dp", "fsdp"), axis=0, tiled=True),
-        lax.all_gather(qkv_weight, ("dp", "fsdp"), axis=0, tiled=True),
-        lax.all_gather(proj_weight, ("dp", "fsdp"), axis=0, tiled=True),
-        lax.all_gather(up_weight, ("dp", "fsdp"), axis=0, tiled=True),
-        lax.all_gather(down_weight, ("dp", "fsdp"), axis=0, tiled=True),
+        gain_one, gain_two, w_qkv, w_proj, w_up, w_down
     )
     grad_wide = grad_rows.astype(jnp.float32)
     bias_grad = jnp.sum(grad_wide, axis=0)
@@ -251,35 +356,32 @@
     input_grad = (
         (grad_wide + dx_one + dx_two).astype(jnp.bfloat16).reshape(seq_count, length, model_width)
     )
-    shards = (
-        lax.psum_scatter(grad_gain_one, ("dp", "fsdp"), scatter_dimension=0, tiled=True),
-        lax.psum_scatter(grad_shift_one, ("dp", "fsdp"), scatter_dimension=0, tiled=True),
-        lax.psum_scatter(grad_gain_two, ("dp", "fsdp"), scatter_dimension=0, tiled=True),
-        lax.psum_scatter(grad_shift_two, ("dp", "fsdp"), scatter_dimension=0, tiled=True),
-        lax.psum_scatter(grad_qkv, ("dp", "fsdp"), scatter_dimension=0, tiled=True),
-        lax.psum_scatter(grad_qkv_bias, ("dp", "fsdp"), scatter_dimension=0, tiled=True),
-        lax.psum_scatter(grad_proj, ("dp", "fsdp"), scatter_dimension=0, tiled=True),
-        lax.psum_scatter(bias_grad, ("dp", "fsdp"), scatter_dimension=0, tiled=True),
-        lax.psum_scatter(grad_up, ("dp", "fsdp"), scatter_dimension=0, tiled=True),
-        lax.psum_scatter(grad_up_bias, ("dp", "fsdp"), scatter_dimension=0, tiled=True),
-        lax.psum_scatter(grad_down, ("dp", "fsdp"), scatter_dimension=0, tiled=True),
-        lax.psum_scatter(bias_grad, ("dp", "fsdp"), scatter_dimension=0, tiled=True),
-    )
+    n = grid.total
+    sums = (grad_gain_one, grad_shift_one, grad_gain_two, grad_shift_two, grad_qkv_bias, bias_grad, grad_up_bias)
+    vectors = jnp.concatenate([entry.reshape(n, -1) for entry in sums], axis=1)
+    vectors = jnp.pad(vectors, ((0, 0), (0, -vectors.shape[1] % 128)))
+    total = scatter_small(grid, vectors)
+    outs, at = [], 0
+    for entry in sums:
+        width = entry.shape[0] // n
+        outs.append(total[0, at : at + width])
+        at += width
+    low = [scatter_sum(grid, entry.astype(jnp.bfloat16)) for entry in (grad_qkv, grad_proj, grad_up, grad_down)]
     return (
         layer_out,
         input_grad,
-        shards[0],
-        shards[1],
-        shards[2],
-        shards[3],
-        shards[4],
-        shards[5],
-        shards[6],
-        shards[7],
-        shards[8],
-        shards[9],
-        shards[10],
-        shards[11],
+        outs[0],
+        outs[1],
+        outs[2],
+        outs[3],
+        low[0],
+        outs[4],
+        low[1],
+        outs[5],
+        low[2],
+        outs[6],
+        low[3],
+        outs[5],
     )
 
 
@@ -317,4 +419,5 @@
         P(("dp", "fsdp"), None),
         P(("dp", "fsdp")),
     )
-    return jax.shard_map(body, mesh=mesh, in_specs=in_specs, out_specs=out_specs, check_vma=False)
+    grid = Grid((mesh.shape["dp"], mesh.shape["fsdp"]))
+    return jax.shard_map(partial(body, grid), mesh=mesh, in_specs=in_specs, out_specs=out_specs, check_vma=False)

time: 1440 us -> 890 us (0.62)
  waiting for transfers between devices: 732 us -> 128 us
  blocking collectives: 146 us -> 0 us
  Pallas kernels: 0 us -> 125 us
  starting transfers between devices: 0.53 us -> 51.1 us
    reduce_scatter x4 -> x0, waiting for transfers between devices: 725 us -> none  [the longest x1 361 us: body(): lax.psum_scatter(grad_down, ('dp', 'fsdp'), scatter_dimension=0, tiled=True)]
    pallas_call x0 -> x24, Pallas kernels: none -> 125 us  [the longest x20 118 us: halves(): pl.pallas_call(split_kernel if come is None else join_kernel, grid_spec=p...]
    all_gather x4, waiting for transfers between devices: 4.33 us -> 96.4 us  [body(): lax.all_gather(entry, AXES, axis=0, tiled=True)]
    unnamed x2 -> x0, blocking collectives: 82.5 us -> none
    all_gather x1 -> x0, blocking collectives: 63.3 us -> none  [body(): lax.all_gather(up_bias, ('dp', 'fsdp'), axis=0, tiled=True)]
    ppermute x0 -> x30, starting transfers between devices: none -> 50.9 us  [swap(): return lax.ppermute(value, AXES, self.pairs(stage))]
    ppermute x0 -> x30, waiting for transfers between devices: none -> 29.5 us  [swap(): return lax.ppermute(value, AXES, self.pairs(stage))]
  transfers between devices with their start and end apart: 8 -> 34, of which waited for: 4 -> 9; matrix products, arithmetic and copies ran while one was open for 37% -> 62% of each run, Pallas kernels for 0% -> 14%
where the time goes in v1:
time: 890 us; the launch traced here: 875 us
  matrix products  378 us (42%)
  other arithmetic  132 us (15%)
  waiting for transfers between devices  128 us (14%)
  Pallas kernels  125 us (14%)
  starting transfers between devices  51.1 us (6%)
  local copies, waits for them, and re-layouts  46.2 us (5%)
  between operations  14.7 us (2%)
    pallas_call x20, Pallas kernels, halves(): pl.pallas_call(split_kernel if come is None else join_kernel, grid_spec=p...  118 us
    all_gather x4, waiting for transfers between devices, body(): lax.all_gather(entry, AXES, axis=0, tiled=True)  96.4 us
    convert_element_type x1, other arithmetic, attend_backward(): d_scores = (probs * (d_probs - inner)).astype(jnp.bfloat16)  54.5 us
    dot_general x1, matrix products, body(): jnp.dot(normed_two, w_up, preferred_element_type=jnp.float32)  51.3 us
    ppermute x30, starting transfers between devices, swap(): return lax.ppermute(value, AXES, self.pairs(stage))  50.9 us
    dot_general x2, matrix products, attend_backward(): jnp.einsum('qhe,khe->hqk', d_out[block_start:block_end], values, preferre...  50.2 us
    dot_general x2, matrix products, attend_backward(): jnp.einsum('hqk,qhe->khe', probs.astype(jnp.bfloat16), d_out[block_start:...  33.8 us
    dot_general x2, matrix products, attend_forward(): jnp.einsum('qhe,khe->hqk', query[block_start:block_start + block_rows], k...  31.5 us
  transfers between devices with their start and end apart: 34, of which 9 were waited for; matrix products, arithmetic and copies ran while one was open for 62% of the time, Pallas kernels for 14%

profile of v1, /device:TPU:1, one launch (start us, length us, event | category | flops | bytes accessed | tf_op | source)
XLA Modules:
  0.0 874.7 jit_solution(16316645765857548894)
XLA Ops:
  9.5 5.4 concatenate.104
  39.0 31.2 %all-gather.7.cloned.1.call-done = bf16[1024,1024]{1,0:T(8,128)(2,1)} async-done(((bf16[32,1024]{1,0:T(8,128)(2,1)}), bf16[1024,1024]{1,0:T(8,128)(2,1)}) %all-gather.7.cloned.1.call-update) | async-done | bytes 2097168 | tf_op jit(solution)/shard_map/all_gather | solution.py:279
  70.2 4.6 multiply_convert_fusion.3
  76.4 65.1 %all-gather.5.cloned.1.call-done = bf16[1024,3072]{1,0:T(8,128)(2,1)} async-done(((bf16[32,3072]{1,0:T(8,128)(2,1)}), bf16[1024,3072]{1,0:T(8,128)(2,1)}) %all-gather.5.cloned.1.call-update) | async-done | bytes 6291472 | tf_op jit(solution)/shard_map/all_gather | solution.py:279
  141.5 13.1 %broadcast_add_fusion = f32[1024,3072]{1,0:T(8,128)} fusion(f32[3072]{0:T(1024)S(1)} %reshape.703, bf16[1024,3072]{1,0:T(8,128)(2,1)} %all-gather.5.cloned.1.call-done, bf16[1,1024,1024]{2,1,0:T(8,128)(2,1)} %param.15, f32[1024]{0:T(1024)S(1)} %reshape.702, f32[1024]{0:T(1024)S(1)} %reshape.701, f32[1024]{0:T(1024)S(1)} %fusion.96, ...), kind=kOutput, calls=%fused_computation.50 | convolution fusion | flops 6451888128 | bytes 21000192 | tf_op jit(solution)/shard_map/dot_general | solution.py:291
  154.6 12.7 %copy.32 = f32[1024,3072]{0,1:T(8,128)} copy(f32[1024,3072]{1,0:T(8,128)} %broadcast_add_fusion) | data formatting | bytes 25165824 | tf_op jit(solution)/shard_map/add | solution.py:291
  167.3 4.5 slice_bitcast_fusion
  175.8 15.6 %select_reduce_fusion = (f32[16,512]{1,0:T(8,128)S(1)}, f32[16,512,1024]{2,1,0:T(8,128)}) fusion(pred[512,1024]{1,0:T(8,128)(4,1)S(1)} %get-tuple-element.190, bf16[1024,16,48]{0,2,1:T(8,128)(2,1)} %fusion.87, bf16[1024,16,8]{0,2,1:T(8,128)(2,1)S(1)} %get-tuple-element.166, bf16[1024,16,8]{0,2,1:T(8,128)(2,1)S(1)} %get-tuple-element.165, ...), kind=kOutput, calls=%fused_computation.12 | convolution fusion | flops 1096802304 | bytes 37257216 | tf_op jit(solution)/shard_map/while/body/eval_jaxpr/qhe,khe->hqk/dot_general | solution.py:74
  191.4 15.7 %fusion.1 = f32[16,512]{1,0:T(8,128)S(1)} fusion(f32[16,512,1024]{2,1,0:T(8,128)} %get-tuple-element.199, f32[16,512]{1,0:T(8,128)S(1)} %get-tuple-element.198, pred[512,1024]{1,0:T(8,128)(4,1)S(1)} %get-tuple-element.190), kind=kLoop, calls=%fused_computation.11 | loop fusion | flops 25157632 | bytes 34144256 | tf_op jit(solution)/shard_map/while/body/eval_jaxpr/reduce_sum | solution.py:83
  207.1 15.5 %fusion.21 = f32[16,64,512]{2,1,0:T(8,128)} fusion(f32[16,512,1024]{2,1,0:T(8,128)} %get-tuple-element.199, f32[16,512]{1,0:T(8,128)S(1)} %fusion.1, f32[16,512]{1,0:T(8,128)S(1)} %get-tuple-element.198, pred[512,1024]{1,0:T(8,128)(4,1)S(1)} %get-tuple-element.190, f32[1,1024,3,16,64]{1,4,3,2,0:T(8,128)S(1)} %bitcast.230), kind=kOutput, calls=%fused_computation.43 | convolution fusion | flops 1107296256 | bytes 38338560 | tf_op jit(solution)/shard_map/while/body/eval_jaxpr/hqk,khe->qhe/dot_general | solution.py:86
  222.6 17.0 %fusion.4 = f32[16,64,1024]{2,1,0:T(8,128)} fusion(bf16[512,16,64]{0,2,1:T(8,128)(2,1)} %bitcast.243, f32[16,512,1024]{2,1,0:T(8,128)} %get-tuple-element.199, f32[16,512]{1,0:T(8,128)S(1)} %log_add_fusion, pred[512,1024]{1,0:T(8,128)(4,1)S(1)} %get-tuple-element.190), kind=kOutput, calls=%fused_computation.17 | convolution fusion | flops 1098907648 | bytes 39354368 | tf_op jit(solution)/shard_map/while/body/eval_jaxpr/hqk,qhe->khe/dot_general | solution.py:112
  239.6 25.6 %multiply_reduce_fusion = (f32[16,512]{1,0:T(8,128)S(1)}, f32[16,512,1024]{2,1,0:T(8,128)}) fusion(f32[16,512,1024]{2,1,0:T(8,128)} %get-tuple-element.199, f32[16,512]{1,0:T(8,128)S(1)} %log_add_fusion, pred[512,1024]{1,0:T(8,128)(4,1)S(1)} %get-tuple-element.190, bf16[512,16,64]{0,2,1:T(8,128)(2,1)S(1)} %bitcast.244, f32[1,1024,3,16,64]{1,4,3,2,0:T(8,128)} %bitcast.227), kind=kOutput, calls=%fused_computation.1 | convolution fusion | flops 1107288064 | bytes 70844416 | tf_op jit(solution)/shard_map/while/body/eval_jaxpr/qhe,khe->hqk/dot_general | solution.py:107
  265.2 15.9 %select_reduce_fusion.1 = (f32[16,512]{1,0:T(8,128)S(1)}, f32[16,512,1024]{2,1,0:T(8,128)}) fusion(pred[512,1024]{1,0:T(8,128)(4,1)S(1)} %copy-done.1, bf16[1024,16,48]{0,2,1:T(8,128)(2,1)} %fusion.87, bf16[1024,16,8]{0,2,1:T(8,128)(2,1)S(1)} %copy-done.18, bf16[1024,16,8]{0,2,1:T(8,128)(2,1)S(1)} %get-tuple-element.165, bf16[1,1024,16,64]{1,3,2,0:T(8,128)(2,1)} %fusion.51), kind=kOutput, calls=%fused_computation.13 | convolution fusion | flops 1096802304 | bytes 37257216 | tf_op jit(solution)/shard_map/while/body/eval_jaxpr/qhe,khe->hqk/dot_general | solution.py:74
  281.1 15.5 %fusion = f32[16,512]{1,0:T(8,128)S(1)} fusion(f32[16,512,1024]{2,1,0:T(8,128)} %get-tuple-element.201, f32[16,512]{1,0:T(8,128)S(1)} %get-tuple-element.200, pred[512,1024]{1,0:T(8,128)(4,1)} %get-tuple-element.189), kind=kLoop, calls=%fused_computation.10 | loop fusion | flops 25157632 | bytes 34144256 | tf_op jit(solution)/shard_map/while/body/eval_jaxpr/reduce_sum | solution.py:83
  296.7 14.9 %fusion.20 = f32[16,64,512]{2,1,0:T(8,128)} fusion(f32[16,512,1024]{2,1,0:T(8,128)} %get-tuple-element.201, f32[16,512]{1,0:T(8,128)S(1)} %fusion, f32[16,512]{1,0:T(8,128)S(1)} %get-tuple-element.200, pred[512,1024]{1,0:T(8,128)(4,1)S(1)} %copy-done.2, f32[1,1024,3,16,64]{1,4,3,2,0:T(8,128)S(1)} %bitcast.233), kind=kOutput, calls=%fused_computation.42 | convolution fusion | flops 1107296256 | bytes 38338560 | tf_op jit(solution)/shard_map/while/body/eval_jaxpr/hqk,khe->qhe/dot_general | solution.py:86
  311.5 24.7 %multiply_reduce_fusion.1 = (f32[16,512]{1,0:T(8,128)S(1)}, f32[16,512,1024]{2,1,0:T(8,128)}) fusion(f32[16,512,1024]{2,1,0:T(8,128)} %get-tuple-element.201, f32[16,512]{1,0:T(8,128)S(1)} %log_add_fusion.1, pred[512,1024]{1,0:T(8,128)(4,1)} %get-tuple-element.189, bf16[512,16,64]{0,2,1:T(8,128)(2,1)} %bitcast.241, f32[1,1024,3,16,64]{1,4,3,2,0:T(8,128)S(1)} %bitcast.234), kind=kOutput, calls=%fused_computation.4 | convolution fusion | flops 1107288064 | bytes 70844416 | tf_op jit(solution)/shard_map/while/body/eval_jaxpr/qhe,khe->hqk/dot_general | solution.py:107
  336.2 54.5 %multiply_convert_fusion = (bf16[16,512,1024]{2,1,0:T(8,128)(2,1)}, bf16[16,512,1024]{2,1,0:T(8,128)(2,1)}) fusion(f32[16,512,1024]{2,1,0:T(8,128)} %get-tuple-element.204, f32[16,512,1024]{2,1,0:T(8,128)} %get-tuple-element.199, f32[16,512]{1,0:T(8,128)S(1)} %get-tuple-element.203, f32[16,512]{1,0:T(8,128)S(1)} %log_add_fusion, ...), kind=kLoop, calls=%fused_computation | loop fusion | flops 83886080 | bytes 168951808 | tf_op jit(solution)/shard_map/while/body/eval_jaxpr/convert_element_type | solution.py:111
  390.8 12.3 %convolution_bitcast_fusion.1 = f32[1,512,16,64]{1,3,2,0:T(8,128)} fusion(bf16[16,512,1024]{2,1,0:T(8,128)(2,1)} %get-tuple-element.211, bf16[1024,16,48]{0,2,1:T(8,128)(2,1)S(1)} %copy-done, bf16[1024,16,8]{0,2,1:T(8,128)(2,1)S(1)} %copy-done.19, bf16[1024,16,8]{0,2,1:T(8,128)(2,1)S(1)} %copy-done.16), kind=kOutput, calls=%fused_computation.129 | convolution fusion | flops 1080033280 | bytes 20971520 | tf_op jit(solution)/shard_map/while/body/eval_jaxpr/hqk,khe->qhe/dot_general | solution.py:119
  403.0 11.1 %fusion.88 = f32[16,64,1024]{2,1,0:T(8,128)} fusion(bf16[16,512,1024]{2,1,0:T(8,128)(2,1)} %get-tuple-element.211, bf16[1,1024,16,64]{1,3,2,0:T(8,128)(2,1)} %fusion.51), kind=kOutput, calls=%fused_computation.133 | convolution fusion | flops 1073741824 | bytes 22020096 | tf_op jit(solution)/shard_map/while/body/eval_jaxpr/hqk,qhe->khe/dot_general | solution.py:121
  414.1 12.3 %convolution_bitcast_fusion = f32[1,512,16,64]{1,3,2,0:T(8,128)} fusion(bf16[16,512,1024]{2,1,0:T(8,128)(2,1)} %get-tuple-element.210, bf16[1024,16,48]{0,2,1:T(8,128)(2,1)S(1)} %copy-done, bf16[1024,16,8]{0,2,1:T(8,128)(2,1)S(1)} %copy-done.19, bf16[1024,16,8]{0,2,1:T(8,128)(2,1)S(1)} %copy-done.16), kind=kOutput, calls=%fused_computation.128 | convolution fusion | flops 1080033280 | bytes 20971520 | tf_op jit(solution)/shard_map/while/body/eval_jaxpr/hqk,khe->qhe/dot_general | solution.py:119
  426.4 10.5 %add_bitcast_fusion.2 = f32[1,1024,16,64]{1,3,2,0:T(8,128)S(1)} fusion(f32[16,64,1024]{2,1,0:T(8,128)} %fusion.88, bf16[16,512,1024]{2,1,0:T(8,128)(2,1)} %get-tuple-element.210, bf16[1,1024,16,64]{1,3,2,0:T(8,128)(2,1)} %fusion.51), kind=kOutput, calls=%fused_computation.99 | convolution fusion | flops 1074790400 | bytes 26214400 | tf_op jit(solution)/shard_map/while/body/eval_jaxpr/hqk,qhe->khe/dot_general | solution.py:121
  450.0 10.2 %shard_map.263 = (bf16[16,32,1024]{2,1,0:T(8,128)(2,1)}, bf16[16,32,1024]{2,1,0:T(8,128)(2,1)}) custom-call(s32[2]{0:T(128)} %pad_add_fusion.4.plan, bf16[32,32,1024]{2,1,0:T(8,128)(2,1)} %bitcast.245, bf16[32,32,1024]{2,1,0:T(8,128)(2,1)} %bitcast.246), custom_call_target="tpu_custom_call" | custom-call | flops 1048576 | bytes 4194304 | tf_op jit(solution)/shard_map/pallas_call | solution.py:198
  465.4 16.8 %add_bitcast_fusion = bf16[1,1024,1,16,64]{1,4,3,2,0:T(8,128)(2,1)} fusion(f32[16,64,1024]{2,1,0:T(8,128)} %fusion.4, bf16[512,16,64]{0,2,1:T(8,128)(2,1)S(1)} %bitcast.242, f32[16,512,1024]{2,1,0:T(8,128)} %get-tuple-element.201, f32[16,512]{1,0:T(8,128)S(1)} %log_add_fusion.1, pred[512,1024]{1,0:T(8,128)(4,1)S(1)} %copy-done.3), kind=kOutput, calls=%fused_computation.97 | convolution fusion | flops 1101004800 | bytes 41451520 | tf_op jit(solution)/shard_map/while/body/eval_jaxpr/hqk,qhe->khe/dot_general | solution.py:112
  482.2 6.3 convert_reduce_fusion.1
  489.2 12.1 %convolution_convert_fusion.2 = bf16[1024,3072]{1,0:T(8,128)(2,1)} fusion(bf16[1024,3072]{0,1:T(8,128)(2,1)} %bitcast.247, bf16[1,1024,1024]{2,1,0:T(8,128)(2,1)S(1)} %copy-done.6, f32[1024]{0:T(1024)S(1)} %copy-done.59, f32[1024]{0:T(1024)S(1)} %copy-done.49, f32[1024]{0:T(1024)S(1)} %copy-done.52, f32[1024]{0:T(1024)S(1)} %copy-done.44), kind=kOutput, calls=%fused_computation.54 | convolution fusion | flops 6451888128 | bytes 14696448 | tf_op jit(solution)/shard_map/rd,rc->dc/dot_general | solution.py:351
  501.3 11.9 %shard_map.257 = (bf16[16,32,3072]{2,1,0:T(8,128)(2,1)}, bf16[16,32,3072]{2,1,0:T(8,128)(2,1)}) custom-call(s32[2]{0:T(128)} %pad_add_fusion.4.plan, bf16[32,32,3072]{2,1,0:T(8,128)(2,1)} %bitcast.239, bf16[32,32,3072]{2,1,0:T(8,128)(2,1)} %bitcast.240), custom_call_target="tpu_custom_call" | custom-call | flops 3145728 | bytes 12582912 | tf_op jit(solution)/shard_map/pallas_call | solution.py:198
  513.3 6.0 shard_map.264
  521.0 51.3 %multiply_convert_fusion.2 = (bf16[1024,4096]{1,0:T(8,128)(2,1)}, f32[1024,4096]{1,0:T(8,128)}, f32[1024,4096]{1,0:T(8,128)}) fusion(f32[4096]{0:T(1024)S(1)} %copy-done.53, bf16[1024,4096]{1,0:T(8,128)(2,1)} %all-gather.9.cloned.1.call-done, bf16[1,1024,1024]{2,1,0:T(8,128)(2,1)S(1)} %copy-done.6, f32[1024]{0:T(1024)S(1)} %copy-done.57, ...), kind=kOutput, calls=%fused_computation.24 | convolution fusion | flops 8873050112 | bytes 52461568 | tf_op jit(solution)/shard_map/dot_general | solution.py:313
  572.3 24.0 %convert_reduce_fusion = (f32[4096]{0:T(1024)S(1)}, bf16[1024,4096]{1,0:T(8,128)(2,1)}) fusion(f32[1024,4096]{1,0:T(8,128)} %get-tuple-element.158, bf16[4096,1024]{1,0:T(8,128)(2,1)} %all-gather.11.cloned.1.call-done, bf16[1,1024,1024]{2,1,0:T(8,128)(2,1)} %param.17, f32[1024,4096]{1,0:T(8,128)} %get-tuple-element.202, f32[4096]{0:T(1024)S(1)} %copy-done.53), kind=kOutput, calls=%fused_computation.20 | convolution fusion | flops 8661233664 | bytes 52461568 | tf_op jit(solution)/shard_map/rd,fd->rf/dot_general | solution.py:327
  596.3 15.0 %convolution_convert_fusion.1 = bf16[1024,4096]{1,0:T(8,128)(2,1)} fusion(bf16[1024,4096]{1,0:T(8,128)(2,1)} %get-tuple-element.209, bf16[1,1024,1024]{2,1,0:T(8,128)(2,1)S(1)} %copy-done.6, f32[1024]{0:T(1024)S(1)} %copy-done.57, f32[1024]{0:T(1024)S(1)} %copy-done.47, f32[1024]{0:T(1024)S(1)} %copy-done.52, f32[1024]{0:T(1024)S(1)} %copy-done.44), kind=kOutput, calls=%fused_computation.47 | convolution fusion | flops 8600420352 | bytes 18890752 | tf_op jit(solution)/shard_map/rd,rf->df/dot_general | solution.py:331
  611.3 12.5 %shard_map.269 = (bf16[16,32,4096]{2,1,0:T(8,128)(2,1)}, bf16[16,32,4096]{2,1,0:T(8,128)(2,1)}) custom-call(s32[2]{0:T(128)} %pad_add_fusion.4.plan, bf16[32,32,4096]{2,1,0:T(8,128)(2,1)} %bitcast.235, bf16[32,32,4096]{2,1,0:T(8,128)(2,1)} %bitcast.236), custom_call_target="tpu_custom_call" | custom-call | flops 4194304 | bytes 16777216 | tf_op jit(solution)/shard_map/pallas_call | solution.py:198
  623.8 15.2 %convolution_convert_fusion = bf16[4096,1024]{1,0:T(8,128)(2,1)} fusion(bf16[1024,4096]{1,0:T(8,128)(2,1)} %get-tuple-element.157, bf16[1,1024,1024]{2,1,0:T(8,128)(2,1)} %param.17), kind=kOutput, calls=%fused_computation.46 | convolution fusion | flops 8594128896 | bytes 18874368 | tf_op jit(solution)/shard_map/rf,rd->fd/dot_general | solution.py:326
  639.0 12.5 %shard_map.275 = (bf16[16,128,1024]{2,1,0:T(8,128)(2,1)}, bf16[16,128,1024]{2,1,0:T(8,128)(2,1)}) custom-call(s32[2]{0:T(128)} %pad_add_fusion.4.plan, bf16[32,128,1024]{2,1,0:T(8,128)(2,1)} %bitcast.237, bf16[32,128,1024]{2,1,0:T(8,128)(2,1)} %bitcast.238), custom_call_target="tpu_custom_call" | custom-call | flops 4194304 | bytes 16777216 | tf_op jit(solution)/shard_map/pallas_call | solution.py:198
  652.2 12.8 %fusion.118 = f32[1024,1024]{1,0:T(8,128)S(1)} fusion(bf16[1024,4096]{1,0:T(8,128)(2,1)} %get-tuple-element.209, bf16[1024,4096]{1,0:T(8,128)(2,1)} %all-gather.9.cloned.1.call-done), kind=kOutput, calls=%fused_computation.219 | convolution fusion | flops 8589934592 | bytes 20971520 | tf_op jit(solution)/shard_map/rf,df->rd/dot_general | solution.py:332
  665.1 12.2 %fusion.109 = (f32[1024]{0:T(1024)S(1)}, f32[1024]{0:T(1024)S(1)}, f32[1024]{0:T(1024)S(1)}, f32[1024]{0:T(1024)S(1)}, f32[1024,1024]{1,0:T(8,128)S(1)}) fusion(f32[1024]{0:T(1024)S(1)} %copy-done.50, f32[1024]{0:T(1024)S(1)} %copy-done.44, bf16[1,1024,1024]{2,1,0:T(8,128)(2,1)S(1)} %copy-done.6, f32[1024,1024]{1,0:T(8,128)S(1)} %fusion.118, ...), kind=kOutput, calls=%fused_computation.215 | convolution fusion | flops 6452932608 | bytes 23097344 | tf_op jit(solution)/shard_map/rc,dc->rd/dot_general | solution.py:352
  681.3 8.2 shard_map.276
  689.8 8.2 shard_map.270
  699.3 6.6 convert_reduce_fusion.3
  712.9 4.8 pad_maximum_fusion
  724.3 7.5 shard_map.258
  733.4 4.1 fusion.53
  742.7 4.9 shard_map.277
  747.9 5.3 shard_map.271
  754.5 23.9 %collective-permute-start.8 = (f32[2,384]{1,0:T(2,128)S(1)}, f32[2,384]{1,0:T(2,128)S(1)}, u32[]{:S(2)}, u32[]{:S(2)}) collective-permute-start(f32[2,384]{1,0:T(2,128)S(1)} %broadcast_select_fusion.1), channel_id=1, source_target_pairs={{0,2},{1,3},{2,0},{3,1},{4,6},{5,7},{6,4},{7,5},{8,10},{9,11},{10,... | collective-permute-start | bytes 9224 | tf_op jit(solution)/shard_map/ppermute | solution.py:155
  778.4 6.6 fusion.117
  787.4 4.7 shard_map.259
  802.8 15.4 %fusion.59 = bf16[1,1024,1024]{2,1,0:T(8,128)(2,1)} fusion(f32[1024,1024]{1,0:T(8,128)} %fusion.117, bf16[1,1024,1024]{2,1,0:T(8,128)(2,1)S(1)} %copy-done.6, f32[1024]{0:T(1024)S(1)} %reshape.709, f32[1024]{0:T(1024)S(1)} %reshape.705, bf16[1024,4096]{1,0:T(8,128)(2,1)} %get-tuple-element.157, bf16[4096,1024]{1,0:T(8,128)(2,1)} %all-gather.11.cloned.1.call-done), kind=kOutput, calls=%fused_computation.106 | convolution fusion | flops 8596226048 | bytes 25174016 | tf_op jit(solution)/shard_map/dot_general | solution.py:317
  838.4 21.5 %collective-permute-done.14.come = bf16[1,32,3072]{2,1,0:T(8,128)(2,1)S(1)} collective-permute-done((bf16[1,32,3072]{2,1,0:T(8,128)(2,1)}, bf16[1,32,3072]{2,1,0:T(8,128)(2,1)S(1)}, u32[]{:S(2)}, u32[]{:S(2)}) %collective-permute-start.14) | collective-permute-done | bytes 196640 | tf_op jit(solution)/shard_map/ppermute | solution.py:155
  (304 shorter events, 122.0 us)
Async XLA Ops:
  7.2 63.0 %all-gather.7.cloned.1.call-start = ((), (), s32[]{:S(2)}) async-start(), calls=%async_computation.1 | async-start | bytes 2162688 | tf_op jit(solution)/shard_map/all_gather | solution.py:279
  7.9 133.6 %all-gather.5.cloned.1.call-start = ((), (), s32[]{:S(2)}) async-start(), calls=%async_computation | async-start | bytes 6488064 | tf_op jit(solution)/shard_map/all_gather | solution.py:279
  8.7 512.3 %all-gather.9.cloned.1.call-start = ((), (), s32[]{:S(2)}) async-start(), calls=%async_computation.2 | async-start | bytes 8650752 | tf_op jit(solution)/shard_map/all_gather | solution.py:279
  9.4 562.9 %all-gather.11.cloned.1.call-start = ((), (), s32[]{:S(2)}) async-start(), calls=%async_computation.3 | async-start | bytes 8650752 | tf_op jit(solution)/shard_map/all_gather | solution.py:279
  14.9 10.0 %collective-permute-start = (bf16[1,512]{1,0:T(2,128)(2,1)S(1)}, bf16[1,512]{1,0:T(2,128)(2,1)S(1)}, u32[]{:S(2)}, u32[]{:S(2)}) collective-permute-start(bf16[1,512]{1,0:T(2,128)(2,1)S(1)} %broadcast_in_dim.129), channel_id=1, source_target_pairs={{0,1},{1,0},{2,3},{3,2},{4,5},{5,4},{6,7},{7,6},{8,9},{9,8},{10,11... | collective-permute-start | bytes 3080 | tf_op jit(solution)/shard_map/ppermute | solution.py:155
  17.8 57.0 %copy-start.54 = (f32[1,1024]{1,0:T(1,128)}, f32[1,1024]{1,0:T(1,128)S(1)}, u32[]{:S(2)}) copy-start(f32[1,1024]{1,0:T(1,128)S(1)} %compare_convert_fusion) | copy-start | bytes 12292
  22.2 119.4 %copy-start.43 = (f32[1024]{0:T(1024)}, f32[1024]{0:T(1024)S(1)}, u32[]{:S(2)}) copy-start(f32[1024]{0:T(1024)S(1)} %broadcast_multiply_fusion) | copy-start | bytes 12292
  22.9 118.6 %copy-start.51 = (f32[1024]{0:T(1024)}, f32[1024]{0:T(1024)S(1)}, u32[]{:S(2)}) copy-start(f32[1024]{0:T(1024)S(1)} %fusion.96) | copy-start | bytes 12292
  23.1 150.3 %copy-start.31 = (f32[1024,8]{0,1:T(8,128)}, f32[1024,8]{0,1:T(8,128)S(1)}, u32[]{:S(2)}) copy-start(f32[1024,8]{0,1:T(8,128)S(1)} %get-tuple-element.185) | copy-start | bytes 98308
  23.1 150.3 %copy-start.33 = (f32[1024,8]{0,1:T(8,128)}, f32[1024,8]{0,1:T(8,128)S(1)}, u32[]{:S(2)}) copy-start(f32[1024,8]{0,1:T(8,128)S(1)} %get-tuple-element.186) | copy-start | bytes 98308
  24.9 214.7 %copy-start.4 = (pred[512,1024]{1,0:T(8,128)(4,1)}, pred[512,1024]{1,0:T(8,128)(4,1)S(1)}, u32[]{:S(2)}) copy-start(pred[512,1024]{1,0:T(8,128)(4,1)S(1)} %get-tuple-element.190) | copy-start | bytes 1572868
  24.9 1.9 collective-permute-start.1
  26.8 2.9 collective-permute-start.2
  29.7 3.0 collective-permute-start.3
  32.7 3.5 collective-permute-start.4
  38.3 103.3 %copy-start.48 = (f32[1024]{0:T(1024)}, f32[1024]{0:T(1024)S(1)}, u32[]{:S(2)}) copy-start(f32[1024]{0:T(1024)S(1)} %reshape.701) | copy-start | bytes 12292
  39.0 102.5 %copy-start.58 = (f32[1024]{0:T(1024)}, f32[1024]{0:T(1024)S(1)}, u32[]{:S(2)}) copy-start(f32[1024]{0:T(1024)S(1)} %reshape.702) | copy-start | bytes 12292
  173.8 91.4 %copy-start.15 = (bf16[1024,16,8]{0,2,1:T(8,128)(2,1)}, bf16[1024,16,8]{0,2,1:T(8,128)(2,1)S(1)}, u32[]{:S(2)}) copy-start(bf16[1024,16,8]{0,2,1:T(8,128)(2,1)S(1)} %get-tuple-element.165) | copy-start | bytes 786436
  265.2 31.5 %slice-start.3 = ((s8[12582912]{0:T(1024)(128)(4,1)}), s8[4194304]{0:T(1024)(128)(4,1)S(1)}, s32[]{:S(2)}) async-start(s8[12582912]{0:T(1024)(128)(4,1)} %bitcast.231), calls=%async_computation.7 | async-start | bytes 8388608
  336.2 54.5 %copy-start = (bf16[1024,16,48]{0,2,1:T(8,128)(2,1)S(1)}, bf16[1024,16,48]{0,2,1:T(8,128)(2,1)}, u32[]{:S(2)}) copy-start(bf16[1024,16,48]{0,2,1:T(8,128)(2,1)} %fusion.87) | copy-start | bytes 4718596
  336.2 54.5 %copy-start.16 = (bf16[1024,16,8]{0,2,1:T(8,128)(2,1)S(1)}, bf16[1024,16,8]{0,2,1:T(8,128)(2,1)}, u32[]{:S(2)}) copy-start(bf16[1024,16,8]{0,2,1:T(8,128)(2,1)} %copy-done.15) | copy-start | bytes 786436
  336.2 54.5 %copy-start.19 = (bf16[1024,16,8]{0,2,1:T(8,128)(2,1)S(1)}, bf16[1024,16,8]{0,2,1:T(8,128)(2,1)}, u32[]{:S(2)}) copy-start(bf16[1024,16,8]{0,2,1:T(8,128)(2,1)} %copy-done.17) | copy-start | bytes 786436
  460.2 53.2 %collective-permute-start.15 = (bf16[16,32,1024]{2,1,0:T(8,128)(2,1)}, bf16[16,32,1024]{2,1,0:T(8,128)(2,1)}, u32[]{:S(2)}, u32[]{:S(2)}) collective-permute-start(bf16[16,32,1024]{2,1,0:T(8,128)(2,1)} %get-tuple-element.116), channel_id=1, source_target_pairs={{0,2},{1,3},{2,0},{3,1},{4,6},{5,7},{6,4},{7,5},{8,10},{9,11},{10,... | collective-permute-start | bytes 3145736 | tf_op jit(solution)/shard_map/ppermute | solution.py:155
  513.3 211.1 %collective-permute-start.10 = (bf16[16,32,3072]{2,1,0:T(8,128)(2,1)}, bf16[16,32,3072]{2,1,0:T(8,128)(2,1)}, u32[]{:S(2)}, u32[]{:S(2)}) collective-permute-start(bf16[16,32,3072]{2,1,0:T(8,128)(2,1)} %get-tuple-element.106), channel_id=1, source_target_pairs={{0,2},{1,3},{2,0},{3,1},{4,6},{5,7},{6,4},{7,5},{8,10},{9,11},{10,... | collective-permute-start | bytes 9437192 | tf_op jit(solution)/shard_map/ppermute | solution.py:155
  519.4 189.2 %collective-permute-start.16 = (bf16[8,32,1024]{2,1,0:T(8,128)(2,1)}, bf16[8,32,1024]{2,1,0:T(8,128)(2,1)}, u32[]{:S(2)}, u32[]{:S(2)}) collective-permute-start(bf16[8,32,1024]{2,1,0:T(8,128)(2,1)} %get-tuple-element.118), channel_id=1, source_target_pairs={{0,4},{1,5},{2,3},{3,2},{4,0},{5,1},{6,7},{7,6},{8,12},{9,13},{10,... | collective-permute-start | bytes 1572872 | tf_op jit(solution)/shard_map/ppermute | solution.py:155
  651.5 29.8 %collective-permute-start.25 = (bf16[16,128,1024]{2,1,0:T(8,128)(2,1)}, bf16[16,128,1024]{2,1,0:T(8,128)(2,1)}, u32[]{:S(2)}, u32[]{:S(2)}) collective-permute-start(bf16[16,128,1024]{2,1,0:T(8,128)(2,1)} %get-tuple-element.136), channel_id=1, source_target_pairs={{0,2},{1,3},{2,0},{3,1},{4,6},{5,7},{6,4},{7,5},{8,10},{9,11},{10,... | collective-permute-start | bytes 12582920 | tf_op jit(solution)/shard_map/ppermute | solution.py:155
  652.1 37.7 %collective-permute-start.20 = (bf16[16,32,4096]{2,1,0:T(8,128)(2,1)}, bf16[16,32,4096]{2,1,0:T(8,128)(2,1)}, u32[]{:S(2)}, u32[]{:S(2)}) collective-permute-start(bf16[16,32,4096]{2,1,0:T(8,128)(2,1)} %get-tuple-element.126), channel_id=1, source_target_pairs={{0,2},{1,3},{2,0},{3,1},{4,6},{5,7},{6,4},{7,5},{8,10},{9,11},{10,... | collective-permute-start | bytes 12582920 | tf_op jit(solution)/shard_map/ppermute | solution.py:155
  689.5 53.2 %collective-permute-start.26 = (bf16[8,128,1024]{2,1,0:T(8,128)(2,1)}, bf16[8,128,1024]{2,1,0:T(8,128)(2,1)}, u32[]{:S(2)}, u32[]{:S(2)}) collective-permute-start(bf16[8,128,1024]{2,1,0:T(8,128)(2,1)} %get-tuple-element.138), channel_id=1, source_target_pairs={{0,4},{1,5},{2,3},{3,2},{4,0},{5,1},{6,7},{7,6},{8,12},{9,13},{10,... | collective-permute-start | bytes 6291464 | tf_op jit(solution)/shard_map/ppermute | solution.py:155
  698.0 49.9 %collective-permute-start.21 = (bf16[8,32,4096]{2,1,0:T(8,128)(2,1)}, bf16[8,32,4096]{2,1,0:T(8,128)(2,1)}, u32[]{:S(2)}, u32[]{:S(2)}) collective-permute-start(bf16[8,32,4096]{2,1,0:T(8,128)(2,1)} %get-tuple-element.128), channel_id=1, source_target_pairs={{0,4},{1,5},{2,3},{3,2},{4,0},{5,1},{6,7},{7,6},{8,12},{9,13},{10,... | collective-permute-start | bytes 6291464 | tf_op jit(solution)/shard_map/ppermute | solution.py:155
  706.3 6.5 collective-permute-start.5
  712.5 8.7 collective-permute-start.17
  712.8 19.3 %collective-permute-start.6 = (f32[8,384]{1,0:T(8,128)S(1)}, f32[8,384]{1,0:T(8,128)S(1)}, u32[]{:S(2)}, u32[]{:S(2)}) collective-permute-start(f32[8,384]{1,0:T(8,128)S(1)} %slice_select_fusion.1), channel_id=1, source_target_pairs={{0,8},{1,9},{2,10},{3,11},{4,12},{5,13},{6,14},{7,15},{8,0},{9,1},... | collective-permute-start | bytes 36872 | tf_op jit(solution)/shard_map/ppermute | solution.py:155
  724.3 13.2 %collective-permute-start.18 = (bf16[2,32,1024]{2,1,0:T(8,128)(2,1)}, bf16[2,32,1024]{2,1,0:T(8,128)(2,1)S(1)}, u32[]{:S(2)}, u32[]{:S(2)}) collective-permute-start(bf16[2,32,1024]{2,1,0:T(8,128)(2,1)} %get-tuple-element.122), channel_id=1, source_target_pairs={{0,8},{1,9},{2,10},{3,11},{4,12},{5,13},{6,14},{7,15},{8,0},{9,1},... | collective-permute-start | bytes 393224 | tf_op jit(solution)/shard_map/ppermute | solution.py:155
  731.8 55.6 %collective-permute-start.11 = (bf16[8,32,3072]{2,1,0:T(8,128)(2,1)}, bf16[8,32,3072]{2,1,0:T(8,128)(2,1)}, u32[]{:S(2)}, u32[]{:S(2)}) collective-permute-start(bf16[8,32,3072]{2,1,0:T(8,128)(2,1)} %get-tuple-element.108), channel_id=1, source_target_pairs={{0,4},{1,5},{2,3},{3,2},{4,0},{5,1},{6,7},{7,6},{8,12},{9,13},{10,... | collective-permute-start | bytes 4718600 | tf_op jit(solution)/shard_map/ppermute | solution.py:155
  732.1 10.6 %collective-permute-start.7 = (f32[4,384]{1,0:T(4,128)S(1)}, f32[4,384]{1,0:T(4,128)S(1)}, u32[]{:S(2)}, u32[]{:S(2)}) collective-permute-start(f32[4,384]{1,0:T(4,128)S(1)} %slice_select_fusion.2), channel_id=1, source_target_pairs={{0,4},{1,5},{2,6},{3,7},{4,0},{5,1},{6,2},{7,3},{8,12},{9,13},{10,... | collective-permute-start | bytes 18440 | tf_op jit(solution)/shard_map/ppermute | solution.py:155
  740.5 44.6 %collective-permute-start.19 = (bf16[1,32,1024]{2,1,0:T(8,128)(2,1)}, bf16[1,32,1024]{2,1,0:T(8,128)(2,1)S(1)}, u32[]{:S(2)}, u32[]{:S(2)}) collective-permute-start(bf16[1,32,1024]{2,1,0:T(8,128)(2,1)} %get-tuple-element.124), channel_id=1, source_target_pairs={{0,16},{1,17},{2,18},{3,19},{4,20},{5,21},{6,22},{7,23},{8,24},{9,... | collective-permute-start | bytes 196616 | tf_op jit(solution)/shard_map/ppermute | solution.py:155
  747.6 46.1 %collective-permute-start.27 = (bf16[4,128,1024]{2,1,0:T(8,128)(2,1)}, bf16[4,128,1024]{2,1,0:T(8,128)(2,1)S(1)}, u32[]{:S(2)}, u32[]{:S(2)}) collective-permute-start(bf16[4,128,1024]{2,1,0:T(8,128)(2,1)} %get-tuple-element.140), channel_id=1, source_target_pairs={{0,1},{1,0},{2,6},{3,7},{4,5},{5,4},{6,2},{7,3},{8,9},{9,8},{10,14... | collective-permute-start | bytes 3145736 | tf_op jit(solution)/shard_map/ppermute | solution.py:155
  753.2 46.5 %collective-permute-start.22 = (bf16[4,32,4096]{2,1,0:T(8,128)(2,1)}, bf16[4,32,4096]{2,1,0:T(8,128)(2,1)}, u32[]{:S(2)}, u32[]{:S(2)}) collective-permute-start(bf16[4,32,4096]{2,1,0:T(8,128)(2,1)} %get-tuple-element.130), channel_id=1, source_target_pairs={{0,1},{1,0},{2,6},{3,7},{4,5},{5,4},{6,2},{7,3},{8,9},{9,8},{10,14... | collective-permute-start | bytes 3145736 | tf_op jit(solution)/shard_map/ppermute | solution.py:155
  754.5 32.7 %collective-permute-start.8 = (f32[2,384]{1,0:T(2,128)S(1)}, f32[2,384]{1,0:T(2,128)S(1)}, u32[]{:S(2)}, u32[]{:S(2)}) collective-permute-start(f32[2,384]{1,0:T(2,128)S(1)} %broadcast_select_fusion.1), channel_id=1, source_target_pairs={{0,2},{1,3},{2,0},{3,1},{4,6},{5,7},{6,4},{7,5},{8,10},{9,11},{10,... | collective-permute-start | bytes 9224 | tf_op jit(solution)/shard_map/ppermute | solution.py:155
  787.2 31.0 %collective-permute-start.9 = (f32[1,384]{1,0:T(1,128)S(1)}, f32[1,384]{1,0:T(1,128)S(1)}, u32[]{:S(2)}, u32[]{:S(2)}) collective-permute-start(f32[1,384]{1,0:T(1,128)S(1)} %broadcast_select_fusion.2), channel_id=1, source_target_pairs={{0,1},{1,0},{2,3},{3,2},{4,5},{5,4},{6,7},{7,6},{8,9},{9,8},{10,11... | collective-permute-start | bytes 4616 | tf_op jit(solution)/shard_map/ppermute | solution.py:155
  792.1 26.1 %collective-permute-start.12 = (bf16[4,32,3072]{2,1,0:T(8,128)(2,1)}, bf16[4,32,3072]{2,1,0:T(8,128)(2,1)}, u32[]{:S(2)}, u32[]{:S(2)}) collective-permute-start(bf16[4,32,3072]{2,1,0:T(8,128)(2,1)} %get-tuple-element.110), channel_id=1, source_target_pairs={{0,1},{1,0},{2,6},{3,7},{4,5},{5,4},{6,2},{7,3},{8,9},{9,8},{10,14... | collective-permute-start | bytes 2359304 | tf_op jit(solution)/shard_map/ppermute | solution.py:155
  797.8 25.4 %collective-permute-start.28 = (bf16[2,128,1024]{2,1,0:T(8,128)(2,1)}, bf16[2,128,1024]{2,1,0:T(8,128)(2,1)S(1)}, u32[]{:S(2)}, u32[]{:S(2)}) collective-permute-start(bf16[2,128,1024]{2,1,0:T(8,128)(2,1)} %get-tuple-element.142), channel_id=1, source_target_pairs={{0,8},{1,9},{2,10},{3,11},{4,12},{5,13},{6,14},{7,15},{8,0},{9,1},... | collective-permute-start | bytes 1572872 | tf_op jit(solution)/shard_map/ppermute | solution.py:155
  802.8 24.6 %collective-permute-start.23 = (bf16[2,32,4096]{2,1,0:T(8,128)(2,1)}, bf16[2,32,4096]{2,1,0:T(8,128)(2,1)S(1)}, u32[]{:S(2)}, u32[]{:S(2)}) collective-permute-start(bf16[2,32,4096]{2,1,0:T(8,128)(2,1)} %get-tuple-element.132), channel_id=1, source_target_pairs={{0,8},{1,9},{2,10},{3,11},{4,12},{5,13},{6,14},{7,15},{8,0},{9,1},... | collective-permute-start | bytes 1572872 | tf_op jit(solution)/shard_map/ppermute | solution.py:155
  821.2 13.3 %collective-permute-start.13 = (bf16[2,32,3072]{2,1,0:T(8,128)(2,1)}, bf16[2,32,3072]{2,1,0:T(8,128)(2,1)S(1)}, u32[]{:S(2)}, u32[]{:S(2)}) collective-permute-start(bf16[2,32,3072]{2,1,0:T(8,128)(2,1)} %get-tuple-element.112), channel_id=1, source_target_pairs={{0,8},{1,9},{2,10},{3,11},{4,12},{5,13},{6,14},{7,15},{8,0},{9,1},... | collective-permute-start | bytes 1179656 | tf_op jit(solution)/shard_map/ppermute | solution.py:155
  823.2 44.3 %copy-start.60 = (f32[32]{0:T(128)}, f32[32]{0:T(128)S(1)}, u32[]{:S(2)}) copy-start(f32[32]{0:T(128)S(1)} %get-tuple-element.239) | copy-start | bytes 388
  826.7 35.6 %collective-permute-start.29 = (bf16[1,128,1024]{2,1,0:T(8,128)(2,1)}, bf16[1,128,1024]{2,1,0:T(8,128)(2,1)S(1)}, u32[]{:S(2)}, u32[]{:S(2)}) collective-permute-start(bf16[1,128,1024]{2,1,0:T(8,128)(2,1)} %get-tuple-element.144), channel_id=1, source_target_pairs={{0,16},{1,17},{2,18},{3,19},{4,20},{5,21},{6,22},{7,23},{8,24},{9,... | collective-permute-start | bytes 786440 | tf_op jit(solution)/shard_map/ppermute | solution.py:155
  830.9 34.0 %collective-permute-start.24 = (bf16[1,32,4096]{2,1,0:T(8,128)(2,1)}, bf16[1,32,4096]{2,1,0:T(8,128)(2,1)S(1)}, u32[]{:S(2)}, u32[]{:S(2)}) collective-permute-start(bf16[1,32,4096]{2,1,0:T(8,128)(2,1)} %get-tuple-element.134), channel_id=1, source_target_pairs={{0,16},{1,17},{2,18},{3,19},{4,20},{5,21},{6,22},{7,23},{8,24},{9,... | collective-permute-start | bytes 786440 | tf_op jit(solution)/shard_map/ppermute | solution.py:155
  837.9 22.0 %collective-permute-start.14 = (bf16[1,32,3072]{2,1,0:T(8,128)(2,1)}, bf16[1,32,3072]{2,1,0:T(8,128)(2,1)S(1)}, u32[]{:S(2)}, u32[]{:S(2)}) collective-permute-start(bf16[1,32,3072]{2,1,0:T(8,128)(2,1)} %get-tuple-element.114), channel_id=1, source_target_pairs={{0,16},{1,17},{2,18},{3,19},{4,20},{5,21},{6,22},{7,23},{8,24},{9,... | collective-permute-start | bytes 589832 | tf_op jit(solution)/shard_map/ppermute | solution.py:155
  (57 other events, 491.2 us)
Sparse Core Ops, SparseCore 0:
  11.1 59.0 all-gather.6
  73.1 68.3 all-gather.4
  144.6 75.9 all-gather.8
  223.6 76.1 all-gather.10

commit v2 on v1

--- a/solution.py
+++ b/solution.py
@@ -5,6 +5,7 @@
 from jax import lax
 from jax.experimental import pallas as pl
 from jax.experimental.pallas import tpu as pltpu
+from jax.sharding import Mesh
 from jax.sharding import PartitionSpec as P
 
 AXES = ("dp", "fsdp")
@@ -385,39 +386,692 @@
     )
 
 
+NT = (((1,), (1,)), ((), ()))
+NN = (((1,), (0,)), ((), ()))
+TN = (((0,), (0,)), ((), ()))
+PAIR = 2 * HEAD
+ROWS = 256
+
+
+def mul(left, right, dims):
+    return lax.dot_general(left, right, dims, preferred_element_type=jnp.float32)
+
+
+def params(**more):
+    return pltpu.CompilerParams(vmem_limit_bytes=60 << 20, **more)
+
+
+def cost(flops, moved, special=0):
+    return pl.CostEstimate(flops=int(flops), transcendentals=int(special), bytes_accessed=int(moved))
+
+
+def fixed(shape):
+    return pl.BlockSpec(shape, lambda *_: (0,) * len(shape), pipeline_mode=pl.Buffered(1))
+
+
+def middle_swap(value):
+    quarter = (lax.broadcasted_iota(jnp.int32, value.shape, 1) % 128) // 32
+    width = value.shape[1]
+    up, down = pltpu.roll(value, width - 32, 1), pltpu.roll(value, 32, 1)
+    return jnp.where(quarter == 1, up, jnp.where(quarter == 2, down, value))
+
+
+def norm_kernel(mine, theirs, gmine, gtheirs, scales, one, two, grads):
+    def work(source, cotangent):
+        value = source[...].astype(jnp.float32)
+        center = value - jnp.mean(value, axis=1, keepdims=True)
+        spread = jnp.mean(center * center, axis=1, keepdims=True)
+        hat = center * lax.rsqrt(spread + norm_eps)
+        table = scales[...].astype(jnp.float32)
+        one[...] = middle_swap(hat * table[0:1] + table[1:2]).astype(jnp.bfloat16)
+        two[...] = middle_swap(hat * table[2:3] + table[3:4]).astype(jnp.bfloat16)
+        grads[...] = cotangent[...]
+
+    first = pl.program_id(0) == 0
+    pl.when(first)(lambda: work(mine, gmine))
+    pl.when(jnp.logical_not(first))(lambda: work(theirs, gtheirs))
+
+
+def norms(mine, theirs, gmine, gtheirs, scales):
+    length, width = mine.shape
+    block = (ROWS, width)
+    steps = length // ROWS
+    own = pl.BlockSpec(block, lambda s, i: (jnp.where(s == 0, i, steps - 1), 0))
+    other = pl.BlockSpec(block, lambda s, i: (jnp.where(s == 0, 0, i), 0))
+    out = pl.BlockSpec(block, lambda s, i: (s * steps + i, 0))
+    shape = jax.ShapeDtypeStruct((2 * length, width), jnp.bfloat16)
+    return pl.pallas_call(
+        norm_kernel,
+        grid=(2, steps),
+        in_specs=[own, other, own, other, fixed(scales.shape)],
+        out_specs=[out] * 3,
+        out_shape=[shape] * 3,
+        compiler_params=params(),
+        cost_estimate=cost(40 * length * width, 20 * length * width),
+    )(mine, theirs, gmine, gtheirs, scales)
+
+
+def turn(value, cosine, sine):
+    lane = lax.broadcasted_iota(jnp.int32, value.shape, 1) % HEAD
+    half = ROT // 2
+    up, down = pltpu.roll(value, value.shape[1] - half, 1), pltpu.roll(value, half, 1)
+    return value * cosine + jnp.where(lane < half, up, down) * sine
+
+
+def project_kernel(normed, grads, weight, bias, cosine, sine, valid, out):
+    part = pl.program_id(0)
+    tokens = normed.shape[0]
+    width = weight.shape[-1]
+    held = weight[...].reshape(-1, width)
+    for start in range(0, tokens, 2 * ROWS):
+        rows = slice(start, start + 2 * ROWS)
+
+        @pl.when(part < 3)
+        def _():
+            value = mul(normed[rows, :], held, NN) + bias[0].astype(jnp.float32)
+
+            @pl.when(part < 2)
+            def _():
+                scale = jnp.where(part == 0, HEAD ** (-0.5), 1.0)
+                for at in range(0, width, PAIR):
+                    turned = turn(value[:, at : at + PAIR], cosine[rows, :], sine[rows, :])
+                    out[0, rows, at : at + PAIR] = (turned * scale).astype(out.dtype)
+
+            @pl.when(part == 2)
+            def _():
+                out[0, rows, :] = value.astype(out.dtype)
+
+        @pl.when(part == 3)
+        def _():
+            pieces = weight[...].reshape(-1, 2, weight.shape[2] // 2, width)
+            total = None
+            for half in range(2):
+                term = mul(
+                    grads[rows, half * width : (half + 1) * width],
+                    pieces[:, half].reshape(-1, width),
+                    NT,
+                )
+                total = term if total is None else total + term
+            out[0, rows, :] = (total * valid[rows, :]).astype(out.dtype)
+
+
+def project(normed, grads, packed, bias, cosine, sine, valid):
+    tokens, model = normed.shape
+    chips, parts, rows, width = packed.shape
+    return pl.pallas_call(
+        project_kernel,
+        grid=(parts,),
+        in_specs=[
+            fixed(normed.shape),
+            fixed(grads.shape),
+            pl.BlockSpec((chips, 1, rows, width), lambda p: (0, p, 0, 0)),
+            pl.BlockSpec((1, 1, width), lambda p: (jnp.minimum(p, 2), 0, 0)),
+            fixed(cosine.shape),
+            fixed(sine.shape),
+            fixed(valid.shape),
+        ],
+        out_specs=pl.BlockSpec((1, tokens, width), lambda p: (p, 0, 0)),
+        out_shape=jax.ShapeDtypeStruct((parts, tokens, width), jnp.bfloat16),
+        compiler_params=params(),
+        cost_estimate=cost(7 * tokens * model * width, 40 * tokens * width),
+    )(normed, grads, packed, bias, cosine, sine, valid)
+
+
+def attention_kernel(
+    q_ref, k_ref, v_ref, g_ref, cosine, sine, seg_row, seg_col, valid, out, d_out, mask, dk_sum, dv_sum
+):
+    length = q_ref.shape[1]
+    blocks = length // ROWS
+
+    @pl.when(pl.program_id(1) == 0)
+    def _():
+        for block in range(blocks):
+            start = block * ROWS
+            end = start + ROWS
+            key_pos = lax.broadcasted_iota(jnp.int32, (ROWS, end), 1)
+            query_pos = lax.broadcasted_iota(jnp.int32, (ROWS, end), 0) + start
+            allowed = (key_pos <= query_pos) & (seg_col[start:end, :] == seg_row[0, :, :end])
+            mask[start:end, :end] = jnp.where(allowed, 0.0, masked_score)
+
+    lane = lax.broadcasted_iota(jnp.int32, (ROWS, PAIR), 1)
+    for block in range(blocks - 1, -1, -1):
+        start = block * ROWS
+        end = start + ROWS
+        rows = slice(start, end)
+        keys, values = k_ref[0, :end, :], v_ref[0, :end, :]
+        query, grads = q_ref[0, rows, :], g_ref[0, rows, :]
+        hide = mask[rows, :end]
+        pieces = []
+        for head in range(2):
+            mine = lane < HEAD if head == 0 else lane >= HEAD
+            own_query = jnp.where(mine, query, jnp.zeros_like(query))
+            own_grads = jnp.where(mine, grads, jnp.zeros_like(grads))
+            scores = mul(own_query, keys, NT) + hide
+            exponent = jnp.exp(scores - jnp.max(scores, axis=1, keepdims=True))
+            probs = exponent * (1.0 / jnp.sum(exponent, axis=1, keepdims=True))
+            low = probs.astype(jnp.bfloat16)
+            mixed = mul(low, values, NN)
+            d_probs = mul(own_grads, values, NT)
+            inner = jnp.sum(own_grads.astype(jnp.float32) * mixed, axis=1, keepdims=True)
+            d_scores = (probs * (d_probs - inner)).astype(jnp.bfloat16)
+            pieces.append((mixed, mul(d_scores, keys, NN)))
+            d_keys, d_values = mul(d_scores, own_query, TN), mul(low, own_grads, TN)
+            if block == blocks - 1 and head == 0:
+                dk_sum[:end, :] = d_keys
+                dv_sum[:end, :] = d_values
+            else:
+                dk_sum[:end, :] += d_keys
+                dv_sum[:end, :] += d_values
+        mine = lane < HEAD
+        out[rows, :] = (jnp.where(mine, pieces[0][0], pieces[1][0]) * valid[rows, :]).astype(out.dtype)
+        d_query = turn(jnp.where(mine, pieces[0][1], pieces[1][1]), cosine[rows, :], -sine[rows, :])
+        d_out[0, rows, :] = (d_query * HEAD ** (-0.5)).astype(d_out.dtype)
+    d_out[1] = turn(dk_sum[...], cosine[...], -sine[...]).astype(d_out.dtype)
+    d_out[2] = dv_sum[...].astype(d_out.dtype)
+
+
+def attention(parts, cosine, sine, segments, valid):
+    sequences, length = segments.shape
+    tokens, width = parts.shape[1:]
+    part = lambda p: pl.BlockSpec((1, length, PAIR), lambda s, j: (p, s, j))
+    table = lambda n: pl.BlockSpec((length, n), lambda s, j: (s, 0))
+    return pl.pallas_call(
+        attention_kernel,
+        grid=(sequences, width // PAIR),
+        in_specs=[
+            part(0),
+            part(1),
+            part(2),
+            part(3),
+            table(PAIR),
+            table(PAIR),
+            pl.BlockSpec((1, 1, length), lambda s, j: (s, 0, 0)),
+            table(1),
+            table(1),
+        ],
+        out_specs=[
+            pl.BlockSpec((length, PAIR), lambda s, j: (s, j)),
+            pl.BlockSpec((3, length, PAIR), lambda s, j: (0, s, j)),
+        ],
+        out_shape=[
+            jax.ShapeDtypeStruct((tokens, width), jnp.bfloat16),
+            jax.ShapeDtypeStruct((3, tokens, width), jnp.bfloat16),
+        ],
+        scratch_shapes=[pltpu.VMEM((length, length), jnp.float32)] + [pltpu.VMEM((length, PAIR), jnp.float32)] * 2,
+        compiler_params=params(),
+        cost_estimate=cost(8 * tokens * length * width * 4, 16 * tokens * width, tokens * length * width // 100),
+    )(*[parts] * 4, cosine, sine, segments[:, None, :], segments.reshape(tokens, 1), valid)
+
+
+def attention_grads_kernel(normed, grads, weight, d_mixed, attended, packed, d_mine, d_send, p_mine, p_send, sums, total):
+    part = pl.program_id(0)
+    tokens = normed.shape[0]
+    half_tokens = tokens // 2
+    chips, _, rows, width = weight.shape
+
+    @pl.when(part < 3)
+    def _():
+        change = d_mixed[0]
+        held = weight[...].reshape(-1, width)
+        packed[...] = mul(normed[...], change, TN).astype(packed.dtype).reshape(packed.shape)
+        sums[0] = jnp.sum(change.astype(jnp.float32), axis=0, keepdims=True)
+        for start in range(0, tokens, 2 * ROWS):
+            at = slice(start, start + 2 * ROWS)
+            term = mul(d_mixed[0, at, :], held, NT)
+
+            @pl.when(part == 0)
+            def _():
+                total[at, :] = term
+
+            @pl.when(part == 1)
+            def _():
+                total[at, :] += term
+
+            @pl.when(part == 2)
+            def _():
+                both = total[at, :] + term
+                if start < half_tokens:
+                    d_mine[at, :] = both
+                else:
+                    d_send[start - half_tokens : start - half_tokens + 2 * ROWS, :] = both.astype(d_send.dtype)
+
+    @pl.when(part == 3)
+    def _():
+        sums[0] = jnp.zeros_like(sums[0])
+        pieces = weight[...].reshape(-1, 2, rows // 2, width)
+        for half in range(2):
+            columns = slice(half * width, (half + 1) * width)
+            change = mul(attended[...], grads[:, columns], TN).astype(packed.dtype)
+            packed[:, 0, half * rows // 2 : (half + 1) * rows // 2, :] = change.reshape(chips, rows // 2, width)
+            term = mul(attended[...], pieces[:, half].reshape(-1, width), NN)
+            p_mine[:, columns] = term[:half_tokens]
+            p_send[:, columns] = term[half_tokens:].astype(p_send.dtype)
+
+
+def attention_grads(normed, grads, weights, d_mixed, attended):
+    tokens, model = normed.shape
+    chips, parts, rows, width = weights.shape
+    wide = pl.BlockSpec((chips, 1, rows, width), lambda p: (0, p, 0, 0))
+    half = (tokens // 2, model)
+    mine, send = jax.ShapeDtypeStruct(half, jnp.float32), jax.ShapeDtypeStruct(half, jnp.bfloat16)
+    return pl.pallas_call(
+        attention_grads_kernel,
+        grid=(parts,),
+        in_specs=[
+            fixed(normed.shape),
+            fixed(grads.shape),
+            wide,
+            pl.BlockSpec((1, tokens, width), lambda p: (jnp.minimum(p, 2), 0, 0)),
+            fixed(attended.shape),
+        ],
+        out_specs=[wide, fixed(half), fixed(half), fixed(half), fixed(half), pl.BlockSpec((1, 1, width), lambda p: (p, 0, 0))],
+        out_shape=[
+            jax.ShapeDtypeStruct(weights.shape, jnp.bfloat16),
+            mine,
+            send,
+            mine,
+            send,
+            jax.ShapeDtypeStruct((parts, 1, width), jnp.float32),
+        ],
+        scratch_shapes=[pltpu.VMEM((tokens, model), jnp.float32)],
+        compiler_params=params(),
+        cost_estimate=cost(16 * tokens * model * width, 20 * tokens * model),
+    )(normed, grads, weights, d_mixed, attended)
+
+
+def forward_kernel(begins, ends, *refs):
+    normed, grads, up, down, bias = refs[:5]
+    rest = refs[5:] if begins else refs[7:]
+    packed, bias_sum = rest[:2]
+    step = pl.program_id(0)
+    if begins:
+        out_total, d_total, after, d_before = rest[2:]
+    else:
+        results = rest[2:6]
+        after, d_before, out_total, d_total, arrived = rest[6:]
+        loads = [
+            pltpu.make_async_copy(source, target, arrived.at[n])
+            for n, (source, target) in enumerate(zip(refs[5:7], (out_total, d_total)))
+        ]
+
+        @pl.when(step == 0)
+        def _():
+            for load in loads:
+                load.start()
+
+    steps = pl.num_programs(0)
+    tokens = normed.shape[0]
+    half_tokens = tokens // 2
+    chips, _, rows, width = up.shape
+
+    def add(total, at, columns, term):
+        if begins:
+
+            @pl.when(step == 0)
+            def _():
+                total[at, columns] = term
+
+            @pl.when(step > 0)
+            def _():
+                total[at, columns] += term
+        else:
+            total[at, columns] += term
+
+    held_up = up[...].reshape(-1, width)
+    pieces = down[...].reshape(down.shape[0], 2, -1, width)
+    held_down = [pieces[:, half].reshape(-1, width) for half in range(2)]
+    offset = bias[0].astype(jnp.float32)
+    bias_total = jnp.zeros_like(offset)
+    for start in range(0, tokens, ROWS):
+        at = slice(start, start + ROWS)
+        before = mul(normed[at, :], held_up, NN) + offset
+        change = mul(grads[at, :width], held_down[0], NT) + mul(grads[at, width:], held_down[1], NT)
+        share = 0.5 + 0.5 * lax.erf(before * 0.7071067811865476)
+        density = jnp.exp(-0.5 * before * before) * 0.3989422804014327
+        after[at, :] = (before * share).astype(after.dtype)
+        low = (change * (share + before * density)).astype(d_before.dtype)
+        d_before[at, :] = low
+        bias_total += jnp.sum(low.astype(jnp.float32), axis=0, keepdims=True)
+    bias_sum[0] = bias_total
+    if not begins:
+
+        @pl.when(step == 0)
+        def _():
+            for load in loads:
+                load.wait()
+
+    for start in range(0, tokens, ROWS):
+        at = slice(start, start + ROWS)
+        for half in range(2):
+            columns = slice(half * width, (half + 1) * width)
+            term = mul(after[at, :], held_down[half], NN)
+
+            add(out_total, at, columns, term)
+        add(d_total, at, slice(None), mul(d_before[at, :], held_up, NT))
+
+    change = mul(normed[...], d_before[...], TN).astype(packed.dtype)
+    quads = chips // 4
+    for chip in range(chips):
+        z, place = chip // 4, chip % 4
+        start = (z // 2) * steps * rows + step * rows
+        packed[place * 2 + z % 2, pl.ds(pl.multiple_of(start, rows), rows), :] = change[chip * rows : (chip + 1) * rows]
+    below = down.shape[1] * rows // 2
+    for half in range(2):
+        change = mul(after[...], grads[:, half * width : (half + 1) * width], TN).astype(packed.dtype)
+        start = quads // 2 * steps * rows + half * below
+        for place in range(4):
+            packed[place * 2 + step, start : start + below, :] = change[place * below : (place + 1) * below]
+
+    if ends:
+
+        @pl.when(step == steps - 1)
+        def _():
+            results[0][...] = out_total[:half_tokens, :]
+            results[1][...] = out_total[half_tokens:, :].astype(jnp.bfloat16)
+            results[2][...] = d_total[:half_tokens, :]
+            results[3][...] = d_total[half_tokens:, :].astype(jnp.bfloat16)
+
+
+def forward_chunk(which, chunks, normed, grads, weights, bias, sums):
+    tokens, model = normed.shape
+    chips, parts, rows, width = weights.shape
+    steps = parts // 2 // chunks
+    begins, ends = which == 0, which == chunks - 1
+    half, whole = (tokens // 2, model), (tokens, model)
+    first = which * steps
+    in_specs = [
+        fixed(whole),
+        fixed(whole),
+        pl.BlockSpec((chips, 1, rows, width), lambda i: (0, first + i, 0, 0)),
+        pl.BlockSpec((4, parts // 2, rows, width), lambda i: (first + i, 1, 0, 0)),
+        pl.BlockSpec((1, 1, width), lambda i: (first + i, 0, 0)),
+    ] + ([] if begins else [pl.BlockSpec(memory_space=pl.ANY)] * 2)
+    blocks = (8, chips * parts * rows // 2 // chunks // 4, width)
+    mine, send = jax.ShapeDtypeStruct(half, jnp.float32), jax.ShapeDtypeStruct(half, jnp.bfloat16)
+    results = [mine, send, mine, send] if ends else [jax.ShapeDtypeStruct(whole, jnp.float32)] * 2
+    return pl.pallas_call(
+        partial(forward_kernel, begins, ends),
+        grid=(steps,),
+        in_specs=in_specs,
+        out_specs=[fixed(blocks), pl.BlockSpec((1, 1, width), lambda i: (i, 0, 0))] + [fixed(r.shape) for r in results],
+        out_shape=[jax.ShapeDtypeStruct(blocks, jnp.bfloat16), jax.ShapeDtypeStruct((steps, 1, width), jnp.float32)] + results,
+        scratch_shapes=[pltpu.VMEM((tokens, width), jnp.bfloat16)] * 2
+        + ([] if begins else [pltpu.VMEM(whole, jnp.float32)] * 2 + [pltpu.SemaphoreType.DMA((2,))]),
+        compiler_params=params(),
+        cost_estimate=cost(12 * steps * tokens * model * width, 40 * tokens * model, 2 * steps * tokens * width),
+    )(normed, grads, weights, weights, bias, *([] if begins else sums))
+
+
+def finish_kernel(
+    hidden, grads, d1a, d1b, d2a, d2b, pa, pb, fa, fb, scales, layer_out, input_grad, sums
+):
+    value = hidden[...].astype(jnp.float32)
+    cotangent = grads[...].astype(jnp.float32)
+    table = scales[...].astype(jnp.float32)
+    both = pa[...] + pb[...].astype(jnp.float32) + table[2:3]
+    both += fa[...] + fb[...].astype(jnp.float32) + table[3:4]
+    layer_out[...] = (value + both).astype(layer_out.dtype)
+    center = value - jnp.mean(value, axis=1, keepdims=True)
+    scale = lax.rsqrt(jnp.mean(center * center, axis=1, keepdims=True) + norm_eps)
+    hat = center * scale
+    one = middle_swap(d1a[...] + d1b[...].astype(jnp.float32))
+    two = middle_swap(d2a[...] + d2b[...].astype(jnp.float32))
+    gained = one * table[0:1] + two * table[1:2]
+    mean = jnp.mean(gained, axis=1, keepdims=True)
+    slope = jnp.mean(gained * hat, axis=1, keepdims=True)
+    input_grad[...] = (cotangent + (gained - mean - hat * slope) * scale).astype(input_grad.dtype)
+
+    @pl.when(pl.program_id(0) == 0)
+    def _():
+        sums[...] = jnp.zeros_like(sums)
+
+    for row, column in enumerate((one * hat, one, two * hat, two, cotangent)):
+        sums[row : row + 1, :] += jnp.sum(column, axis=0, keepdims=True)
+
+
+def finish(hidden, grads, pieces, scales):
+    length, width = hidden.shape
+    block = pl.BlockSpec((ROWS, width), lambda i: (i, 0))
+    shape = jax.ShapeDtypeStruct(hidden.shape, jnp.bfloat16)
+    return pl.pallas_call(
+        finish_kernel,
+        grid=(length // ROWS,),
+        in_specs=[block] * 10 + [fixed(scales.shape)],
+        out_specs=[block, block, pl.BlockSpec((8, width), lambda i: (0, 0))],
+        out_shape=[shape, shape, jax.ShapeDtypeStruct((8, width), jnp.float32)],
+        compiler_params=params(),
+        cost_estimate=cost(60 * length * width, 32 * length * width),
+    )(hidden, grads, *pieces, scales)
+
+
+BITS = {"y": 0, "core": 1, "x": 2, "z_low": 3, "z_high": 4}
+SPLIT = ("zx", "core", "y")
+
+
+class Pairs:
+    def __init__(self, total):
+        self.total = total
+
+    def here(self):
+        y = lax.axis_size("y")
+        return (lax.axis_index("zx") * 2 + lax.axis_index("core")) * y + lax.axis_index("y")
+
+    def bit(self, name):
+        return (self.here() >> BITS[name]) & 1
+
+    def swap(self, value, names):
+        moves = []
+        for device in range(self.total):
+            name = names[(device >> BITS["core"]) & 1]
+            moves.append((device, device ^ (1 << BITS[name])))
+        return lax.ppermute(value, SPLIT, moves)
+
+    def plan(self, names, order, gone):
+        places, values = [], []
+        for which in (0, 1):
+            left = [n for n in order if n not in [g[which] for g in gone]]
+            places.append(len(left) - 1 - left.index(names[which]))
+            values.append(self.bit(names[which]))
+        first = self.bit("core") == 0
+        return jnp.stack([jnp.where(first, *places), jnp.where(first, *values)]).astype(jnp.int32)
+
+    def scatter(self, held, order, stages):
+        come, gone = None, []
+        for names in stages:
+            keep, send = halves(self.plan(names, order, gone), held, come)
+            come = self.swap(send, names)
+            held = keep
+            gone.append(names)
+        return held, come
+
+
+PLANE = (("x", "y"), ("y", "x"))
+
+
+def add_up(held, come):
+    return held.astype(jnp.float32) + come.astype(jnp.float32)
+
+
+def wide_angles(segments):
+    cosine, sine = angles(segments)
+    tail = cosine.shape[:-1] + (HEAD - ROT,)
+    cosine = jnp.concatenate([cosine, cosine, jnp.ones(tail, jnp.float32)], axis=-1)
+    sine = jnp.concatenate([-sine, sine, jnp.zeros(tail, jnp.float32)], axis=-1)
+    return [jnp.concatenate([t, t], axis=-1).reshape(-1, PAIR) for t in (cosine, sine)]
+
+
+def paired_body(
+    pairs,
+    hidden_in,
+    segment_ids,
+    out_grad,
+    norm1_gain,
+    norm1_bias,
+    norm2_gain,
+    norm2_bias,
+    qkv_weight,
+    qkv_bias,
+    proj_weight,
+    proj_bias,
+    up_weight,
+    up_bias,
+    down_weight,
+    down_bias,
+):
+    core = lax.axis_index("core")
+    cores = ("core", "core")
+    heads, model = HEADS // 2, qkv_weight.shape[1] // 3
+    rows, width = qkv_weight.shape[0], heads * HEAD
+    hidden, grads = hidden_in[0], out_grad[0]
+    length = hidden.shape[0]
+
+    def columns(which):
+        taken = qkv_weight.reshape(rows, 3, heads, 2, HEAD)
+        taken = lax.dynamic_index_in_dim(taken, which, 3, keepdims=False).reshape(rows, 3 * width)
+        more = up_weight.reshape(rows, heads, 2, -1)
+        more = lax.dynamic_index_in_dim(more, which, 2, keepdims=False).reshape(rows, -1)
+        return jnp.concatenate([taken, more], axis=1)
+
+    theirs = pairs.swap(columns(1 - core), cores)
+    mine = columns(core)
+    both = jnp.where(core == 0, jnp.stack([mine, theirs]), jnp.stack([theirs, mine]))
+    both = both.reshape(2 * rows, -1, width).transpose(1, 0, 2)
+    low_proj = proj_weight.reshape(rows, 2, width).transpose(1, 0, 2).reshape(1, 2 * rows, width)
+    low_down = down_weight.reshape(-1, 2, width).transpose(1, 0, 2).reshape(-1, 2 * rows, width)
+    packed_attention = jnp.concatenate([both[:3], low_proj])
+    packed_forward = jnp.concatenate([both[3:], low_down])
+    w_attention = lax.all_gather(packed_attention.reshape(-1, width), ("zx", "y"), axis=0, tiled=True)
+    w_attention = w_attention.reshape((-1,) + packed_attention.shape)
+    w_forward = lax.all_gather(packed_forward.reshape(-1, width), ("zx", "y"), axis=0, tiled=True)
+    w_forward = w_forward.reshape((-1,) + packed_forward.shape)
+
+    small = (norm1_gain, norm1_bias, norm2_gain, norm2_bias, qkv_bias, proj_bias, up_bias, down_bias)
+    sizes = [entry.shape[0] for entry in small]
+    line = jnp.concatenate(small)
+    line = jnp.pad(line, (0, -line.shape[0] % 128))[None]
+    for name in BITS:
+        come = pairs.swap(line, (name, name))
+        line = jnp.where(pairs.bit(name) == 0, jnp.concatenate([line, come]), jnp.concatenate([come, line]))
+    spread, at = [], 0
+    for size in sizes:
+        spread.append(line[:, at : at + size].reshape(-1))
+        at += size
+    gain_one, shift_one, gain_two, shift_two, b_qkv, b_proj, b_up, b_down = spread
+    own_bias = lax.dynamic_index_in_dim(b_qkv.reshape(3, heads, 2, HEAD), core, 2, keepdims=False).reshape(3, 1, width)
+    own_up_bias = lax.dynamic_index_in_dim(b_up.reshape(heads, 2, -1), core, 1, keepdims=False).reshape(-1, 1, width)
+
+    other, other_grads = pairs.swap(hidden, cores), pairs.swap(grads, cores)
+    other_ids = pairs.swap(segment_ids, cores)
+    segments = jnp.concatenate([segment_ids, other_ids])
+    cosine, sine = wide_angles(segments)
+    valid = (segments != DOCS - 1).astype(jnp.float32).reshape(-1, 1)
+    normed_one, normed_two, both_grads = norms(
+        hidden, other, grads, other_grads, jnp.stack([gain_one, shift_one, gain_two, shift_two])
+    )
+
+    parts = project(normed_one, both_grads, w_attention, own_bias, cosine, sine, valid)
+    attended, d_mixed = attention(parts, cosine, sine, segments, valid)
+    packed, d1_mine, d1_send, p_mine, p_send, qkv_sums = attention_grads(
+        normed_one, both_grads, w_attention, d_mixed, attended
+    )
+    d1_come, p_come = pairs.swap(d1_send, cores), pairs.swap(p_send, cores)
+    held, come = pairs.scatter(packed.reshape(packed.shape[0], -1, width), ("z_high", "z_low", "x", "y"),
+                               PLANE + (("z_low", "z_low"), ("z_high", "z_high")))
+    own = add_up(held, come).reshape(4, 2, rows, width)
+    low_qkv, grad_proj = own[:3], own[3]
+
+    totals, kept, up_sums = None, [], []
+    for which in range(2):
+        blocks, sums, *totals = forward_chunk(which, 2, normed_two, both_grads, w_forward, own_up_bias, totals)
+        up_sums.append(sums)
+        held, come = pairs.scatter(blocks, ("x", "y", "z_low"), PLANE + (("z_low", "z_low"),))
+        kept.append(add_up(held, come).astype(jnp.bfloat16)[0])
+    f_mine, f_send, d2_mine, d2_send = totals
+    f_come, d2_come = pairs.swap(f_send, cores), pairs.swap(d2_send, cores)
+    above = kept[0].shape[0] // 2
+    ups = jnp.stack([k[:above].reshape(2, -1, width) for k in kept])
+    downs = jnp.stack([k[above:] for k in kept])
+    high = pairs.bit("z_high")
+    pick = lambda value, axis, which: lax.dynamic_index_in_dim(value, which, axis, keepdims=False)
+    send = jnp.concatenate([pick(ups, 1, 1 - high).reshape(-1, width), pick(downs, 0, 1 - high)])
+    stay = jnp.concatenate([pick(ups, 1, high).reshape(-1, width), pick(downs, 0, high)])
+    own = add_up(stay, pairs.swap(send, ("z_high", "z_high")))
+    low_up = own[: 2 * above // 2].reshape(-1, 2, rows, width)
+    grad_down = own[above:].reshape(2, -1, width).transpose(1, 0, 2).reshape(down_weight.shape)
+    grad_proj = grad_proj.transpose(1, 0, 2).reshape(proj_weight.shape)
+
+    def rows_of(value, which):
+        return lax.dynamic_index_in_dim(value, which, 1, keepdims=False)
+
+    def interleave(value, unit):
+        mine, come = rows_of(value, core), pairs.swap(rows_of(value, 1 - core), cores)
+        flat = [v.transpose(1, 0, 2).reshape(rows, -1, 1, unit) for v in (mine, come)]
+        joined = jnp.where(core == 0, jnp.concatenate(flat, axis=2), jnp.concatenate(flat[::-1], axis=2))
+        return joined.reshape(rows, -1)
+
+    grad_qkv = interleave(low_qkv, HEAD)
+    grad_up = interleave(low_up, up_weight.shape[1] // HEADS)
+
+    layer_out, input_grad, sums = finish(
+        hidden,
+        grads,
+        (d1_mine, d1_come, d2_mine, d2_come, p_mine, p_come, f_mine, f_come),
+        jnp.stack([gain_one, gain_two, b_proj, b_down]),
+    )
+
+    def both_cores(value, unit):
+        own = value.reshape(-1, 1, unit)
+        none = jnp.zeros_like(own)
+        return jnp.where(core == 0, jnp.concatenate([own, none], axis=1), jnp.concatenate([none, own], axis=1)).reshape(-1)
+
+    sum_qkv = both_cores(qkv_sums[:3].reshape(-1), HEAD)
+    sum_up = both_cores(jnp.concatenate(up_sums).reshape(-1), up_weight.shape[1] // HEADS)
+    entries = [sums[0], sums[1], sums[2], sums[3], sum_qkv, sums[4], sum_up]
+    table = jnp.concatenate([entry.reshape(pairs.total, -1) for entry in entries], axis=1)
+    table = jnp.pad(table, ((0, 0), (0, -table.shape[1] % 128)))
+    for name in reversed(BITS):
+        upper = pairs.bit(name) == 1
+        half = table.shape[0] // 2
+        send = jnp.where(upper, table[:half], table[half:])
+        table = jnp.where(upper, table[half:], table[:half]) + pairs.swap(send, (name, name))
+    outs, at = [], 0
+    for entry in entries:
+        size = entry.shape[0] // pairs.total
+        outs.append(table[0, at : at + size])
+        at += size
+    return (
+        layer_out[None],
+        input_grad[None],
+        outs[0],
+        outs[1],
+        outs[2],
+        outs[3],
+        grad_qkv,
+        outs[4],
+        grad_proj,
+        outs[5],
+        grad_up,
+        outs[6],
+        grad_down,
+        outs[5],
+    )
+
+
+def placed(axes):
+    rows, flat = P(axes, None), P(axes)
+    whole = P(axes, None, None)
+    inside = (whole, rows, whole) + (flat,) * 4 + (rows, flat) * 4
+    outside = (whole, whole) + (flat,) * 4 + (rows, flat) * 4
+    return inside, outside
+
+
 def solution(mesh):
-    in_specs = (
-        P(("dp", "fsdp"), None, None),
-        P(("dp", "fsdp"), None),
-        P(("dp", "fsdp"), None, None),
-        P(("dp", "fsdp")),
-        P(("dp", "fsdp")),
-        P(("dp", "fsdp")),
-        P(("dp", "fsdp")),
-        P(("dp", "fsdp"), None),
-        P(("dp", "fsdp")),
-        P(("dp", "fsdp"), None),
-        P(("dp", "fsdp")),
-        P(("dp", "fsdp"), None),
-        P(("dp", "fsdp")),
-        P(("dp", "fsdp"), None),
-        P(("dp", "fsdp")),
-    )
-    out_specs = (
-        P(("dp", "fsdp"), None, None),
-        P(("dp", "fsdp"), None, None),
-        P(("dp", "fsdp")),
-        P(("dp", "fsdp")),
-        P(("dp", "fsdp")),
-        P(("dp", "fsdp")),
-        P(("dp", "fsdp"), None),
-        P(("dp", "fsdp")),
-        P(("dp", "fsdp"), None),
-        P(("dp", "fsdp")),
-        P(("dp", "fsdp"), None),
-        P(("dp", "fsdp")),
-        P(("dp", "fsdp"), None),
-        P(("dp", "fsdp")),
-    )
-    grid = Grid((mesh.shape["dp"], mesh.shape["fsdp"]))
-    return jax.shard_map(partial(body, grid), mesh=mesh, in_specs=in_specs, out_specs=out_specs, check_vma=False)
+    dp, fsdp = mesh.shape["dp"], mesh.shape["fsdp"]
+    if (dp, fsdp) == (16, 2):
+        split = Mesh(mesh.devices.reshape(dp // 2, 2, fsdp), SPLIT)
+        inside, outside = placed(SPLIT)
+        step = partial(paired_body, Pairs(dp * fsdp))
+        return jax.shard_map(step, mesh=split, in_specs=inside, out_specs=outside, check_vma=False)
+    inside, outside = placed(AXES)
+    step = partial(body, Grid((dp, fsdp)))
+    return jax.shard_map(step, mesh=mesh, in_specs=inside, out_specs=outside, check_vma=False)

time: 890 us -> 476 us (0.53)
  matrix products: 378 us -> 0 us
  Pallas kernels: 125 us -> 286 us
  other arithmetic: 132 us -> 14.6 us
  waiting for transfers between devices: 128 us -> 84.7 us
  starting transfers between devices: 51.1 us -> 29.1 us
    dot_general x24 -> x0, matrix products: 378 us -> none  [the longest x1 51.3 us: body(): jnp.dot(normed_two, w_up, preferred_element_type=jnp.float32)]
    pallas_call x4 -> x7, Pallas kernels: 7.1 us -> 242 us  [the longest x2 87.4 us: forward_chunk(): pl.pallas_call(partial(forward_kernel, begins, ends), grid=(steps,), in_s...]
    pallas_call x20 -> x10, Pallas kernels: 118 us -> 44 us  [halves(): pl.pallas_call(split_kernel if come is None else join_kernel, grid_spec=p...]
    all_gather x4 -> x2, waiting for transfers between devices: 96.4 us -> 27.7 us  [the longest x1 27.7 us: paired_body(): lax.all_gather(packed_attention.reshape(-1, width), ('zx', 'y'), axis=0,...]
    convert_element_type x6 -> x3, other arithmetic: 61.8 us -> 2.53 us  [the longest x1 2.27 us: paired_body(): valid = (segments != DOCS - 1).astype(jnp.float32).reshape(-1, 1)]
    reduce_sum x7 -> x0, other arithmetic: 50.7 us -> none  [the longest x2 31.2 us: attend_forward(): total = jnp.sum(exponent, axis=-1, keepdims=True)]
    ppermute x30 -> x31, waiting for transfers between devices: 29.5 us -> 56.9 us  [swap(): return lax.ppermute(value, SPLIT, moves)]
    ppermute x30 -> x31, starting transfers between devices: 50.9 us -> 28.7 us  [swap(): return lax.ppermute(value, SPLIT, moves)]
  transfers between devices with their start and end apart: 34 -> 33, of which waited for: 9 -> 9; matrix products, arithmetic and copies ran while one was open for 62% -> 8% of each run, Pallas kernels for 14% -> 61%
where the time goes in v2:
time: 476 us; the launch traced here: 470 us
  Pallas kernels  286 us (60%)
  waiting for transfers between devices  84.7 us (18%)
  local copies, waits for them, and re-layouts  39.8 us (8%)
  starting transfers between devices  29.1 us (6%)
  between operations  15.1 us (3%)
  other arithmetic  14.6 us (3%)
    pallas_call x2, Pallas kernels, forward_chunk(): pl.pallas_call(partial(forward_kernel, begins, ends), grid=(steps,), in_s...  87.4 us
    pallas_call x1, Pallas kernels, attention(): pl.pallas_call(attention_kernel, grid=(sequences, width // PAIR), in_spec...  68.8 us
    ppermute x31, waiting for transfers between devices, swap(): return lax.ppermute(value, SPLIT, moves)  56.9 us
    pallas_call x10, Pallas kernels, halves(): pl.pallas_call(split_kernel if come is None else join_kernel, grid_spec=p...  44 us
    pallas_call x1, Pallas kernels, attention_grads(): pl.pallas_call(attention_grads_kernel, grid=(parts,), in_specs=[fixed(nor...  32.2 us
    ppermute x31, starting transfers between devices, swap(): return lax.ppermute(value, SPLIT, moves)  28.7 us
    all_gather x1, waiting for transfers between devices, paired_body(): lax.all_gather(packed_attention.reshape(-1, width), ('zx', 'y'), axis=0,...  27.7 us
    pallas_call x1, Pallas kernels, project(): pl.pallas_call(project_kernel, grid=(parts,), in_specs=[fixed(normed.shap...  23.6 us
  transfers between devices with their start and end apart: 33, of which 9 were waited for; matrix products, arithmetic and copies ran while one was open for 8% of the time, Pallas kernels for 61%

profile of v2, /device:TPU:1, one launch (start us, length us, event | category | flops | bytes accessed | tf_op | source)
XLA Modules:
  0.0 469.5 jit_solution(18232500690808226545)
XLA Ops:
  7.2 1.3 reshape.223
  8.5 2.6 dynamic-slice_reduce_fusion.1
  11.5 1.5 dynamic-slice_reduce_fusion.3
  19.0 2.4 collective-permute-start.2
  23.7 2.1 collective-permute-done.3
  25.9 1.3 collective-permute-start.4
  28.4 3.7 multiply_sine_fusion
  32.2 1.4 collective-permute-start.5
  33.6 1.4 copy.152
  35.2 2.2 collective-permute-start.6
  37.4 2.3 compare_convert_fusion.valid
  41.3 4.5 concatenate.117.cosine
  45.8 3.0 concatenate.118.sine
  51.5 14.4 %shard_map.254 = (bf16[2048,1024]{1,0:T(8,128)(2,1)}, bf16[2048,1024]{1,0:T(8,128)(2,1)}, bf16[2048,1024]{1,0:T(8,128)(2,1)}) custom-call(bf16[1024,1024]{1,0:T(8,128)(2,1)} %bitcast.mine.hidden, bf16[1024,1024]{1,0:T(8,128)(2,1)} %collective-permute-done.theirs, bf16[1024,1024]{1,0:T(8,128)(2,1)} %bitcast.1.gmine.grads, ...), custom_call_target="tpu_custom_call" | custom-call | flops 41943040 | bytes 20971520 | tf_op jit(solution)/shard_map/pallas_call | solution.py:443
  65.9 27.7 %all-gather.3.cloned.1.call-done = bf16[4096,512]{1,0:T(8,128)(2,1)} async-done(((bf16[256,512]{1,0:T(8,128)(2,1)}), bf16[4096,512]{1,0:T(8,128)(2,1)}) %all-gather.3.cloned.1.call-update) | async-done | bytes 4194320 | tf_op jit(solution)/shard_map/all_gather | solution.py:943
  93.7 23.6 %shard_map.255.q_ref.k_ref.v_ref.g_ref = bf16[4,2048,512]{2,1,0:T(8,128)(2,1)} custom-call(bf16[2048,1024]{1,0:T(8,128)(2,1)} %get-tuple-element.58.normed, bf16[2048,1024]{1,0:T(8,128)(2,1)} %get-tuple-element.59.grads.refs_1_, bf16[16,4,64,512]{3,2,1,0:T(8,128)(2,1)} %bitcast.142, bf16[3,1,512]{2,1,0:T(2,128)(2,1)} %reshape.252.bias, ...), custom_call_target="tpu_custom_call" | custom-call | flops 7516192768 | bytes 41943040 | tf_op jit(solution)/shard_map/pallas_call | solution.py:501
  117.3 68.8 %shard_map.256 = (bf16[2048,512]{1,0:T(8,128)(2,1)}, bf16[3,2048,512]{2,1,0:T(8,128)(2,1)}) custom-call(bf16[4,2048,512]{2,1,0:T(8,128)(2,1)} %shard_map.255.q_ref.k_ref.v_ref.g_ref, bf16[4,2048,512]{2,1,0:T(8,128)(2,1)} %shard_map.255.q_ref.k_ref.v_ref.g_ref, bf16[4,2048,512]{2,1,0:T(8,128)(2,1)} %shard_map.255.q_ref.k_ref.v_ref.g_ref, ...), custom_call_target="tpu_custom_call" | custom-call | flops 34359738368 | bytes 16777216 | tf_op jit(solution)/shard_map/pallas_call | solution.py:578
  186.0 32.2 %shard_map.257 = (bf16[16,4,64,512]{3,2,1,0:T(8,128)(2,1)}, f32[1024,1024]{1,0:T(8,128)}, bf16[1024,1024]{1,0:T(8,128)(2,1)}, f32[1024,1024]{1,0:T(8,128)}, bf16...) custom-call(bf16[2048,1024]{1,0:T(8,128)(2,1)} %get-tuple-element.58.normed, ...), custom_call_target="tpu_custom_call" | custom-call | flops 17179869184 | bytes 41943040 | tf_op jit(solution)/shard_map/pallas_call | solution.py:657
  218.2 7.3 %shard_map.261 = (bf16[8,256,512]{2,1,0:T(8,128)(2,1)}, bf16[8,256,512]{2,1,0:T(8,128)(2,1)}) custom-call(s32[2]{0:T(128)} %get-tuple-element.185.plan, bf16[16,256,512]{2,1,0:T(8,128)(2,1)} %bitcast.105, bf16[16,256,512]{2,1,0:T(8,128)(2,1)} %bitcast.106), custom_call_target="tpu_custom_call" | custom-call | flops 2097152 | bytes 8388608 | tf_op jit(solution)/shard_map/pallas_call | solution.py:199
  225.5 1.2 collective-permute-start.18
  226.7 2.3 collective-permute-start.11
  228.9 46.8 %shard_map.258 = (bf16[8,512,512]{2,1,0:T(8,128)(2,1)}, f32[2,1,512]{2,1,0:T(1,128)}, f32[2048,1024]{1,0:T(8,128)}, f32[2048,1024]{1,0:T(8,128)}) custom-call(bf16[2048,1024]{1,0:T(8,128)(2,1)} %get-tuple-element.64.refs_0_, bf16[2048,1024]{1,0:T(8,128)(2,1)} %get-tuple-element.59.grads.refs_1_, bf16[16,8,64,512]{3,2,1,0:T(8,128)(2,1)} %bitcast.138, ...), custom_call_target="tpu_custom_call" | custom-call | flops 25769803776 | bytes 83886080 | tf_op jit(solution)/shard_map/pallas_call | solution.py:792
  275.8 40.5 %shard_map.259 = (bf16[8,512,512]{2,1,0:T(8,128)(2,1)}, f32[2,1,512]{2,1,0:T(1,128)}, f32[1024,1024]{1,0:T(8,128)}, bf16[1024,1024]{1,0:T(8,128)(2,1)}, f32[1024...) custom-call(bf16[2048,1024]{1,0:T(8,128)(2,1)} %get-tuple-element.64.refs_0_, ...), custom_call_target="tpu_custom_call" | custom-call | flops 25769803776 | bytes 83886080 | tf_op jit(solution)/shard_map/pallas_call | solution.py:792
  317.5 1.3 copy-done.1
  318.9 4.9 %shard_map.262 = (bf16[4,256,512]{2,1,0:T(8,128)(2,1)}, bf16[4,256,512]{2,1,0:T(8,128)(2,1)}) custom-call(s32[2]{0:T(128)} %pad_add_fusion.1.plan, bf16[8,256,512]{2,1,0:T(8,128)(2,1)} %get-tuple-element.80.own_keep.own_send, bf16[8,256,512]{2,1,0:T(8,128)(2,1)} %get-tuple-element.80.own_keep.own_send, bf16[8,256,512]{2,1,0:T(8,128)(2,1)} %copy-done.1, ...), custom_call_target="tpu_custom_call" | custom-call | flops 1048576 | bytes 8388608 | tf_op jit(solution)/shard_map/pallas_call | solution.py:199
  324.0 5.3 %shard_map.268 = (bf16[4,512,512]{2,1,0:T(8,128)(2,1)}, bf16[4,512,512]{2,1,0:T(8,128)(2,1)}) custom-call(s32[2]{0:T(128)} %get-tuple-element.186.plan, bf16[8,512,512]{2,1,0:T(8,128)(2,1)} %get-tuple-element.95.own_keep.own_send, bf16[8,512,512]{2,1,0:T(8,128)(2,1)} %get-tuple-element.95.own_keep.own_send), custom_call_target="tpu_custom_call" | custom-call | flops 2097152 | bytes 8388608 | tf_op jit(solution)/shard_map/pallas_call | solution.py:199
  330.5 5.5 %shard_map.265 = (bf16[4,512,512]{2,1,0:T(8,128)(2,1)}, bf16[4,512,512]{2,1,0:T(8,128)(2,1)}) custom-call(s32[2]{0:T(128)} %get-tuple-element.186.plan, bf16[8,512,512]{2,1,0:T(8,128)(2,1)} %get-tuple-element.88.own_keep.own_send, bf16[8,512,512]{2,1,0:T(8,128)(2,1)} %get-tuple-element.88.own_keep.own_send), custom_call_target="tpu_custom_call" | custom-call | flops 2097152 | bytes 8388608 | tf_op jit(solution)/shard_map/pallas_call | solution.py:199
  336.1 6.3 %collective-permute-done.19.come_keep.come_send = bf16[4,256,512]{2,1,0:T(8,128)(2,1)S(1)} collective-permute-done((bf16[4,256,512]{2,1,0:T(8,128)(2,1)}, bf16[4,256,512]{2,1,0:T(8,128)(2,1)S(1)}, u32[]{:S(2)}, u32[]{:S(2)}) %collective-permute-start.19) | collective-permute-done | bytes 1048608 | tf_op jit(solution)/shard_map/ppermute | solution.py:867
  343.9 3.2 shard_map.263
  347.2 1.3 collective-permute-start.20
  348.5 15.9 %shard_map.260 = (bf16[1024,1024]{1,0:T(8,128)(2,1)}, bf16[1024,1024]{1,0:T(8,128)(2,1)}, f32[8,1024]{1,0:T(8,128)}) custom-call(bf16[1024,1024]{1,0:T(8,128)(2,1)} %bitcast.mine.hidden, bf16[1024,1024]{1,0:T(8,128)(2,1)} %bitcast.1.gmine.grads, f32[1024,1024]{1,0:T(8,128)} %get-tuple-element.62.d1a, bf16[1024,1024]{1,0:T(8,128)(2,1)} %collective-permute-done.9.d1b, ...), custom_call_target="tpu_custom_call" | custom-call | flops 62914560 | bytes 33554432 | tf_op jit(solution)/shard_map/pallas_call | solution.py:836
  367.8 2.7 shard_map.264
  370.5 1.9 collective-permute-start.21
  372.4 4.2 shard_map.269
  376.6 1.3 collective-permute-start.27
  378.8 5.4 %collective-permute-done.21 = bf16[1,256,512]{2,1,0:T(8,128)(2,1)} collective-permute-done((bf16[1,256,512]{2,1,0:T(8,128)(2,1)}, bf16[1,256,512]{2,1,0:T(8,128)(2,1)}, u32[]{:S(2)}, u32[]{:S(2)}) %collective-permute-start.21) | collective-permute-done | bytes 262176 | tf_op jit(solution)/shard_map/ppermute | solution.py:867
  386.0 1.3 copy-done
  387.3 4.2 shard_map.266
  391.5 1.2 collective-permute-start.24
  394.5 2.5 collective-permute-start.22
  397.0 8.8 %collective-permute-done.15 = f32[4,384]{1,0:T(4,128)S(1)} collective-permute-done((f32[4,384]{1,0:T(4,128)S(1)}, f32[4,384]{1,0:T(4,128)S(1)}, u32[]{:S(2)}, u32[]{:S(2)}) %collective-permute-start.15) | collective-permute-done | bytes 6176 | tf_op jit(solution)/shard_map/ppermute | solution.py:867
  406.7 3.4 shard_map.270
  413.5 3.4 shard_map.267
  418.7 11.4 %collective-permute-done.25 = bf16[1,512,512]{2,1,0:T(8,128)(2,1)S(1)} collective-permute-done((bf16[1,512,512]{2,1,0:T(8,128)(2,1)}, bf16[1,512,512]{2,1,0:T(8,128)(2,1)S(1)}, u32[]{:S(2)}, u32[]{:S(2)}) %collective-permute-start.25) | collective-permute-done | bytes 524320 | tf_op jit(solution)/shard_map/ppermute | solution.py:867
  430.6 1.3 collective-permute-start.29
  432.6 1.4 select_n.256
  434.6 21.7 %collective-permute-done.29 = bf16[512,512]{1,0:T(8,128)(2,1)S(1)} collective-permute-done((bf16[512,512]{1,0:T(8,128)(2,1)S(1)}, bf16[512,512]{1,0:T(8,128)(2,1)S(1)}, u32[]{:S(2)}, u32[]{:S(2)}) %collective-permute-start.29) | collective-permute-done | bytes 524320 | tf_op jit(solution)/shard_map/ppermute | solution.py:867
  460.7 1.2 select_n.262
  (226 shorter events, 39.0 us)
Async XLA Ops:
  7.2 4.1 copy-start.9
  7.2 86.5 %all-gather.3.cloned.1.call-start = ((), (), s32[]{:S(2)}) async-start(), calls=%async_computation | async-start | bytes 4456448 | tf_op jit(solution)/shard_map/all_gather | solution.py:943
  8.5 4.9 %copy-start.13 = (bf16[32,1024]{1,0:T(8,128)(2,1)S(1)}, bf16[32,1024]{1,0:T(8,128)(2,1)}, u32[]{:S(2)}) copy-start(bf16[32,1024]{1,0:T(8,128)(2,1)} %param.24) | copy-start | bytes 196612
  13.1 1.6 collective-permute-start.7
  13.6 3.1 copy-start.10
  16.4 212.5 %all-gather.5.cloned.1.call-start = ((), (), s32[]{:S(2)}) async-start(), calls=%async_computation.1 | async-start | bytes 8912896 | tf_op jit(solution)/shard_map/all_gather | solution.py:945
  16.9 1.9 copy-start.18
  17.0 5.1 %copy-start.14 = (s32[1,1024]{1,0:T(1,128)S(1)}, s32[1,1024]{1,0:T(1,128)}, u32[]{:S(2)}) copy-start(s32[1,1024]{1,0:T(1,128)} %param.16) | copy-start | bytes 12292
  19.0 4.2 collective-permute-start.2
  21.4 30.1 %collective-permute-start = (bf16[1024,1024]{1,0:T(8,128)(2,1)}, bf16[1024,1024]{1,0:T(8,128)(2,1)}, u32[]{:S(2)}, u32[]{:S(2)}) collective-permute-start(bf16[1024,1024]{1,0:T(8,128)(2,1)} %bitcast.mine.hidden), channel_id=1, source_target_pairs={{0,2},{1,3},{2,0},{3,1},{4,6},{5,7},{6,4},{7,5},{8,10},{9,11},{10,... | collective-permute-start | bytes 6291464 | tf_op jit(solution)/shard_map/ppermute | solution.py:867
  22.1 29.5 %collective-permute-start.1 = (bf16[1024,1024]{1,0:T(8,128)(2,1)}, bf16[1024,1024]{1,0:T(8,128)(2,1)}, u32[]{:S(2)}, u32[]{:S(2)}) collective-permute-start(bf16[1024,1024]{1,0:T(8,128)(2,1)} %bitcast.1.gmine.grads), channel_id=1, source_target_pairs={{0,2},{1,3},{2,0},{3,1},{4,6},{5,7},{6,4},{7,5},{8,10},{9,11},{10,... | collective-permute-start | bytes 6291464 | tf_op jit(solution)/shard_map/ppermute | solution.py:867
  22.1 5.1 %collective-permute-start.8 = (s32[1,1024]{1,0:T(1,128)S(1)}, s32[1,1024]{1,0:T(1,128)S(1)}, u32[]{:S(2)}, u32[]{:S(2)}) collective-permute-start(s32[1,1024]{1,0:T(1,128)S(1)} %copy-done.14), channel_id=1, source_target_pairs={{0,2},{1,3},{2,0},{3,1},{4,6},{5,7},{6,4},{7,5},{8,10},{9,11},{10,... | collective-permute-start | bytes 12296 | tf_op jit(solution)/shard_map/ppermute | solution.py:867
  23.2 2.7 collective-permute-start.3
  25.9 6.3 %collective-permute-start.4 = (bf16[4,512]{1,0:T(4,128)(2,1)S(1)}, bf16[4,512]{1,0:T(4,128)(2,1)S(1)}, u32[]{:S(2)}, u32[]{:S(2)}) collective-permute-start(bf16[4,512]{1,0:T(4,128)(2,1)S(1)} %maximum_select_fusion.6), channel_id=1, source_target_pairs={{0,4},{1,5},{2,6},{3,7},{4,0},{5,1},{6,2},{7,3},{8,12},{9,13},{10,... | collective-permute-start | bytes 12296 | tf_op jit(solution)/shard_map/ppermute | solution.py:867
  32.2 3.0 collective-permute-start.5
  35.2 13.6 %collective-permute-start.6 = (bf16[16,512]{1,0:T(8,128)(2,1)S(1)}, bf16[16,512]{1,0:T(8,128)(2,1)S(1)}, u32[]{:S(2)}, u32[]{:S(2)}) collective-permute-start(bf16[16,512]{1,0:T(8,128)(2,1)S(1)} %maximum_select_fusion.4), channel_id=1, source_target_pairs={{0,16},{1,17},{2,18},{3,19},{4,20},{5,21},{6,22},{7,23},{8,24},{9,... | collective-permute-start | bytes 49160 | tf_op jit(solution)/shard_map/ppermute | solution.py:867
  225.5 92.1 %collective-permute-start.18 = (bf16[8,256,512]{2,1,0:T(8,128)(2,1)}, bf16[8,256,512]{2,1,0:T(8,128)(2,1)S(1)}, u32[]{:S(2)}, u32[]{:S(2)}) collective-permute-start(bf16[8,256,512]{2,1,0:T(8,128)(2,1)} %get-tuple-element.81), channel_id=1, source_target_pairs={{0,4},{1,5},{2,3},{3,2},{4,0},{5,1},{6,7},{7,6},{8,12},{9,13},{10,... | collective-permute-start | bytes 6291464 | tf_op jit(solution)/shard_map/ppermute | solution.py:867
  226.7 102.7 %collective-permute-start.11 = (bf16[1024,1024]{1,0:T(8,128)(2,1)}, bf16[1024,1024]{1,0:T(8,128)(2,1)}, u32[]{:S(2)}, u32[]{:S(2)}) collective-permute-start(bf16[1024,1024]{1,0:T(8,128)(2,1)} %get-tuple-element.70), channel_id=1, source_target_pairs={{0,2},{1,3},{2,0},{3,1},{4,6},{5,7},{6,4},{7,5},{8,10},{9,11},{10,... | collective-permute-start | bytes 6291464 | tf_op jit(solution)/shard_map/ppermute | solution.py:867
  228.9 118.2 %collective-permute-start.9 = (bf16[1024,1024]{1,0:T(8,128)(2,1)}, bf16[1024,1024]{1,0:T(8,128)(2,1)}, u32[]{:S(2)}, u32[]{:S(2)}) collective-permute-start(bf16[1024,1024]{1,0:T(8,128)(2,1)} %get-tuple-element.63), channel_id=1, source_target_pairs={{0,2},{1,3},{2,0},{3,1},{4,6},{5,7},{6,4},{7,5},{8,10},{9,11},{10,... | collective-permute-start | bytes 6291464 | tf_op jit(solution)/shard_map/ppermute | solution.py:867
  316.3 32.2 %collective-permute-start.10 = (bf16[1024,1024]{1,0:T(8,128)(2,1)}, bf16[1024,1024]{1,0:T(8,128)(2,1)}, u32[]{:S(2)}, u32[]{:S(2)}) collective-permute-start(bf16[1024,1024]{1,0:T(8,128)(2,1)} %get-tuple-element.68), channel_id=1, source_target_pairs={{0,2},{1,3},{2,0},{3,1},{4,6},{5,7},{6,4},{7,5},{8,10},{9,11},{10,... | collective-permute-start | bytes 6291464 | tf_op jit(solution)/shard_map/ppermute | solution.py:867
  316.9 31.6 %collective-permute-start.12 = (bf16[1024,1024]{1,0:T(8,128)(2,1)}, bf16[1024,1024]{1,0:T(8,128)(2,1)}, u32[]{:S(2)}, u32[]{:S(2)}) collective-permute-start(bf16[1024,1024]{1,0:T(8,128)(2,1)} %get-tuple-element.72), channel_id=1, source_target_pairs={{0,2},{1,3},{2,0},{3,1},{4,6},{5,7},{6,4},{7,5},{8,10},{9,11},{10,... | collective-permute-start | bytes 6291464 | tf_op jit(solution)/shard_map/ppermute | solution.py:867
  323.7 18.7 %collective-permute-start.19 = (bf16[4,256,512]{2,1,0:T(8,128)(2,1)}, bf16[4,256,512]{2,1,0:T(8,128)(2,1)S(1)}, u32[]{:S(2)}, u32[]{:S(2)}) collective-permute-start(bf16[4,256,512]{2,1,0:T(8,128)(2,1)} %get-tuple-element.83), channel_id=1, source_target_pairs={{0,1},{1,0},{2,6},{3,7},{4,5},{5,4},{6,2},{7,3},{8,9},{9,8},{10,14... | collective-permute-start | bytes 3145736 | tf_op jit(solution)/shard_map/ppermute | solution.py:867
  329.3 43.1 %collective-permute-start.26 = (bf16[4,512,512]{2,1,0:T(8,128)(2,1)}, bf16[4,512,512]{2,1,0:T(8,128)(2,1)}, u32[]{:S(2)}, u32[]{:S(2)}) collective-permute-start(bf16[4,512,512]{2,1,0:T(8,128)(2,1)} %get-tuple-element.97), channel_id=1, source_target_pairs={{0,4},{1,5},{2,3},{3,2},{4,0},{5,1},{6,7},{7,6},{8,12},{9,13},{10,... | collective-permute-start | bytes 6291464 | tf_op jit(solution)/shard_map/ppermute | solution.py:867
  330.5 13.1 %copy-start.15 = (f32[4,1,512]{2,1,0:T(1,128)S(1)}, f32[4,1,512]{2,1,0:T(1,128)}, u32[]{:S(2)}) copy-start(f32[4,1,512]{2,1,0:T(1,128)} %get-tuple-element.76) | copy-start | bytes 24580
  342.4 42.8 %collective-permute-start.23 = (bf16[4,512,512]{2,1,0:T(8,128)(2,1)}, bf16[4,512,512]{2,1,0:T(8,128)(2,1)S(1)}, u32[]{:S(2)}, u32[]{:S(2)}) collective-permute-start(bf16[4,512,512]{2,1,0:T(8,128)(2,1)} %get-tuple-element.90), channel_id=1, source_target_pairs={{0,4},{1,5},{2,3},{3,2},{4,0},{5,1},{6,7},{7,6},{8,12},{9,13},{10,... | collective-permute-start | bytes 6291464 | tf_op jit(solution)/shard_map/ppermute | solution.py:867
  343.9 3.2 copy-start.16
  343.9 3.2 copy-start.17
  347.2 19.9 %collective-permute-start.20 = (bf16[2,256,512]{2,1,0:T(8,128)(2,1)}, bf16[2,256,512]{2,1,0:T(8,128)(2,1)S(1)}, u32[]{:S(2)}, u32[]{:S(2)}) collective-permute-start(bf16[2,256,512]{2,1,0:T(8,128)(2,1)} %get-tuple-element.85), channel_id=1, source_target_pairs={{0,8},{1,9},{2,10},{3,11},{4,12},{5,13},{6,14},{7,15},{8,0},{9,1},... | collective-permute-start | bytes 1572872 | tf_op jit(solution)/shard_map/ppermute | solution.py:867
  365.9 12.0 %collective-permute-start.13 = (f32[16,384]{1,0:T(8,128)S(1)}, f32[16,384]{1,0:T(8,128)S(1)}, u32[]{:S(2)}, u32[]{:S(2)}) collective-permute-start(f32[16,384]{1,0:T(8,128)S(1)} %slice_select_fusion), channel_id=1, source_target_pairs={{0,16},{1,17},{2,18},{3,19},{4,20},{5,21},{6,22},{7,23},{8,24},{9,... | collective-permute-start | bytes 73736 | tf_op jit(solution)/shard_map/ppermute | solution.py:867
  370.5 13.6 %collective-permute-start.21 = (bf16[1,256,512]{2,1,0:T(8,128)(2,1)}, bf16[1,256,512]{2,1,0:T(8,128)(2,1)}, u32[]{:S(2)}, u32[]{:S(2)}) collective-permute-start(bf16[1,256,512]{2,1,0:T(8,128)(2,1)} %get-tuple-element.87), channel_id=1, source_target_pairs={{0,16},{1,17},{2,18},{3,19},{4,20},{5,21},{6,22},{7,23},{8,24},{9,... | collective-permute-start | bytes 786440 | tf_op jit(solution)/shard_map/ppermute | solution.py:867
  372.4 11.7 %copy-start.11 = (bf16[1,256,512]{2,1,0:T(8,128)(2,1)S(1)}, bf16[1,256,512]{2,1,0:T(8,128)(2,1)}, u32[]{:S(2)}) copy-start(bf16[1,256,512]{2,1,0:T(8,128)(2,1)} %get-tuple-element.86) | copy-start | bytes 786436
  376.6 29.2 %collective-permute-start.27 = (bf16[2,512,512]{2,1,0:T(8,128)(2,1)}, bf16[2,512,512]{2,1,0:T(8,128)(2,1)S(1)}, u32[]{:S(2)}, u32[]{:S(2)}) collective-permute-start(bf16[2,512,512]{2,1,0:T(8,128)(2,1)} %get-tuple-element.99), channel_id=1, source_target_pairs={{0,1},{1,0},{2,6},{3,7},{4,5},{5,4},{6,2},{7,3},{8,9},{9,8},{10,14... | collective-permute-start | bytes 3145736 | tf_op jit(solution)/shard_map/ppermute | solution.py:867
  377.9 6.2 %copy-start.12 = (f32[16,384]{1,0:T(8,128)}, f32[16,384]{1,0:T(8,128)S(1)}, u32[]{:S(2)}) copy-start(f32[16,384]{1,0:T(8,128)S(1)} %select_add_fusion) | copy-start | bytes 73732
  378.6 14.1 %collective-permute-start.14 = (f32[8,384]{1,0:T(8,128)}, f32[8,384]{1,0:T(8,128)S(1)}, u32[]{:S(2)}, u32[]{:S(2)}) collective-permute-start(f32[8,384]{1,0:T(8,128)} %slice_select_fusion.1), channel_id=1, source_target_pairs={{0,8},{1,9},{2,10},{3,11},{4,12},{5,13},{6,14},{7,15},{8,0},{9,1},... | collective-permute-start | bytes 36872 | tf_op jit(solution)/shard_map/ppermute | solution.py:867
  387.3 6.4 %slice-start = ((f32[1,256,512]{2,1,0:T(8,128)}), f32[1,192,512]{2,1,0:T(8,128)S(1)}, s32[]{:S(2)}) async-start(f32[1,256,512]{2,1,0:T(8,128)} %copy-done.6), calls=%async_computation.2 | async-start | bytes 786432 | tf_op jit(solution)/shard_map/slice | solution.py:981
  391.5 21.0 %collective-permute-start.24 = (bf16[2,512,512]{2,1,0:T(8,128)(2,1)}, bf16[2,512,512]{2,1,0:T(8,128)(2,1)S(1)}, u32[]{:S(2)}, u32[]{:S(2)}) collective-permute-start(bf16[2,512,512]{2,1,0:T(8,128)(2,1)} %get-tuple-element.92), channel_id=1, source_target_pairs={{0,1},{1,0},{2,6},{3,7},{4,5},{5,4},{6,2},{7,3},{8,9},{9,8},{10,14... | collective-permute-start | bytes 3145736 | tf_op jit(solution)/shard_map/ppermute | solution.py:867
  393.4 12.3 %collective-permute-start.15 = (f32[4,384]{1,0:T(4,128)S(1)}, f32[4,384]{1,0:T(4,128)S(1)}, u32[]{:S(2)}, u32[]{:S(2)}) collective-permute-start(f32[4,384]{1,0:T(4,128)S(1)} %slice_select_fusion.2), channel_id=1, source_target_pairs={{0,4},{1,5},{2,6},{3,7},{4,0},{5,1},{6,2},{7,3},{8,12},{9,13},{10,... | collective-permute-start | bytes 18440 | tf_op jit(solution)/shard_map/ppermute | solution.py:867
  394.5 17.6 %collective-permute-start.22 = (f32[3,32,512]{2,1,0:T(8,128)}, f32[3,32,512]{2,1,0:T(8,128)S(1)}, u32[]{:S(2)}, u32[]{:S(2)}) collective-permute-start(f32[3,32,512]{2,1,0:T(8,128)} %get-tuple-element.166), channel_id=1, source_target_pairs={{0,2},{1,3},{2,0},{3,1},{4,6},{5,7},{6,4},{7,5},{8,10},{9,11},{10,... | collective-permute-start | bytes 589832 | tf_op jit(solution)/shard_map/ppermute | solution.py:867
  406.7 4.7 slice-start.1
  410.1 8.4 %collective-permute-start.28 = (bf16[1,512,512]{2,1,0:T(8,128)(2,1)}, bf16[1,512,512]{2,1,0:T(8,128)(2,1)S(1)}, u32[]{:S(2)}, u32[]{:S(2)}) collective-permute-start(bf16[1,512,512]{2,1,0:T(8,128)(2,1)} %get-tuple-element.101), channel_id=1, source_target_pairs={{0,8},{1,9},{2,10},{3,11},{4,12},{5,13},{6,14},{7,15},{8,0},{9,1},... | collective-permute-start | bytes 1572872 | tf_op jit(solution)/shard_map/ppermute | solution.py:867
  411.1 1.4 collective-permute-start.16
  413.5 5.1 %copy-start.7 = (bf16[1,512,512]{2,1,0:T(8,128)(2,1)S(1)}, bf16[1,512,512]{2,1,0:T(8,128)(2,1)}, u32[]{:S(2)}) copy-start(bf16[1,512,512]{2,1,0:T(8,128)(2,1)} %get-tuple-element.100) | copy-start | bytes 1572868
  416.9 13.2 %copy-start.8 = (bf16[1,512,512]{2,1,0:T(8,128)(2,1)S(1)}, bf16[1,512,512]{2,1,0:T(8,128)(2,1)}, u32[]{:S(2)}) copy-start(bf16[1,512,512]{2,1,0:T(8,128)(2,1)} %get-tuple-element.93) | copy-start | bytes 1572868
  416.9 13.2 %collective-permute-start.25 = (bf16[1,512,512]{2,1,0:T(8,128)(2,1)}, bf16[1,512,512]{2,1,0:T(8,128)(2,1)S(1)}, u32[]{:S(2)}, u32[]{:S(2)}) collective-permute-start(bf16[1,512,512]{2,1,0:T(8,128)(2,1)} %get-tuple-element.94), channel_id=1, source_target_pairs={{0,8},{1,9},{2,10},{3,11},{4,12},{5,13},{6,14},{7,15},{8,0},{9,1},... | collective-permute-start | bytes 1572872 | tf_op jit(solution)/shard_map/ppermute | solution.py:867
  417.4 16.6 %collective-permute-start.17 = (f32[1,384]{1,0:T(1,128)S(1)}, f32[1,384]{1,0:T(1,128)S(1)}, u32[]{:S(2)}, u32[]{:S(2)}) collective-permute-start(f32[1,384]{1,0:T(1,128)S(1)} %broadcast_select_fusion.2), channel_id=1, source_target_pairs={{0,1},{1,0},{2,3},{3,2},{4,5},{5,4},{6,7},{7,6},{8,9},{9,8},{10,11... | collective-permute-start | bytes 4616 | tf_op jit(solution)/shard_map/ppermute | solution.py:867
  430.6 25.7 %collective-permute-start.29 = (bf16[512,512]{1,0:T(8,128)(2,1)S(1)}, bf16[512,512]{1,0:T(8,128)(2,1)S(1)}, u32[]{:S(2)}, u32[]{:S(2)}) collective-permute-start(bf16[512,512]{1,0:T(8,128)(2,1)S(1)} %pad_maximum_fusion.1), channel_id=1, source_target_pairs={{0,16},{1,17},{2,18},{3,19},{4,20},{5,21},{6,22},{7,23},{8,24},{9,... | collective-permute-start | bytes 1572872 | tf_op jit(solution)/shard_map/ppermute | solution.py:867
  434.6 27.3 %copy-start.26 = (f32[32]{0:T(128)}, f32[32]{0:T(128)S(1)}, u32[]{:S(2)}) copy-start(f32[32]{0:T(128)S(1)} %get-tuple-element.214) | copy-start | bytes 388
  456.6 3.4 collective-permute-start.30
  (14 other events, 20.7 us)
Sparse Core Ops, SparseCore 0:
  16.5 77.0 all-gather.2
  97.0 111.9 all-gather.4

commit v3 on v1

--- a/solution.py
+++ b/solution.py
@@ -5,6 +5,7 @@
 from jax import lax
 from jax.experimental import pallas as pl
 from jax.experimental.pallas import tpu as pltpu
+from jax.sharding import Mesh
 from jax.sharding import PartitionSpec as P
 
 AXES = ("dp", "fsdp")
@@ -385,39 +386,876 @@
     )
 
 
+NT = (((1,), (1,)), ((), ()))
+NN = (((1,), (0,)), ((), ()))
+TN = (((0,), (0,)), ((), ()))
+PAIR = 2 * HEAD
+ROWS = 256
+TOKENS = 512
+
+
+def mul(left, right, dims):
+    return lax.dot_general(left, right, dims, preferred_element_type=jnp.float32)
+
+
+def params(mebibytes):
+    return pltpu.CompilerParams(vmem_limit_bytes=mebibytes << 20)
+
+
+def cost(flops, moved, special=0):
+    return pl.CostEstimate(flops=int(flops), transcendentals=int(special), bytes_accessed=int(moved))
+
+
+def fixed(shape, at=None):
+    place = (0,) * len(shape) if at is None else at
+    return pl.BlockSpec(shape, lambda *_: place, pipeline_mode=pl.Buffered(1))
+
+
+def middle_swap(value):
+    quarter = (lax.broadcasted_iota(jnp.int32, value.shape, 1) % 128) // 32
+    width = value.shape[1]
+    up, down = pltpu.roll(value, width - 32, 1), pltpu.roll(value, 32, 1)
+    return jnp.where(quarter == 1, up, jnp.where(quarter == 2, down, value))
+
+
+def norm_kernel(mine, theirs, gmine, gtheirs, scales, one, two, grads):
+    def work(source, cotangent):
+        value = source[...].astype(jnp.float32)
+        center = value - jnp.mean(value, axis=1, keepdims=True)
+        spread = jnp.mean(center * center, axis=1, keepdims=True)
+        hat = middle_swap(center * lax.rsqrt(spread + norm_eps))
+        table = scales[...].astype(jnp.float32)
+        one[...] = (hat * table[0:1] + table[1:2]).astype(jnp.bfloat16)
+        two[...] = (hat * table[2:3] + table[3:4]).astype(jnp.bfloat16)
+        grads[...] = cotangent[...]
+
+    first = pl.program_id(0) == 0
+    pl.when(first)(lambda: work(mine, gmine))
+    pl.when(jnp.logical_not(first))(lambda: work(theirs, gtheirs))
+
+
+def norms(mine, theirs, gmine, gtheirs, scales):
+    length, width = mine.shape
+    block = (ROWS, width)
+    steps = length // ROWS
+    own = pl.BlockSpec(block, lambda s, i: (jnp.where(s == 0, i, steps - 1), 0))
+    other = pl.BlockSpec(block, lambda s, i: (jnp.where(s == 0, 0, i), 0))
+    out = pl.BlockSpec(block, lambda s, i: (s * steps + i, 0))
+    shape = jax.ShapeDtypeStruct((2 * length, width), jnp.bfloat16)
+    return pl.pallas_call(
+        norm_kernel,
+        grid=(2, steps),
+        in_specs=[own, other, own, other, fixed(scales.shape)],
+        out_specs=[out] * 3,
+        out_shape=[shape] * 3,
+        compiler_params=params(16),
+        cost_estimate=cost(40 * length * width, 20 * length * width),
+    )(mine, theirs, gmine, gtheirs, scales)
+
+
+def turn(value, cosine, sine):
+    lane = lax.broadcasted_iota(jnp.int32, value.shape, 1) % HEAD
+    half = ROT // 2
+    up, down = pltpu.roll(value, value.shape[1] - half, 1), pltpu.roll(value, half, 1)
+    return value * cosine + jnp.where(lane < half, up, down) * sine
+
+
+def chosen(place, chip, near, far, *index):
+    spot, half = place[chip], near.shape[0]
+    return jnp.where(spot < half, near[(spot % half, *index)], far[(spot % half, *index)])
+
+
+def arrange(place, half, weights, ordered, ordered_proj):
+    chips = 2 * weights[0].shape[0]
+    for part in range(3):
+        near, far = weights[2 * part : 2 * part + 2]
+        rows, width = near.shape[1:]
+        for chip in range(chips):
+            block = chosen(place, chip, near, far)
+            ordered[chip * rows : (chip + 1) * rows, part * width : (part + 1) * width] = block
+    near, far = weights[6:]
+    below = near.shape[1] // 4
+    for chip in range(chips // 2):
+        block = chosen(place, half * chips // 2 + chip, near, far)
+        for n in range(4):
+            ordered_proj[chip * below : (chip + 1) * below, n * width : (n + 1) * width] = block[n * below : (n + 1) * below]
+
+
+def weight_specs(weights, first):
+    chips, _, width = weights[0].shape
+    found = [fixed((chips, 64, width), (0, first + part, 0)) for part in range(3) for _ in weights]
+    return found + [fixed((chips, 128, width))] * 2
+
+
+def weight_scratch(weights):
+    chips, _, width = weights[0].shape
+    return [pltpu.VMEM((128 * chips, 3 * width), jnp.bfloat16), pltpu.VMEM((32 * chips, 4 * width), jnp.bfloat16)]
+
+
+def project_kernel(half, place, normed, grads, *refs):
+    weights = refs[:8]
+    bias, cosine, sine, segments, out, ordered, ordered_proj = refs[8:]
+    width = out.shape[-1]
+
+    @pl.when(pl.program_id(0) == 0)
+    def _():
+        arrange(place, half, weights, ordered, ordered_proj)
+
+    for part in range(3):
+        columns = slice(part * width, (part + 1) * width)
+        value = mul(normed[...], ordered[:, columns], NN) + bias[part].astype(jnp.float32)
+        if part == 2:
+            out[part] = value.astype(out.dtype)
+            continue
+        for at in range(0, width, PAIR):
+            turned = turn(value[:, at : at + PAIR], cosine[...], sine[...])
+            out[part, :, at : at + PAIR] = (turned * (HEAD ** (-0.5) if part == 0 else 1.0)).astype(out.dtype)
+    valid = (segments[...] != DOCS - 1).astype(jnp.float32)
+    out[3] = (mul(grads[...], ordered_proj[...], NT) * valid).astype(out.dtype)
+
+
+def project(half, place, normed, grads, weights, first, proj, bias, cosine, sine, segments):
+    tokens, model = normed.shape
+    width = weights[0].shape[-1]
+    rows = lambda n: pl.BlockSpec((TOKENS, n), lambda i, *_: (i, 0))
+    return pl.pallas_call(
+        partial(project_kernel, half),
+        grid_spec=pltpu.PrefetchScalarGridSpec(
+            num_scalar_prefetch=1,
+            grid=(tokens // TOKENS,),
+            in_specs=[rows(model), rows(model)]
+            + weight_specs(weights, first)
+            + [fixed(bias.shape), rows(PAIR), rows(PAIR), rows(1)],
+            out_specs=pl.BlockSpec((4, TOKENS, width), lambda i, *_: (0, i, 0)),
+            scratch_shapes=weight_scratch(weights),
+        ),
+        out_shape=jax.ShapeDtypeStruct((4, tokens, width), jnp.bfloat16),
+        compiler_params=params(20),
+        cost_estimate=cost(8 * tokens * model * width, 6 * tokens * model),
+    )(place, normed, grads, *weights * 3, *proj, bias, cosine, sine, segments)
+
+
+def attention_kernel(
+    q_ref, k_ref, v_ref, g_ref, cosine, sine, seg_row, seg_col, *rest
+):
+    out, d_out, mask, dk_sum, dv_sum = rest[-5:]
+    length = q_ref.shape[1]
+    blocks = length // ROWS
+
+    @pl.when(pl.program_id(0) == 0)
+    def _():
+        for block in range(blocks):
+            start = block * ROWS
+            end = start + ROWS
+            key_pos = lax.broadcasted_iota(jnp.int32, (ROWS, end), 1)
+            query_pos = lax.broadcasted_iota(jnp.int32, (ROWS, end), 0) + start
+            allowed = (key_pos <= query_pos) & (seg_col[start:end, :] == seg_row[0, :, :end])
+            mask[start:end, :end] = jnp.where(allowed, 0.0, masked_score)
+
+    lane = lax.broadcasted_iota(jnp.int32, (ROWS, PAIR), 1)
+    for block in range(blocks - 1, -1, -1):
+        start = block * ROWS
+        end = start + ROWS
+        rows = slice(start, end)
+        keys, values = k_ref[0, :end, :], v_ref[0, :end, :]
+        query, grads = q_ref[0, rows, :], g_ref[0, rows, :]
+        hide = mask[rows, :end]
+        pieces = []
+        for head in range(2):
+            mine = lane < HEAD if head == 0 else lane >= HEAD
+            own_query = jnp.where(mine, query, jnp.zeros_like(query))
+            own_grads = jnp.where(mine, grads, jnp.zeros_like(grads))
+            scores = mul(own_query, keys, NT) + hide
+            exponent = jnp.exp(scores - jnp.max(scores, axis=1, keepdims=True))
+            probs = exponent * (1.0 / jnp.sum(exponent, axis=1, keepdims=True))
+            low = probs.astype(jnp.bfloat16)
+            mixed = mul(low, values, NN)
+            d_probs = mul(own_grads, values, NT)
+            inner = jnp.sum(own_grads.astype(jnp.float32) * mixed, axis=1, keepdims=True)
+            d_scores = (probs * (d_probs - inner)).astype(jnp.bfloat16)
+            pieces.append((mixed, mul(d_scores, keys, NN)))
+            d_keys, d_values = mul(d_scores, own_query, TN), mul(low, own_grads, TN)
+            if block == blocks - 1 and head == 0:
+                dk_sum[:end, :] = d_keys
+                dv_sum[:end, :] = d_values
+            else:
+                dk_sum[:end, :] += d_keys
+                dv_sum[:end, :] += d_values
+        mine = lane < HEAD
+        valid = (seg_col[rows, :] != DOCS - 1).astype(jnp.float32)
+        out[rows, :] = (jnp.where(mine, pieces[0][0], pieces[1][0]) * valid).astype(out.dtype)
+        d_query = turn(jnp.where(mine, pieces[0][1], pieces[1][1]), cosine[rows, :], -sine[rows, :])
+        d_out[0, rows, :] = (d_query * HEAD ** (-0.5)).astype(d_out.dtype)
+    d_out[1] = turn(dk_sum[...], cosine[...], -sine[...]).astype(d_out.dtype)
+    d_out[2] = dv_sum[...].astype(d_out.dtype)
+
+
+def attention(sequence, parts, cosine, sine, segments, before):
+    length = segments.shape[1]
+    tokens, width = parts.shape[1:]
+    part = lambda p: pl.BlockSpec((1, length, PAIR), lambda j: (p, sequence, j))
+    table = lambda n: pl.BlockSpec((length, n), lambda j: (sequence, 0))
+    anywhere = pl.BlockSpec(memory_space=pl.ANY)
+    return pl.pallas_call(
+        attention_kernel,
+        grid=(width // PAIR,),
+        in_specs=[
+            part(0),
+            part(1),
+            part(2),
+            part(3),
+            table(PAIR),
+            table(PAIR),
+            pl.BlockSpec((1, 1, length), lambda j: (sequence, 0, 0)),
+            table(1),
+        ]
+        + [anywhere] * len(before),
+        out_specs=[
+            pl.BlockSpec((length, PAIR), lambda j: (sequence, j)),
+            pl.BlockSpec((3, length, PAIR), lambda j: (0, sequence, j)),
+        ],
+        out_shape=[
+            jax.ShapeDtypeStruct((tokens, width), jnp.bfloat16),
+            jax.ShapeDtypeStruct((3, tokens, width), jnp.bfloat16),
+        ],
+        input_output_aliases={8 + n: n for n in range(len(before))},
+        scratch_shapes=[pltpu.VMEM((length, length), jnp.float32)] + [pltpu.VMEM((length, PAIR), jnp.float32)] * 2,
+        compiler_params=params(20),
+        cost_estimate=cost(24 * tokens * length * width, 8 * tokens * width, tokens * length * width // 200),
+    )(*[parts] * 4, cosine, sine, segments[:, None, :], segments.reshape(tokens, 1), *before)
+
+
+def put_out(staged, keep, send, done):
+    half = keep.shape[0]
+    copies = [
+        pltpu.make_async_copy(staged.at[pl.ds(n * half, half)], target, done.at[n])
+        for n, target in enumerate((keep, send))
+    ]
+    for copy in copies:
+        copy.start()
+    for copy in copies:
+        copy.wait()
+
+
+def attention_grads_kernel(place, *refs):
+    normed, d_mixed = refs[:2]
+    more = refs[2:-7]
+    keep, send, sums, totals, proj_total, staged, done = refs[-7:]
+    step, last = pl.program_id(0), pl.num_programs(0) - 1
+    width = d_mixed.shape[-1]
+    chips = staged.shape[0]
+    parts = totals.shape[0]
+    rows = totals.shape[1] // chips
+
+    @pl.when(step == 0)
+    def _():
+        totals[...] = jnp.zeros_like(totals)
+        sums[...] = jnp.zeros_like(sums)
+        if more:
+            proj_total[...] = jnp.zeros_like(proj_total)
+
+    for part in range(parts):
+        totals[part] += mul(normed[...], d_mixed[part], TN)
+        sums[part] += jnp.sum(d_mixed[part].astype(jnp.float32), axis=0, keepdims=True)
+    if more:
+        for n, attended in enumerate(more[:2]):
+            proj_total[n * width : (n + 1) * width, :] += mul(attended[...], more[2][...], TN)
+
+    @pl.when(step == last)
+    def _():
+        for chip in range(chips):
+            spot = place[chip]
+            for part in range(parts):
+                change = totals[part, chip * rows : (chip + 1) * rows, :]
+                staged[spot, part * rows : (part + 1) * rows, :] = change.astype(staged.dtype)
+            if more:
+                below = proj_total.shape[0] // chips
+                for n in range(4):
+                    change = proj_total[chip * below : (chip + 1) * below, n * width : (n + 1) * width]
+                    start = parts * rows + n * below
+                    staged[spot, start : start + below, :] = change.astype(staged.dtype)
+        put_out(staged, keep, send, done)
+
+
+def attention_grads(place, normed, d_mixed, more):
+    tokens, model = normed.shape
+    parts, _, width = d_mixed.shape
+    chips = place.shape[0]
+    rows = parts * model // chips + (4 * 2 * width // chips if more else 0)
+    token = lambda n: pl.BlockSpec((TOKENS, n), lambda i, *_: (i, 0))
+    half = jax.ShapeDtypeStruct((chips // 2, rows, width), jnp.bfloat16)
+    anywhere = pl.BlockSpec(memory_space=pl.ANY)
+    return pl.pallas_call(
+        attention_grads_kernel,
+        grid_spec=pltpu.PrefetchScalarGridSpec(
+            num_scalar_prefetch=1,
+            grid=(tokens // TOKENS,),
+            in_specs=[token(model), pl.BlockSpec((parts, TOKENS, width), lambda i, *_: (0, i, 0))]
+            + ([token(width), token(width), token(model)] if more else []),
+            out_specs=[anywhere, anywhere, pl.BlockSpec((parts, 1, width), lambda i, *_: (0, 0, 0))],
+            scratch_shapes=[
+                pltpu.VMEM((parts, model, width), jnp.float32),
+                pltpu.VMEM((2 * width, model), jnp.float32),
+                pltpu.VMEM((chips, rows, width), jnp.bfloat16),
+                pltpu.SemaphoreType.DMA((2,)),
+            ],
+        ),
+        out_shape=[half, half, jax.ShapeDtypeStruct((parts, 1, width), jnp.float32)],
+        compiler_params=params(26),
+        cost_estimate=cost(8 * tokens * model * width, 6 * tokens * model),
+    )(place, normed, d_mixed, *more)
+
+
+def share_out(step, steps, before, mine, send, value):
+    for own, ref, earlier in ((True, mine, before[:1]), (False, send, before[1:])):
+
+        @pl.when((step < steps // 2) == own)
+        def _():
+            total = value
+            for one in earlier:
+                total = total + one[...].astype(jnp.float32)
+            ref[...] = total.astype(ref.dtype)
+
+
+def attention_back_kernel(half, place, d_mixed, attended, *refs):
+    weights, before = refs[:8], refs[8:-6]
+    d_mine, d_send, p_mine, p_send, ordered, ordered_proj = refs[-6:]
+    step, steps = pl.program_id(0), pl.num_programs(0)
+
+    @pl.when(step == 0)
+    def _():
+        arrange(place, half, weights, ordered, ordered_proj)
+
+    change = jnp.concatenate([d_mixed[part] for part in range(3)], axis=1)
+    share_out(step, steps, before[:2], d_mine, d_send, mul(change, ordered[...], NT))
+    share_out(step, steps, before[2:], p_mine, p_send, mul(attended[...], ordered_proj[...], NN))
+
+
+def attention_back(half, place, d_mixed, attended, weights, first, proj, before):
+    parts, tokens, width = d_mixed.shape
+    model = 128 * weights[0].shape[0]
+    steps = tokens // TOKENS
+    own = pl.BlockSpec((TOKENS, model), lambda i, *_: (jnp.minimum(i, steps // 2 - 1), 0))
+    other = pl.BlockSpec((TOKENS, model), lambda i, *_: (jnp.maximum(i - steps // 2, 0), 0))
+    shape = jax.ShapeDtypeStruct((tokens // 2, model), jnp.bfloat16)
+    return pl.pallas_call(
+        partial(attention_back_kernel, half),
+        grid_spec=pltpu.PrefetchScalarGridSpec(
+            num_scalar_prefetch=1,
+            grid=(steps,),
+            in_specs=[
+                pl.BlockSpec((parts, TOKENS, width), lambda i, *_: (0, i, 0)),
+                pl.BlockSpec((TOKENS, width), lambda i, *_: (i, 0)),
+            ]
+            + weight_specs(weights, first)
+            + [own, other] * (len(before) // 2),
+            out_specs=[own, other] * 2,
+            scratch_shapes=weight_scratch(weights),
+        ),
+        out_shape=[shape] * 4,
+        compiler_params=params(24),
+        cost_estimate=cost(8 * tokens * model * width, 8 * tokens * model),
+    )(place, d_mixed, attended, *weights * 3, *proj, *before)
+
+
+def forward_kernel(place, normed, grads, near, far, bias, *refs):
+    earlier, refs = refs[:-18], refs[-18:]
+    keep, send, sums = refs[:3]
+    outs = refs[3:7]
+    own_normed, own_grads, up, down, after, d_before, results, staged, arrived, shared, left = refs[7:18]
+    tokens, model = own_normed.shape
+    hidden = up.shape[1]
+    half_tokens = tokens // 2
+    rows = near.shape[1] // 2
+    chips = 2 * near.shape[0]
+    blocks = tokens // ROWS
+
+    def pieces(chip):
+        at = pl.ds(chip * rows, rows)
+        return ((0, up.at[at], 2 * chip), (rows, down.at[at], 2 * chip + 1))
+
+    def row_loads(block):
+        at = pl.ds(block * ROWS, ROWS)
+        return [
+            pltpu.make_async_copy(source.at[at], target.at[at], arrived.at[2 * chips + 2 * block + n])
+            for n, (source, target) in enumerate(((normed, own_normed), (grads, own_grads)))
+        ]
+
+    loads = [pltpu.make_async_copy(ref, results.at[n], shared.at[n]) for n, ref in enumerate(earlier)]
+    for chip in range(chips):
+        spot = place[chip]
+        for start, target, n in pieces(chip):
+            for own, source in ((True, near), (False, far)):
+
+                @pl.when((spot < chips // 2) == own)
+                def _():
+                    held = source.at[spot % (chips // 2), pl.ds(start, rows)]
+                    pltpu.make_async_copy(held, target, arrived.at[n]).start()
+
+    for block in range(blocks):
+        for load in row_loads(block):
+            load.start()
+    for load in loads:
+        load.start()
+    for chip in range(chips):
+        for start, target, n in pieces(chip):
+            pltpu.make_async_copy(near.at[0, pl.ds(start, rows)], target, arrived.at[n]).wait()
+    offset = bias[...].astype(jnp.float32)
+    bias_total = jnp.zeros_like(offset)
+    for block in range(blocks):
+        at = slice(block * ROWS, (block + 1) * ROWS)
+        for load in row_loads(block):
+            load.wait()
+        before = mul(own_normed[at, :], up[...], NN) + offset
+        change = mul(own_grads[at, :], down[...], NT)
+        share = 0.5 + 0.5 * lax.erf(before * 0.7071067811865476)
+        density = jnp.exp(-0.5 * before * before) * 0.3989422804014327
+        after[at, :] = (before * share).astype(after.dtype)
+        low = (change * (share + before * density)).astype(d_before.dtype)
+        d_before[at, :] = low
+        bias_total += jnp.sum(low.astype(jnp.float32), axis=0, keepdims=True)
+    sums[...] = bias_total
+    for load in loads:
+        load.wait()
+    stores = []
+    for block in range(blocks):
+        at = slice(block * ROWS, (block + 1) * ROWS)
+        side = 0 if block * ROWS < half_tokens else 1
+        own = pl.ds(block * ROWS - side * half_tokens, ROWS)
+        for which, value in enumerate((mul(after[at, :], down[...], NN), mul(d_before[at, :], up[...], NT))):
+            n = 2 * which + side
+            if n < len(earlier):
+                value += results[n, own, :].astype(jnp.float32)
+            results[n, own, :] = value.astype(results.dtype)
+            store = pltpu.make_async_copy(results.at[n, own], outs[n].at[own], left.at[2 + 2 * block + which])
+            store.start()
+            stores.append(store)
+    tile = 256
+    for start in range(0, hidden, tile):
+        change = mul(own_normed[...], d_before[:, start : start + tile], TN).astype(staged.dtype)
+        for chip in range(chips):
+            staged[place[chip], :rows, start : start + tile] = change[chip * rows : (chip + 1) * rows]
+        change = mul(after[:, start : start + tile], own_grads[...], TN).astype(staged.dtype)
+        for n in range(tile // rows):
+            staged[place[start // rows + n], rows:, :] = change[n * rows : (n + 1) * rows]
+    half = keep.shape[0]
+    for n, target in enumerate((keep, send)):
+        store = pltpu.make_async_copy(staged.at[pl.ds(n * half, half)], target, left.at[n])
+        store.start()
+        stores.append(store)
+    for store in stores:
+        store.wait()
+
+
+def forward_chunk(place, normed, grads, weights, bias, earlier):
+    tokens, model = normed.shape
+    chips, both_rows, hidden = weights[0].shape
+    chips *= 2
+    low = lambda *shape: pltpu.VMEM(shape, jnp.bfloat16)
+    blocks = jax.ShapeDtypeStruct((chips // 2, both_rows, model), jnp.bfloat16)
+    anywhere = pl.BlockSpec(memory_space=pl.ANY)
+    share = jax.ShapeDtypeStruct((tokens // 2, model), jnp.bfloat16)
+    small = pl.BlockSpec((1, hidden), lambda i, *_: (0, 0))
+    counts = (2 * chips + 2 * (tokens // ROWS), 4, 2 + 2 * (tokens // ROWS))
+    return pl.pallas_call(
+        forward_kernel,
+        grid_spec=pltpu.PrefetchScalarGridSpec(
+            num_scalar_prefetch=1,
+            grid=(1,),
+            in_specs=[anywhere] * 4 + [small] + [anywhere] * len(earlier),
+            out_specs=[anywhere, anywhere, small] + [anywhere] * 4,
+            scratch_shapes=[
+                low(tokens, model),
+                low(tokens, model),
+                low(model, hidden),
+                low(hidden, model),
+                low(tokens, hidden),
+                low(tokens, hidden),
+                low(4, tokens // 2, model),
+                low(chips, both_rows, model),
+            ]
+            + [pltpu.SemaphoreType.DMA((count,)) for count in counts],
+        ),
+        out_shape=[blocks, blocks, jax.ShapeDtypeStruct((1, hidden), jnp.float32)] + [share] * 4,
+        compiler_params=params(44),
+        cost_estimate=cost(12 * tokens * model * hidden, 16 * tokens * model, 2 * tokens * hidden),
+    )(place, normed, grads, *weights, bias, *earlier)
+
+
+def both_of(left, right):
+    return left[...].astype(jnp.float32) + right[...].astype(jnp.float32)
+
+
+def finish_out_kernel(hidden, mine, come, scales, layer_out):
+    table = scales[...].astype(jnp.float32)
+    total = both_of(mine, come) + table[0:1] + table[1:2]
+    layer_out[...] = (hidden[...].astype(jnp.float32) + total).astype(layer_out.dtype)
+
+
+def finish_grad_kernel(hidden, grads, one_mine, one_come, two_mine, two_come, scales, input_grad, sums):
+    value = hidden[...].astype(jnp.float32)
+    cotangent = grads[...].astype(jnp.float32)
+    table = scales[...].astype(jnp.float32)
+    center = value - jnp.mean(value, axis=1, keepdims=True)
+    scale = lax.rsqrt(jnp.mean(center * center, axis=1, keepdims=True) + norm_eps)
+    hat = center * scale
+    one, two = middle_swap(both_of(one_mine, one_come)), middle_swap(both_of(two_mine, two_come))
+    gained = one * table[0:1] + two * table[1:2]
+    mean = jnp.mean(gained, axis=1, keepdims=True)
+    slope = jnp.mean(gained * hat, axis=1, keepdims=True)
+    input_grad[...] = (cotangent + (gained - mean - hat * slope) * scale).astype(input_grad.dtype)
+
+    @pl.when(pl.program_id(0) == 0)
+    def _():
+        sums[...] = jnp.zeros_like(sums)
+
+    for row, column in enumerate((one * hat, one, two * hat, two, cotangent)):
+        sums[row : row + 1, :] += jnp.sum(column, axis=0, keepdims=True)
+
+
+def finish(kernel, arrays, scales, with_sums):
+    length, width = arrays[0].shape
+    block = pl.BlockSpec((ROWS, width), lambda i: (i, 0))
+    shape = jax.ShapeDtypeStruct((length, width), jnp.bfloat16)
+    more = [pl.BlockSpec((8, width), lambda i: (0, 0))] if with_sums else []
+    return pl.pallas_call(
+        kernel,
+        grid=(length // ROWS,),
+        in_specs=[block] * len(arrays) + [fixed(scales.shape)],
+        out_specs=[block] + more,
+        out_shape=[shape] + [jax.ShapeDtypeStruct((8, width), jnp.float32)] * len(more),
+        compiler_params=params(16),
+        cost_estimate=cost(40 * length * width, 2 * (len(arrays) + 1) * length * width),
+    )(*arrays, scales)
+
+
+BITS = {"y": 0, "core": 1, "x": 2, "z_low": 3, "z_high": 4}
+SPLIT = ("zx", "core", "y")
+CORES = ("core", "core")
+STAGES = (("x", "y"), ("y", "x"), ("z_low", "z_low"), ("z_high", "z_high"))
+
+
+class Pairs:
+    def __init__(self, total):
+        self.total = total
+
+    def here(self):
+        y = lax.axis_size("y")
+        return (lax.axis_index("zx") * 2 + lax.axis_index("core")) * y + lax.axis_index("y")
+
+    def bit(self, name):
+        return (self.here() >> BITS[name]) & 1
+
+    def swap(self, value, names):
+        moves = []
+        for device in range(self.total):
+            name = names[(device >> BITS["core"]) & 1]
+            moves.append((device, device ^ (1 << BITS[name])))
+        return lax.ppermute(value, SPLIT, moves)
+
+    def places(self):
+        chip = jnp.arange(self.total // 2, dtype=jnp.int32)
+        bits = {"y": chip & 1, "x": (chip >> 1) & 1, "z_low": (chip >> 2) & 1, "z_high": (chip >> 3) & 1}
+        differs = {name: bits[name] ^ self.bit(name) for name in bits}
+        place = jnp.zeros_like(chip)
+        for first, second in STAGES:
+            place = 2 * place + jnp.where(lax.axis_index("core") == 0, differs[first], differs[second])
+        return place
+
+
+class Sum:
+    def __init__(self, pairs, keep, send):
+        self.pairs, self.arrays, self.stage = pairs, (keep, send), 0
+
+    def ready(self, arrays):
+        if self.stage == 0:
+            return arrays
+        keep, come = arrays
+        half = keep.shape[0] // 2
+        return add_low(keep[:half], come[:half]), add_low(keep[half:], come[half:])
+
+    def move(self, arrays):
+        keep, send = arrays
+        self.arrays = keep, self.pairs.swap(send, STAGES[self.stage])
+        self.stage += 1
+
+    def result(self):
+        keep, come = self.arrays
+        return keep[0].astype(jnp.float32) + come[0].astype(jnp.float32)
+
+
+class Gather:
+    def __init__(self, pairs, own):
+        self.pairs, self.arrays, self.stage = pairs, (own[None],), 0
+
+    def ready(self, arrays):
+        return arrays if self.stage == 0 else (jnp.concatenate(arrays),)
+
+    def move(self, arrays):
+        self.stage += 1
+        self.arrays = arrays[0], self.pairs.swap(arrays[0], STAGES[-self.stage])
+
+    def result(self):
+        return self.arrays
+
+
+class Trade:
+    def __init__(self, pairs, *arrays):
+        self.pairs, self.arrays, self.stage = pairs, arrays, 0
+
+    def ready(self, arrays):
+        return arrays
+
+    def move(self, arrays):
+        if self.stage == 0:
+            arrays = tuple(self.pairs.swap(array, CORES) for array in arrays)
+        self.arrays = arrays
+        self.stage += 1
+
+    def result(self):
+        return self.arrays
+
+
+def hold(value, tasks):
+    value, arrays = lax.optimization_barrier((value, [task.arrays for task in tasks]))
+    for task, own in zip(tasks, arrays):
+        task.arrays = tuple(own)
+    return value
+
+
+def tick(after, value, *tasks, done=()):
+    if after is not None:
+        after = hold(after, tasks + tuple(done))
+    for task in tasks:
+        task.arrays = task.ready(task.arrays)
+    after, value = hold((after, value), tasks)
+    for task in tasks:
+        task.move(task.arrays)
+    return after, value
+
+
+def add_low(left, right):
+    return (left.astype(jnp.float32) + right.astype(jnp.float32)).astype(jnp.bfloat16)
+
+
+def wide_angles(segments):
+    position = lax.broadcasted_iota(jnp.int32, segments.shape, 1)
+    change = jnp.concatenate([jnp.ones_like(segments[:, :1], jnp.bool_), segments[:, 1:] != segments[:, :-1]], axis=1)
+    place = position - lax.cummax(jnp.where(change, position, 0), axis=1)
+    lane = jnp.arange(PAIR) % HEAD
+    half = ROT // 2
+    freqs = 10000.0 ** (-((lane % half) * 2).astype(jnp.float32) / ROT)
+    freqs = jnp.where(lane < ROT, freqs, 0.0)
+    theta = place.reshape(-1, 1).astype(jnp.float32) * freqs
+    return jnp.cos(theta), jnp.sin(theta) * jnp.where(lane < half, -1.0, 1.0)
+
+
+def pick(value, which, axis):
+    return lax.dynamic_index_in_dim(value, which, axis, keepdims=False)
+
+
+def paired_body(
+    pairs,
+    hidden_in,
+    segment_ids,
+    out_grad,
+    norm1_gain,
+    norm1_bias,
+    norm2_gain,
+    norm2_bias,
+    qkv_weight,
+    qkv_bias,
+    proj_weight,
+    proj_bias,
+    up_weight,
+    up_bias,
+    down_weight,
+    down_bias,
+):
+    core = lax.axis_index("core")
+    heads = HEADS // 2
+    rows, model = qkv_weight.shape[0], proj_weight.shape[1]
+    width = heads * HEAD // 2
+    unit = down_weight.shape[0] // 2
+    hidden, grads = hidden_in[0], out_grad[0]
+
+    def columns(which):
+        taken = pick(qkv_weight.reshape(rows, 3, heads, 2, HEAD), which, 3).reshape(rows, 3 * 2 * width)
+        more = pick(up_weight.reshape(rows, heads, 2, 2, 2, unit), which, 2).transpose(0, 3, 1, 2, 4).reshape(rows, -1)
+        return jnp.concatenate([taken, more], axis=1)
+
+    theirs = pairs.swap(columns(1 - core), CORES)
+    mine = columns(core)
+    both = jnp.where(core == 0, jnp.stack([mine, theirs]), jnp.stack([theirs, mine])).reshape(2 * rows, -1)
+    low_qkv = both[:, : 6 * width].reshape(2 * rows, 3, 2, width).transpose(2, 1, 0, 3)
+    low_proj = proj_weight.reshape(rows, 4, width).transpose(1, 0, 2).reshape(2, 2 * rows, width)
+    low_up = both[:, 6 * width :].reshape(2 * rows, 2, -1).transpose(1, 0, 2)
+    low_down = down_weight.reshape(2, unit, model)
+
+    other, other_grads = pairs.swap(hidden, CORES), pairs.swap(grads, CORES)
+    segments = jnp.concatenate([segment_ids, pairs.swap(segment_ids, CORES)])
+    column = segments.reshape(-1, 1)
+    cosine, sine = wide_angles(segments)
+    place = pairs.places()
+
+    small = (norm1_gain, norm1_bias, norm2_gain, norm2_bias, qkv_bias, proj_bias, up_bias, down_bias)
+    line = jnp.concatenate(small)
+    line = jnp.pad(line, (0, -line.shape[0] % 128))
+    come = pairs.swap(line, CORES)
+    lines = Gather(pairs, jnp.where(core == 0, jnp.stack([line, come]), jnp.stack([come, line])).reshape(-1))
+    first = Gather(pairs, jnp.concatenate([low_proj, low_qkv[0]]).reshape(-1, width))
+    chunks = [Gather(pairs, jnp.concatenate([low_up[h], low_down[h]])) for h in range(2)]
+    second = Gather(pairs, low_qkv[1].reshape(-1, width))
+    tick(None, (), first, lines)
+    tick(None, (), first, lines)
+    tick(None, (), first, lines, chunks[0])
+    tick(None, (), first, lines, chunks[0])
+    w_first = first.result()
+    table = jnp.concatenate(lines.result())[place]
+    table = table.reshape(heads, 2, 2, -1).swapaxes(1, 2).reshape(pairs.total, -1)
+    spread, at = [], 0
+    for entry in small:
+        size = entry.shape[0]
+        spread.append(table[:, at : at + size].reshape(-1))
+        at += size
+    gain_one, shift_one, gain_two, shift_two, b_qkv, b_proj, b_up, b_down = spread
+    own_bias = pick(b_qkv.reshape(3, heads, 2, HEAD), core, 2).reshape(3, 2, 1, width)
+    own_up_bias = pick(b_up.reshape(heads, 2, 2, 2, unit), core, 1).transpose(2, 0, 1, 3).reshape(2, 1, -1)
+    scales = jnp.stack([gain_one, shift_one, gain_two, shift_two])
+    normed_one, normed_two, both_grads = norms(
+        hidden, other, grads, other_grads, scales.reshape(4, -1, 2, 2, rows).swapaxes(2, 3).reshape(4, model)
+    )
+
+    (normed_one, cosine, sine), _ = tick((normed_one, cosine, sine), (), chunks[0], chunks[1])
+    parts = project(
+        0, place, normed_one, both_grads, w_first, 2, w_first, own_bias[:, 0], cosine, sine, column
+    )
+    parts, _ = tick(parts, (), chunks[0], chunks[1])
+    before = attention(0, parts, cosine, sine, segments, ())
+    before, parts = tick(before, parts, chunks[1])
+    attended_one, d_mixed = attention(1, parts, cosine, sine, segments, before)
+    (attended_one, d_mixed), _ = tick((attended_one, d_mixed), (), chunks[1], second)
+    keep, send, qkv_sums_one = attention_grads(place, normed_one, d_mixed, ())
+    sum_one = Sum(pairs, keep, send)
+    _, d_mixed = tick(None, d_mixed, sum_one, second)
+    d1, d1_send, out, out_send = attention_back(0, place, d_mixed, attended_one, w_first, 2, w_first, ())
+
+    sum_forward, up_sums = [], []
+    before = (out, out_send)
+    for chunk in range(2):
+        before, normed_two = tick(before, normed_two, sum_one, second, *sum_forward)
+        keep, send, sums, *before = forward_chunk(
+            place, normed_two, both_grads, chunks[chunk].result(), own_up_bias[chunk], before
+        )
+        up_sums.append(sums)
+        sum_forward.append(Sum(pairs, keep, send))
+    out, out_send, d2, d2_send = before
+    (out, out_send, d2_send), normed_one = tick(
+        (out, out_send, d2_send), normed_one, sum_one, sum_forward[0], done=(second,)
+    )
+    w_second = second.result()
+    trade_two = Trade(pairs, d2_send)
+    parts = project(
+        1, place, normed_one, both_grads, w_second, 0, w_first, own_bias[:, 1], cosine, sine, column
+    )
+    parts, _ = tick(parts, (), sum_forward[0], sum_forward[1], trade_two, done=(sum_one,))
+    before = attention(0, parts, cosine, sine, segments, ())
+    before, parts = tick(before, parts, sum_forward[0], done=(trade_two,))
+    attended_two, d_mixed = attention(1, parts, cosine, sine, segments, before)
+    (attended_two, d_mixed), _ = tick((attended_two, d_mixed), (), sum_forward[1], done=sum_forward[:1])
+    keep, send, qkv_sums_two = attention_grads(place, normed_one, d_mixed, (attended_one, attended_two, both_grads))
+    sum_two = Sum(pairs, keep, send)
+    qkv_sums_two, d_mixed = tick(qkv_sums_two, d_mixed, sum_forward[1], sum_two)
+    back = attention_back(1, place, d_mixed, attended_two, w_second, 0, w_first, (d1, d1_send, out, out_send))
+    (d1, d1_send, out, out_send), _ = tick(back, (), sum_forward[1], sum_two)
+    trade = Trade(pairs, d1_send, out_send)
+    tick(None, (), trade)
+    d1_come, out_come = trade.result()
+    input_grad, sums = finish(
+        finish_grad_kernel,
+        [hidden, grads, d1, d1_come, d2, *trade_two.result()],
+        jnp.stack([gain_one, gain_two]),
+        True,
+    )
+    (input_grad, sums), out = tick((input_grad, sums), out, sum_two, done=sum_forward[1:])
+    layer_out = finish(finish_out_kernel, [hidden, out, out_come], jnp.stack([b_proj, b_down]), False)[0]
+    layer_out, _ = tick(layer_out, (), sum_two)
+    low_qkv_one, low_qkv_two = sum_one.result(), sum_two.result()
+    low_forward = [task.result() for task in sum_forward]
+
+    def whole_rows(value):
+        mine, come = pick(value, core, 0), pairs.swap(pick(value, 1 - core, 0), CORES)
+        return jnp.where(core == 0, jnp.stack([mine, come], 2), jnp.stack([come, mine], 2))
+
+    third = 3 * 2 * rows
+    both = jnp.stack([low_qkv_one, low_qkv_two[:third]]).reshape(2, 3, 2, rows, heads // 2, HEAD)
+    grad_qkv = whole_rows(both.transpose(2, 3, 1, 0, 4, 5).reshape(2, rows, 3 * heads, HEAD)).reshape(rows, -1)
+    grad_proj = low_qkv_two[third:].reshape(4, rows, width).transpose(1, 0, 2).reshape(rows, model)
+    ups = jnp.stack([entry[: 2 * rows] for entry in low_forward]).reshape(2, 2, rows, heads, 2, unit)
+    grad_up = whole_rows(ups.transpose(1, 2, 3, 4, 0, 5).reshape(2, rows, heads, 4 * unit)).reshape(rows, -1)
+    grad_down = jnp.concatenate([entry[2 * rows :] for entry in low_forward])
+
+    def both_cores(own):
+        own = own[:, None]
+        none = jnp.zeros_like(own)
+        return jnp.where(core == 0, jnp.concatenate([own, none], axis=1), jnp.concatenate([none, own], axis=1)).reshape(-1)
+
+    sum_qkv = jnp.stack([qkv_sums_one.reshape(3, -1), qkv_sums_two.reshape(3, -1)], axis=1)
+    sum_up = jnp.stack([entry.reshape(heads, 2, unit) for entry in up_sums], axis=2)
+    entries = [
+        sums[0],
+        sums[1],
+        sums[2],
+        sums[3],
+        both_cores(sum_qkv.reshape(-1, HEAD)),
+        sums[4],
+        both_cores(sum_up.reshape(heads, -1)),
+    ]
+    table = jnp.concatenate([entry.reshape(pairs.total, -1) for entry in entries], axis=1)
+    table = jnp.pad(table, ((0, 0), (0, -table.shape[1] % 128)))
+    for name in reversed(BITS):
+        upper = pairs.bit(name) == 1
+        half = table.shape[0] // 2
+        send = jnp.where(upper, table[:half], table[half:])
+        table = jnp.where(upper, table[half:], table[:half]) + pairs.swap(send, (name, name))
+    outs, at = [], 0
+    for entry in entries:
+        size = entry.shape[0] // pairs.total
+        outs.append(table[0, at : at + size])
+        at += size
+    return (
+        layer_out[None],
+        input_grad[None],
+        outs[0],
+        outs[1],
+        outs[2],
+        outs[3],
+        grad_qkv,
+        outs[4],
+        grad_proj,
+        outs[5],
+        grad_up,
+        outs[6],
+        grad_down,
+        outs[5],
+    )
+
+
+def placed(axes):
+    rows, flat = P(axes, None), P(axes)
+    whole = P(axes, None, None)
+    inside = (whole, rows, whole) + (flat,) * 4 + (rows, flat) * 4
+    outside = (whole, whole) + (flat,) * 4 + (rows, flat) * 4
+    return inside, outside
+
+
 def solution(mesh):
-    in_specs = (
-        P(("dp", "fsdp"), None, None),
-        P(("dp", "fsdp"), None),
-        P(("dp", "fsdp"), None, None),
-        P(("dp", "fsdp")),
-        P(("dp", "fsdp")),
-        P(("dp", "fsdp")),
-        P(("dp", "fsdp")),
-        P(("dp", "fsdp"), None),
-        P(("dp", "fsdp")),
-        P(("dp", "fsdp"), None),
-        P(("dp", "fsdp")),
-        P(("dp", "fsdp"), None),
-        P(("dp", "fsdp")),
-        P(("dp", "fsdp"), None),
-        P(("dp", "fsdp")),
-    )
-    out_specs = (
-        P(("dp", "fsdp"), None, None),
-        P(("dp", "fsdp"), None, None),
-        P(("dp", "fsdp")),
-        P(("dp", "fsdp")),
-        P(("dp", "fsdp")),
-        P(("dp", "fsdp")),
-        P(("dp", "fsdp"), None),
-        P(("dp", "fsdp")),
-        P(("dp", "fsdp"), None),
-        P(("dp", "fsdp")),
-        P(("dp", "fsdp"), None),
-        P(("dp", "fsdp")),
-        P(("dp", "fsdp"), None),
-        P(("dp", "fsdp")),
-    )
-    grid = Grid((mesh.shape["dp"], mesh.shape["fsdp"]))
-    return jax.shard_map(partial(body, grid), mesh=mesh, in_specs=in_specs, out_specs=out_specs, check_vma=False)
+    dp, fsdp = mesh.shape["dp"], mesh.shape["fsdp"]
+    if (dp, fsdp) == (16, 2):
+        split = Mesh(mesh.devices.reshape(dp // 2, 2, fsdp), SPLIT)
+        inside, outside = placed(SPLIT)
+        step = partial(paired_body, Pairs(dp * fsdp))
+        return jax.shard_map(step, mesh=split, in_specs=inside, out_specs=outside, check_vma=False)
+    inside, outside = placed(AXES)
+    step = partial(body, Grid((dp, fsdp)))
+    return jax.shard_map(step, mesh=mesh, in_specs=inside, out_specs=outside, check_vma=False)

time: 890 us -> 426 us (0.48); the launches traced: 875 us -> 420 us
  matrix products: 378 us -> 0 us
  other arithmetic: 132 us -> 37.4 us
  Pallas kernels: 125 us -> 215 us
  waiting for transfers between devices: 128 us -> 50.3 us
  local copies, waits for them, and re-layouts: 46.2 us -> 67.4 us
  between operations: 14.7 us -> 2.2 us
    dot_general x24 -> x0, matrix products: 378 us -> none  [the longest x1 51.3 us: body(): jnp.dot(normed_two, w_up, preferred_element_type=jnp.float32)]
    all_gather x4 -> x0, waiting for transfers between devices: 96.4 us -> none  [body(): lax.all_gather(entry, AXES, axis=0, tiled=True)]
    pallas_call x24 -> x15, Pallas kernels: 125 us -> 215 us  [the longest x2 73 us: forward_chunk(): pl.pallas_call(forward_kernel, grid_spec=pltpu.PrefetchScalarGridSpec(num...]
    reduce_sum x7 -> x0, other arithmetic: 50.7 us -> none  [the longest x2 31.2 us: attend_forward(): total = jnp.sum(exponent, axis=-1, keepdims=True)]
    convert_element_type x7 -> x13, other arithmetic: 61.9 us -> 13.7 us  [the longest x12 13.6 us: add_low(): (left.astype(jnp.float32) + right.astype(jnp.float32)).astype(jnp.bfloat16)]
    ppermute x30 -> x51, waiting for transfers between devices: 29.5 us -> 50.3 us  [swap(): return lax.ppermute(value, SPLIT, moves)]
    unnamed x139 -> x140, local copies, waits for them, and re-layouts: 15 us -> 35.1 us
    add x1 -> x0, local copies, waits for them, and re-layouts: 12.7 us -> none  [body(): jnp.dot(normed_one, w_qkv, preferred_element_type=jnp.float32)]
  transfers between devices with their start and end apart: 34 -> 51, of which waited for: 9 -> 12; matrix products, arithmetic and copies ran while one was open for 62% -> 12% of each run, Pallas kernels for 14% -> 51%
where the time goes in v3:
time: 426 us; the launch traced here: 420 us
  Pallas kernels  215 us (50%)
  local copies, waits for them, and re-layouts  67.4 us (16%)
  waiting for transfers between devices  50.3 us (12%)
  starting transfers between devices  47.6 us (11%)
  other arithmetic  37.4 us (9%)
    pallas_call x2, Pallas kernels, forward_chunk(): pl.pallas_call(forward_kernel, grid_spec=pltpu.PrefetchScalarGridSpec(num...  73 us
    pallas_call x4, Pallas kernels, attention(): pl.pallas_call(attention_kernel, grid=(width // PAIR,), in_specs=[part(0)...  68.8 us
    ppermute x51, waiting for transfers between devices, swap(): return lax.ppermute(value, SPLIT, moves)  50.3 us
    ppermute x51, starting transfers between devices, swap(): return lax.ppermute(value, SPLIT, moves)  47.6 us
    unnamed x140, local copies, waits for them, and re-layouts  35.1 us
    pallas_call x2, Pallas kernels, attention_back(): pl.pallas_call(partial(attention_back_kernel, half), grid_spec=pltpu.Pref...  18.3 us
    pallas_call x2, Pallas kernels, finish(): pl.pallas_call(kernel, grid=(length // ROWS,), in_specs=[block] * len(arr...  16.8 us
    pallas_call x2, Pallas kernels, attention_grads(): pl.pallas_call(attention_grads_kernel, grid_spec=pltpu.PrefetchScalarGrid...  14.5 us
  transfers between devices with their start and end apart: 51, of which 12 were waited for; matrix products, arithmetic and copies ran while one was open for 12% of the time, Pallas kernels for 51%

profile of v3, /device:TPU:1, one launch (start us, length us, event | category | flops | bytes accessed | tf_op | source)
XLA Modules:
  0.0 420.1 jit_solution(2094911564159124768)
XLA Ops:
  0.7 5.5 %concatenate.96 = bf16[416]{0:T(512)(128)(2,1)S(1)} concatenate(bf16[32]{0:T(256)(128)(2,1)} %param.18, bf16[32]{0:T(256)(128)(2,1)} %param.19, bf16[32]{0:T(256)(128)(2,1)} %param.20, bf16[32]{0:T(256)(128)(2,1)} %param.21, bf16[96]{0:T(256)(128)(2,1)} %param.23, bf16[32]{0:T(256)(128)(2,1)} %param.25, bf16[128]{0:T(256)(128)(2,1)} %param.27, bf16[32]{0:T(256)(128)(2,1)} %param.29), dimensions={0} | concatenate | bytes 1664 | tf_op jit(solution)/shard_map/concatenate | solution.py:1102
  7.9 2.6 dynamic-slice_reduce_fusion.1
  17.2 3.8 collective-permute-start.5
  22.0 8.8 %collective-permute-done.4 = bf16[1,320,256]{2,1,0:T(8,128)(2,1)S(1)} collective-permute-done((bf16[1,320,256]{2,1,0:T(8,128)(2,1)S(1)}, bf16[1,320,256]{2,1,0:T(8,128)(2,1)S(1)}, u32[]{:S(2)}, u32[]{:S(2)}) %collective-permute-start.4) | collective-permute-done | bytes 163872 | tf_op jit(solution)/shard_map/ppermute | solution.py:954
  32.6 6.5 %collective-permute-done.7 = bf16[2,1024]{1,0:T(2,128)(2,1)S(1)} collective-permute-done((bf16[2,1024]{1,0:T(2,128)(2,1)S(1)}, bf16[2,1024]{1,0:T(2,128)(2,1)S(1)}, u32[]{:S(2)}, u32[]{:S(2)}) %collective-permute-start.7) | collective-permute-done | bytes 4128 | tf_op jit(solution)/shard_map/ppermute | solution.py:954
  42.5 5.6 %fusion = (f32[2048,128]{1,0:T(8,128)}, f32[2048,128]{1,0:T(8,128)}) fusion(f32[128]{0:T(128)S(1)} %get-tuple-element.520, f32[128]{0:T(128)S(1)} %get-tuple-element.521, f32[2048]{0:T(1024)S(1)} %fusion.5), kind=kLoop, calls=%fused_computation.12 | loop fusion | flops 524288 | bytes 2106368 | tf_op jit(solution)/shard_map/mul | solution.py:1050
  48.1 6.8 %collective-permute-done.10 = bf16[1,128,1024]{2,1,0:T(8,128)(2,1)S(1)} collective-permute-done((bf16[1,128,1024]{2,1,0:T(8,128)(2,1)S(1)}, bf16[1,128,1024]{2,1,0:T(8,128)(2,1)S(1)}, u32[]{:S(2)}, u32[]{:S(2)}) %collective-permute-start.10) | collective-permute-done | bytes 262176 | tf_op jit(solution)/shard_map/ppermute | solution.py:954
  59.9 10.6 %shard_map.254 = (bf16[2048,1024]{1,0:T(8,128)(2,1)S(1)}, bf16[2048,1024]{1,0:T(8,128)(2,1)S(1)}, bf16[2048,1024]{1,0:T(8,128)(2,1)S(1)}) custom-call(bf16[1024,1024]{1,0:T(8,128)(2,1)} %bitcast.mine.hidden, bf16[1024,1024]{1,0:T(8,128)(2,1)} %collective-permute-done.theirs, bf16[1024,1024]{1,0:T(8,128)(2,1)} %bitcast.1.gmine.grads, ...), custom_call_target="tpu_custom_call" | custom-call | flops 41943040 | bytes 20971520 | tf_op jit(solution)/shard_map/pallas_call | solution.py:445
  70.5 1.9 copy-done
  72.5 2.0 copy-done.4
  74.4 1.9 copy-done.30
  76.4 2.1 pad_maximum_fusion.3
  81.1 2.4 collective-permute-start.16
  83.6 2.2 copy-done.1
  85.8 2.2 copy-done.5
  91.6 6.6 %shard_map.255.q_ref.k_ref.v_ref.g_ref = bf16[4,2048,256]{2,1,0:T(8,128)(2,1)S(1)} custom-call(s32[16]{0:T(128)S(1)} %xor_add_fusion.place, bf16[2048,1024]{1,0:T(8,128)(2,1)S(1)} %copy-done.1, bf16[2048,1024]{1,0:T(8,128)(2,1)S(1)} %copy-done.5, bf16[8,320,256]{2,1,0:T(8,128)(2,1)S(1)} %pad_maximum_fusion.2.refs_0_.refs_2_.refs_4_.refs_6_, ...), custom_call_target="tpu_custom_call" | custom-call | flops 4294967296 | bytes 12582912 | tf_op jit(solution)/shard_map/pallas_call | solution.py:521
  98.3 3.1 pad_maximum_fusion.near
  103.7 17.2 %shard_map.256 = (bf16[2048,256]{1,0:T(8,128)(2,1)S(1)}, bf16[3,2048,256]{2,1,0:T(8,128)(2,1)S(1)}) custom-call(bf16[4,2048,256]{2,1,0:T(8,128)(2,1)S(1)} %shard_map.255.q_ref.k_ref.v_ref.g_ref, bf16[4,2048,256]{2,1,0:T(8,128)(2,1)S(1)} %shard_map.255.q_ref.k_ref.v_ref.g_ref, bf16[4,2048,256]{2,1,0:T(8,128)(2,1)S(1)} %shard_map.255.q_ref.k_ref.v_ref.g_ref, ...), custom_call_target="tpu_custom_call" | custom-call | flops 12884901888 | bytes 4194304 | tf_op jit(solution)/shard_map/pallas_call | solution.py:599
  122.4 17.3 %shard_map.257 = (bf16[2048,256]{1,0:T(8,128)(2,1)S(1)}, bf16[3,2048,256]{2,1,0:T(8,128)(2,1)S(1)}) custom-call(bf16[4,2048,256]{2,1,0:T(8,128)(2,1)S(1)} %shard_map.255.q_ref.k_ref.v_ref.g_ref, bf16[4,2048,256]{2,1,0:T(8,128)(2,1)S(1)} %shard_map.255.q_ref.k_ref.v_ref.g_ref, ...), custom_call_target="tpu_custom_call", output_to_operand_aliasing={{0}: (8, {}), {1}: (9, {})} | custom-call | flops 12884901888 | bytes 4194304 | tf_op jit(solution)/shard_map/pallas_call | solution.py:599
  139.6 3.1 collective-permute-done.18
  145.7 6.5 %shard_map.258 = (bf16[8,192,256]{2,1,0:T(8,128)(2,1)S(1)}, bf16[8,192,256]{2,1,0:T(8,128)(2,1)}, f32[3,1,256]{2,1,0:T(1,128)S(1)}) custom-call(s32[16]{0:T(128)S(1)} %xor_add_fusion.place, bf16[2048,1024]{1,0:T(8,128)(2,1)S(1)} %copy-done.2, bf16[3,2048,256]{2,1,0:T(8,128)(2,1)S(1)} %get-tuple-element.285.refs_1_.d_mixed), custom_call_target="tpu_custom_call" | custom-call | flops 4294967296 | bytes 12582912 | tf_op jit(solution)/shard_map/pallas_call | solution.py:688
  154.8 1.9 copy-done.35
  157.9 8.4 %shard_map.259 = (bf16[1024,1024]{1,0:T(8,128)(2,1)S(1)}, bf16[1024,1024]{1,0:T(8,128)(2,1)S(1)}, bf16[1024,1024]{1,0:T(8,128)(2,1)S(1)}, bf16[1024,1024]{1,0:T(8,128)(2,1)S(1)}) custom-call(s32[16]{0:T(128)S(1)} %xor_add_fusion.place, bf16[3,2048,256]{2,1,0:T(8,128)(2,1)S(1)} %copy-done.35, bf16[2048,256]{1,0:T(8,128)(2,1)S(1)} %copy-done.39, ...), custom_call_target="tpu_custom_call" | custom-call | flops 4294967296 | bytes 16777216 | tf_op jit(solution)/shard_map/pallas_call | solution.py:741
  170.4 1.9 add_convert_fusion.10
  173.8 36.5 %shard_map.260 = (bf16[8,128,1024]{2,1,0:T(8,128)(2,1)S(1)}, bf16[8,128,1024]{2,1,0:T(8,128)(2,1)}, f32[1,1024]{1,0:T(1,128)S(1)}, bf16[1024,1024]{1,0:T(8,128)(...) custom-call(s32[16]{0:T(128)S(1)} %xor_add_fusion.place, ...), custom_call_target="tpu_custom_call" | custom-call | flops 25769803776 | bytes 33554432 | tf_op jit(solution)/shard_map/pallas_call | solution.py:860
  214.8 36.4 %shard_map.261 = (bf16[8,128,1024]{2,1,0:T(8,128)(2,1)S(1)}, bf16[8,128,1024]{2,1,0:T(8,128)(2,1)S(1)}, f32[1,1024]{1,0:T(1,128)S(1)}, bf16[1024,1024]{1,0:T(8,1...) custom-call(s32[16]{0:T(128)S(1)} %xor_add_fusion.place, ...), custom_call_target="tpu_custom_call" | custom-call | flops 25769803776 | bytes 33554432 | tf_op jit(solution)/shard_map/pallas_call | solution.py:860
  253.4 3.3 add_convert_fusion.2
  258.0 2.2 copy-done.6
  260.2 6.6 %shard_map.262.q_ref.k_ref.v_ref.g_ref = bf16[4,2048,256]{2,1,0:T(8,128)(2,1)S(1)} custom-call(s32[16]{0:T(128)S(1)} %xor_add_fusion.place, bf16[2048,1024]{1,0:T(8,128)(2,1)S(1)} %copy-done.3, bf16[2048,1024]{1,0:T(8,128)(2,1)S(1)} %copy-done.6, bf16[8,192,256]{2,1,0:T(8,128)(2,1)S(1)} %pad_maximum_fusion.5.refs_0_.refs_2_.refs_4_, ...), custom_call_target="tpu_custom_call" | custom-call | flops 4294967296 | bytes 12582912 | tf_op jit(solution)/shard_map/pallas_call | solution.py:521
  266.9 3.8 collective-permute-done.29
  271.2 3.6 collective-permute-start.32
  276.1 17.0 %shard_map.263 = (bf16[2048,256]{1,0:T(8,128)(2,1)S(1)}, bf16[3,2048,256]{2,1,0:T(8,128)(2,1)S(1)}) custom-call(bf16[4,2048,256]{2,1,0:T(8,128)(2,1)S(1)} %shard_map.262.q_ref.k_ref.v_ref.g_ref, bf16[4,2048,256]{2,1,0:T(8,128)(2,1)S(1)} %shard_map.262.q_ref.k_ref.v_ref.g_ref, bf16[4,2048,256]{2,1,0:T(8,128)(2,1)S(1)} %shard_map.262.q_ref.k_ref.v_ref.g_ref, ...), custom_call_target="tpu_custom_call" | custom-call | flops 12884901888 | bytes 4194304 | tf_op jit(solution)/shard_map/pallas_call | solution.py:599
  295.1 17.4 %shard_map.264 = (bf16[2048,256]{1,0:T(8,128)(2,1)S(1)}, bf16[3,2048,256]{2,1,0:T(8,128)(2,1)S(1)}) custom-call(bf16[4,2048,256]{2,1,0:T(8,128)(2,1)S(1)} %shard_map.262.q_ref.k_ref.v_ref.g_ref, bf16[4,2048,256]{2,1,0:T(8,128)(2,1)S(1)} %shard_map.262.q_ref.k_ref.v_ref.g_ref, ...), custom_call_target="tpu_custom_call", output_to_operand_aliasing={{0}: (8, {}), {1}: (9, {})} | custom-call | flops 12884901888 | bytes 4194304 | tf_op jit(solution)/shard_map/pallas_call | solution.py:599
  315.7 8.0 %shard_map.265 = (bf16[8,320,256]{2,1,0:T(8,128)(2,1)S(1)}, bf16[8,320,256]{2,1,0:T(8,128)(2,1)S(1)}, f32[3,1,256]{2,1,0:T(1,128)S(1)}) custom-call(s32[16]{0:T(128)S(1)} %xor_add_fusion.place, bf16[2048,1024]{1,0:T(8,128)(2,1)S(1)} %copy-done.3, bf16[3,2048,256]{2,1,0:T(8,128)(2,1)S(1)} %get-tuple-element.394.refs_1_.d_mixed, ...), custom_call_target="tpu_custom_call" | custom-call | flops 4294967296 | bytes 12582912 | tf_op jit(solution)/shard_map/pallas_call | solution.py:688
  323.7 4.6 %collective-permute-done.35 = bf16[4,128,1024]{2,1,0:T(8,128)(2,1)S(1)} collective-permute-done((bf16[4,128,1024]{2,1,0:T(8,128)(2,1)S(1)}, bf16[4,128,1024]{2,1,0:T(8,128)(2,1)S(1)}, u32[]{:S(2)}, u32[]{:S(2)}) %collective-permute-start.35) | collective-permute-done | bytes 1048608 | tf_op jit(solution)/shard_map/ppermute | solution.py:954
  330.0 9.8 %shard_map.266 = (bf16[1024,1024]{1,0:T(8,128)(2,1)S(1)}, bf16[1024,1024]{1,0:T(8,128)(2,1)}, bf16[1024,1024]{1,0:T(8,128)(2,1)S(1)}, bf16[1024,1024]{1,0:T(8,128)(2,1)S(1)}) custom-call(s32[16]{0:T(128)S(1)} %xor_add_fusion.place, bf16[3,2048,256]{2,1,0:T(8,128)(2,1)S(1)} %get-tuple-element.394.refs_1_.d_mixed, ...), custom_call_target="tpu_custom_call" | custom-call | flops 4294967296 | bytes 16777216 | tf_op jit(solution)/shard_map/pallas_call | solution.py:741
  341.1 4.3 %collective-permute-done.37 = bf16[8,320,256]{2,1,0:T(8,128)(2,1)S(1)} collective-permute-done((bf16[8,320,256]{2,1,0:T(8,128)(2,1)S(1)}, bf16[8,320,256]{2,1,0:T(8,128)(2,1)S(1)}, u32[]{:S(2)}, u32[]{:S(2)}) %collective-permute-start.37) | collective-permute-done | bytes 1310752 | tf_op jit(solution)/shard_map/ppermute | solution.py:954
  347.8 2.6 collective-permute-start.38
  357.8 2.1 stack.121
  364.9 12.1 %shard_map.267 = (bf16[1024,1024]{1,0:T(8,128)(2,1)}, f32[8,1024]{1,0:T(8,128)S(1)}) custom-call(bf16[1024,1024]{1,0:T(8,128)(2,1)} %bitcast.mine.hidden, bf16[1024,1024]{1,0:T(8,128)(2,1)} %bitcast.1.gmine.grads, bf16[1024,1024]{1,0:T(8,128)(2,1)S(1)} %copy-done.21, bf16[1024,1024]{1,0:T(8,128)(2,1)} %collective-permute-done.38.one_come, ...), custom_call_target="tpu_custom_call" | custom-call | flops 41943040 | bytes 14680064 | tf_op jit(solution)/shard_map/pallas_call | solution.py:921
  376.9 2.1 add_convert_fusion.12
  384.7 2.1 maximum_bitcast_fusion
  386.8 2.2 reshape.338
  389.4 1.8 collective-permute-start.50
  391.6 2.7 collective-permute-start.46
  394.3 1.8 pad_maximum_fusion.11
  396.4 4.8 %shard_map.268 = bf16[1024,1024]{1,0:T(8,128)(2,1)} custom-call(bf16[1024,1024]{1,0:T(8,128)(2,1)} %bitcast.mine.hidden, bf16[1024,1024]{1,0:T(8,128)(2,1)S(1)} %copy-done.17, bf16[1024,1024]{1,0:T(8,128)(2,1)} %collective-permute-done.41.come, bf16[2,1024]{1,0:T(2,128)(2,1)S(1)} %pad_maximum_fusion.24.scales), custom_call_target="tpu_custom_call" | custom-call | flops 41943040 | bytes 8388608 | tf_op jit(solution)/shard_map/pallas_call | solution.py:921
  403.6 9.5 %collective-permute-done.48 = bf16[1,320,256]{2,1,0:T(8,128)(2,1)S(1)} collective-permute-done((bf16[1,320,256]{2,1,0:T(8,128)(2,1)S(1)}, bf16[1,320,256]{2,1,0:T(8,128)(2,1)S(1)}, u32[]{:S(2)}, u32[]{:S(2)}) %collective-permute-start.48) | collective-permute-done | bytes 163872 | tf_op jit(solution)/shard_map/ppermute | solution.py:954
  (378 shorter events, 89.5 us)
Async XLA Ops:
  6.1 8.2 %collective-permute-start.3 = (bf16[512]{0:T(512)(128)(2,1)S(1)}, bf16[512]{0:T(512)(128)(2,1)S(1)}, u32[]{:S(2)}, u32[]{:S(2)}) collective-permute-start(bf16[512]{0:T(512)(128)(2,1)S(1)} %pad.9), channel_id=1, source_target_pairs={{0,2},{1,3},{2,0},{3,1},{4,6},{5,7},{6,4},{7,5},{8,10},{9,11},{10,... | collective-permute-start | bytes 3080 | tf_op jit(solution)/shard_map/ppermute | solution.py:954
  6.2 8.1 %collective-permute-start.12 = (s32[1,1024]{1,0:T(1,128)}, s32[1,1024]{1,0:T(1,128)S(1)}, u32[]{:S(2)}, u32[]{:S(2)}) collective-permute-start(s32[1,1024]{1,0:T(1,128)} %param.16), channel_id=1, source_target_pairs={{0,2},{1,3},{2,0},{3,1},{4,6},{5,7},{6,4},{7,5},{8,10},{9,11},{10,... | collective-permute-start | bytes 12296 | tf_op jit(solution)/shard_map/ppermute | solution.py:954
  12.3 3.7 collective-permute-start.2
  12.5 47.4 %collective-permute-start = (bf16[1024,1024]{1,0:T(8,128)(2,1)}, bf16[1024,1024]{1,0:T(8,128)(2,1)}, u32[]{:S(2)}, u32[]{:S(2)}) collective-permute-start(bf16[1024,1024]{1,0:T(8,128)(2,1)} %bitcast.mine.hidden), channel_id=1, source_target_pairs={{0,2},{1,3},{2,0},{3,1},{4,6},{5,7},{6,4},{7,5},{8,10},{9,11},{10,... | collective-permute-start | bytes 6291464 | tf_op jit(solution)/shard_map/ppermute | solution.py:954
  12.9 46.9 %collective-permute-start.1 = (bf16[1024,1024]{1,0:T(8,128)(2,1)}, bf16[1024,1024]{1,0:T(8,128)(2,1)}, u32[]{:S(2)}, u32[]{:S(2)}) collective-permute-start(bf16[1024,1024]{1,0:T(8,128)(2,1)} %bitcast.1.gmine.grads), channel_id=1, source_target_pairs={{0,2},{1,3},{2,0},{3,1},{4,6},{5,7},{6,4},{7,5},{8,10},{9,11},{10,... | collective-permute-start | bytes 6291464 | tf_op jit(solution)/shard_map/ppermute | solution.py:954
  17.2 4.8 %collective-permute-start.5 = (bf16[1,1024]{1,0:T(2,128)(2,1)S(1)}, bf16[1,1024]{1,0:T(2,128)(2,1)S(1)}, u32[]{:S(2)}, u32[]{:S(2)}) collective-permute-start(bf16[1,1024]{1,0:T(2,128)(2,1)S(1)} %bitcast.167), channel_id=1, source_target_pairs={{0,16},{1,17},{2,18},{3,19},{4,20},{5,21},{6,22},{7,23},{8,24},{9,... | collective-permute-start | bytes 6152 | tf_op jit(solution)/shard_map/ppermute | solution.py:954
  21.0 9.9 %collective-permute-start.4 = (bf16[1,320,256]{2,1,0:T(8,128)(2,1)S(1)}, bf16[1,320,256]{2,1,0:T(8,128)(2,1)S(1)}, u32[]{:S(2)}, u32[]{:S(2)}) collective-permute-start(bf16[1,320,256]{2,1,0:T(8,128)(2,1)S(1)} %bitcast.145), channel_id=1, source_target_pairs={{0,16},{1,17},{2,18},{3,19},{4,20},{5,21},{6,22},{7,23},{8,24},{9,... | collective-permute-start | bytes 491528 | tf_op jit(solution)/shard_map/ppermute | solution.py:954
  30.9 8.2 %collective-permute-start.6 = (bf16[2,320,256]{2,1,0:T(8,128)(2,1)S(1)}, bf16[2,320,256]{2,1,0:T(8,128)(2,1)S(1)}, u32[]{:S(2)}, u32[]{:S(2)}) collective-permute-start(bf16[2,320,256]{2,1,0:T(8,128)(2,1)S(1)} %pad_maximum_fusion.13), channel_id=1, source_target_pairs={{0,8},{1,9},{2,10},{3,11},{4,12},{5,13},{6,14},{7,15},{8,0},{9,1},... | collective-permute-start | bytes 983048 | tf_op jit(solution)/shard_map/ppermute | solution.py:954
  31.0 8.1 %collective-permute-start.7 = (bf16[2,1024]{1,0:T(2,128)(2,1)S(1)}, bf16[2,1024]{1,0:T(2,128)(2,1)S(1)}, u32[]{:S(2)}, u32[]{:S(2)}) collective-permute-start(bf16[2,1024]{1,0:T(2,128)(2,1)S(1)} %pad_maximum_fusion.22), channel_id=1, source_target_pairs={{0,8},{1,9},{2,10},{3,11},{4,12},{5,13},{6,14},{7,15},{8,0},{9,1},... | collective-permute-start | bytes 12296 | tf_op jit(solution)/shard_map/ppermute | solution.py:954
  39.2 8.9 %collective-permute-start.9 = (bf16[4,1024]{1,0:T(4,128)(2,1)S(1)}, bf16[4,1024]{1,0:T(4,128)(2,1)S(1)}, u32[]{:S(2)}, u32[]{:S(2)}) collective-permute-start(bf16[4,1024]{1,0:T(4,128)(2,1)S(1)} %pad_maximum_fusion.20), channel_id=1, source_target_pairs={{0,1},{1,0},{2,6},{3,7},{4,5},{5,4},{6,2},{7,3},{8,9},{9,8},{10,14... | collective-permute-start | bytes 24584 | tf_op jit(solution)/shard_map/ppermute | solution.py:954
  40.5 14.4 %collective-permute-start.10 = (bf16[1,128,1024]{2,1,0:T(8,128)(2,1)S(1)}, bf16[1,128,1024]{2,1,0:T(8,128)(2,1)S(1)}, u32[]{:S(2)}, u32[]{:S(2)}) collective-permute-start(bf16[1,128,1024]{2,1,0:T(8,128)(2,1)S(1)} %maximum_bitcast_fusion.1), channel_id=1, source_target_pairs={{0,16},{1,17},{2,18},{3,19},{4,20},{5,21},{6,22},{7,23},{8,24},{9,... | collective-permute-start | bytes 786440 | tf_op jit(solution)/shard_map/ppermute | solution.py:954
  42.2 12.7 %collective-permute-start.8 = (bf16[4,320,256]{2,1,0:T(8,128)(2,1)S(1)}, bf16[4,320,256]{2,1,0:T(8,128)(2,1)S(1)}, u32[]{:S(2)}, u32[]{:S(2)}) collective-permute-start(bf16[4,320,256]{2,1,0:T(8,128)(2,1)S(1)} %pad_maximum_fusion.7), channel_id=1, source_target_pairs={{0,1},{1,0},{2,6},{3,7},{4,5},{5,4},{6,2},{7,3},{8,9},{9,8},{10,14... | collective-permute-start | bytes 1966088 | tf_op jit(solution)/shard_map/ppermute | solution.py:954
  56.4 20.0 %collective-permute-start.13 = (bf16[2,128,1024]{2,1,0:T(8,128)(2,1)S(1)}, bf16[2,128,1024]{2,1,0:T(8,128)(2,1)}, u32[]{:S(2)}, u32[]{:S(2)}) collective-permute-start(bf16[2,128,1024]{2,1,0:T(8,128)(2,1)S(1)} %pad_maximum_fusion.8), channel_id=1, source_target_pairs={{0,8},{1,9},{2,10},{3,11},{4,12},{5,13},{6,14},{7,15},{8,0},{9,1},... | collective-permute-start | bytes 1572872 | tf_op jit(solution)/shard_map/ppermute | solution.py:954
  56.5 27.1 %collective-permute-start.14 = (bf16[8,320,256]{2,1,0:T(8,128)(2,1)S(1)}, bf16[8,320,256]{2,1,0:T(8,128)(2,1)S(1)}, u32[]{:S(2)}, u32[]{:S(2)}) collective-permute-start(bf16[8,320,256]{2,1,0:T(8,128)(2,1)S(1)} %pad_maximum_fusion.2.refs_0_.refs_2_.refs_4_.refs_6_), channel_id=1, source_target_pairs={{0,4},{1,5},{2,3},{3,2},{4,0},{5,1},{6,7},{7,6},{8,12},{9,13},{10,... | collective-permute-start | bytes 3932168 | tf_op jit(solution)/shard_map/ppermute | solution.py:954
  78.5 19.8 %collective-permute-start.15 = (bf16[4,128,1024]{2,1,0:T(8,128)(2,1)}, bf16[4,128,1024]{2,1,0:T(8,128)(2,1)}, u32[]{:S(2)}, u32[]{:S(2)}) collective-permute-start(bf16[4,128,1024]{2,1,0:T(8,128)(2,1)} %pad_maximum_fusion.3), channel_id=1, source_target_pairs={{0,1},{1,0},{2,6},{3,7},{4,5},{5,4},{6,2},{7,3},{8,9},{9,8},{10,14... | collective-permute-start | bytes 3145736 | tf_op jit(solution)/shard_map/ppermute | solution.py:954
  81.1 17.1 %collective-permute-start.16 = (bf16[1,128,1024]{2,1,0:T(8,128)(2,1)S(1)}, bf16[1,128,1024]{2,1,0:T(8,128)(2,1)S(1)}, u32[]{:S(2)}, u32[]{:S(2)}) collective-permute-start(bf16[1,128,1024]{2,1,0:T(8,128)(2,1)S(1)} %maximum_bitcast_fusion.2), channel_id=1, source_target_pairs={{0,16},{1,17},{2,18},{3,19},{4,20},{5,21},{6,22},{7,23},{8,24},{9,... | collective-permute-start | bytes 786440 | tf_op jit(solution)/shard_map/ppermute | solution.py:954
  101.4 19.5 %collective-permute-start.17 = (bf16[2,128,1024]{2,1,0:T(8,128)(2,1)S(1)}, bf16[2,128,1024]{2,1,0:T(8,128)(2,1)S(1)}, u32[]{:S(2)}, u32[]{:S(2)}) collective-permute-start(bf16[2,128,1024]{2,1,0:T(8,128)(2,1)S(1)} %pad_maximum_fusion.9), channel_id=1, source_target_pairs={{0,8},{1,9},{2,10},{3,11},{4,12},{5,13},{6,14},{7,15},{8,0},{9,1},... | collective-permute-start | bytes 1572872 | tf_op jit(solution)/shard_map/ppermute | solution.py:954
  102.5 71.3 %collective-permute-start.22 = (bf16[8,128,1024]{2,1,0:T(8,128)(2,1)}, bf16[8,128,1024]{2,1,0:T(8,128)(2,1)}, u32[]{:S(2)}, u32[]{:S(2)}) collective-permute-start(bf16[8,128,1024]{2,1,0:T(8,128)(2,1)} %pad_maximum_fusion.near), channel_id=1, source_target_pairs={{0,4},{1,5},{2,3},{3,2},{4,0},{5,1},{6,7},{7,6},{8,12},{9,13},{10,... | collective-permute-start | bytes 6291464 | tf_op jit(solution)/shard_map/ppermute | solution.py:954
  121.1 21.7 %collective-permute-start.18 = (bf16[4,128,1024]{2,1,0:T(8,128)(2,1)S(1)}, bf16[4,128,1024]{2,1,0:T(8,128)(2,1)S(1)}, u32[]{:S(2)}, u32[]{:S(2)}) collective-permute-start(bf16[4,128,1024]{2,1,0:T(8,128)(2,1)S(1)} %pad_maximum_fusion.4), channel_id=1, source_target_pairs={{0,1},{1,0},{2,6},{3,7},{4,5},{5,4},{6,2},{7,3},{8,9},{9,8},{10,14... | collective-permute-start | bytes 3145736 | tf_op jit(solution)/shard_map/ppermute | solution.py:954
  144.3 7.9 %collective-permute-start.19 = (bf16[1,192,256]{2,1,0:T(8,128)(2,1)S(1)}, bf16[1,192,256]{2,1,0:T(8,128)(2,1)S(1)}, u32[]{:S(2)}, u32[]{:S(2)}) collective-permute-start(bf16[1,192,256]{2,1,0:T(8,128)(2,1)S(1)} %bitcast.150), channel_id=1, source_target_pairs={{0,16},{1,17},{2,18},{3,19},{4,20},{5,21},{6,22},{7,23},{8,24},{9,... | collective-permute-start | bytes 294920 | tf_op jit(solution)/shard_map/ppermute | solution.py:954
  152.9 17.4 %collective-permute-start.20 = (bf16[8,192,256]{2,1,0:T(8,128)(2,1)}, bf16[8,192,256]{2,1,0:T(8,128)(2,1)}, u32[]{:S(2)}, u32[]{:S(2)}) collective-permute-start(bf16[8,192,256]{2,1,0:T(8,128)(2,1)} %get-tuple-element.290), channel_id=1, source_target_pairs={{0,4},{1,5},{2,3},{3,2},{4,0},{5,1},{6,7},{7,6},{8,12},{9,13},{10,... | collective-permute-start | bytes 2359304 | tf_op jit(solution)/shard_map/ppermute | solution.py:954
  153.5 61.3 %collective-permute-start.25 = (bf16[8,128,1024]{2,1,0:T(8,128)(2,1)}, bf16[8,128,1024]{2,1,0:T(8,128)(2,1)}, u32[]{:S(2)}, u32[]{:S(2)}) collective-permute-start(bf16[8,128,1024]{2,1,0:T(8,128)(2,1)} %pad_maximum_fusion.1.near), channel_id=1, source_target_pairs={{0,4},{1,5},{2,3},{3,2},{4,0},{5,1},{6,7},{7,6},{8,12},{9,13},{10,... | collective-permute-start | bytes 6291464 | tf_op jit(solution)/shard_map/ppermute | solution.py:954
  154.7 15.6 %collective-permute-start.21 = (bf16[2,192,256]{2,1,0:T(8,128)(2,1)}, bf16[2,192,256]{2,1,0:T(8,128)(2,1)S(1)}, u32[]{:S(2)}, u32[]{:S(2)}) collective-permute-start(bf16[2,192,256]{2,1,0:T(8,128)(2,1)} %pad_maximum_fusion.15), channel_id=1, source_target_pairs={{0,8},{1,9},{2,10},{3,11},{4,12},{5,13},{6,14},{7,15},{8,0},{9,1},... | collective-permute-start | bytes 589832 | tf_op jit(solution)/shard_map/ppermute | solution.py:954
  172.3 39.4 %collective-permute-start.23 = (bf16[4,192,256]{2,1,0:T(8,128)(2,1)S(1)}, bf16[4,192,256]{2,1,0:T(8,128)(2,1)S(1)}, u32[]{:S(2)}, u32[]{:S(2)}) collective-permute-start(bf16[4,192,256]{2,1,0:T(8,128)(2,1)S(1)} %get-tuple-element.308), channel_id=1, source_target_pairs={{0,1},{1,0},{2,6},{3,7},{4,5},{5,4},{6,2},{7,3},{8,9},{9,8},{10,14... | collective-permute-start | bytes 1179656 | tf_op jit(solution)/shard_map/ppermute | solution.py:954
  172.6 39.1 %collective-permute-start.24 = (bf16[4,192,256]{2,1,0:T(8,128)(2,1)S(1)}, bf16[4,192,256]{2,1,0:T(8,128)(2,1)S(1)}, u32[]{:S(2)}, u32[]{:S(2)}) collective-permute-start(bf16[4,192,256]{2,1,0:T(8,128)(2,1)S(1)} %pad_maximum_fusion.12), channel_id=1, source_target_pairs={{0,1},{1,0},{2,6},{3,7},{4,5},{5,4},{6,2},{7,3},{8,9},{9,8},{10,14... | collective-permute-start | bytes 1179656 | tf_op jit(solution)/shard_map/ppermute | solution.py:954
  211.9 40.7 %collective-permute-start.26 = (bf16[2,192,256]{2,1,0:T(8,128)(2,1)S(1)}, bf16[2,192,256]{2,1,0:T(8,128)(2,1)S(1)}, u32[]{:S(2)}, u32[]{:S(2)}) collective-permute-start(bf16[2,192,256]{2,1,0:T(8,128)(2,1)S(1)} %get-tuple-element.332), channel_id=1, source_target_pairs={{0,8},{1,9},{2,10},{3,11},{4,12},{5,13},{6,14},{7,15},{8,0},{9,1},... | collective-permute-start | bytes 589832 | tf_op jit(solution)/shard_map/ppermute | solution.py:954
  213.3 39.3 %collective-permute-start.28 = (bf16[8,192,256]{2,1,0:T(8,128)(2,1)S(1)}, bf16[8,192,256]{2,1,0:T(8,128)(2,1)S(1)}, u32[]{:S(2)}, u32[]{:S(2)}) collective-permute-start(bf16[8,192,256]{2,1,0:T(8,128)(2,1)S(1)} %pad_maximum_fusion.5.refs_0_.refs_2_.refs_4_), channel_id=1, source_target_pairs={{0,4},{1,5},{2,3},{3,2},{4,0},{5,1},{6,7},{7,6},{8,12},{9,13},{10,... | collective-permute-start | bytes 2359304 | tf_op jit(solution)/shard_map/ppermute | solution.py:954
  213.5 39.0 %collective-permute-start.27 = (bf16[8,128,1024]{2,1,0:T(8,128)(2,1)}, bf16[8,128,1024]{2,1,0:T(8,128)(2,1)}, u32[]{:S(2)}, u32[]{:S(2)}) collective-permute-start(bf16[8,128,1024]{2,1,0:T(8,128)(2,1)} %get-tuple-element.334), channel_id=1, source_target_pairs={{0,4},{1,5},{2,3},{3,2},{4,0},{5,1},{6,7},{7,6},{8,12},{9,13},{10,... | collective-permute-start | bytes 6291464 | tf_op jit(solution)/shard_map/ppermute | solution.py:954
  256.7 14.0 %collective-permute-start.29 = (bf16[4,128,1024]{2,1,0:T(8,128)(2,1)S(1)}, bf16[4,128,1024]{2,1,0:T(8,128)(2,1)S(1)}, u32[]{:S(2)}, u32[]{:S(2)}) collective-permute-start(bf16[4,128,1024]{2,1,0:T(8,128)(2,1)S(1)} %get-tuple-element.347), channel_id=1, source_target_pairs={{0,1},{1,0},{2,6},{3,7},{4,5},{5,4},{6,2},{7,3},{8,9},{9,8},{10,14... | collective-permute-start | bytes 3145736 | tf_op jit(solution)/shard_map/ppermute | solution.py:954
  257.0 9.8 %collective-permute-start.30 = (bf16[1,192,256]{2,1,0:T(8,128)(2,1)S(1)}, bf16[1,192,256]{2,1,0:T(8,128)(2,1)S(1)}, u32[]{:S(2)}, u32[]{:S(2)}) collective-permute-start(bf16[1,192,256]{2,1,0:T(8,128)(2,1)S(1)} %get-tuple-element.352), channel_id=1, source_target_pairs={{0,16},{1,17},{2,18},{3,19},{4,20},{5,21},{6,22},{7,23},{8,24},{9,... | collective-permute-start | bytes 294920 | tf_op jit(solution)/shard_map/ppermute | solution.py:954
  271.2 21.9 %collective-permute-start.32 = (bf16[1024,1024]{1,0:T(8,128)(2,1)S(1)}, bf16[1024,1024]{1,0:T(8,128)(2,1)S(1)}, u32[]{:S(2)}, u32[]{:S(2)}) collective-permute-start(bf16[1024,1024]{1,0:T(8,128)(2,1)S(1)} %copy-done.66), channel_id=1, source_target_pairs={{0,2},{1,3},{2,0},{3,1},{4,6},{5,7},{6,4},{7,5},{8,10},{9,11},{10,... | collective-permute-start | bytes 6291464 | tf_op jit(solution)/shard_map/ppermute | solution.py:954
  274.8 18.3 %collective-permute-start.31 = (bf16[2,128,1024]{2,1,0:T(8,128)(2,1)S(1)}, bf16[2,128,1024]{2,1,0:T(8,128)(2,1)S(1)}, u32[]{:S(2)}, u32[]{:S(2)}) collective-permute-start(bf16[2,128,1024]{2,1,0:T(8,128)(2,1)S(1)} %get-tuple-element.363), channel_id=1, source_target_pairs={{0,8},{1,9},{2,10},{3,11},{4,12},{5,13},{6,14},{7,15},{8,0},{9,1},... | collective-permute-start | bytes 1572872 | tf_op jit(solution)/shard_map/ppermute | solution.py:954
  274.9 37.6 %collective-permute-start.33 = (bf16[8,128,1024]{2,1,0:T(8,128)(2,1)S(1)}, bf16[8,128,1024]{2,1,0:T(8,128)(2,1)S(1)}, u32[]{:S(2)}, u32[]{:S(2)}) collective-permute-start(bf16[8,128,1024]{2,1,0:T(8,128)(2,1)S(1)} %copy-done.33), channel_id=1, source_target_pairs={{0,4},{1,5},{2,3},{3,2},{4,0},{5,1},{6,7},{7,6},{8,12},{9,13},{10,... | collective-permute-start | bytes 6291464 | tf_op jit(solution)/shard_map/ppermute | solution.py:954
  294.2 18.2 %collective-permute-start.34 = (bf16[1,128,1024]{2,1,0:T(8,128)(2,1)S(1)}, bf16[1,128,1024]{2,1,0:T(8,128)(2,1)S(1)}, u32[]{:S(2)}, u32[]{:S(2)}) collective-permute-start(bf16[1,128,1024]{2,1,0:T(8,128)(2,1)S(1)} %get-tuple-element.377), channel_id=1, source_target_pairs={{0,16},{1,17},{2,18},{3,19},{4,20},{5,21},{6,22},{7,23},{8,24},{9,... | collective-permute-start | bytes 786440 | tf_op jit(solution)/shard_map/ppermute | solution.py:954
  314.2 14.0 %collective-permute-start.35 = (bf16[4,128,1024]{2,1,0:T(8,128)(2,1)S(1)}, bf16[4,128,1024]{2,1,0:T(8,128)(2,1)S(1)}, u32[]{:S(2)}, u32[]{:S(2)}) collective-permute-start(bf16[4,128,1024]{2,1,0:T(8,128)(2,1)S(1)} %get-tuple-element.386), channel_id=1, source_target_pairs={{0,1},{1,0},{2,6},{3,7},{4,5},{5,4},{6,2},{7,3},{8,9},{9,8},{10,14... | collective-permute-start | bytes 3145736 | tf_op jit(solution)/shard_map/ppermute | solution.py:954
  328.7 16.8 %collective-permute-start.37 = (bf16[8,320,256]{2,1,0:T(8,128)(2,1)S(1)}, bf16[8,320,256]{2,1,0:T(8,128)(2,1)S(1)}, u32[]{:S(2)}, u32[]{:S(2)}) collective-permute-start(bf16[8,320,256]{2,1,0:T(8,128)(2,1)S(1)} %get-tuple-element.406), channel_id=1, source_target_pairs={{0,4},{1,5},{2,3},{3,2},{4,0},{5,1},{6,7},{7,6},{8,12},{9,13},{10,... | collective-permute-start | bytes 3932168 | tf_op jit(solution)/shard_map/ppermute | solution.py:954
  329.0 12.2 %collective-permute-start.36 = (bf16[2,128,1024]{2,1,0:T(8,128)(2,1)S(1)}, bf16[2,128,1024]{2,1,0:T(8,128)(2,1)S(1)}, u32[]{:S(2)}, u32[]{:S(2)}) collective-permute-start(bf16[2,128,1024]{2,1,0:T(8,128)(2,1)S(1)} %get-tuple-element.404), channel_id=1, source_target_pairs={{0,8},{1,9},{2,10},{3,11},{4,12},{5,13},{6,14},{7,15},{8,0},{9,1},... | collective-permute-start | bytes 1572872 | tf_op jit(solution)/shard_map/ppermute | solution.py:954
  347.8 13.9 %collective-permute-start.38 = (bf16[1024,1024]{1,0:T(8,128)(2,1)}, bf16[1024,1024]{1,0:T(8,128)(2,1)}, u32[]{:S(2)}, u32[]{:S(2)}) collective-permute-start(bf16[1024,1024]{1,0:T(8,128)(2,1)} %get-tuple-element.418), channel_id=1, source_target_pairs={{0,2},{1,3},{2,0},{3,1},{4,6},{5,7},{6,4},{7,5},{8,10},{9,11},{10,... | collective-permute-start | bytes 6291464 | tf_op jit(solution)/shard_map/ppermute | solution.py:954
  354.0 22.9 %collective-permute-start.39 = (bf16[4,320,256]{2,1,0:T(8,128)(2,1)}, bf16[4,320,256]{2,1,0:T(8,128)(2,1)}, u32[]{:S(2)}, u32[]{:S(2)}) collective-permute-start(bf16[4,320,256]{2,1,0:T(8,128)(2,1)} %get-tuple-element.424), channel_id=1, source_target_pairs={{0,1},{1,0},{2,6},{3,7},{4,5},{5,4},{6,2},{7,3},{8,9},{9,8},{10,14... | collective-permute-start | bytes 1966088 | tf_op jit(solution)/shard_map/ppermute | solution.py:954
  355.4 21.6 %collective-permute-start.40 = (bf16[1,128,1024]{2,1,0:T(8,128)(2,1)}, bf16[1,128,1024]{2,1,0:T(8,128)(2,1)}, u32[]{:S(2)}, u32[]{:S(2)}) collective-permute-start(bf16[1,128,1024]{2,1,0:T(8,128)(2,1)} %get-tuple-element.426), channel_id=1, source_target_pairs={{0,16},{1,17},{2,18},{3,19},{4,20},{5,21},{6,22},{7,23},{8,24},{9,... | collective-permute-start | bytes 786440 | tf_op jit(solution)/shard_map/ppermute | solution.py:954
  360.2 36.2 %collective-permute-start.41 = (bf16[1024,1024]{1,0:T(8,128)(2,1)}, bf16[1024,1024]{1,0:T(8,128)(2,1)}, u32[]{:S(2)}, u32[]{:S(2)}) collective-permute-start(bf16[1024,1024]{1,0:T(8,128)(2,1)} %copy-done.31), channel_id=1, source_target_pairs={{0,2},{1,3},{2,0},{3,1},{4,6},{5,7},{6,4},{7,5},{8,10},{9,11},{10,... | collective-permute-start | bytes 6291464 | tf_op jit(solution)/shard_map/ppermute | solution.py:954
  379.6 3.6 collective-permute-start.43
  383.2 5.8 %collective-permute-start.44 = (f32[8,384]{1,0:T(8,128)S(1)}, f32[8,384]{1,0:T(8,128)S(1)}, u32[]{:S(2)}, u32[]{:S(2)}) collective-permute-start(f32[8,384]{1,0:T(8,128)S(1)} %slice_select_fusion.1), channel_id=1, source_target_pairs={{0,8},{1,9},{2,10},{3,11},{4,12},{5,13},{6,14},{7,15},{8,0},{9,1},... | collective-permute-start | bytes 36872 | tf_op jit(solution)/shard_map/ppermute | solution.py:954
  389.4 14.0 %collective-permute-start.50 = (f32[32,8,256]{2,1,0:T(8,128)S(1)}, f32[32,8,256]{2,1,0:T(8,128)S(1)}, u32[]{:S(2)}, u32[]{:S(2)}) collective-permute-start(f32[32,8,256]{2,1,0:T(8,128)S(1)} %get-tuple-element.489), channel_id=1, source_target_pairs={{0,2},{1,3},{2,0},{3,1},{4,6},{5,7},{6,4},{7,5},{8,10},{9,11},{10,... | collective-permute-start | bytes 786440 | tf_op jit(solution)/shard_map/ppermute | solution.py:954
  391.2 11.4 %collective-permute-start.42 = (bf16[2,320,256]{2,1,0:T(8,128)(2,1)}, bf16[2,320,256]{2,1,0:T(8,128)(2,1)S(1)}, u32[]{:S(2)}, u32[]{:S(2)}) collective-permute-start(bf16[2,320,256]{2,1,0:T(8,128)(2,1)} %get-tuple-element.435), channel_id=1, source_target_pairs={{0,8},{1,9},{2,10},{3,11},{4,12},{5,13},{6,14},{7,15},{8,0},{9,1},... | collective-permute-start | bytes 983048 | tf_op jit(solution)/shard_map/ppermute | solution.py:954
  391.6 4.5 %collective-permute-start.46 = (f32[2,384]{1,0:T(2,128)S(1)}, f32[2,384]{1,0:T(2,128)S(1)}, u32[]{:S(2)}, u32[]{:S(2)}) collective-permute-start(f32[2,384]{1,0:T(2,128)S(1)} %broadcast_select_fusion.1), channel_id=1, source_target_pairs={{0,2},{1,3},{2,0},{3,1},{4,6},{5,7},{6,4},{7,5},{8,10},{9,11},{10,... | collective-permute-start | bytes 9224 | tf_op jit(solution)/shard_map/ppermute | solution.py:954
  396.1 5.3 %collective-permute-start.47 = (f32[1,384]{1,0:T(1,128)S(1)}, f32[1,384]{1,0:T(1,128)S(1)}, u32[]{:S(2)}, u32[]{:S(2)}) collective-permute-start(f32[1,384]{1,0:T(1,128)S(1)} %broadcast_select_fusion.2), channel_id=1, source_target_pairs={{0,1},{1,0},{2,3},{3,2},{4,5},{5,4},{6,7},{7,6},{8,9},{9,8},{10,11... | collective-permute-start | bytes 4616 | tf_op jit(solution)/shard_map/ppermute | solution.py:954
  402.7 10.4 %collective-permute-start.48 = (bf16[1,320,256]{2,1,0:T(8,128)(2,1)S(1)}, bf16[1,320,256]{2,1,0:T(8,128)(2,1)S(1)}, u32[]{:S(2)}, u32[]{:S(2)}) collective-permute-start(bf16[1,320,256]{2,1,0:T(8,128)(2,1)S(1)} %get-tuple-element.449), channel_id=1, source_target_pairs={{0,16},{1,17},{2,18},{3,19},{4,20},{5,21},{6,22},{7,23},{8,24},{9,... | collective-permute-start | bytes 491528 | tf_op jit(solution)/shard_map/ppermute | solution.py:954
  (72 other events, 393.8 us)

commit v4 on v3

--- a/solution.py
+++ b/solution.py
@@ -418,39 +418,34 @@
     return jnp.where(quarter == 1, up, jnp.where(quarter == 2, down, value))
 
 
-def norm_kernel(mine, theirs, gmine, gtheirs, scales, one, two, grads):
-    def work(source, cotangent):
-        value = source[...].astype(jnp.float32)
-        center = value - jnp.mean(value, axis=1, keepdims=True)
-        spread = jnp.mean(center * center, axis=1, keepdims=True)
-        hat = middle_swap(center * lax.rsqrt(spread + norm_eps))
-        table = scales[...].astype(jnp.float32)
-        one[...] = (hat * table[0:1] + table[1:2]).astype(jnp.bfloat16)
-        two[...] = (hat * table[2:3] + table[3:4]).astype(jnp.bfloat16)
-        grads[...] = cotangent[...]
-
-    first = pl.program_id(0) == 0
-    pl.when(first)(lambda: work(mine, gmine))
-    pl.when(jnp.logical_not(first))(lambda: work(theirs, gtheirs))
-
-
-def norms(mine, theirs, gmine, gtheirs, scales):
-    length, width = mine.shape
-    block = (ROWS, width)
+def norm_kernel(source, cotangent, scales, *refs):
+    one, two, grads = refs[-3:]
+    value = source[...].astype(jnp.float32)
+    center = value - jnp.mean(value, axis=1, keepdims=True)
+    spread = jnp.mean(center * center, axis=1, keepdims=True)
+    hat = middle_swap(center * lax.rsqrt(spread + norm_eps))
+    table = scales[...].astype(jnp.float32)
+    one[...] = (hat * table[0:1] + table[1:2]).astype(jnp.bfloat16)
+    two[...] = (hat * table[2:3] + table[3:4]).astype(jnp.bfloat16)
+    grads[...] = cotangent[...]
+
+
+def norms(sequence, source, cotangent, scales, before):
+    length, width = source.shape
     steps = length // ROWS
-    own = pl.BlockSpec(block, lambda s, i: (jnp.where(s == 0, i, steps - 1), 0))
-    other = pl.BlockSpec(block, lambda s, i: (jnp.where(s == 0, 0, i), 0))
-    out = pl.BlockSpec(block, lambda s, i: (s * steps + i, 0))
+    block = pl.BlockSpec((ROWS, width), lambda i: (i, 0))
+    out = pl.BlockSpec((ROWS, width), lambda i: (sequence * steps + i, 0))
     shape = jax.ShapeDtypeStruct((2 * length, width), jnp.bfloat16)
     return pl.pallas_call(
         norm_kernel,
-        grid=(2, steps),
-        in_specs=[own, other, own, other, fixed(scales.shape)],
+        grid=(steps,),
+        in_specs=[block, block, fixed(scales.shape)] + [pl.BlockSpec(memory_space=pl.ANY)] * len(before),
         out_specs=[out] * 3,
         out_shape=[shape] * 3,
-        compiler_params=params(16),
-        cost_estimate=cost(40 * length * width, 20 * length * width),
-    )(mine, theirs, gmine, gtheirs, scales)
+        input_output_aliases={3 + n: n for n in range(len(before))},
+        compiler_params=params(60),
+        cost_estimate=cost(20 * length * width, 10 * length * width),
+    )(source, cotangent, scales, *before)
 
 
 def turn(value, cosine, sine):
@@ -530,7 +525,7 @@
             scratch_shapes=weight_scratch(weights),
         ),
         out_shape=jax.ShapeDtypeStruct((4, tokens, width), jnp.bfloat16),
-        compiler_params=params(20),
+        compiler_params=params(60),
         cost_estimate=cost(8 * tokens * model * width, 6 * tokens * model),
     )(place, normed, grads, *weights * 3, *proj, bias, cosine, sine, segments)
 
@@ -701,25 +696,29 @@
             ],
         ),
         out_shape=[half, half, jax.ShapeDtypeStruct((parts, 1, width), jnp.float32)],
-        compiler_params=params(26),
+        compiler_params=params(60 if more else 26),
         cost_estimate=cost(8 * tokens * model * width, 6 * tokens * model),
     )(place, normed, d_mixed, *more)
 
 
-def share_out(step, steps, before, mine, send, value):
-    for own, ref, earlier in ((True, mine, before[:1]), (False, send, before[1:])):
-
-        @pl.when((step < steps // 2) == own)
+def share_out(step, steps, earlier, mine, sends, value):
+    each = steps // 2 // len(sends)
+    for start, end, ref, more in [(0, steps // 2, mine, earlier[:1])] + [
+        (steps // 2 + n * each, steps // 2 + (n + 1) * each, send, earlier[1:]) for n, send in enumerate(sends)
+    ]:
+
+        @pl.when((step >= start) & (step < end))
         def _():
             total = value
-            for one in earlier:
+            for one in more:
                 total = total + one[...].astype(jnp.float32)
             ref[...] = total.astype(ref.dtype)
 
 
-def attention_back_kernel(half, place, d_mixed, attended, *refs):
-    weights, before = refs[:8], refs[8:-6]
-    d_mine, d_send, p_mine, p_send, ordered, ordered_proj = refs[-6:]
+def attention_back_kernel(half, pieces, place, d_mixed, attended, *refs):
+    count = 2 * (1 + pieces) + 2
+    weights, before, results = refs[:8], refs[8:-count], refs[-count:-2]
+    ordered, ordered_proj = refs[-2:]
     step, steps = pl.program_id(0), pl.num_programs(0)
 
     @pl.when(step == 0)
@@ -727,19 +726,24 @@
         arrange(place, half, weights, ordered, ordered_proj)
 
     change = jnp.concatenate([d_mixed[part] for part in range(3)], axis=1)
-    share_out(step, steps, before[:2], d_mine, d_send, mul(change, ordered[...], NT))
-    share_out(step, steps, before[2:], p_mine, p_send, mul(attended[...], ordered_proj[...], NN))
-
-
-def attention_back(half, place, d_mixed, attended, weights, first, proj, before):
+    share_out(step, steps, before[:2], results[0], results[1 : 1 + pieces], mul(change, ordered[...], NT))
+    share_out(step, steps, before[2:], results[1 + pieces], results[2 + pieces :], mul(attended[...], ordered_proj[...], NN))
+
+
+def attention_back(half, pieces, place, d_mixed, attended, weights, first, proj, before):
     parts, tokens, width = d_mixed.shape
     model = 128 * weights[0].shape[0]
     steps = tokens // TOKENS
     own = pl.BlockSpec((TOKENS, model), lambda i, *_: (jnp.minimum(i, steps // 2 - 1), 0))
     other = pl.BlockSpec((TOKENS, model), lambda i, *_: (jnp.maximum(i - steps // 2, 0), 0))
-    shape = jax.ShapeDtypeStruct((tokens // 2, model), jnp.bfloat16)
+    each = steps // 2 // pieces
+    shape = lambda n: jax.ShapeDtypeStruct((n * TOKENS, model), jnp.bfloat16)
+    sent = [
+        pl.BlockSpec((TOKENS, model), lambda i, *_, n=n: (jnp.clip(i - steps // 2 - n * each, 0, each - 1), 0))
+        for n in range(pieces)
+    ]
     return pl.pallas_call(
-        partial(attention_back_kernel, half),
+        partial(attention_back_kernel, half, pieces),
         grid_spec=pltpu.PrefetchScalarGridSpec(
             num_scalar_prefetch=1,
             grid=(steps,),
@@ -749,11 +753,11 @@
             ]
             + weight_specs(weights, first)
             + [own, other] * (len(before) // 2),
-            out_specs=[own, other] * 2,
+            out_specs=([own] + sent) * 2,
             scratch_shapes=weight_scratch(weights),
         ),
-        out_shape=[shape] * 4,
-        compiler_params=params(24),
+        out_shape=([shape(steps // 2)] + [shape(each)] * pieces) * 2,
+        compiler_params=params(60),
         cost_estimate=cost(8 * tokens * model * width, 8 * tokens * model),
     )(place, d_mixed, attended, *weights * 3, *proj, *before)
 
@@ -882,8 +886,11 @@
     )(place, normed, grads, *weights, bias, *earlier)
 
 
-def both_of(left, right):
-    return left[...].astype(jnp.float32) + right[...].astype(jnp.float32)
+def both_of(left, *right):
+    come = right[0][...]
+    if len(right) > 1:
+        come = jnp.where(pl.program_id(0) < pl.num_programs(0) // 2, come, right[1][...])
+    return left[...].astype(jnp.float32) + come.astype(jnp.float32)
 
 
 def finish_out_kernel(hidden, mine, come, scales, layer_out):
@@ -916,17 +923,66 @@
 def finish(kernel, arrays, scales, with_sums):
     length, width = arrays[0].shape
     block = pl.BlockSpec((ROWS, width), lambda i: (i, 0))
+    steps, specs = length // ROWS, []
+    for array in arrays:
+        if isinstance(array, tuple):
+            specs.append(pl.BlockSpec((ROWS, width), lambda i: (jnp.minimum(i, steps // 2 - 1), 0)))
+            specs.append(pl.BlockSpec((ROWS, width), lambda i: (jnp.maximum(i - steps // 2, 0), 0)))
+        else:
+            specs.append(block)
+    arrays = jax.tree.leaves(arrays)
     shape = jax.ShapeDtypeStruct((length, width), jnp.bfloat16)
     more = [pl.BlockSpec((8, width), lambda i: (0, 0))] if with_sums else []
     return pl.pallas_call(
         kernel,
         grid=(length // ROWS,),
-        in_specs=[block] * len(arrays) + [fixed(scales.shape)],
+        in_specs=specs + [fixed(scales.shape)],
         out_specs=[block] + more,
         out_shape=[shape] + [jax.ShapeDtypeStruct((8, width), jnp.float32)] * len(more),
-        compiler_params=params(16),
+        compiler_params=params(60),
         cost_estimate=cost(40 * length * width, 2 * (len(arrays) + 1) * length * width),
     )(*arrays, scales)
+
+
+def by_core(core, mine, come):
+    return jnp.where(core == 0, mine, come), jnp.where(core == 0, come, mine)
+
+
+def qkv_rows_kernel(core, mine_one, come_one, mine_two, come_two, out):
+    parts, _, width = mine_one.shape
+    for part in range(parts):
+        for half, (mine, come) in enumerate(((mine_one, come_one), (mine_two, come_two))):
+            even, odd = by_core(core[0], mine[part], come[part])
+            for head in range(width // HEAD):
+                at = slice(head * HEAD, (head + 1) * HEAD)
+                start = (part * 2 + half) * 2 * width + head * PAIR
+                out[:, start : start + PAIR] = jnp.concatenate([even[:, at], odd[:, at]], axis=1)
+
+
+def up_rows_kernel(core, mine_one, come_one, mine_two, come_two, out):
+    width = mine_one.shape[2]
+    first, second = by_core(core[0], mine_one[0], come_one[0]), by_core(core[0], mine_two[0], come_two[0])
+    for chip in range(width // 64):
+        at = slice(chip * 64, (chip + 1) * 64)
+        for which in range(2):
+            start = ((chip // 2) * 2 + which) * 256 + (chip % 2) * 128
+            out[:, start : start + 128] = jnp.concatenate([first[which][:, at], second[which][:, at]], axis=1)
+
+
+def whole_rows(kernel, core, halves, shape):
+    operands = [array for half in halves for array in half]
+    return pl.pallas_call(
+        kernel,
+        grid_spec=pltpu.PrefetchScalarGridSpec(
+            num_scalar_prefetch=1,
+            grid=(1,),
+            in_specs=[fixed(array.shape) for array in operands],
+            out_specs=pl.BlockSpec(shape, lambda i, *_: (0, 0)),
+        ),
+        out_shape=jax.ShapeDtypeStruct(shape, jnp.float32),
+        compiler_params=params(16),
+        cost_estimate=cost(0, 16 * shape[0] * shape[1]),
+    )(core, *operands)
 
 
 BITS = {"y": 0, "core": 1, "x": 2, "z_low": 3, "z_high": 4}
@@ -1099,18 +1155,18 @@
     place = pairs.places()
 
     small = (norm1_gain, norm1_bias, norm2_gain, norm2_bias, qkv_bias, proj_bias, up_bias, down_bias)
-    line = jnp.concatenate(small)
-    line = jnp.pad(line, (0, -line.shape[0] % 128))
+    ends = [sum(entry.shape[0] for entry in small[: n + 1]) for n in range(len(small))]
+    long = ends[-1] + -ends[-1] % 128
+    line = sum(jnp.pad(entry, (end - entry.shape[0], long - end)) for entry, end in zip(small, ends))
     come = pairs.swap(line, CORES)
     lines = Gather(pairs, jnp.where(core == 0, jnp.stack([line, come]), jnp.stack([come, line])).reshape(-1))
     first = Gather(pairs, jnp.concatenate([low_proj, low_qkv[0]]).reshape(-1, width))
     chunks = [Gather(pairs, jnp.concatenate([low_up[h], low_down[h]])) for h in range(2)]
     second = Gather(pairs, low_qkv[1].reshape(-1, width))
     tick(None, (), first, lines)
+    tick(None, (), lines)
     tick(None, (), first, lines)
-    tick(None, (), first, lines, chunks[0])
-    tick(None, (), first, lines, chunks[0])
-    w_first = first.result()
+    tick(None, (), lines)
     table = jnp.concatenate(lines.result())[place]
     table = table.reshape(heads, 2, 2, -1).swapaxes(1, 2).reshape(pairs.total, -1)
     spread, at = [], 0
@@ -1122,34 +1178,46 @@
     own_bias = pick(b_qkv.reshape(3, heads, 2, HEAD), core, 2).reshape(3, 2, 1, width)
     own_up_bias = pick(b_up.reshape(heads, 2, 2, 2, unit), core, 1).transpose(2, 0, 1, 3).reshape(2, 1, -1)
     scales = jnp.stack([gain_one, shift_one, gain_two, shift_two])
-    normed_one, normed_two, both_grads = norms(
-        hidden, other, grads, other_grads, scales.reshape(4, -1, 2, 2, rows).swapaxes(2, 3).reshape(4, model)
-    )
-
-    (normed_one, cosine, sine), _ = tick((normed_one, cosine, sine), (), chunks[0], chunks[1])
+    scales = scales.reshape(4, -1, 2, 2, rows).swapaxes(2, 3).reshape(4, model)
+    _, scales = tick(None, scales, first)
+    before = norms(0, hidden, grads, scales, ())
+    before, (scales, segments) = tick(before, (scales, segments), first, chunks[0])
+    column = segments.reshape(-1, 1)
+    cosine, sine = wide_angles(segments)
+    normed_one, normed_two, both_grads = norms(1, other, other_grads, scales, before)
+    (normed_one, cosine, sine), _ = tick((normed_one, cosine, sine), (), chunks[0], done=(first,))
+    w_first = first.result()
+
     parts = project(
         0, place, normed_one, both_grads, w_first, 2, w_first, own_bias[:, 0], cosine, sine, column
     )
     parts, _ = tick(parts, (), chunks[0], chunks[1])
     before = attention(0, parts, cosine, sine, segments, ())
-    before, parts = tick(before, parts, chunks[1])
+    before, parts = tick(before, parts, chunks[0], chunks[1])
     attended_one, d_mixed = attention(1, parts, cosine, sine, segments, before)
     (attended_one, d_mixed), _ = tick((attended_one, d_mixed), (), chunks[1], second)
     keep, send, qkv_sums_one = attention_grads(place, normed_one, d_mixed, ())
     sum_one = Sum(pairs, keep, send)
-    _, d_mixed = tick(None, d_mixed, sum_one, second)
-    d1, d1_send, out, out_send = attention_back(0, place, d_mixed, attended_one, w_first, 2, w_first, ())
+    qkv_sums_one, d_mixed = tick(qkv_sums_one, d_mixed, sum_one, second)
+    d1, d1_send, out, out_send = attention_back(0, 1, place, d_mixed, attended_one, w_first, 2, w_first, ())
 
     sum_forward, up_sums = [], []
     before = (out, out_send)
     for chunk in range(2):
-        before, normed_two = tick(before, normed_two, sum_one, second, *sum_forward)
+        more = [] if chunk else chunks[1:]
+        before, normed_two = tick(before, normed_two, *more, sum_one, second, *sum_forward, done=(chunks[chunk],))
         keep, send, sums, *before = forward_chunk(
-            place, normed_two, both_grads, chunks[chunk].result(), own_up_bias[chunk], before
+            place,
+            normed_two,
+            both_grads,
+            chunks[chunk].result(),
+            own_up_bias[chunk],
+            before,
         )
         up_sums.append(sums)
         sum_forward.append(Sum(pairs, keep, send))
     out, out_send, d2, d2_send = before
+
     (out, out_send, d2_send), normed_one = tick(
         (out, out_send, d2_send), normed_one, sum_one, sum_forward[0], done=(second,)
     )
@@ -1163,13 +1231,14 @@
     before, parts = tick(before, parts, sum_forward[0], done=(trade_two,))
     attended_two, d_mixed = attention(1, parts, cosine, sine, segments, before)
     (attended_two, d_mixed), _ = tick((attended_two, d_mixed), (), sum_forward[1], done=sum_forward[:1])
+    d1, d1_send, out, out_send = attention_back(
+        1, 1, place, d_mixed, attended_two, w_second, 0, w_first, (d1, d1_send, out, out_send)
+    )
+    trade = Trade(pairs, d1_send, out_send)
+    (d1, out), d_mixed = tick((d1, out), d_mixed, sum_forward[1], trade)
     keep, send, qkv_sums_two = attention_grads(place, normed_one, d_mixed, (attended_one, attended_two, both_grads))
     sum_two = Sum(pairs, keep, send)
-    qkv_sums_two, d_mixed = tick(qkv_sums_two, d_mixed, sum_forward[1], sum_two)
-    back = attention_back(1, place, d_mixed, attended_two, w_second, 0, w_first, (d1, d1_send, out, out_send))
-    (d1, d1_send, out, out_send), _ = tick(back, (), sum_forward[1], sum_two)
-    trade = Trade(pairs, d1_send, out_send)
-    tick(None, (), trade)
+    (qkv_sums_two, d1, out), _ = tick((qkv_sums_two, d1, out), (), sum_two, done=(trade,))
     d1_come, out_come = trade.result()
     input_grad, sums = finish(
         finish_grad_kernel,
@@ -1177,28 +1246,19 @@
         jnp.stack([gain_one, gain_two]),
         True,
     )
-    (input_grad, sums), out = tick((input_grad, sums), out, sum_two, done=sum_forward[1:])
-    layer_out = finish(finish_out_kernel, [hidden, out, out_come], jnp.stack([b_proj, b_down]), False)[0]
-    layer_out, _ = tick(layer_out, (), sum_two)
-    low_qkv_one, low_qkv_two = sum_one.result(), sum_two.result()
-    low_forward = [task.result() for task in sum_forward]
-
-    def whole_rows(value):
-        mine, come = pick(value, core, 0), pairs.swap(pick(value, 1 - core, 0), CORES)
-        return jnp.where(core == 0, jnp.stack([mine, come], 2), jnp.stack([come, mine], 2))
-
-    third = 3 * 2 * rows
-    both = jnp.stack([low_qkv_one, low_qkv_two[:third]]).reshape(2, 3, 2, rows, heads // 2, HEAD)
-    grad_qkv = whole_rows(both.transpose(2, 3, 1, 0, 4, 5).reshape(2, rows, 3 * heads, HEAD)).reshape(rows, -1)
-    grad_proj = low_qkv_two[third:].reshape(4, rows, width).transpose(1, 0, 2).reshape(rows, model)
-    ups = jnp.stack([entry[: 2 * rows] for entry in low_forward]).reshape(2, 2, rows, heads, 2, unit)
-    grad_up = whole_rows(ups.transpose(1, 2, 3, 4, 0, 5).reshape(2, rows, heads, 4 * unit)).reshape(rows, -1)
-    grad_down = jnp.concatenate([entry[2 * rows :] for entry in low_forward])
-
+    (input_grad, sums, qkv_sums_one, qkv_sums_two, up_sums), _ = tick(
+        (input_grad, sums, qkv_sums_one, qkv_sums_two, up_sums), (), sum_two, sum_forward[1]
+    )
     def both_cores(own):
         own = own[:, None]
         none = jnp.zeros_like(own)
         return jnp.where(core == 0, jnp.concatenate([own, none], axis=1), jnp.concatenate([none, own], axis=1)).reshape(-1)
+
+    def halve(table, name):
+        upper = pairs.bit(name) == 1
+        half = table.shape[0] // 2
+        send = jnp.where(upper, table[:half], table[half:])
+        return jnp.where(upper, table[half:], table[:half]) + pairs.swap(send, (name, name))
 
     sum_qkv = jnp.stack([qkv_sums_one.reshape(3, -1), qkv_sums_two.reshape(3, -1)], axis=1)
     sum_up = jnp.stack([entry.reshape(heads, 2, unit) for entry in up_sums], axis=2)
@@ -1213,11 +1273,29 @@
     ]
     table = jnp.concatenate([entry.reshape(pairs.total, -1) for entry in entries], axis=1)
     table = jnp.pad(table, ((0, 0), (0, -table.shape[1] % 128)))
-    for name in reversed(BITS):
-        upper = pairs.bit(name) == 1
-        half = table.shape[0] // 2
-        send = jnp.where(upper, table[:half], table[half:])
-        table = jnp.where(upper, table[half:], table[:half]) + pairs.swap(send, (name, name))
+    names = list(reversed(BITS))
+    for name in names[:1]:
+        table = halve(table, name)
+    table, out = tick(table, out, sum_two)
+    layer_out = finish(finish_out_kernel, [hidden, out, out_come], jnp.stack([b_proj, b_down]), False)[0]
+    table = halve(halve(table, names[1]), names[2])
+    (table, layer_out), _ = tick((table, layer_out), (), sum_two, done=(sum_one, *sum_forward))
+    for name in names[3:]:
+        table = halve(table, name)
+    low_qkv_one, low_qkv_two = sum_one.result(), sum_two.result()
+    low_forward = [task.result() for task in sum_forward]
+
+    def trade_rows(value):
+        split = value.reshape(value.shape[0], 2, rows, -1)
+        return pick(split, core, 1), pairs.swap(pick(split, 1 - core, 1), CORES)
+
+    which = core.astype(jnp.int32).reshape(1)
+    low = (low_qkv_one.reshape(3, 2 * rows, width), low_qkv_two[: 6 * rows].reshape(3, 2 * rows, width))
+    grad_qkv = whole_rows(qkv_rows_kernel, which, [trade_rows(value) for value in low], qkv_weight.shape)
+    grad_proj = low_qkv_two[6 * rows :].reshape(4, rows, width).transpose(1, 0, 2).reshape(rows, model)
+    ups = [trade_rows(entry[: 2 * rows].reshape(1, 2 * rows, -1)) for entry in low_forward]
+    grad_up = whole_rows(up_rows_kernel, which, ups, up_weight.shape)
+    grad_down = jnp.concatenate([entry[2 * rows :] for entry in low_forward])
     outs, at = [], 0
     for entry in entries:
         size = entry.shape[0] // pairs.total

time: 426 us -> 405 us (0.951)
  local copies, waits for them, and re-layouts: 67.4 us -> 26.4 us
  Pallas kernels: 215 us -> 243 us
  waiting for transfers between devices: 50.3 us -> 42.1 us
  other arithmetic: 37.4 us -> 32.9 us
    unnamed x140 -> x110, local copies, waits for them, and re-layouts: 35.1 us -> 11.6 us
    pallas_call x5 -> x8, Pallas kernels: 45.7 us -> 61.5 us  [the longest x2 26.2 us: attention_back(): pl.pallas_call(partial(attention_back_kernel, half, pieces), grid_spec=pl...]
    pallas_call x2, Pallas kernels: 13.2 us -> 21.6 us  [project(): pl.pallas_call(partial(project_kernel, half), grid_spec=pltpu.PrefetchSca...]
    ppermute x51 -> x53, waiting for transfers between devices: 50.3 us -> 42.1 us  [swap(): return lax.ppermute(value, SPLIT, moves)]
    concatenate x1 -> x0, local copies, waits for them, and re-layouts: 5.47 us -> none  [paired_body(): line = jnp.concatenate(small)]
    ppermute x51 -> x53, starting transfers between devices: 47.6 us -> 51 us  [swap(): return lax.ppermute(value, SPLIT, moves)]
  transfers between devices with their start and end apart: 51 -> 53, of which waited for: 12 -> 14; matrix products, arithmetic and copies ran while one was open for 12% -> 7% of each run, Pallas kernels for 51% -> 61%
where the time goes in v4:
time: 405 us; the launch traced here: 398 us
  Pallas kernels  243 us (60%)
  starting transfers between devices  51 us (13%)
  waiting for transfers between devices  42.1 us (10%)
  other arithmetic  32.9 us (8%)
  local copies, waits for them, and re-layouts  26.4 us (7%)
    pallas_call x2, Pallas kernels, forward_chunk(): pl.pallas_call(forward_kernel, grid_spec=pltpu.PrefetchScalarGridSpec(num...  73.1 us
    pallas_call x4, Pallas kernels, attention(): pl.pallas_call(attention_kernel, grid=(width // PAIR,), in_specs=[part(0)...  68.8 us
    ppermute x53, starting transfers between devices, swap(): return lax.ppermute(value, SPLIT, moves)  51 us
    ppermute x53, waiting for transfers between devices, swap(): return lax.ppermute(value, SPLIT, moves)  42.1 us
    pallas_call x2, Pallas kernels, attention_back(): pl.pallas_call(partial(attention_back_kernel, half, pieces), grid_spec=pl...  26.2 us
    pallas_call x2, Pallas kernels, project(): pl.pallas_call(partial(project_kernel, half), grid_spec=pltpu.PrefetchSca...  21.6 us
    pallas_call x2, Pallas kernels, attention_grads(): pl.pallas_call(attention_grads_kernel, grid_spec=pltpu.PrefetchScalarGrid...  18.3 us
    pallas_call x2, Pallas kernels, finish(): pl.pallas_call(kernel, grid=(length // ROWS,), in_specs=specs + [fixed(sc...  18.2 us
  transfers between devices with their start and end apart: 53, of which 14 were waited for; matrix products, arithmetic and copies ran while one was open for 7% of the time, Pallas kernels for 61%

profile of v4, /device:TPU:1, one launch (start us, length us, event | category | flops | bytes accessed | tf_op | source)
XLA Modules:
  0.0 398.0 jit_solution(13270530225867116429)
XLA Ops:
  2.9 2.6 dynamic-slice_reduce_fusion.1
  9.4 3.7 collective-permute-start.5
  14.1 1.4 collective-permute-start.6
  15.6 2.1 collective-permute-done.6
  17.7 6.6 %collective-permute-done.4 = bf16[1,320,256]{2,1,0:T(8,128)(2,1)S(1)} collective-permute-done((bf16[1,320,256]{2,1,0:T(8,128)(2,1)S(1)}, bf16[1,320,256]{2,1,0:T(8,128)(2,1)S(1)}, u32[]{:S(2)}, u32[]{:S(2)}) %collective-permute-start.4) | collective-permute-done | bytes 163872 | tf_op jit(solution)/shard_map/ppermute | solution.py:1010
  26.9 1.3 collective-permute-start.8
  28.2 1.3 collective-permute-done.8
  32.3 2.9 collective-permute-done.9
  35.2 2.2 collective-permute-start.10
  38.7 7.7 %shard_map.254 = (bf16[2048,1024]{1,0:T(8,128)(2,1)}, bf16[2048,1024]{1,0:T(8,128)(2,1)}, bf16[2048,1024]{1,0:T(8,128)(2,1)}) custom-call(bf16[1024,1024]{1,0:T(8,128)(2,1)} %bitcast.source.hidden, bf16[1024,1024]{1,0:T(8,128)(2,1)} %bitcast.1.cotangent.grads, bf16[4,1024]{1,0:T(4,128)(2,1)} %reshape.310.scales), custom_call_target="tpu_custom_call" | custom-call | flops 20971520 | bytes 10485760 | tf_op jit(solution)/shard_map/pallas_call | solution.py:439
  51.1 6.3 %fusion = (f32[2048,128]{1,0:T(8,128)}, f32[2048,128]{1,0:T(8,128)}) fusion(f32[128]{0:T(128)} %get-tuple-element.616, f32[128]{0:T(128)} %get-tuple-element.617, f32[2048]{0:T(1024)S(1)} %fusion.2), kind=kLoop, calls=%fused_computation.12 | loop fusion | flops 524288 | bytes 2106368 | tf_op jit(solution)/shard_map/mul | solution.py:1106
  57.4 7.5 %shard_map.255 = (bf16[2048,1024]{1,0:T(8,128)(2,1)}, bf16[2048,1024]{1,0:T(8,128)(2,1)}, bf16[2048,1024]{1,0:T(8,128)(2,1)}) custom-call(bf16[1024,1024]{1,0:T(8,128)(2,1)} %collective-permute-done.source, bf16[1024,1024]{1,0:T(8,128)(2,1)} %collective-permute-done.1.cotangent, ...), custom_call_target="tpu_custom_call", output_to_operand_aliasing={{0}: (3, {}), {1}: (4, {}), {2}: (5, {})} | custom-call | flops 20971520 | bytes 10485760 | tf_op jit(solution)/shard_map/pallas_call | solution.py:439
  67.6 1.3 copy.152
  69.0 10.8 %shard_map.256.q_ref.k_ref.v_ref.g_ref = bf16[4,2048,256]{2,1,0:T(8,128)(2,1)} custom-call(s32[16]{0:T(128)} %xor_add_fusion.place, bf16[2048,1024]{1,0:T(8,128)(2,1)} %get-tuple-element.417.normed.refs_0_, bf16[2048,1024]{1,0:T(8,128)(2,1)} %get-tuple-element.310.grads.refs_4_, bf16[8,320,256]{2,1,0:T(8,128)(2,1)} %copy-done.22, ...), custom_call_target="tpu_custom_call" | custom-call | flops 4294967296 | bytes 12582912 | tf_op jit(solution)/shard_map/pallas_call | solution.py:516
  79.8 1.4 pad_maximum_fusion.3
  82.6 2.2 copy-done.8
  84.7 17.2 %shard_map.257 = (bf16[2048,256]{1,0:T(8,128)(2,1)S(1)}, bf16[3,2048,256]{2,1,0:T(8,128)(2,1)S(1)}) custom-call(bf16[4,2048,256]{2,1,0:T(8,128)(2,1)S(1)} %copy-done.8, bf16[4,2048,256]{2,1,0:T(8,128)(2,1)S(1)} %copy-done.8, bf16[4,2048,256]{2,1,0:T(8,128)(2,1)S(1)} %copy-done.8, bf16[4,2048,256]{2,1,0:T(8,128)(2,1)S(1)} %copy-done.8, ...), custom_call_target="tpu_custom_call" | custom-call | flops 12884901888 | bytes 4194304 | tf_op jit(solution)/shard_map/pallas_call | solution.py:594
  102.0 1.5 pad_maximum_fusion.near
  104.7 1.3 collective-permute-start.22
  106.1 17.4 %shard_map.258 = (bf16[2048,256]{1,0:T(8,128)(2,1)S(1)}, bf16[3,2048,256]{2,1,0:T(8,128)(2,1)S(1)}) custom-call(bf16[4,2048,256]{2,1,0:T(8,128)(2,1)S(1)} %copy-done.9, bf16[4,2048,256]{2,1,0:T(8,128)(2,1)S(1)} %copy-done.9, bf16[4,2048,256]{2,1,0:T(8,128)(2,1)S(1)} %copy-done.9, ...), custom_call_target="tpu_custom_call", output_to_operand_aliasing={{0}: (8, {}), {1}: (9, {})} | custom-call | flops 12884901888 | bytes 4194304 | tf_op jit(solution)/shard_map/pallas_call | solution.py:594
  126.4 5.8 %shard_map.259 = (bf16[8,192,256]{2,1,0:T(8,128)(2,1)S(1)}, bf16[8,192,256]{2,1,0:T(8,128)(2,1)S(1)}, f32[3,1,256]{2,1,0:T(1,128)S(1)}) custom-call(s32[16]{0:T(128)S(1)} %copy-done.16, bf16[2048,1024]{1,0:T(8,128)(2,1)S(1)} %copy-done, bf16[3,2048,256]{2,1,0:T(8,128)(2,1)S(1)} %get-tuple-element.352.refs_1_.d_mixed), custom_call_target="tpu_custom_call" | custom-call | flops 4294967296 | bytes 12582912 | tf_op jit(solution)/shard_map/pallas_call | solution.py:683
  134.0 12.2 %shard_map.260 = (bf16[1024,1024]{1,0:T(8,128)(2,1)}, bf16[1024,1024]{1,0:T(8,128)(2,1)}, bf16[1024,1024]{1,0:T(8,128)(2,1)}, bf16[1024,1024]{1,0:T(8,128)(2,1)}) custom-call(s32[16]{0:T(128)} %xor_add_fusion.place, bf16[3,2048,256]{2,1,0:T(8,128)(2,1)} %copy-done.18, bf16[2048,256]{1,0:T(8,128)(2,1)} %copy-done.19, bf16[8,320,256]{2,1,0:T(8,128)(2,1)} %copy-done.22, ...), custom_call_target="tpu_custom_call" | custom-call | flops 4294967296 | bytes 16777216 | tf_op jit(solution)/shard_map/pallas_call | solution.py:745
  146.2 5.8 %collective-permute-done.20 = bf16[8,192,256]{2,1,0:T(8,128)(2,1)S(1)} collective-permute-done((bf16[8,192,256]{2,1,0:T(8,128)(2,1)S(1)}, bf16[8,192,256]{2,1,0:T(8,128)(2,1)S(1)}, u32[]{:S(2)}, u32[]{:S(2)}) %collective-permute-start.20) | collective-permute-done | bytes 786464 | tf_op jit(solution)/shard_map/ppermute | solution.py:1010
  152.3 1.7 pad_maximum_fusion.1.near
  156.7 35.8 %shard_map.261 = (bf16[8,128,1024]{2,1,0:T(8,128)(2,1)S(1)}, bf16[8,128,1024]{2,1,0:T(8,128)(2,1)S(1)}, f32[1,1024]{1,0:T(1,128)S(1)}, bf16[1024,1024]{1,0:T(8,1...) custom-call(s32[16]{0:T(128)S(1)} %copy-done.17, ...), custom_call_target="tpu_custom_call" | custom-call | flops 25769803776 | bytes 33554432 | tf_op jit(solution)/shard_map/pallas_call | solution.py:864
  196.2 37.3 %shard_map.262 = (bf16[8,128,1024]{2,1,0:T(8,128)(2,1)S(1)}, bf16[8,128,1024]{2,1,0:T(8,128)(2,1)}, f32[1,1024]{1,0:T(1,128)S(1)}, bf16[1024,1024]{1,0:T(8,128)(...) custom-call(s32[16]{0:T(128)S(1)} %copy-done.17, ...), custom_call_target="tpu_custom_call" | custom-call | flops 25769803776 | bytes 33554432 | tf_op jit(solution)/shard_map/pallas_call | solution.py:864
  233.6 2.6 add_convert_fusion.2
  238.6 10.8 %shard_map.263.q_ref.k_ref.v_ref.g_ref = bf16[4,2048,256]{2,1,0:T(8,128)(2,1)} custom-call(s32[16]{0:T(128)} %xor_add_fusion.place, bf16[2048,1024]{1,0:T(8,128)(2,1)} %get-tuple-element.417.normed.refs_0_, bf16[2048,1024]{1,0:T(8,128)(2,1)} %get-tuple-element.310.grads.refs_4_, bf16[8,192,256]{2,1,0:T(8,128)(2,1)} %copy-done.24, ...), custom_call_target="tpu_custom_call" | custom-call | flops 4294967296 | bytes 12582912 | tf_op jit(solution)/shard_map/pallas_call | solution.py:516
  249.5 1.3 collective-permute-done.29
  250.9 1.6 add_convert_fusion.8
  252.4 5.5 %collective-permute-start.32 = (bf16[1024,1024]{1,0:T(8,128)(2,1)}, bf16[1024,1024]{1,0:T(8,128)(2,1)S(1)}, u32[]{:S(2)}, u32[]{:S(2)}) collective-permute-start(bf16[1024,1024]{1,0:T(8,128)(2,1)} %get-tuple-element.438), channel_id=1, source_target_pairs={{0,2},{1,3},{2,0},{3,1},{4,6},{5,7},{6,4},{7,5},{8,10},{9,11},{10,... | collective-permute-start | bytes 6291464 | tf_op jit(solution)/shard_map/ppermute | solution.py:1010
  259.7 2.2 copy-done.7
  261.9 17.0 %shard_map.264 = (bf16[2048,256]{1,0:T(8,128)(2,1)S(1)}, bf16[3,2048,256]{2,1,0:T(8,128)(2,1)S(1)}) custom-call(bf16[4,2048,256]{2,1,0:T(8,128)(2,1)S(1)} %copy-done.7, bf16[4,2048,256]{2,1,0:T(8,128)(2,1)S(1)} %copy-done.7, bf16[4,2048,256]{2,1,0:T(8,128)(2,1)S(1)} %copy-done.7, bf16[4,2048,256]{2,1,0:T(8,128)(2,1)S(1)} %copy-done.7, ...), custom_call_target="tpu_custom_call" | custom-call | flops 12884901888 | bytes 4194304 | tf_op jit(solution)/shard_map/pallas_call | solution.py:594
  281.4 17.2 %shard_map.265 = (bf16[2048,256]{1,0:T(8,128)(2,1)S(1)}, bf16[3,2048,256]{2,1,0:T(8,128)(2,1)S(1)}) custom-call(bf16[4,2048,256]{2,1,0:T(8,128)(2,1)S(1)} %copy-done.7, bf16[4,2048,256]{2,1,0:T(8,128)(2,1)S(1)} %copy-done.7, bf16[4,2048,256]{2,1,0:T(8,128)(2,1)S(1)} %copy-done.7, ...), custom_call_target="tpu_custom_call", output_to_operand_aliasing={{0}: (8, {}), {1}: (9, {})} | custom-call | flops 12884901888 | bytes 4194304 | tf_op jit(solution)/shard_map/pallas_call | solution.py:594
  299.6 2.4 add_convert_fusion
  302.3 14.0 %shard_map.266 = (bf16[1024,1024]{1,0:T(8,128)(2,1)}, bf16[1024,1024]{1,0:T(8,128)(2,1)}, bf16[1024,1024]{1,0:T(8,128)(2,1)}, bf16[1024,1024]{1,0:T(8,128)(2,1)}) custom-call(s32[16]{0:T(128)} %xor_add_fusion.place, bf16[3,2048,256]{2,1,0:T(8,128)(2,1)} %copy-done.10, bf16[2048,256]{1,0:T(8,128)(2,1)} %copy-done.15, bf16[8,192,256]{2,1,0:T(8,128)(2,1)} %copy-done.24, ...), custom_call_target="tpu_custom_call" | custom-call | flops 4294967296 | bytes 16777216 | tf_op jit(solution)/shard_map/pallas_call | solution.py:745
  318.8 12.5 %shard_map.267 = (bf16[8,320,256]{2,1,0:T(8,128)(2,1)}, bf16[8,320,256]{2,1,0:T(8,128)(2,1)}, f32[3,1,256]{2,1,0:T(1,128)}) custom-call(s32[16]{0:T(128)} %xor_add_fusion.place, bf16[2048,1024]{1,0:T(8,128)(2,1)} %get-tuple-element.417.normed.refs_0_, bf16[3,2048,256]{2,1,0:T(8,128)(2,1)} %copy-done.10, bf16[2048,256]{1,0:T(8,128)(2,1)} %copy-done.19, ...), custom_call_target="tpu_custom_call" | custom-call | flops 4294967296 | bytes 12582912 | tf_op jit(solution)/shard_map/pallas_call | solution.py:683
  332.0 1.5 collective-permute-start.39
  334.3 13.0 %shard_map.268 = (bf16[1024,1024]{1,0:T(8,128)(2,1)}, f32[8,1024]{1,0:T(8,128)}) custom-call(bf16[1024,1024]{1,0:T(8,128)(2,1)} %bitcast.source.hidden, bf16[1024,1024]{1,0:T(8,128)(2,1)} %bitcast.1.cotangent.grads, bf16[1024,1024]{1,0:T(8,128)(2,1)} %get-tuple-element.487.one_mine, bf16[1024,1024]{1,0:T(8,128)(2,1)} %collective-permute-done.36.one_come, ...), custom_call_target="tpu_custom_call" | custom-call | flops 41943040 | bytes 14680064 | tf_op jit(solution)/shard_map/pallas_call | solution.py:936
  349.3 2.4 add_convert_fusion.4
  357.2 2.4 collective-permute-done.40
  359.6 4.4 %collective-permute-done.41 = bf16[4,320,256]{2,1,0:T(8,128)(2,1)S(1)} collective-permute-done((bf16[4,320,256]{2,1,0:T(8,128)(2,1)}, bf16[4,320,256]{2,1,0:T(8,128)(2,1)S(1)}, u32[]{:S(2)}, u32[]{:S(2)}) %collective-permute-start.41) | collective-permute-done | bytes 655392 | tf_op jit(solution)/shard_map/ppermute | solution.py:1010
  364.2 1.6 collective-permute-start.42
  366.6 1.4 collective-permute-start.44
  369.0 5.2 %shard_map.269 = bf16[1024,1024]{1,0:T(8,128)(2,1)} custom-call(bf16[1024,1024]{1,0:T(8,128)(2,1)} %bitcast.source.hidden, bf16[1024,1024]{1,0:T(8,128)(2,1)} %get-tuple-element.523.mine, bf16[1024,1024]{1,0:T(8,128)(2,1)} %collective-permute-done.37.come, bf16[2,1024]{1,0:T(2,128)(2,1)} %pad_maximum_fusion.22.scales), custom_call_target="tpu_custom_call" | custom-call | flops 41943040 | bytes 8388608 | tf_op jit(solution)/shard_map/pallas_call | solution.py:936
  374.2 6.3 %collective-permute-done.45 = bf16[1,128,1024]{2,1,0:T(8,128)(2,1)S(1)} collective-permute-done((bf16[1,128,1024]{2,1,0:T(8,128)(2,1)}, bf16[1,128,1024]{2,1,0:T(8,128)(2,1)S(1)}, u32[]{:S(2)}, u32[]{:S(2)}) %collective-permute-start.45) | collective-permute-done | bytes 262176 | tf_op jit(solution)/shard_map/ppermute | solution.py:1010
  380.5 2.1 collective-permute-start.48
  388.1 5.2 %collective-permute-done.49 = bf16[1,320,256]{2,1,0:T(8,128)(2,1)S(1)} collective-permute-done((bf16[1,320,256]{2,1,0:T(8,128)(2,1)S(1)}, bf16[1,320,256]{2,1,0:T(8,128)(2,1)S(1)}, u32[]{:S(2)}, u32[]{:S(2)}) %collective-permute-start.49) | collective-permute-done | bytes 163872 | tf_op jit(solution)/shard_map/ppermute | solution.py:1010
  (337 shorter events, 65.8 us)
Async XLA Ops:
  1.6 6.8 %collective-permute-start.3 = (bf16[512]{0:T(512)(128)(2,1)S(1)}, bf16[512]{0:T(512)(128)(2,1)S(1)}, u32[]{:S(2)}, u32[]{:S(2)}) collective-permute-start(bf16[512]{0:T(512)(128)(2,1)S(1)} %pad_add_fusion.1), channel_id=1, source_target_pairs={{0,2},{1,3},{2,0},{3,1},{4,6},{5,7},{6,4},{7,5},{8,10},{9,11},{10,... | collective-permute-start | bytes 3080 | tf_op jit(solution)/shard_map/ppermute | solution.py:1010
  9.4 4.7 %collective-permute-start.5 = (bf16[1,1024]{1,0:T(2,128)(2,1)S(1)}, bf16[1,1024]{1,0:T(2,128)(2,1)S(1)}, u32[]{:S(2)}, u32[]{:S(2)}) collective-permute-start(bf16[1,1024]{1,0:T(2,128)(2,1)S(1)} %bitcast.174), channel_id=1, source_target_pairs={{0,16},{1,17},{2,18},{3,19},{4,20},{5,21},{6,22},{7,23},{8,24},{9,... | collective-permute-start | bytes 6152 | tf_op jit(solution)/shard_map/ppermute | solution.py:1010
  13.1 25.4 %collective-permute-start.11 = (s32[1,1024]{1,0:T(1,128)S(1)}, s32[1,1024]{1,0:T(1,128)S(1)}, u32[]{:S(2)}, u32[]{:S(2)}) collective-permute-start(s32[1,1024]{1,0:T(1,128)S(1)} %copy-done.48), channel_id=1, source_target_pairs={{0,2},{1,3},{2,0},{3,1},{4,6},{5,7},{6,4},{7,5},{8,10},{9,11},{10,... | collective-permute-start | bytes 12296 | tf_op jit(solution)/shard_map/ppermute | solution.py:1010
  13.6 43.9 %collective-permute-start = (bf16[1024,1024]{1,0:T(8,128)(2,1)}, bf16[1024,1024]{1,0:T(8,128)(2,1)}, u32[]{:S(2)}, u32[]{:S(2)}) collective-permute-start(bf16[1024,1024]{1,0:T(8,128)(2,1)} %bitcast.source.hidden), channel_id=1, source_target_pairs={{0,2},{1,3},{2,0},{3,1},{4,6},{5,7},{6,4},{7,5},{8,10},{9,11},{10,... | collective-permute-start | bytes 6291464 | tf_op jit(solution)/shard_map/ppermute | solution.py:1010
  13.6 43.8 %collective-permute-start.1 = (bf16[1024,1024]{1,0:T(8,128)(2,1)}, bf16[1024,1024]{1,0:T(8,128)(2,1)}, u32[]{:S(2)}, u32[]{:S(2)}) collective-permute-start(bf16[1024,1024]{1,0:T(8,128)(2,1)} %bitcast.1.cotangent.grads), channel_id=1, source_target_pairs={{0,2},{1,3},{2,0},{3,1},{4,6},{5,7},{6,4},{7,5},{8,10},{9,11},{10,... | collective-permute-start | bytes 6291464 | tf_op jit(solution)/shard_map/ppermute | solution.py:1010
  14.1 10.2 %collective-permute-start.4 = (bf16[1,320,256]{2,1,0:T(8,128)(2,1)S(1)}, bf16[1,320,256]{2,1,0:T(8,128)(2,1)S(1)}, u32[]{:S(2)}, u32[]{:S(2)}) collective-permute-start(bf16[1,320,256]{2,1,0:T(8,128)(2,1)S(1)} %bitcast.153), channel_id=1, source_target_pairs={{0,16},{1,17},{2,18},{3,19},{4,20},{5,21},{6,22},{7,23},{8,24},{9,... | collective-permute-start | bytes 491528 | tf_op jit(solution)/shard_map/ppermute | solution.py:1010
  14.1 3.5 collective-permute-start.6
  28.2 6.9 %collective-permute-start.9 = (bf16[2,320,256]{2,1,0:T(8,128)(2,1)S(1)}, bf16[2,320,256]{2,1,0:T(8,128)(2,1)S(1)}, u32[]{:S(2)}, u32[]{:S(2)}) collective-permute-start(bf16[2,320,256]{2,1,0:T(8,128)(2,1)S(1)} %pad_maximum_fusion.11), channel_id=1, source_target_pairs={{0,8},{1,9},{2,10},{3,11},{4,12},{5,13},{6,14},{7,15},{8,0},{9,1},... | collective-permute-start | bytes 983048 | tf_op jit(solution)/shard_map/ppermute | solution.py:1010
  35.2 11.2 %collective-permute-start.10 = (bf16[4,320,256]{2,1,0:T(8,128)(2,1)S(1)}, bf16[4,320,256]{2,1,0:T(8,128)(2,1)S(1)}, u32[]{:S(2)}, u32[]{:S(2)}) collective-permute-start(bf16[4,320,256]{2,1,0:T(8,128)(2,1)S(1)} %pad_maximum_fusion.6), channel_id=1, source_target_pairs={{0,1},{1,0},{2,6},{3,7},{4,5},{5,4},{6,2},{7,3},{8,9},{9,8},{10,14... | collective-permute-start | bytes 1966088 | tf_op jit(solution)/shard_map/ppermute | solution.py:1010
  46.5 18.4 %collective-permute-start.13 = (bf16[8,320,256]{2,1,0:T(8,128)(2,1)S(1)}, bf16[8,320,256]{2,1,0:T(8,128)(2,1)S(1)}, u32[]{:S(2)}, u32[]{:S(2)}) collective-permute-start(bf16[8,320,256]{2,1,0:T(8,128)(2,1)S(1)} %pad_maximum_fusion.2.refs_0_.refs_2_.refs_4_.refs_6_), channel_id=1, source_target_pairs={{0,4},{1,5},{2,3},{3,2},{4,0},{5,1},{6,7},{7,6},{8,12},{9,13},{10,... | collective-permute-start | bytes 3932168 | tf_op jit(solution)/shard_map/ppermute | solution.py:1010
  49.3 15.6 %collective-permute-start.12 = (bf16[1,128,1024]{2,1,0:T(8,128)(2,1)S(1)}, bf16[1,128,1024]{2,1,0:T(8,128)(2,1)S(1)}, u32[]{:S(2)}, u32[]{:S(2)}) collective-permute-start(bf16[1,128,1024]{2,1,0:T(8,128)(2,1)S(1)} %maximum_bitcast_fusion), channel_id=1, source_target_pairs={{0,16},{1,17},{2,18},{3,19},{4,20},{5,21},{6,22},{7,23},{8,24},{9,... | collective-permute-start | bytes 786440 | tf_op jit(solution)/shard_map/ppermute | solution.py:1010
  65.9 13.9 %collective-permute-start.14 = (bf16[2,128,1024]{2,1,0:T(8,128)(2,1)}, bf16[2,128,1024]{2,1,0:T(8,128)(2,1)}, u32[]{:S(2)}, u32[]{:S(2)}) collective-permute-start(bf16[2,128,1024]{2,1,0:T(8,128)(2,1)} %pad_maximum_fusion.7), channel_id=1, source_target_pairs={{0,8},{1,9},{2,10},{3,11},{4,12},{5,13},{6,14},{7,15},{8,0},{9,1},... | collective-permute-start | bytes 1572872 | tf_op jit(solution)/shard_map/ppermute | solution.py:1010
  81.2 20.7 %collective-permute-start.16 = (bf16[1,128,1024]{2,1,0:T(8,128)(2,1)S(1)}, bf16[1,128,1024]{2,1,0:T(8,128)(2,1)S(1)}, u32[]{:S(2)}, u32[]{:S(2)}) collective-permute-start(bf16[1,128,1024]{2,1,0:T(8,128)(2,1)S(1)} %maximum_bitcast_fusion.1), channel_id=1, source_target_pairs={{0,16},{1,17},{2,18},{3,19},{4,20},{5,21},{6,22},{7,23},{8,24},{9,... | collective-permute-start | bytes 786440 | tf_op jit(solution)/shard_map/ppermute | solution.py:1010
  81.8 20.2 %collective-permute-start.15 = (bf16[4,128,1024]{2,1,0:T(8,128)(2,1)S(1)}, bf16[4,128,1024]{2,1,0:T(8,128)(2,1)S(1)}, u32[]{:S(2)}, u32[]{:S(2)}) collective-permute-start(bf16[4,128,1024]{2,1,0:T(8,128)(2,1)S(1)} %pad_maximum_fusion.3), channel_id=1, source_target_pairs={{0,1},{1,0},{2,6},{3,7},{4,5},{5,4},{6,2},{7,3},{8,9},{9,8},{10,14... | collective-permute-start | bytes 3145736 | tf_op jit(solution)/shard_map/ppermute | solution.py:1010
  103.5 20.0 %collective-permute-start.17 = (bf16[2,128,1024]{2,1,0:T(8,128)(2,1)S(1)}, bf16[2,128,1024]{2,1,0:T(8,128)(2,1)S(1)}, u32[]{:S(2)}, u32[]{:S(2)}) collective-permute-start(bf16[2,128,1024]{2,1,0:T(8,128)(2,1)S(1)} %pad_maximum_fusion.8), channel_id=1, source_target_pairs={{0,8},{1,9},{2,10},{3,11},{4,12},{5,13},{6,14},{7,15},{8,0},{9,1},... | collective-permute-start | bytes 1572872 | tf_op jit(solution)/shard_map/ppermute | solution.py:1010
  104.7 47.3 %collective-permute-start.22 = (bf16[8,128,1024]{2,1,0:T(8,128)(2,1)}, bf16[8,128,1024]{2,1,0:T(8,128)(2,1)}, u32[]{:S(2)}, u32[]{:S(2)}) collective-permute-start(bf16[8,128,1024]{2,1,0:T(8,128)(2,1)} %pad_maximum_fusion.near), channel_id=1, source_target_pairs={{0,4},{1,5},{2,3},{3,2},{4,0},{5,1},{6,7},{7,6},{8,12},{9,13},{10,... | collective-permute-start | bytes 6291464 | tf_op jit(solution)/shard_map/ppermute | solution.py:1010
  124.6 7.6 %collective-permute-start.18 = (bf16[1,192,256]{2,1,0:T(8,128)(2,1)S(1)}, bf16[1,192,256]{2,1,0:T(8,128)(2,1)S(1)}, u32[]{:S(2)}, u32[]{:S(2)}) collective-permute-start(bf16[1,192,256]{2,1,0:T(8,128)(2,1)S(1)} %bitcast.156), channel_id=1, source_target_pairs={{0,16},{1,17},{2,18},{3,19},{4,20},{5,21},{6,22},{7,23},{8,24},{9,... | collective-permute-start | bytes 294920 | tf_op jit(solution)/shard_map/ppermute | solution.py:1010
  125.7 26.4 %collective-permute-start.19 = (bf16[4,128,1024]{2,1,0:T(8,128)(2,1)}, bf16[4,128,1024]{2,1,0:T(8,128)(2,1)}, u32[]{:S(2)}, u32[]{:S(2)}) collective-permute-start(bf16[4,128,1024]{2,1,0:T(8,128)(2,1)} %pad_maximum_fusion.4), channel_id=1, source_target_pairs={{0,1},{1,0},{2,6},{3,7},{4,5},{5,4},{6,2},{7,3},{8,9},{9,8},{10,14... | collective-permute-start | bytes 3145736 | tf_op jit(solution)/shard_map/ppermute | solution.py:1010
  132.2 19.8 %collective-permute-start.20 = (bf16[8,192,256]{2,1,0:T(8,128)(2,1)S(1)}, bf16[8,192,256]{2,1,0:T(8,128)(2,1)S(1)}, u32[]{:S(2)}, u32[]{:S(2)}) collective-permute-start(bf16[8,192,256]{2,1,0:T(8,128)(2,1)S(1)} %get-tuple-element.358), channel_id=1, source_target_pairs={{0,4},{1,5},{2,3},{3,2},{4,0},{5,1},{6,7},{7,6},{8,12},{9,13},{10,... | collective-permute-start | bytes 2359304 | tf_op jit(solution)/shard_map/ppermute | solution.py:1010
  133.7 12.5 %collective-permute-start.21 = (bf16[2,192,256]{2,1,0:T(8,128)(2,1)S(1)}, bf16[2,192,256]{2,1,0:T(8,128)(2,1)S(1)}, u32[]{:S(2)}, u32[]{:S(2)}) collective-permute-start(bf16[2,192,256]{2,1,0:T(8,128)(2,1)S(1)} %pad_maximum_fusion.13), channel_id=1, source_target_pairs={{0,8},{1,9},{2,10},{3,11},{4,12},{5,13},{6,14},{7,15},{8,0},{9,1},... | collective-permute-start | bytes 589832 | tf_op jit(solution)/shard_map/ppermute | solution.py:1010
  154.0 39.7 %collective-permute-start.23 = (bf16[4,192,256]{2,1,0:T(8,128)(2,1)S(1)}, bf16[4,192,256]{2,1,0:T(8,128)(2,1)S(1)}, u32[]{:S(2)}, u32[]{:S(2)}) collective-permute-start(bf16[4,192,256]{2,1,0:T(8,128)(2,1)S(1)} %get-tuple-element.380), channel_id=1, source_target_pairs={{0,1},{1,0},{2,6},{3,7},{4,5},{5,4},{6,2},{7,3},{8,9},{9,8},{10,14... | collective-permute-start | bytes 1179656 | tf_op jit(solution)/shard_map/ppermute | solution.py:1010
  154.9 38.9 %collective-permute-start.24 = (bf16[4,192,256]{2,1,0:T(8,128)(2,1)S(1)}, bf16[4,192,256]{2,1,0:T(8,128)(2,1)S(1)}, u32[]{:S(2)}, u32[]{:S(2)}) collective-permute-start(bf16[4,192,256]{2,1,0:T(8,128)(2,1)S(1)} %pad_maximum_fusion.10), channel_id=1, source_target_pairs={{0,1},{1,0},{2,6},{3,7},{4,5},{5,4},{6,2},{7,3},{8,9},{9,8},{10,14... | collective-permute-start | bytes 1179656 | tf_op jit(solution)/shard_map/ppermute | solution.py:1010
  155.6 38.2 %collective-permute-start.25 = (bf16[8,128,1024]{2,1,0:T(8,128)(2,1)S(1)}, bf16[8,128,1024]{2,1,0:T(8,128)(2,1)S(1)}, u32[]{:S(2)}, u32[]{:S(2)}) collective-permute-start(bf16[8,128,1024]{2,1,0:T(8,128)(2,1)S(1)} %pad_maximum_fusion.1.near), channel_id=1, source_target_pairs={{0,4},{1,5},{2,3},{3,2},{4,0},{5,1},{6,7},{7,6},{8,12},{9,13},{10,... | collective-permute-start | bytes 6291464 | tf_op jit(solution)/shard_map/ppermute | solution.py:1010
  194.0 39.5 %collective-permute-start.26 = (bf16[2,192,256]{2,1,0:T(8,128)(2,1)S(1)}, bf16[2,192,256]{2,1,0:T(8,128)(2,1)S(1)}, u32[]{:S(2)}, u32[]{:S(2)}) collective-permute-start(bf16[2,192,256]{2,1,0:T(8,128)(2,1)S(1)} %get-tuple-element.406), channel_id=1, source_target_pairs={{0,8},{1,9},{2,10},{3,11},{4,12},{5,13},{6,14},{7,15},{8,0},{9,1},... | collective-permute-start | bytes 589832 | tf_op jit(solution)/shard_map/ppermute | solution.py:1010
  194.3 39.2 %collective-permute-start.28 = (bf16[8,192,256]{2,1,0:T(8,128)(2,1)S(1)}, bf16[8,192,256]{2,1,0:T(8,128)(2,1)S(1)}, u32[]{:S(2)}, u32[]{:S(2)}) collective-permute-start(bf16[8,192,256]{2,1,0:T(8,128)(2,1)S(1)} %pad_maximum_fusion.5.refs_0_.refs_2_.refs_4_), channel_id=1, source_target_pairs={{0,4},{1,5},{2,3},{3,2},{4,0},{5,1},{6,7},{7,6},{8,12},{9,13},{10,... | collective-permute-start | bytes 2359304 | tf_op jit(solution)/shard_map/ppermute | solution.py:1010
  195.8 37.8 %collective-permute-start.27 = (bf16[8,128,1024]{2,1,0:T(8,128)(2,1)S(1)}, bf16[8,128,1024]{2,1,0:T(8,128)(2,1)S(1)}, u32[]{:S(2)}, u32[]{:S(2)}) collective-permute-start(bf16[8,128,1024]{2,1,0:T(8,128)(2,1)S(1)} %get-tuple-element.408), channel_id=1, source_target_pairs={{0,4},{1,5},{2,3},{3,2},{4,0},{5,1},{6,7},{7,6},{8,12},{9,13},{10,... | collective-permute-start | bytes 6291464 | tf_op jit(solution)/shard_map/ppermute | solution.py:1010
  236.6 14.3 %collective-permute-start.29 = (bf16[4,128,1024]{2,1,0:T(8,128)(2,1)}, bf16[4,128,1024]{2,1,0:T(8,128)(2,1)}, u32[]{:S(2)}, u32[]{:S(2)}) collective-permute-start(bf16[4,128,1024]{2,1,0:T(8,128)(2,1)} %get-tuple-element.421), channel_id=1, source_target_pairs={{0,1},{1,0},{2,6},{3,7},{4,5},{5,4},{6,2},{7,3},{8,9},{9,8},{10,14... | collective-permute-start | bytes 3145736 | tf_op jit(solution)/shard_map/ppermute | solution.py:1010
  237.4 12.1 %collective-permute-start.30 = (bf16[1,192,256]{2,1,0:T(8,128)(2,1)S(1)}, bf16[1,192,256]{2,1,0:T(8,128)(2,1)S(1)}, u32[]{:S(2)}, u32[]{:S(2)}) collective-permute-start(bf16[1,192,256]{2,1,0:T(8,128)(2,1)S(1)} %get-tuple-element.426), channel_id=1, source_target_pairs={{0,16},{1,17},{2,18},{3,19},{4,20},{5,21},{6,22},{7,23},{8,24},{9,... | collective-permute-start | bytes 294920 | tf_op jit(solution)/shard_map/ppermute | solution.py:1010
  252.4 26.5 %collective-permute-start.32 = (bf16[1024,1024]{1,0:T(8,128)(2,1)}, bf16[1024,1024]{1,0:T(8,128)(2,1)S(1)}, u32[]{:S(2)}, u32[]{:S(2)}) collective-permute-start(bf16[1024,1024]{1,0:T(8,128)(2,1)} %get-tuple-element.438), channel_id=1, source_target_pairs={{0,2},{1,3},{2,0},{3,1},{4,6},{5,7},{6,4},{7,5},{8,10},{9,11},{10,... | collective-permute-start | bytes 6291464 | tf_op jit(solution)/shard_map/ppermute | solution.py:1010
  257.9 21.0 %collective-permute-start.31 = (bf16[2,128,1024]{2,1,0:T(8,128)(2,1)S(1)}, bf16[2,128,1024]{2,1,0:T(8,128)(2,1)S(1)}, u32[]{:S(2)}, u32[]{:S(2)}) collective-permute-start(bf16[2,128,1024]{2,1,0:T(8,128)(2,1)S(1)} %get-tuple-element.437), channel_id=1, source_target_pairs={{0,8},{1,9},{2,10},{3,11},{4,12},{5,13},{6,14},{7,15},{8,0},{9,1},... | collective-permute-start | bytes 1572872 | tf_op jit(solution)/shard_map/ppermute | solution.py:1010
  258.7 40.9 %collective-permute-start.33 = (bf16[8,128,1024]{2,1,0:T(8,128)(2,1)}, bf16[8,128,1024]{2,1,0:T(8,128)(2,1)S(1)}, u32[]{:S(2)}, u32[]{:S(2)}) collective-permute-start(bf16[8,128,1024]{2,1,0:T(8,128)(2,1)} %get-tuple-element.449), channel_id=1, source_target_pairs={{0,4},{1,5},{2,3},{3,2},{4,0},{5,1},{6,7},{7,6},{8,12},{9,13},{10,... | collective-permute-start | bytes 6291464 | tf_op jit(solution)/shard_map/ppermute | solution.py:1010
  280.3 19.3 %collective-permute-start.34 = (bf16[1,128,1024]{2,1,0:T(8,128)(2,1)S(1)}, bf16[1,128,1024]{2,1,0:T(8,128)(2,1)S(1)}, u32[]{:S(2)}, u32[]{:S(2)}) collective-permute-start(bf16[1,128,1024]{2,1,0:T(8,128)(2,1)S(1)} %get-tuple-element.451), channel_id=1, source_target_pairs={{0,16},{1,17},{2,18},{3,19},{4,20},{5,21},{6,22},{7,23},{8,24},{9,... | collective-permute-start | bytes 786440 | tf_op jit(solution)/shard_map/ppermute | solution.py:1010
  302.0 14.3 %collective-permute-start.35 = (bf16[4,128,1024]{2,1,0:T(8,128)(2,1)}, bf16[4,128,1024]{2,1,0:T(8,128)(2,1)S(1)}, u32[]{:S(2)}, u32[]{:S(2)}) collective-permute-start(bf16[4,128,1024]{2,1,0:T(8,128)(2,1)} %get-tuple-element.465), channel_id=1, source_target_pairs={{0,1},{1,0},{2,6},{3,7},{4,5},{5,4},{6,2},{7,3},{8,9},{9,8},{10,14... | collective-permute-start | bytes 3145736 | tf_op jit(solution)/shard_map/ppermute | solution.py:1010
  317.6 13.7 %collective-permute-start.36 = (bf16[1024,1024]{1,0:T(8,128)(2,1)}, bf16[1024,1024]{1,0:T(8,128)(2,1)}, u32[]{:S(2)}, u32[]{:S(2)}) collective-permute-start(bf16[1024,1024]{1,0:T(8,128)(2,1)} %get-tuple-element.480), channel_id=1, source_target_pairs={{0,2},{1,3},{2,0},{3,1},{4,6},{5,7},{6,4},{7,5},{8,10},{9,11},{10,... | collective-permute-start | bytes 6291464 | tf_op jit(solution)/shard_map/ppermute | solution.py:1010
  318.8 12.5 %collective-permute-start.37 = (bf16[1024,1024]{1,0:T(8,128)(2,1)}, bf16[1024,1024]{1,0:T(8,128)(2,1)}, u32[]{:S(2)}, u32[]{:S(2)}) collective-permute-start(bf16[1024,1024]{1,0:T(8,128)(2,1)} %get-tuple-element.481), channel_id=1, source_target_pairs={{0,2},{1,3},{2,0},{3,1},{4,6},{5,7},{6,4},{7,5},{8,10},{9,11},{10,... | collective-permute-start | bytes 6291464 | tf_op jit(solution)/shard_map/ppermute | solution.py:1010
  331.2 17.1 %collective-permute-start.38 = (bf16[8,320,256]{2,1,0:T(8,128)(2,1)}, bf16[8,320,256]{2,1,0:T(8,128)(2,1)}, u32[]{:S(2)}, u32[]{:S(2)}) collective-permute-start(bf16[8,320,256]{2,1,0:T(8,128)(2,1)} %get-tuple-element.498), channel_id=1, source_target_pairs={{0,4},{1,5},{2,3},{3,2},{4,0},{5,1},{6,7},{7,6},{8,12},{9,13},{10,... | collective-permute-start | bytes 3932168 | tf_op jit(solution)/shard_map/ppermute | solution.py:1010
  332.0 15.3 %collective-permute-start.39 = (bf16[2,128,1024]{2,1,0:T(8,128)(2,1)}, bf16[2,128,1024]{2,1,0:T(8,128)(2,1)S(1)}, u32[]{:S(2)}, u32[]{:S(2)}) collective-permute-start(bf16[2,128,1024]{2,1,0:T(8,128)(2,1)} %get-tuple-element.500), channel_id=1, source_target_pairs={{0,8},{1,9},{2,10},{3,11},{4,12},{5,13},{6,14},{7,15},{8,0},{9,1},... | collective-permute-start | bytes 1572872 | tf_op jit(solution)/shard_map/ppermute | solution.py:1010
  354.0 10.0 %collective-permute-start.41 = (bf16[4,320,256]{2,1,0:T(8,128)(2,1)}, bf16[4,320,256]{2,1,0:T(8,128)(2,1)S(1)}, u32[]{:S(2)}, u32[]{:S(2)}) collective-permute-start(bf16[4,320,256]{2,1,0:T(8,128)(2,1)} %get-tuple-element.517), channel_id=1, source_target_pairs={{0,1},{1,0},{2,6},{3,7},{4,5},{5,4},{6,2},{7,3},{8,9},{9,8},{10,14... | collective-permute-start | bytes 1966088 | tf_op jit(solution)/shard_map/ppermute | solution.py:1010
  355.9 3.7 collective-permute-start.40
  364.2 3.9 collective-permute-start.42
  365.9 14.6 %collective-permute-start.45 = (bf16[1,128,1024]{2,1,0:T(8,128)(2,1)}, bf16[1,128,1024]{2,1,0:T(8,128)(2,1)S(1)}, u32[]{:S(2)}, u32[]{:S(2)}) collective-permute-start(bf16[1,128,1024]{2,1,0:T(8,128)(2,1)} %get-tuple-element.532), channel_id=1, source_target_pairs={{0,16},{1,17},{2,18},{3,19},{4,20},{5,21},{6,22},{7,23},{8,24},{9,... | collective-permute-start | bytes 786440 | tf_op jit(solution)/shard_map/ppermute | solution.py:1010
  366.6 13.9 %collective-permute-start.44 = (bf16[2,320,256]{2,1,0:T(8,128)(2,1)S(1)}, bf16[2,320,256]{2,1,0:T(8,128)(2,1)S(1)}, u32[]{:S(2)}, u32[]{:S(2)}) collective-permute-start(bf16[2,320,256]{2,1,0:T(8,128)(2,1)S(1)} %get-tuple-element.526), channel_id=1, source_target_pairs={{0,8},{1,9},{2,10},{3,11},{4,12},{5,13},{6,14},{7,15},{8,0},{9,1},... | collective-permute-start | bytes 983048 | tf_op jit(solution)/shard_map/ppermute | solution.py:1010
  368.1 6.1 %collective-permute-start.43 = (f32[4,384]{1,0:T(4,128)S(1)}, f32[4,384]{1,0:T(4,128)S(1)}, u32[]{:S(2)}, u32[]{:S(2)}) collective-permute-start(f32[4,384]{1,0:T(4,128)S(1)} %slice_select_fusion.2), channel_id=1, source_target_pairs={{0,4},{1,5},{2,6},{3,7},{4,0},{5,1},{6,2},{7,3},{8,12},{9,13},{10,... | collective-permute-start | bytes 18440 | tf_op jit(solution)/shard_map/ppermute | solution.py:1010
  380.5 15.6 %collective-permute-start.48 = (f32[3,32,256]{2,1,0:T(8,128)S(1)}, f32[3,32,256]{2,1,0:T(8,128)S(1)}, u32[]{:S(2)}, u32[]{:S(2)}) collective-permute-start(f32[3,32,256]{2,1,0:T(8,128)S(1)} %get-tuple-element.595), channel_id=1, source_target_pairs={{0,2},{1,3},{2,0},{3,1},{4,6},{5,7},{6,4},{7,5},{8,10},{9,11},{10,... | collective-permute-start | bytes 294920 | tf_op jit(solution)/shard_map/ppermute | solution.py:1010
  382.8 10.5 %collective-permute-start.49 = (bf16[1,320,256]{2,1,0:T(8,128)(2,1)S(1)}, bf16[1,320,256]{2,1,0:T(8,128)(2,1)S(1)}, u32[]{:S(2)}, u32[]{:S(2)}) collective-permute-start(bf16[1,320,256]{2,1,0:T(8,128)(2,1)S(1)} %get-tuple-element.543), channel_id=1, source_target_pairs={{0,16},{1,17},{2,18},{3,19},{4,20},{5,21},{6,22},{7,23},{8,24},{9,... | collective-permute-start | bytes 491528 | tf_op jit(solution)/shard_map/ppermute | solution.py:1010
  383.5 11.0 %collective-permute-start.51 = (f32[1,32,1024]{2,1,0:T(8,128)S(1)}, f32[1,32,1024]{2,1,0:T(8,128)S(1)}, u32[]{:S(2)}, u32[]{:S(2)}) collective-permute-start(f32[1,32,1024]{2,1,0:T(8,128)S(1)} %get-tuple-element.587), channel_id=1, source_target_pairs={{0,2},{1,3},{2,0},{3,1},{4,6},{5,7},{6,4},{7,5},{8,10},{9,11},{10,... | collective-permute-start | bytes 393224 | tf_op jit(solution)/shard_map/ppermute | solution.py:1010
  384.4 10.1 %collective-permute-start.52 = (f32[1,32,1024]{2,1,0:T(8,128)S(1)}, f32[1,32,1024]{2,1,0:T(8,128)S(1)}, u32[]{:S(2)}, u32[]{:S(2)}) collective-permute-start(f32[1,32,1024]{2,1,0:T(8,128)S(1)} %get-tuple-element.585), channel_id=1, source_target_pairs={{0,2},{1,3},{2,0},{3,1},{4,6},{5,7},{6,4},{7,5},{8,10},{9,11},{10,... | collective-permute-start | bytes 393224 | tf_op jit(solution)/shard_map/ppermute | solution.py:1010
  393.4 2.8 collective-permute-start.50
  (59 other events, 495.1 us)

commit v5 on v4

--- a/solution.py
+++ b/solution.py
@@ -1238,7 +1238,7 @@
     (d1, out), d_mixed = tick((d1, out), d_mixed, sum_forward[1], trade)
     keep, send, qkv_sums_two = attention_grads(place, normed_one, d_mixed, (attended_one, attended_two, both_grads))
     sum_two = Sum(pairs, keep, send)
-    (qkv_sums_two, d1, out), _ = tick((qkv_sums_two, d1, out), (), sum_two, done=(trade,))
+    (qkv_sums_two, d1, out), _ = tick((qkv_sums_two, d1, out), (), sum_two, sum_forward[1], done=(trade,))
     d1_come, out_come = trade.result()
     input_grad, sums = finish(
         finish_grad_kernel,
@@ -1247,7 +1247,7 @@
         True,
     )
     (input_grad, sums, qkv_sums_one, qkv_sums_two, up_sums), _ = tick(
-        (input_grad, sums, qkv_sums_one, qkv_sums_two, up_sums), (), sum_two, sum_forward[1]
+        (input_grad, sums, qkv_sums_one, qkv_sums_two, up_sums), (), sum_two, done=(sum_forward[1],)
     )
     def both_cores(own):
         own = own[:, None]

time: 405 us -> 400 us (0.988)
  waiting for transfers between devices: 42.1 us -> 36.4 us
    ppermute x53, waiting for transfers between devices: 42.1 us -> 36.4 us  [swap(): return lax.ppermute(value, SPLIT, moves)]
  transfers between devices with their start and end apart: 53 -> 53, of which waited for: 14 -> 14; matrix products, arithmetic and copies ran while one was open for 7% -> 7% of each run, Pallas kernels for 61% -> 62%
where the time goes in v5:
time: 400 us; the launch traced here: 393 us
  Pallas kernels  243 us (61%)
  starting transfers between devices  53.3 us (13%)
  waiting for transfers between devices  36.4 us (9%)
  other arithmetic  31.4 us (8%)
  local copies, waits for them, and re-layouts  26.5 us (7%)
    pallas_call x2, Pallas kernels, forward_chunk(): pl.pallas_call(forward_kernel, grid_spec=pltpu.PrefetchScalarGridSpec(num...  73.1 us
    pallas_call x4, Pallas kernels, attention(): pl.pallas_call(attention_kernel, grid=(width // PAIR,), in_specs=[part(0)...  68.8 us
    ppermute x53, starting transfers between devices, swap(): return lax.ppermute(value, SPLIT, moves)  53.3 us
    ppermute x53, waiting for transfers between devices, swap(): return lax.ppermute(value, SPLIT, moves)  36.4 us
    pallas_call x2, Pallas kernels, attention_back(): pl.pallas_call(partial(attention_back_kernel, half, pieces), grid_spec=pl...  26.2 us
    pallas_call x2, Pallas kernels, project(): pl.pallas_call(partial(project_kernel, half), grid_spec=pltpu.PrefetchSca...  21.6 us
    pallas_call x2, Pallas kernels, finish(): pl.pallas_call(kernel, grid=(length // ROWS,), in_specs=specs + [fixed(sc...  18.3 us
    pallas_call x2, Pallas kernels, attention_grads(): pl.pallas_call(attention_grads_kernel, grid_spec=pltpu.PrefetchScalarGrid...  18.2 us
  transfers between devices with their start and end apart: 53, of which 14 were waited for; matrix products, arithmetic and copies ran while one was open for 7% of the time, Pallas kernels for 62%

profile of v5, /device:TPU:1, one launch (start us, length us, event | category | flops | bytes accessed | tf_op | source)
XLA Modules:
  0.0 393.3 jit_solution(17518036506859206678)
XLA Ops:
  2.9 2.6 dynamic-slice_reduce_fusion.1
  9.4 3.7 collective-permute-start.5
  14.1 1.4 collective-permute-start.6
  15.6 2.1 collective-permute-done.6
  17.7 6.6 %collective-permute-done.4 = bf16[1,320,256]{2,1,0:T(8,128)(2,1)S(1)} collective-permute-done((bf16[1,320,256]{2,1,0:T(8,128)(2,1)S(1)}, bf16[1,320,256]{2,1,0:T(8,128)(2,1)S(1)}, u32[]{:S(2)}, u32[]{:S(2)}) %collective-permute-start.4) | collective-permute-done | bytes 163872 | tf_op jit(solution)/shard_map/ppermute | solution.py:1010
  26.9 1.3 collective-permute-start.8
  28.2 1.3 collective-permute-done.8
  32.3 2.9 collective-permute-done.9
  35.2 2.2 collective-permute-start.10
  38.7 7.7 %shard_map.254 = (bf16[2048,1024]{1,0:T(8,128)(2,1)}, bf16[2048,1024]{1,0:T(8,128)(2,1)}, bf16[2048,1024]{1,0:T(8,128)(2,1)}) custom-call(bf16[1024,1024]{1,0:T(8,128)(2,1)} %bitcast.source.hidden, bf16[1024,1024]{1,0:T(8,128)(2,1)} %bitcast.1.cotangent.grads, bf16[4,1024]{1,0:T(4,128)(2,1)} %reshape.310.scales), custom_call_target="tpu_custom_call" | custom-call | flops 20971520 | bytes 10485760 | tf_op jit(solution)/shard_map/pallas_call | solution.py:439
  51.1 6.3 %fusion = (f32[2048,128]{1,0:T(8,128)}, f32[2048,128]{1,0:T(8,128)}) fusion(f32[128]{0:T(128)} %get-tuple-element.620, f32[128]{0:T(128)} %get-tuple-element.621, f32[2048]{0:T(1024)S(1)} %fusion.2), kind=kLoop, calls=%fused_computation.12 | loop fusion | flops 524288 | bytes 2106368 | tf_op jit(solution)/shard_map/mul | solution.py:1106
  57.4 7.5 %shard_map.255 = (bf16[2048,1024]{1,0:T(8,128)(2,1)}, bf16[2048,1024]{1,0:T(8,128)(2,1)}, bf16[2048,1024]{1,0:T(8,128)(2,1)}) custom-call(bf16[1024,1024]{1,0:T(8,128)(2,1)} %collective-permute-done.source, bf16[1024,1024]{1,0:T(8,128)(2,1)} %collective-permute-done.1.cotangent, ...), custom_call_target="tpu_custom_call", output_to_operand_aliasing={{0}: (3, {}), {1}: (4, {}), {2}: (5, {})} | custom-call | flops 20971520 | bytes 10485760 | tf_op jit(solution)/shard_map/pallas_call | solution.py:439
  67.6 1.3 copy.152
  69.0 10.8 %shard_map.256.q_ref.k_ref.v_ref.g_ref = bf16[4,2048,256]{2,1,0:T(8,128)(2,1)} custom-call(s32[16]{0:T(128)} %xor_add_fusion.place, bf16[2048,1024]{1,0:T(8,128)(2,1)} %get-tuple-element.419.normed.refs_0_, bf16[2048,1024]{1,0:T(8,128)(2,1)} %get-tuple-element.312.grads.refs_4_, bf16[8,320,256]{2,1,0:T(8,128)(2,1)} %copy-done.22, ...), custom_call_target="tpu_custom_call" | custom-call | flops 4294967296 | bytes 12582912 | tf_op jit(solution)/shard_map/pallas_call | solution.py:516
  79.8 1.4 pad_maximum_fusion.3
  82.5 2.2 copy-done.8
  84.7 17.2 %shard_map.257 = (bf16[2048,256]{1,0:T(8,128)(2,1)S(1)}, bf16[3,2048,256]{2,1,0:T(8,128)(2,1)S(1)}) custom-call(bf16[4,2048,256]{2,1,0:T(8,128)(2,1)S(1)} %copy-done.8, bf16[4,2048,256]{2,1,0:T(8,128)(2,1)S(1)} %copy-done.8, bf16[4,2048,256]{2,1,0:T(8,128)(2,1)S(1)} %copy-done.8, bf16[4,2048,256]{2,1,0:T(8,128)(2,1)S(1)} %copy-done.8, ...), custom_call_target="tpu_custom_call" | custom-call | flops 12884901888 | bytes 4194304 | tf_op jit(solution)/shard_map/pallas_call | solution.py:594
  102.0 1.5 pad_maximum_fusion.near
  104.7 1.3 collective-permute-start.22
  106.1 17.4 %shard_map.258 = (bf16[2048,256]{1,0:T(8,128)(2,1)S(1)}, bf16[3,2048,256]{2,1,0:T(8,128)(2,1)S(1)}) custom-call(bf16[4,2048,256]{2,1,0:T(8,128)(2,1)S(1)} %copy-done.9, bf16[4,2048,256]{2,1,0:T(8,128)(2,1)S(1)} %copy-done.9, bf16[4,2048,256]{2,1,0:T(8,128)(2,1)S(1)} %copy-done.9, ...), custom_call_target="tpu_custom_call", output_to_operand_aliasing={{0}: (8, {}), {1}: (9, {})} | custom-call | flops 12884901888 | bytes 4194304 | tf_op jit(solution)/shard_map/pallas_call | solution.py:594
  126.4 5.8 %shard_map.259 = (bf16[8,192,256]{2,1,0:T(8,128)(2,1)S(1)}, bf16[8,192,256]{2,1,0:T(8,128)(2,1)S(1)}, f32[3,1,256]{2,1,0:T(1,128)S(1)}) custom-call(s32[16]{0:T(128)S(1)} %copy-done.16, bf16[2048,1024]{1,0:T(8,128)(2,1)S(1)} %copy-done, bf16[3,2048,256]{2,1,0:T(8,128)(2,1)S(1)} %get-tuple-element.354.refs_1_.d_mixed), custom_call_target="tpu_custom_call" | custom-call | flops 4294967296 | bytes 12582912 | tf_op jit(solution)/shard_map/pallas_call | solution.py:683
  134.0 12.2 %shard_map.260 = (bf16[1024,1024]{1,0:T(8,128)(2,1)}, bf16[1024,1024]{1,0:T(8,128)(2,1)}, bf16[1024,1024]{1,0:T(8,128)(2,1)}, bf16[1024,1024]{1,0:T(8,128)(2,1)}) custom-call(s32[16]{0:T(128)} %xor_add_fusion.place, bf16[3,2048,256]{2,1,0:T(8,128)(2,1)} %copy-done.18, bf16[2048,256]{1,0:T(8,128)(2,1)} %copy-done.19, bf16[8,320,256]{2,1,0:T(8,128)(2,1)} %copy-done.22, ...), custom_call_target="tpu_custom_call" | custom-call | flops 4294967296 | bytes 16777216 | tf_op jit(solution)/shard_map/pallas_call | solution.py:745
  146.2 5.8 %collective-permute-done.20 = bf16[8,192,256]{2,1,0:T(8,128)(2,1)S(1)} collective-permute-done((bf16[8,192,256]{2,1,0:T(8,128)(2,1)S(1)}, bf16[8,192,256]{2,1,0:T(8,128)(2,1)S(1)}, u32[]{:S(2)}, u32[]{:S(2)}) %collective-permute-start.20) | collective-permute-done | bytes 786464 | tf_op jit(solution)/shard_map/ppermute | solution.py:1010
  152.3 1.7 pad_maximum_fusion.1.near
  156.7 35.8 %shard_map.261 = (bf16[8,128,1024]{2,1,0:T(8,128)(2,1)S(1)}, bf16[8,128,1024]{2,1,0:T(8,128)(2,1)S(1)}, f32[1,1024]{1,0:T(1,128)S(1)}, bf16[1024,1024]{1,0:T(8,1...) custom-call(s32[16]{0:T(128)S(1)} %copy-done.17, ...), custom_call_target="tpu_custom_call" | custom-call | flops 25769803776 | bytes 33554432 | tf_op jit(solution)/shard_map/pallas_call | solution.py:864
  192.5 1.3 copy-done.21
  196.2 37.3 %shard_map.262 = (bf16[8,128,1024]{2,1,0:T(8,128)(2,1)S(1)}, bf16[8,128,1024]{2,1,0:T(8,128)(2,1)}, f32[1,1024]{1,0:T(1,128)S(1)}, bf16[1024,1024]{1,0:T(8,128)(...) custom-call(s32[16]{0:T(128)S(1)} %copy-done.17, ...), custom_call_target="tpu_custom_call" | custom-call | flops 25769803776 | bytes 33554432 | tf_op jit(solution)/shard_map/pallas_call | solution.py:864
  233.6 2.6 add_convert_fusion.2
  238.6 10.8 %shard_map.263.q_ref.k_ref.v_ref.g_ref = bf16[4,2048,256]{2,1,0:T(8,128)(2,1)} custom-call(s32[16]{0:T(128)} %xor_add_fusion.place, bf16[2048,1024]{1,0:T(8,128)(2,1)} %get-tuple-element.419.normed.refs_0_, bf16[2048,1024]{1,0:T(8,128)(2,1)} %get-tuple-element.312.grads.refs_4_, bf16[8,192,256]{2,1,0:T(8,128)(2,1)} %copy-done.24, ...), custom_call_target="tpu_custom_call" | custom-call | flops 4294967296 | bytes 12582912 | tf_op jit(solution)/shard_map/pallas_call | solution.py:516
  249.5 1.4 collective-permute-done.29
  250.9 1.6 add_convert_fusion.8
  252.4 5.5 %collective-permute-start.32 = (bf16[1024,1024]{1,0:T(8,128)(2,1)}, bf16[1024,1024]{1,0:T(8,128)(2,1)S(1)}, u32[]{:S(2)}, u32[]{:S(2)}) collective-permute-start(bf16[1024,1024]{1,0:T(8,128)(2,1)} %get-tuple-element.440), channel_id=1, source_target_pairs={{0,2},{1,3},{2,0},{3,1},{4,6},{5,7},{6,4},{7,5},{8,10},{9,11},{10,... | collective-permute-start | bytes 6291464 | tf_op jit(solution)/shard_map/ppermute | solution.py:1010
  259.7 2.2 copy-done.7
  261.9 17.0 %shard_map.264 = (bf16[2048,256]{1,0:T(8,128)(2,1)S(1)}, bf16[3,2048,256]{2,1,0:T(8,128)(2,1)S(1)}) custom-call(bf16[4,2048,256]{2,1,0:T(8,128)(2,1)S(1)} %copy-done.7, bf16[4,2048,256]{2,1,0:T(8,128)(2,1)S(1)} %copy-done.7, bf16[4,2048,256]{2,1,0:T(8,128)(2,1)S(1)} %copy-done.7, bf16[4,2048,256]{2,1,0:T(8,128)(2,1)S(1)} %copy-done.7, ...), custom_call_target="tpu_custom_call" | custom-call | flops 12884901888 | bytes 4194304 | tf_op jit(solution)/shard_map/pallas_call | solution.py:594
  281.3 17.2 %shard_map.265 = (bf16[2048,256]{1,0:T(8,128)(2,1)S(1)}, bf16[3,2048,256]{2,1,0:T(8,128)(2,1)S(1)}) custom-call(bf16[4,2048,256]{2,1,0:T(8,128)(2,1)S(1)} %copy-done.7, bf16[4,2048,256]{2,1,0:T(8,128)(2,1)S(1)} %copy-done.7, bf16[4,2048,256]{2,1,0:T(8,128)(2,1)S(1)} %copy-done.7, ...), custom_call_target="tpu_custom_call", output_to_operand_aliasing={{0}: (8, {}), {1}: (9, {})} | custom-call | flops 12884901888 | bytes 4194304 | tf_op jit(solution)/shard_map/pallas_call | solution.py:594
  299.5 2.4 add_convert_fusion
  302.3 14.0 %shard_map.266 = (bf16[1024,1024]{1,0:T(8,128)(2,1)}, bf16[1024,1024]{1,0:T(8,128)(2,1)}, bf16[1024,1024]{1,0:T(8,128)(2,1)}, bf16[1024,1024]{1,0:T(8,128)(2,1)}) custom-call(s32[16]{0:T(128)} %xor_add_fusion.place, bf16[3,2048,256]{2,1,0:T(8,128)(2,1)} %copy-done.10, bf16[2048,256]{1,0:T(8,128)(2,1)} %copy-done.15, bf16[8,192,256]{2,1,0:T(8,128)(2,1)} %copy-done.24, ...), custom_call_target="tpu_custom_call" | custom-call | flops 4294967296 | bytes 16777216 | tf_op jit(solution)/shard_map/pallas_call | solution.py:745
  318.1 1.5 collective-permute-start.36
  319.6 12.4 %shard_map.267 = (bf16[8,320,256]{2,1,0:T(8,128)(2,1)}, bf16[8,320,256]{2,1,0:T(8,128)(2,1)}, f32[3,1,256]{2,1,0:T(1,128)}) custom-call(s32[16]{0:T(128)} %xor_add_fusion.place, bf16[2048,1024]{1,0:T(8,128)(2,1)} %get-tuple-element.419.normed.refs_0_, bf16[3,2048,256]{2,1,0:T(8,128)(2,1)} %copy-done.10, bf16[2048,256]{1,0:T(8,128)(2,1)} %copy-done.19, ...), custom_call_target="tpu_custom_call" | custom-call | flops 4294967296 | bytes 12582912 | tf_op jit(solution)/shard_map/pallas_call | solution.py:683
  335.1 13.1 %shard_map.268 = (bf16[1024,1024]{1,0:T(8,128)(2,1)}, f32[8,1024]{1,0:T(8,128)}) custom-call(bf16[1024,1024]{1,0:T(8,128)(2,1)} %bitcast.source.hidden, bf16[1024,1024]{1,0:T(8,128)(2,1)} %bitcast.1.cotangent.grads, bf16[1024,1024]{1,0:T(8,128)(2,1)} %get-tuple-element.493.one_mine, bf16[1024,1024]{1,0:T(8,128)(2,1)} %collective-permute-done.37.one_come, ...), custom_call_target="tpu_custom_call" | custom-call | flops 41943040 | bytes 14680064 | tf_op jit(solution)/shard_map/pallas_call | solution.py:936
  349.4 2.4 add_convert_fusion.4
  355.1 1.7 collective-permute-start.41
  356.7 2.0 collective-permute-done.41
  358.7 5.4 %collective-permute-done.42 = bf16[4,320,256]{2,1,0:T(8,128)(2,1)S(1)} collective-permute-done((bf16[4,320,256]{2,1,0:T(8,128)(2,1)}, bf16[4,320,256]{2,1,0:T(8,128)(2,1)S(1)}, u32[]{:S(2)}, u32[]{:S(2)}) %collective-permute-start.42) | collective-permute-done | bytes 655392 | tf_op jit(solution)/shard_map/ppermute | solution.py:1010
  367.8 5.2 %shard_map.269 = bf16[1024,1024]{1,0:T(8,128)(2,1)} custom-call(bf16[1024,1024]{1,0:T(8,128)(2,1)} %bitcast.source.hidden, bf16[1024,1024]{1,0:T(8,128)(2,1)} %get-tuple-element.527.mine, bf16[1024,1024]{1,0:T(8,128)(2,1)} %collective-permute-done.38.come, bf16[2,1024]{1,0:T(2,128)(2,1)} %pad_maximum_fusion.22.scales), custom_call_target="tpu_custom_call" | custom-call | flops 41943040 | bytes 8388608 | tf_op jit(solution)/shard_map/pallas_call | solution.py:936
  373.1 4.7 %collective-permute-start.48 = (f32[3,32,256]{2,1,0:T(8,128)S(1)}, f32[3,32,256]{2,1,0:T(8,128)S(1)}, u32[]{:S(2)}, u32[]{:S(2)}) collective-permute-start(f32[3,32,256]{2,1,0:T(8,128)S(1)} %get-tuple-element.599), channel_id=1, source_target_pairs={{0,2},{1,3},{2,0},{3,1},{4,6},{5,7},{6,4},{7,5},{8,10},{9,11},{10,... | collective-permute-start | bytes 294920 | tf_op jit(solution)/shard_map/ppermute | solution.py:1010
  377.9 1.3 collective-permute-start.49
  384.1 4.2 %collective-permute-done.49 = bf16[1,320,256]{2,1,0:T(8,128)(2,1)S(1)} collective-permute-done((bf16[1,320,256]{2,1,0:T(8,128)(2,1)S(1)}, bf16[1,320,256]{2,1,0:T(8,128)(2,1)S(1)}, u32[]{:S(2)}, u32[]{:S(2)}) %collective-permute-start.49) | collective-permute-done | bytes 163872 | tf_op jit(solution)/shard_map/ppermute | solution.py:1010
  (337 shorter events, 63.8 us)
Async XLA Ops:
  1.6 6.8 %collective-permute-start.3 = (bf16[512]{0:T(512)(128)(2,1)S(1)}, bf16[512]{0:T(512)(128)(2,1)S(1)}, u32[]{:S(2)}, u32[]{:S(2)}) collective-permute-start(bf16[512]{0:T(512)(128)(2,1)S(1)} %pad_add_fusion.1), channel_id=1, source_target_pairs={{0,2},{1,3},{2,0},{3,1},{4,6},{5,7},{6,4},{7,5},{8,10},{9,11},{10,... | collective-permute-start | bytes 3080 | tf_op jit(solution)/shard_map/ppermute | solution.py:1010
  9.4 4.7 %collective-permute-start.5 = (bf16[1,1024]{1,0:T(2,128)(2,1)S(1)}, bf16[1,1024]{1,0:T(2,128)(2,1)S(1)}, u32[]{:S(2)}, u32[]{:S(2)}) collective-permute-start(bf16[1,1024]{1,0:T(2,128)(2,1)S(1)} %bitcast.174), channel_id=1, source_target_pairs={{0,16},{1,17},{2,18},{3,19},{4,20},{5,21},{6,22},{7,23},{8,24},{9,... | collective-permute-start | bytes 6152 | tf_op jit(solution)/shard_map/ppermute | solution.py:1010
  13.1 25.4 %collective-permute-start.11 = (s32[1,1024]{1,0:T(1,128)S(1)}, s32[1,1024]{1,0:T(1,128)S(1)}, u32[]{:S(2)}, u32[]{:S(2)}) collective-permute-start(s32[1,1024]{1,0:T(1,128)S(1)} %copy-done.48), channel_id=1, source_target_pairs={{0,2},{1,3},{2,0},{3,1},{4,6},{5,7},{6,4},{7,5},{8,10},{9,11},{10,... | collective-permute-start | bytes 12296 | tf_op jit(solution)/shard_map/ppermute | solution.py:1010
  13.6 43.8 %collective-permute-start = (bf16[1024,1024]{1,0:T(8,128)(2,1)}, bf16[1024,1024]{1,0:T(8,128)(2,1)}, u32[]{:S(2)}, u32[]{:S(2)}) collective-permute-start(bf16[1024,1024]{1,0:T(8,128)(2,1)} %bitcast.source.hidden), channel_id=1, source_target_pairs={{0,2},{1,3},{2,0},{3,1},{4,6},{5,7},{6,4},{7,5},{8,10},{9,11},{10,... | collective-permute-start | bytes 6291464 | tf_op jit(solution)/shard_map/ppermute | solution.py:1010
  13.6 43.8 %collective-permute-start.1 = (bf16[1024,1024]{1,0:T(8,128)(2,1)}, bf16[1024,1024]{1,0:T(8,128)(2,1)}, u32[]{:S(2)}, u32[]{:S(2)}) collective-permute-start(bf16[1024,1024]{1,0:T(8,128)(2,1)} %bitcast.1.cotangent.grads), channel_id=1, source_target_pairs={{0,2},{1,3},{2,0},{3,1},{4,6},{5,7},{6,4},{7,5},{8,10},{9,11},{10,... | collective-permute-start | bytes 6291464 | tf_op jit(solution)/shard_map/ppermute | solution.py:1010
  14.1 10.2 %collective-permute-start.4 = (bf16[1,320,256]{2,1,0:T(8,128)(2,1)S(1)}, bf16[1,320,256]{2,1,0:T(8,128)(2,1)S(1)}, u32[]{:S(2)}, u32[]{:S(2)}) collective-permute-start(bf16[1,320,256]{2,1,0:T(8,128)(2,1)S(1)} %bitcast.153), channel_id=1, source_target_pairs={{0,16},{1,17},{2,18},{3,19},{4,20},{5,21},{6,22},{7,23},{8,24},{9,... | collective-permute-start | bytes 491528 | tf_op jit(solution)/shard_map/ppermute | solution.py:1010
  14.1 3.5 collective-permute-start.6
  26.9 2.7 collective-permute-start.8
  28.2 6.9 %collective-permute-start.9 = (bf16[2,320,256]{2,1,0:T(8,128)(2,1)S(1)}, bf16[2,320,256]{2,1,0:T(8,128)(2,1)S(1)}, u32[]{:S(2)}, u32[]{:S(2)}) collective-permute-start(bf16[2,320,256]{2,1,0:T(8,128)(2,1)S(1)} %pad_maximum_fusion.11), channel_id=1, source_target_pairs={{0,8},{1,9},{2,10},{3,11},{4,12},{5,13},{6,14},{7,15},{8,0},{9,1},... | collective-permute-start | bytes 983048 | tf_op jit(solution)/shard_map/ppermute | solution.py:1010
  35.2 11.2 %collective-permute-start.10 = (bf16[4,320,256]{2,1,0:T(8,128)(2,1)S(1)}, bf16[4,320,256]{2,1,0:T(8,128)(2,1)S(1)}, u32[]{:S(2)}, u32[]{:S(2)}) collective-permute-start(bf16[4,320,256]{2,1,0:T(8,128)(2,1)S(1)} %pad_maximum_fusion.6), channel_id=1, source_target_pairs={{0,1},{1,0},{2,6},{3,7},{4,5},{5,4},{6,2},{7,3},{8,9},{9,8},{10,14... | collective-permute-start | bytes 1966088 | tf_op jit(solution)/shard_map/ppermute | solution.py:1010
  46.5 18.4 %collective-permute-start.13 = (bf16[8,320,256]{2,1,0:T(8,128)(2,1)S(1)}, bf16[8,320,256]{2,1,0:T(8,128)(2,1)S(1)}, u32[]{:S(2)}, u32[]{:S(2)}) collective-permute-start(bf16[8,320,256]{2,1,0:T(8,128)(2,1)S(1)} %pad_maximum_fusion.2.refs_0_.refs_2_.refs_4_.refs_6_), channel_id=1, source_target_pairs={{0,4},{1,5},{2,3},{3,2},{4,0},{5,1},{6,7},{7,6},{8,12},{9,13},{10,... | collective-permute-start | bytes 3932168 | tf_op jit(solution)/shard_map/ppermute | solution.py:1010
  49.3 15.6 %collective-permute-start.12 = (bf16[1,128,1024]{2,1,0:T(8,128)(2,1)S(1)}, bf16[1,128,1024]{2,1,0:T(8,128)(2,1)S(1)}, u32[]{:S(2)}, u32[]{:S(2)}) collective-permute-start(bf16[1,128,1024]{2,1,0:T(8,128)(2,1)S(1)} %maximum_bitcast_fusion), channel_id=1, source_target_pairs={{0,16},{1,17},{2,18},{3,19},{4,20},{5,21},{6,22},{7,23},{8,24},{9,... | collective-permute-start | bytes 786440 | tf_op jit(solution)/shard_map/ppermute | solution.py:1010
  65.8 13.9 %collective-permute-start.14 = (bf16[2,128,1024]{2,1,0:T(8,128)(2,1)}, bf16[2,128,1024]{2,1,0:T(8,128)(2,1)}, u32[]{:S(2)}, u32[]{:S(2)}) collective-permute-start(bf16[2,128,1024]{2,1,0:T(8,128)(2,1)} %pad_maximum_fusion.7), channel_id=1, source_target_pairs={{0,8},{1,9},{2,10},{3,11},{4,12},{5,13},{6,14},{7,15},{8,0},{9,1},... | collective-permute-start | bytes 1572872 | tf_op jit(solution)/shard_map/ppermute | solution.py:1010
  81.2 20.7 %collective-permute-start.16 = (bf16[1,128,1024]{2,1,0:T(8,128)(2,1)S(1)}, bf16[1,128,1024]{2,1,0:T(8,128)(2,1)S(1)}, u32[]{:S(2)}, u32[]{:S(2)}) collective-permute-start(bf16[1,128,1024]{2,1,0:T(8,128)(2,1)S(1)} %maximum_bitcast_fusion.1), channel_id=1, source_target_pairs={{0,16},{1,17},{2,18},{3,19},{4,20},{5,21},{6,22},{7,23},{8,24},{9,... | collective-permute-start | bytes 786440 | tf_op jit(solution)/shard_map/ppermute | solution.py:1010
  81.8 20.2 %collective-permute-start.15 = (bf16[4,128,1024]{2,1,0:T(8,128)(2,1)S(1)}, bf16[4,128,1024]{2,1,0:T(8,128)(2,1)S(1)}, u32[]{:S(2)}, u32[]{:S(2)}) collective-permute-start(bf16[4,128,1024]{2,1,0:T(8,128)(2,1)S(1)} %pad_maximum_fusion.3), channel_id=1, source_target_pairs={{0,1},{1,0},{2,6},{3,7},{4,5},{5,4},{6,2},{7,3},{8,9},{9,8},{10,14... | collective-permute-start | bytes 3145736 | tf_op jit(solution)/shard_map/ppermute | solution.py:1010
  103.5 20.0 %collective-permute-start.17 = (bf16[2,128,1024]{2,1,0:T(8,128)(2,1)S(1)}, bf16[2,128,1024]{2,1,0:T(8,128)(2,1)S(1)}, u32[]{:S(2)}, u32[]{:S(2)}) collective-permute-start(bf16[2,128,1024]{2,1,0:T(8,128)(2,1)S(1)} %pad_maximum_fusion.8), channel_id=1, source_target_pairs={{0,8},{1,9},{2,10},{3,11},{4,12},{5,13},{6,14},{7,15},{8,0},{9,1},... | collective-permute-start | bytes 1572872 | tf_op jit(solution)/shard_map/ppermute | solution.py:1010
  104.7 47.3 %collective-permute-start.22 = (bf16[8,128,1024]{2,1,0:T(8,128)(2,1)}, bf16[8,128,1024]{2,1,0:T(8,128)(2,1)}, u32[]{:S(2)}, u32[]{:S(2)}) collective-permute-start(bf16[8,128,1024]{2,1,0:T(8,128)(2,1)} %pad_maximum_fusion.near), channel_id=1, source_target_pairs={{0,4},{1,5},{2,3},{3,2},{4,0},{5,1},{6,7},{7,6},{8,12},{9,13},{10,... | collective-permute-start | bytes 6291464 | tf_op jit(solution)/shard_map/ppermute | solution.py:1010
  124.6 7.6 %collective-permute-start.18 = (bf16[1,192,256]{2,1,0:T(8,128)(2,1)S(1)}, bf16[1,192,256]{2,1,0:T(8,128)(2,1)S(1)}, u32[]{:S(2)}, u32[]{:S(2)}) collective-permute-start(bf16[1,192,256]{2,1,0:T(8,128)(2,1)S(1)} %bitcast.156), channel_id=1, source_target_pairs={{0,16},{1,17},{2,18},{3,19},{4,20},{5,21},{6,22},{7,23},{8,24},{9,... | collective-permute-start | bytes 294920 | tf_op jit(solution)/shard_map/ppermute | solution.py:1010
  125.7 26.4 %collective-permute-start.19 = (bf16[4,128,1024]{2,1,0:T(8,128)(2,1)}, bf16[4,128,1024]{2,1,0:T(8,128)(2,1)}, u32[]{:S(2)}, u32[]{:S(2)}) collective-permute-start(bf16[4,128,1024]{2,1,0:T(8,128)(2,1)} %pad_maximum_fusion.4), channel_id=1, source_target_pairs={{0,1},{1,0},{2,6},{3,7},{4,5},{5,4},{6,2},{7,3},{8,9},{9,8},{10,14... | collective-permute-start | bytes 3145736 | tf_op jit(solution)/shard_map/ppermute | solution.py:1010
  132.2 19.8 %collective-permute-start.20 = (bf16[8,192,256]{2,1,0:T(8,128)(2,1)S(1)}, bf16[8,192,256]{2,1,0:T(8,128)(2,1)S(1)}, u32[]{:S(2)}, u32[]{:S(2)}) collective-permute-start(bf16[8,192,256]{2,1,0:T(8,128)(2,1)S(1)} %get-tuple-element.360), channel_id=1, source_target_pairs={{0,4},{1,5},{2,3},{3,2},{4,0},{5,1},{6,7},{7,6},{8,12},{9,13},{10,... | collective-permute-start | bytes 2359304 | tf_op jit(solution)/shard_map/ppermute | solution.py:1010
  133.7 12.5 %collective-permute-start.21 = (bf16[2,192,256]{2,1,0:T(8,128)(2,1)S(1)}, bf16[2,192,256]{2,1,0:T(8,128)(2,1)S(1)}, u32[]{:S(2)}, u32[]{:S(2)}) collective-permute-start(bf16[2,192,256]{2,1,0:T(8,128)(2,1)S(1)} %pad_maximum_fusion.13), channel_id=1, source_target_pairs={{0,8},{1,9},{2,10},{3,11},{4,12},{5,13},{6,14},{7,15},{8,0},{9,1},... | collective-permute-start | bytes 589832 | tf_op jit(solution)/shard_map/ppermute | solution.py:1010
  154.0 39.7 %collective-permute-start.23 = (bf16[4,192,256]{2,1,0:T(8,128)(2,1)S(1)}, bf16[4,192,256]{2,1,0:T(8,128)(2,1)S(1)}, u32[]{:S(2)}, u32[]{:S(2)}) collective-permute-start(bf16[4,192,256]{2,1,0:T(8,128)(2,1)S(1)} %get-tuple-element.382), channel_id=1, source_target_pairs={{0,1},{1,0},{2,6},{3,7},{4,5},{5,4},{6,2},{7,3},{8,9},{9,8},{10,14... | collective-permute-start | bytes 1179656 | tf_op jit(solution)/shard_map/ppermute | solution.py:1010
  154.9 38.9 %collective-permute-start.24 = (bf16[4,192,256]{2,1,0:T(8,128)(2,1)S(1)}, bf16[4,192,256]{2,1,0:T(8,128)(2,1)S(1)}, u32[]{:S(2)}, u32[]{:S(2)}) collective-permute-start(bf16[4,192,256]{2,1,0:T(8,128)(2,1)S(1)} %pad_maximum_fusion.10), channel_id=1, source_target_pairs={{0,1},{1,0},{2,6},{3,7},{4,5},{5,4},{6,2},{7,3},{8,9},{9,8},{10,14... | collective-permute-start | bytes 1179656 | tf_op jit(solution)/shard_map/ppermute | solution.py:1010
  155.6 38.2 %collective-permute-start.25 = (bf16[8,128,1024]{2,1,0:T(8,128)(2,1)S(1)}, bf16[8,128,1024]{2,1,0:T(8,128)(2,1)S(1)}, u32[]{:S(2)}, u32[]{:S(2)}) collective-permute-start(bf16[8,128,1024]{2,1,0:T(8,128)(2,1)S(1)} %pad_maximum_fusion.1.near), channel_id=1, source_target_pairs={{0,4},{1,5},{2,3},{3,2},{4,0},{5,1},{6,7},{7,6},{8,12},{9,13},{10,... | collective-permute-start | bytes 6291464 | tf_op jit(solution)/shard_map/ppermute | solution.py:1010
  194.0 39.5 %collective-permute-start.26 = (bf16[2,192,256]{2,1,0:T(8,128)(2,1)S(1)}, bf16[2,192,256]{2,1,0:T(8,128)(2,1)S(1)}, u32[]{:S(2)}, u32[]{:S(2)}) collective-permute-start(bf16[2,192,256]{2,1,0:T(8,128)(2,1)S(1)} %get-tuple-element.408), channel_id=1, source_target_pairs={{0,8},{1,9},{2,10},{3,11},{4,12},{5,13},{6,14},{7,15},{8,0},{9,1},... | collective-permute-start | bytes 589832 | tf_op jit(solution)/shard_map/ppermute | solution.py:1010
  194.3 39.2 %collective-permute-start.28 = (bf16[8,192,256]{2,1,0:T(8,128)(2,1)S(1)}, bf16[8,192,256]{2,1,0:T(8,128)(2,1)S(1)}, u32[]{:S(2)}, u32[]{:S(2)}) collective-permute-start(bf16[8,192,256]{2,1,0:T(8,128)(2,1)S(1)} %pad_maximum_fusion.5.refs_0_.refs_2_.refs_4_), channel_id=1, source_target_pairs={{0,4},{1,5},{2,3},{3,2},{4,0},{5,1},{6,7},{7,6},{8,12},{9,13},{10,... | collective-permute-start | bytes 2359304 | tf_op jit(solution)/shard_map/ppermute | solution.py:1010
  195.8 37.8 %collective-permute-start.27 = (bf16[8,128,1024]{2,1,0:T(8,128)(2,1)S(1)}, bf16[8,128,1024]{2,1,0:T(8,128)(2,1)S(1)}, u32[]{:S(2)}, u32[]{:S(2)}) collective-permute-start(bf16[8,128,1024]{2,1,0:T(8,128)(2,1)S(1)} %get-tuple-element.410), channel_id=1, source_target_pairs={{0,4},{1,5},{2,3},{3,2},{4,0},{5,1},{6,7},{7,6},{8,12},{9,13},{10,... | collective-permute-start | bytes 6291464 | tf_op jit(solution)/shard_map/ppermute | solution.py:1010
  236.6 14.3 %collective-permute-start.29 = (bf16[4,128,1024]{2,1,0:T(8,128)(2,1)}, bf16[4,128,1024]{2,1,0:T(8,128)(2,1)}, u32[]{:S(2)}, u32[]{:S(2)}) collective-permute-start(bf16[4,128,1024]{2,1,0:T(8,128)(2,1)} %get-tuple-element.423), channel_id=1, source_target_pairs={{0,1},{1,0},{2,6},{3,7},{4,5},{5,4},{6,2},{7,3},{8,9},{9,8},{10,14... | collective-permute-start | bytes 3145736 | tf_op jit(solution)/shard_map/ppermute | solution.py:1010
  237.3 12.1 %collective-permute-start.30 = (bf16[1,192,256]{2,1,0:T(8,128)(2,1)S(1)}, bf16[1,192,256]{2,1,0:T(8,128)(2,1)S(1)}, u32[]{:S(2)}, u32[]{:S(2)}) collective-permute-start(bf16[1,192,256]{2,1,0:T(8,128)(2,1)S(1)} %get-tuple-element.428), channel_id=1, source_target_pairs={{0,16},{1,17},{2,18},{3,19},{4,20},{5,21},{6,22},{7,23},{8,24},{9,... | collective-permute-start | bytes 294920 | tf_op jit(solution)/shard_map/ppermute | solution.py:1010
  252.4 26.5 %collective-permute-start.32 = (bf16[1024,1024]{1,0:T(8,128)(2,1)}, bf16[1024,1024]{1,0:T(8,128)(2,1)S(1)}, u32[]{:S(2)}, u32[]{:S(2)}) collective-permute-start(bf16[1024,1024]{1,0:T(8,128)(2,1)} %get-tuple-element.440), channel_id=1, source_target_pairs={{0,2},{1,3},{2,0},{3,1},{4,6},{5,7},{6,4},{7,5},{8,10},{9,11},{10,... | collective-permute-start | bytes 6291464 | tf_op jit(solution)/shard_map/ppermute | solution.py:1010
  257.9 21.0 %collective-permute-start.31 = (bf16[2,128,1024]{2,1,0:T(8,128)(2,1)S(1)}, bf16[2,128,1024]{2,1,0:T(8,128)(2,1)S(1)}, u32[]{:S(2)}, u32[]{:S(2)}) collective-permute-start(bf16[2,128,1024]{2,1,0:T(8,128)(2,1)S(1)} %get-tuple-element.439), channel_id=1, source_target_pairs={{0,8},{1,9},{2,10},{3,11},{4,12},{5,13},{6,14},{7,15},{8,0},{9,1},... | collective-permute-start | bytes 1572872 | tf_op jit(solution)/shard_map/ppermute | solution.py:1010
  258.7 40.8 %collective-permute-start.33 = (bf16[8,128,1024]{2,1,0:T(8,128)(2,1)}, bf16[8,128,1024]{2,1,0:T(8,128)(2,1)S(1)}, u32[]{:S(2)}, u32[]{:S(2)}) collective-permute-start(bf16[8,128,1024]{2,1,0:T(8,128)(2,1)} %get-tuple-element.451), channel_id=1, source_target_pairs={{0,4},{1,5},{2,3},{3,2},{4,0},{5,1},{6,7},{7,6},{8,12},{9,13},{10,... | collective-permute-start | bytes 6291464 | tf_op jit(solution)/shard_map/ppermute | solution.py:1010
  280.2 19.3 %collective-permute-start.34 = (bf16[1,128,1024]{2,1,0:T(8,128)(2,1)S(1)}, bf16[1,128,1024]{2,1,0:T(8,128)(2,1)S(1)}, u32[]{:S(2)}, u32[]{:S(2)}) collective-permute-start(bf16[1,128,1024]{2,1,0:T(8,128)(2,1)S(1)} %get-tuple-element.453), channel_id=1, source_target_pairs={{0,16},{1,17},{2,18},{3,19},{4,20},{5,21},{6,22},{7,23},{8,24},{9,... | collective-permute-start | bytes 786440 | tf_op jit(solution)/shard_map/ppermute | solution.py:1010
  302.0 14.4 %collective-permute-start.35 = (bf16[4,128,1024]{2,1,0:T(8,128)(2,1)}, bf16[4,128,1024]{2,1,0:T(8,128)(2,1)S(1)}, u32[]{:S(2)}, u32[]{:S(2)}) collective-permute-start(bf16[4,128,1024]{2,1,0:T(8,128)(2,1)} %get-tuple-element.467), channel_id=1, source_target_pairs={{0,1},{1,0},{2,6},{3,7},{4,5},{5,4},{6,2},{7,3},{8,9},{9,8},{10,14... | collective-permute-start | bytes 3145736 | tf_op jit(solution)/shard_map/ppermute | solution.py:1010
  316.8 15.3 %collective-permute-start.37 = (bf16[1024,1024]{1,0:T(8,128)(2,1)}, bf16[1024,1024]{1,0:T(8,128)(2,1)}, u32[]{:S(2)}, u32[]{:S(2)}) collective-permute-start(bf16[1024,1024]{1,0:T(8,128)(2,1)} %get-tuple-element.484), channel_id=1, source_target_pairs={{0,2},{1,3},{2,0},{3,1},{4,6},{5,7},{6,4},{7,5},{8,10},{9,11},{10,... | collective-permute-start | bytes 6291464 | tf_op jit(solution)/shard_map/ppermute | solution.py:1010
  318.0 14.0 %collective-permute-start.38 = (bf16[1024,1024]{1,0:T(8,128)(2,1)}, bf16[1024,1024]{1,0:T(8,128)(2,1)}, u32[]{:S(2)}, u32[]{:S(2)}) collective-permute-start(bf16[1024,1024]{1,0:T(8,128)(2,1)} %get-tuple-element.485), channel_id=1, source_target_pairs={{0,2},{1,3},{2,0},{3,1},{4,6},{5,7},{6,4},{7,5},{8,10},{9,11},{10,... | collective-permute-start | bytes 6291464 | tf_op jit(solution)/shard_map/ppermute | solution.py:1010
  318.1 13.9 %collective-permute-start.36 = (bf16[2,128,1024]{2,1,0:T(8,128)(2,1)S(1)}, bf16[2,128,1024]{2,1,0:T(8,128)(2,1)S(1)}, u32[]{:S(2)}, u32[]{:S(2)}) collective-permute-start(bf16[2,128,1024]{2,1,0:T(8,128)(2,1)S(1)} %get-tuple-element.483), channel_id=1, source_target_pairs={{0,8},{1,9},{2,10},{3,11},{4,12},{5,13},{6,14},{7,15},{8,0},{9,1},... | collective-permute-start | bytes 1572872 | tf_op jit(solution)/shard_map/ppermute | solution.py:1010
  332.2 17.1 %collective-permute-start.39 = (bf16[8,320,256]{2,1,0:T(8,128)(2,1)}, bf16[8,320,256]{2,1,0:T(8,128)(2,1)}, u32[]{:S(2)}, u32[]{:S(2)}) collective-permute-start(bf16[8,320,256]{2,1,0:T(8,128)(2,1)} %get-tuple-element.504), channel_id=1, source_target_pairs={{0,4},{1,5},{2,3},{3,2},{4,0},{5,1},{6,7},{7,6},{8,12},{9,13},{10,... | collective-permute-start | bytes 3932168 | tf_op jit(solution)/shard_map/ppermute | solution.py:1010
  333.0 15.2 %collective-permute-start.40 = (bf16[1,128,1024]{2,1,0:T(8,128)(2,1)S(1)}, bf16[1,128,1024]{2,1,0:T(8,128)(2,1)S(1)}, u32[]{:S(2)}, u32[]{:S(2)}) collective-permute-start(bf16[1,128,1024]{2,1,0:T(8,128)(2,1)S(1)} %get-tuple-element.506), channel_id=1, source_target_pairs={{0,16},{1,17},{2,18},{3,19},{4,20},{5,21},{6,22},{7,23},{8,24},{9,... | collective-permute-start | bytes 786440 | tf_op jit(solution)/shard_map/ppermute | solution.py:1010
  354.1 10.0 %collective-permute-start.42 = (bf16[4,320,256]{2,1,0:T(8,128)(2,1)}, bf16[4,320,256]{2,1,0:T(8,128)(2,1)S(1)}, u32[]{:S(2)}, u32[]{:S(2)}) collective-permute-start(bf16[4,320,256]{2,1,0:T(8,128)(2,1)} %get-tuple-element.521), channel_id=1, source_target_pairs={{0,1},{1,0},{2,6},{3,7},{4,5},{5,4},{6,2},{7,3},{8,9},{9,8},{10,14... | collective-permute-start | bytes 1966088 | tf_op jit(solution)/shard_map/ppermute | solution.py:1010
  355.1 3.6 collective-permute-start.41
  365.1 7.9 %collective-permute-start.45 = (bf16[2,320,256]{2,1,0:T(8,128)(2,1)S(1)}, bf16[2,320,256]{2,1,0:T(8,128)(2,1)S(1)}, u32[]{:S(2)}, u32[]{:S(2)}) collective-permute-start(bf16[2,320,256]{2,1,0:T(8,128)(2,1)S(1)} %get-tuple-element.530), channel_id=1, source_target_pairs={{0,8},{1,9},{2,10},{3,11},{4,12},{5,13},{6,14},{7,15},{8,0},{9,1},... | collective-permute-start | bytes 983048 | tf_op jit(solution)/shard_map/ppermute | solution.py:1010
  366.9 6.1 %collective-permute-start.44 = (f32[4,384]{1,0:T(4,128)S(1)}, f32[4,384]{1,0:T(4,128)S(1)}, u32[]{:S(2)}, u32[]{:S(2)}) collective-permute-start(f32[4,384]{1,0:T(4,128)S(1)} %slice_select_fusion.2), channel_id=1, source_target_pairs={{0,4},{1,5},{2,6},{3,7},{4,0},{5,1},{6,2},{7,3},{8,12},{9,13},{10,... | collective-permute-start | bytes 18440 | tf_op jit(solution)/shard_map/ppermute | solution.py:1010
  373.1 18.3 %collective-permute-start.48 = (f32[3,32,256]{2,1,0:T(8,128)S(1)}, f32[3,32,256]{2,1,0:T(8,128)S(1)}, u32[]{:S(2)}, u32[]{:S(2)}) collective-permute-start(f32[3,32,256]{2,1,0:T(8,128)S(1)} %get-tuple-element.599), channel_id=1, source_target_pairs={{0,2},{1,3},{2,0},{3,1},{4,6},{5,7},{6,4},{7,5},{8,10},{9,11},{10,... | collective-permute-start | bytes 294920 | tf_op jit(solution)/shard_map/ppermute | solution.py:1010
  377.9 10.3 %collective-permute-start.49 = (bf16[1,320,256]{2,1,0:T(8,128)(2,1)S(1)}, bf16[1,320,256]{2,1,0:T(8,128)(2,1)S(1)}, u32[]{:S(2)}, u32[]{:S(2)}) collective-permute-start(bf16[1,320,256]{2,1,0:T(8,128)(2,1)S(1)} %get-tuple-element.547), channel_id=1, source_target_pairs={{0,16},{1,17},{2,18},{3,19},{4,20},{5,21},{6,22},{7,23},{8,24},{9,... | collective-permute-start | bytes 491528 | tf_op jit(solution)/shard_map/ppermute | solution.py:1010
  379.4 10.3 %collective-permute-start.51 = (f32[1,32,1024]{2,1,0:T(8,128)S(1)}, f32[1,32,1024]{2,1,0:T(8,128)S(1)}, u32[]{:S(2)}, u32[]{:S(2)}) collective-permute-start(f32[1,32,1024]{2,1,0:T(8,128)S(1)} %get-tuple-element.591), channel_id=1, source_target_pairs={{0,2},{1,3},{2,0},{3,1},{4,6},{5,7},{6,4},{7,5},{8,10},{9,11},{10,... | collective-permute-start | bytes 393224 | tf_op jit(solution)/shard_map/ppermute | solution.py:1010
  380.4 9.3 %collective-permute-start.52 = (f32[1,32,1024]{2,1,0:T(8,128)S(1)}, f32[1,32,1024]{2,1,0:T(8,128)S(1)}, u32[]{:S(2)}, u32[]{:S(2)}) collective-permute-start(f32[1,32,1024]{2,1,0:T(8,128)S(1)} %get-tuple-element.589), channel_id=1, source_target_pairs={{0,2},{1,3},{2,0},{3,1},{4,6},{5,7},{6,4},{7,5},{8,10},{9,11},{10,... | collective-permute-start | bytes 393224 | tf_op jit(solution)/shard_map/ppermute | solution.py:1010
  388.4 3.0 collective-permute-start.50
  (59 other events, 499.9 us)

commit v6 on v5

--- a/solution.py
+++ b/solution.py
@@ -392,6 +392,7 @@
 PAIR = 2 * HEAD
 ROWS = 256
 TOKENS = 512
+QUERIES = 512
 
 
 def mul(left, right, dims):
@@ -535,22 +536,22 @@
 ):
     out, d_out, mask, dk_sum, dv_sum = rest[-5:]
     length = q_ref.shape[1]
-    blocks = length // ROWS
+    blocks = length // QUERIES
 
     @pl.when(pl.program_id(0) == 0)
     def _():
         for block in range(blocks):
-            start = block * ROWS
-            end = start + ROWS
-            key_pos = lax.broadcasted_iota(jnp.int32, (ROWS, end), 1)
-            query_pos = lax.broadcasted_iota(jnp.int32, (ROWS, end), 0) + start
+            start = block * QUERIES
+            end = start + QUERIES
+            key_pos = lax.broadcasted_iota(jnp.int32, (QUERIES, end), 1)
+            query_pos = lax.broadcasted_iota(jnp.int32, (QUERIES, end), 0) + start
             allowed = (key_pos <= query_pos) & (seg_col[start:end, :] == seg_row[0, :, :end])
             mask[start:end, :end] = jnp.where(allowed, 0.0, masked_score)
 
-    lane = lax.broadcasted_iota(jnp.int32, (ROWS, PAIR), 1)
+    lane = lax.broadcasted_iota(jnp.int32, (QUERIES, PAIR), 1)
     for block in range(blocks - 1, -1, -1):
-        start = block * ROWS
-        end = start + ROWS
+        start = block * QUERIES
+        end = start + QUERIES
         rows = slice(start, end)
         keys, values = k_ref[0, :end, :], v_ref[0, :end, :]
         query, grads = q_ref[0, rows, :], g_ref[0, rows, :]
@@ -615,7 +616,7 @@
         ],
         input_output_aliases={8 + n: n for n in range(len(before))},
         scratch_shapes=[pltpu.VMEM((length, length), jnp.float32)] + [pltpu.VMEM((length, PAIR), jnp.float32)] * 2,
-        compiler_params=params(20),
+        compiler_params=params(32),
         cost_estimate=cost(24 * tokens * length * width, 8 * tokens * width, tokens * length * width // 200),
     )(*[parts] * 4, cosine, sine, segments[:, None, :], segments.reshape(tokens, 1), *before)
 

time: 400 us -> 397 us (level)
    unnamed x110 -> x108, local copies, waits for them, and re-layouts: 11.7 us -> 10.4 us
  transfers between devices with their start and end apart: 53 -> 53, of which waited for: 14 -> 14; matrix products, arithmetic and copies ran while one was open for 7% -> 7% of each run, Pallas kernels for 62% -> 61%
where the time goes in v6:
time: 397 us; the launch traced here: 391 us
  Pallas kernels  241 us (61%)
  starting transfers between devices  53.8 us (14%)
  waiting for transfers between devices  37.1 us (9%)
  other arithmetic  31.7 us (8%)
  local copies, waits for them, and re-layouts  25.2 us (6%)
    pallas_call x2, Pallas kernels, forward_chunk(): pl.pallas_call(forward_kernel, grid_spec=pltpu.PrefetchScalarGridSpec(num...  73 us
    pallas_call x4, Pallas kernels, attention(): pl.pallas_call(attention_kernel, grid=(width // PAIR,), in_specs=[part(0)...  66.2 us
    ppermute x53, starting transfers between devices, swap(): return lax.ppermute(value, SPLIT, moves)  53.8 us
    ppermute x53, waiting for transfers between devices, swap(): return lax.ppermute(value, SPLIT, moves)  37.1 us
    pallas_call x2, Pallas kernels, attention_back(): pl.pallas_call(partial(attention_back_kernel, half, pieces), grid_spec=pl...  26.2 us
    pallas_call x2, Pallas kernels, project(): pl.pallas_call(partial(project_kernel, half), grid_spec=pltpu.PrefetchSca...  21.6 us
    pallas_call x2, Pallas kernels, finish(): pl.pallas_call(kernel, grid=(length // ROWS,), in_specs=specs + [fixed(sc...  18.3 us
    pallas_call x2, Pallas kernels, attention_grads(): pl.pallas_call(attention_grads_kernel, grid_spec=pltpu.PrefetchScalarGrid...  18.2 us
  transfers between devices with their start and end apart: 53, of which 14 were waited for; matrix products, arithmetic and copies ran while one was open for 7% of the time, Pallas kernels for 61%

profile of v6, /device:TPU:1, one launch (start us, length us, event | category | flops | bytes accessed | tf_op | source)
XLA Modules:
  0.0 390.8 jit_solution(1119095645629599462)
XLA Ops:
  2.9 2.6 dynamic-slice_reduce_fusion.1
  9.4 3.7 collective-permute-start.5
  14.1 1.4 collective-permute-start.6
  15.6 2.1 collective-permute-done.6
  17.7 6.6 %collective-permute-done.4 = bf16[1,320,256]{2,1,0:T(8,128)(2,1)S(1)} collective-permute-done((bf16[1,320,256]{2,1,0:T(8,128)(2,1)S(1)}, bf16[1,320,256]{2,1,0:T(8,128)(2,1)S(1)}, u32[]{:S(2)}, u32[]{:S(2)}) %collective-permute-start.4) | collective-permute-done | bytes 163872 | tf_op jit(solution)/shard_map/ppermute | solution.py:1011
  26.9 1.3 collective-permute-start.8
  28.2 1.3 collective-permute-done.8
  32.3 2.9 collective-permute-done.9
  35.2 2.2 collective-permute-start.10
  38.7 7.7 %shard_map.254 = (bf16[2048,1024]{1,0:T(8,128)(2,1)}, bf16[2048,1024]{1,0:T(8,128)(2,1)}, bf16[2048,1024]{1,0:T(8,128)(2,1)}) custom-call(bf16[1024,1024]{1,0:T(8,128)(2,1)} %bitcast.source.hidden, bf16[1024,1024]{1,0:T(8,128)(2,1)} %bitcast.1.cotangent.grads, bf16[4,1024]{1,0:T(4,128)(2,1)} %reshape.310.scales), custom_call_target="tpu_custom_call" | custom-call | flops 20971520 | bytes 10485760 | tf_op jit(solution)/shard_map/pallas_call | solution.py:440
  51.1 6.3 %fusion = (f32[2048,128]{1,0:T(8,128)}, f32[2048,128]{1,0:T(8,128)}) fusion(f32[128]{0:T(128)} %get-tuple-element.620, f32[128]{0:T(128)} %get-tuple-element.621, f32[2048]{0:T(1024)S(1)} %fusion.2), kind=kLoop, calls=%fused_computation.12 | loop fusion | flops 524288 | bytes 2106368 | tf_op jit(solution)/shard_map/mul | solution.py:1107
  57.4 7.5 %shard_map.255 = (bf16[2048,1024]{1,0:T(8,128)(2,1)}, bf16[2048,1024]{1,0:T(8,128)(2,1)}, bf16[2048,1024]{1,0:T(8,128)(2,1)}) custom-call(bf16[1024,1024]{1,0:T(8,128)(2,1)} %collective-permute-done.source, bf16[1024,1024]{1,0:T(8,128)(2,1)} %collective-permute-done.1.cotangent, ...), custom_call_target="tpu_custom_call", output_to_operand_aliasing={{0}: (3, {}), {1}: (4, {}), {2}: (5, {})} | custom-call | flops 20971520 | bytes 10485760 | tf_op jit(solution)/shard_map/pallas_call | solution.py:440
  67.7 1.4 copy.152
  69.0 10.8 %shard_map.256.q_ref.k_ref.v_ref.g_ref = bf16[4,2048,256]{2,1,0:T(8,128)(2,1)} custom-call(s32[16]{0:T(128)} %xor_add_fusion.place, bf16[2048,1024]{1,0:T(8,128)(2,1)} %get-tuple-element.419.normed.refs_0_, bf16[2048,1024]{1,0:T(8,128)(2,1)} %get-tuple-element.312.grads.refs_4_, bf16[8,320,256]{2,1,0:T(8,128)(2,1)} %copy-done.21, ...), custom_call_target="tpu_custom_call" | custom-call | flops 4294967296 | bytes 12582912 | tf_op jit(solution)/shard_map/pallas_call | solution.py:517
  79.8 1.4 pad_maximum_fusion.3
  82.6 2.2 copy-done.8
  84.8 16.5 %shard_map.257 = (bf16[2048,256]{1,0:T(8,128)(2,1)S(1)}, bf16[3,2048,256]{2,1,0:T(8,128)(2,1)S(1)}) custom-call(bf16[4,2048,256]{2,1,0:T(8,128)(2,1)S(1)} %copy-done.8, bf16[4,2048,256]{2,1,0:T(8,128)(2,1)S(1)} %copy-done.8, bf16[4,2048,256]{2,1,0:T(8,128)(2,1)S(1)} %copy-done.8, bf16[4,2048,256]{2,1,0:T(8,128)(2,1)S(1)} %copy-done.8, ...), custom_call_target="tpu_custom_call" | custom-call | flops 12884901888 | bytes 4194304 | tf_op jit(solution)/shard_map/pallas_call | solution.py:595
  101.4 1.5 pad_maximum_fusion.near
  104.1 1.3 collective-permute-start.22
  105.4 16.8 %shard_map.258 = (bf16[2048,256]{1,0:T(8,128)(2,1)S(1)}, bf16[3,2048,256]{2,1,0:T(8,128)(2,1)S(1)}) custom-call(bf16[4,2048,256]{2,1,0:T(8,128)(2,1)S(1)} %copy-done.8, bf16[4,2048,256]{2,1,0:T(8,128)(2,1)S(1)} %copy-done.8, bf16[4,2048,256]{2,1,0:T(8,128)(2,1)S(1)} %copy-done.8, ...), custom_call_target="tpu_custom_call", output_to_operand_aliasing={{0}: (8, {}), {1}: (9, {})} | custom-call | flops 12884901888 | bytes 4194304 | tf_op jit(solution)/shard_map/pallas_call | solution.py:595
  125.1 5.8 %shard_map.259 = (bf16[8,192,256]{2,1,0:T(8,128)(2,1)S(1)}, bf16[8,192,256]{2,1,0:T(8,128)(2,1)S(1)}, f32[3,1,256]{2,1,0:T(1,128)S(1)}) custom-call(s32[16]{0:T(128)S(1)} %copy-done.15, bf16[2048,1024]{1,0:T(8,128)(2,1)S(1)} %copy-done, bf16[3,2048,256]{2,1,0:T(8,128)(2,1)S(1)} %get-tuple-element.354.refs_1_.d_mixed), custom_call_target="tpu_custom_call" | custom-call | flops 4294967296 | bytes 12582912 | tf_op jit(solution)/shard_map/pallas_call | solution.py:684
  132.5 12.2 %shard_map.260 = (bf16[1024,1024]{1,0:T(8,128)(2,1)}, bf16[1024,1024]{1,0:T(8,128)(2,1)}, bf16[1024,1024]{1,0:T(8,128)(2,1)}, bf16[1024,1024]{1,0:T(8,128)(2,1)}) custom-call(s32[16]{0:T(128)} %xor_add_fusion.place, bf16[3,2048,256]{2,1,0:T(8,128)(2,1)} %copy-done.17, bf16[2048,256]{1,0:T(8,128)(2,1)} %copy-done.18, bf16[8,320,256]{2,1,0:T(8,128)(2,1)} %copy-done.21, ...), custom_call_target="tpu_custom_call" | custom-call | flops 4294967296 | bytes 16777216 | tf_op jit(solution)/shard_map/pallas_call | solution.py:746
  144.7 6.0 %collective-permute-done.20 = bf16[8,192,256]{2,1,0:T(8,128)(2,1)S(1)} collective-permute-done((bf16[8,192,256]{2,1,0:T(8,128)(2,1)S(1)}, bf16[8,192,256]{2,1,0:T(8,128)(2,1)S(1)}, u32[]{:S(2)}, u32[]{:S(2)}) %collective-permute-start.20) | collective-permute-done | bytes 786464 | tf_op jit(solution)/shard_map/ppermute | solution.py:1011
  151.0 1.7 pad_maximum_fusion.1.near
  154.4 35.7 %shard_map.261 = (bf16[8,128,1024]{2,1,0:T(8,128)(2,1)S(1)}, bf16[8,128,1024]{2,1,0:T(8,128)(2,1)S(1)}, f32[1,1024]{1,0:T(1,128)S(1)}, bf16[1024,1024]{1,0:T(8,1...) custom-call(s32[16]{0:T(128)S(1)} %copy-done.16, ...), custom_call_target="tpu_custom_call" | custom-call | flops 25769803776 | bytes 33554432 | tf_op jit(solution)/shard_map/pallas_call | solution.py:865
  192.8 1.4 collective-permute-start.28
  194.9 37.3 %shard_map.262 = (bf16[8,128,1024]{2,1,0:T(8,128)(2,1)S(1)}, bf16[8,128,1024]{2,1,0:T(8,128)(2,1)}, f32[1,1024]{1,0:T(1,128)S(1)}, bf16[1024,1024]{1,0:T(8,128)(...) custom-call(s32[16]{0:T(128)S(1)} %copy-done.16, ...), custom_call_target="tpu_custom_call" | custom-call | flops 25769803776 | bytes 33554432 | tf_op jit(solution)/shard_map/pallas_call | solution.py:865
  232.3 2.6 add_convert_fusion.2
  236.0 1.3 collective-permute-start.30
  237.3 10.8 %shard_map.263.q_ref.k_ref.v_ref.g_ref = bf16[4,2048,256]{2,1,0:T(8,128)(2,1)} custom-call(s32[16]{0:T(128)} %xor_add_fusion.place, bf16[2048,1024]{1,0:T(8,128)(2,1)} %get-tuple-element.419.normed.refs_0_, bf16[2048,1024]{1,0:T(8,128)(2,1)} %get-tuple-element.312.grads.refs_4_, bf16[8,192,256]{2,1,0:T(8,128)(2,1)} %copy-done.23, ...), custom_call_target="tpu_custom_call" | custom-call | flops 4294967296 | bytes 12582912 | tf_op jit(solution)/shard_map/pallas_call | solution.py:517
  248.2 1.3 collective-permute-done.29
  249.5 1.6 add_convert_fusion.8
  251.1 6.2 %collective-permute-start.32 = (bf16[1024,1024]{1,0:T(8,128)(2,1)}, bf16[1024,1024]{1,0:T(8,128)(2,1)S(1)}, u32[]{:S(2)}, u32[]{:S(2)}) collective-permute-start(bf16[1024,1024]{1,0:T(8,128)(2,1)} %get-tuple-element.440), channel_id=1, source_target_pairs={{0,2},{1,3},{2,0},{3,1},{4,6},{5,7},{6,4},{7,5},{8,10},{9,11},{10,... | collective-permute-start | bytes 6291464 | tf_op jit(solution)/shard_map/ppermute | solution.py:1011
  259.0 2.2 copy-done.7
  261.2 16.4 %shard_map.264 = (bf16[2048,256]{1,0:T(8,128)(2,1)S(1)}, bf16[3,2048,256]{2,1,0:T(8,128)(2,1)S(1)}) custom-call(bf16[4,2048,256]{2,1,0:T(8,128)(2,1)S(1)} %copy-done.7, bf16[4,2048,256]{2,1,0:T(8,128)(2,1)S(1)} %copy-done.7, bf16[4,2048,256]{2,1,0:T(8,128)(2,1)S(1)} %copy-done.7, bf16[4,2048,256]{2,1,0:T(8,128)(2,1)S(1)} %copy-done.7, ...), custom_call_target="tpu_custom_call" | custom-call | flops 12884901888 | bytes 4194304 | tf_op jit(solution)/shard_map/pallas_call | solution.py:595
  280.2 16.5 %shard_map.265 = (bf16[2048,256]{1,0:T(8,128)(2,1)S(1)}, bf16[3,2048,256]{2,1,0:T(8,128)(2,1)S(1)}) custom-call(bf16[4,2048,256]{2,1,0:T(8,128)(2,1)S(1)} %copy-done.7, bf16[4,2048,256]{2,1,0:T(8,128)(2,1)S(1)} %copy-done.7, bf16[4,2048,256]{2,1,0:T(8,128)(2,1)S(1)} %copy-done.7, ...), custom_call_target="tpu_custom_call", output_to_operand_aliasing={{0}: (8, {}), {1}: (9, {})} | custom-call | flops 12884901888 | bytes 4194304 | tf_op jit(solution)/shard_map/pallas_call | solution.py:595
  296.8 2.7 add_convert_fusion
  299.8 14.0 %shard_map.266 = (bf16[1024,1024]{1,0:T(8,128)(2,1)}, bf16[1024,1024]{1,0:T(8,128)(2,1)}, bf16[1024,1024]{1,0:T(8,128)(2,1)}, bf16[1024,1024]{1,0:T(8,128)(2,1)}) custom-call(s32[16]{0:T(128)} %xor_add_fusion.place, bf16[3,2048,256]{2,1,0:T(8,128)(2,1)} %copy-done.9, bf16[2048,256]{1,0:T(8,128)(2,1)} %copy-done.14, bf16[8,192,256]{2,1,0:T(8,128)(2,1)} %copy-done.23, ...), custom_call_target="tpu_custom_call" | custom-call | flops 4294967296 | bytes 16777216 | tf_op jit(solution)/shard_map/pallas_call | solution.py:746
  315.5 1.6 collective-permute-start.36
  317.1 12.4 %shard_map.267 = (bf16[8,320,256]{2,1,0:T(8,128)(2,1)}, bf16[8,320,256]{2,1,0:T(8,128)(2,1)}, f32[3,1,256]{2,1,0:T(1,128)}) custom-call(s32[16]{0:T(128)} %xor_add_fusion.place, bf16[2048,1024]{1,0:T(8,128)(2,1)} %get-tuple-element.419.normed.refs_0_, bf16[3,2048,256]{2,1,0:T(8,128)(2,1)} %copy-done.9, bf16[2048,256]{1,0:T(8,128)(2,1)} %copy-done.18, ...), custom_call_target="tpu_custom_call" | custom-call | flops 4294967296 | bytes 12582912 | tf_op jit(solution)/shard_map/pallas_call | solution.py:684
  332.5 13.1 %shard_map.268 = (bf16[1024,1024]{1,0:T(8,128)(2,1)}, f32[8,1024]{1,0:T(8,128)}) custom-call(bf16[1024,1024]{1,0:T(8,128)(2,1)} %bitcast.source.hidden, bf16[1024,1024]{1,0:T(8,128)(2,1)} %bitcast.1.cotangent.grads, bf16[1024,1024]{1,0:T(8,128)(2,1)} %get-tuple-element.493.one_mine, bf16[1024,1024]{1,0:T(8,128)(2,1)} %collective-permute-done.37.one_come, ...), custom_call_target="tpu_custom_call" | custom-call | flops 41943040 | bytes 14680064 | tf_op jit(solution)/shard_map/pallas_call | solution.py:937
  346.9 2.4 add_convert_fusion.4
  352.6 1.5 collective-permute-start.41
  354.2 2.1 collective-permute-done.41
  356.3 5.3 %collective-permute-done.42 = bf16[4,320,256]{2,1,0:T(8,128)(2,1)S(1)} collective-permute-done((bf16[4,320,256]{2,1,0:T(8,128)(2,1)}, bf16[4,320,256]{2,1,0:T(8,128)(2,1)S(1)}, u32[]{:S(2)}, u32[]{:S(2)}) %collective-permute-start.42) | collective-permute-done | bytes 655392 | tf_op jit(solution)/shard_map/ppermute | solution.py:1011
  365.4 5.2 %shard_map.269 = bf16[1024,1024]{1,0:T(8,128)(2,1)} custom-call(bf16[1024,1024]{1,0:T(8,128)(2,1)} %bitcast.source.hidden, bf16[1024,1024]{1,0:T(8,128)(2,1)} %get-tuple-element.527.mine, bf16[1024,1024]{1,0:T(8,128)(2,1)} %collective-permute-done.38.come, bf16[2,1024]{1,0:T(2,128)(2,1)} %pad_maximum_fusion.22.scales), custom_call_target="tpu_custom_call" | custom-call | flops 41943040 | bytes 8388608 | tf_op jit(solution)/shard_map/pallas_call | solution.py:937
  370.7 4.7 %collective-permute-start.48 = (f32[3,32,256]{2,1,0:T(8,128)S(1)}, f32[3,32,256]{2,1,0:T(8,128)S(1)}, u32[]{:S(2)}, u32[]{:S(2)}) collective-permute-start(f32[3,32,256]{2,1,0:T(8,128)S(1)} %get-tuple-element.599), channel_id=1, source_target_pairs={{0,2},{1,3},{2,0},{3,1},{4,6},{5,7},{6,4},{7,5},{8,10},{9,11},{10,... | collective-permute-start | bytes 294920 | tf_op jit(solution)/shard_map/ppermute | solution.py:1011
  381.5 4.5 %collective-permute-done.49 = bf16[1,320,256]{2,1,0:T(8,128)(2,1)S(1)} collective-permute-done((bf16[1,320,256]{2,1,0:T(8,128)(2,1)S(1)}, bf16[1,320,256]{2,1,0:T(8,128)(2,1)S(1)}, u32[]{:S(2)}, u32[]{:S(2)}) %collective-permute-start.49) | collective-permute-done | bytes 163872 | tf_op jit(solution)/shard_map/ppermute | solution.py:1011
  (335 shorter events, 62.3 us)
Async XLA Ops:
  1.6 6.8 %collective-permute-start.3 = (bf16[512]{0:T(512)(128)(2,1)S(1)}, bf16[512]{0:T(512)(128)(2,1)S(1)}, u32[]{:S(2)}, u32[]{:S(2)}) collective-permute-start(bf16[512]{0:T(512)(128)(2,1)S(1)} %pad_add_fusion.1), channel_id=1, source_target_pairs={{0,2},{1,3},{2,0},{3,1},{4,6},{5,7},{6,4},{7,5},{8,10},{9,11},{10,... | collective-permute-start | bytes 3080 | tf_op jit(solution)/shard_map/ppermute | solution.py:1011
  9.4 4.7 %collective-permute-start.5 = (bf16[1,1024]{1,0:T(2,128)(2,1)S(1)}, bf16[1,1024]{1,0:T(2,128)(2,1)S(1)}, u32[]{:S(2)}, u32[]{:S(2)}) collective-permute-start(bf16[1,1024]{1,0:T(2,128)(2,1)S(1)} %bitcast.174), channel_id=1, source_target_pairs={{0,16},{1,17},{2,18},{3,19},{4,20},{5,21},{6,22},{7,23},{8,24},{9,... | collective-permute-start | bytes 6152 | tf_op jit(solution)/shard_map/ppermute | solution.py:1011
  13.1 25.4 %collective-permute-start.11 = (s32[1,1024]{1,0:T(1,128)S(1)}, s32[1,1024]{1,0:T(1,128)S(1)}, u32[]{:S(2)}, u32[]{:S(2)}) collective-permute-start(s32[1,1024]{1,0:T(1,128)S(1)} %copy-done.47), channel_id=1, source_target_pairs={{0,2},{1,3},{2,0},{3,1},{4,6},{5,7},{6,4},{7,5},{8,10},{9,11},{10,... | collective-permute-start | bytes 12296 | tf_op jit(solution)/shard_map/ppermute | solution.py:1011
  13.6 43.9 %collective-permute-start = (bf16[1024,1024]{1,0:T(8,128)(2,1)}, bf16[1024,1024]{1,0:T(8,128)(2,1)}, u32[]{:S(2)}, u32[]{:S(2)}) collective-permute-start(bf16[1024,1024]{1,0:T(8,128)(2,1)} %bitcast.source.hidden), channel_id=1, source_target_pairs={{0,2},{1,3},{2,0},{3,1},{4,6},{5,7},{6,4},{7,5},{8,10},{9,11},{10,... | collective-permute-start | bytes 6291464 | tf_op jit(solution)/shard_map/ppermute | solution.py:1011
  13.6 43.8 %collective-permute-start.1 = (bf16[1024,1024]{1,0:T(8,128)(2,1)}, bf16[1024,1024]{1,0:T(8,128)(2,1)}, u32[]{:S(2)}, u32[]{:S(2)}) collective-permute-start(bf16[1024,1024]{1,0:T(8,128)(2,1)} %bitcast.1.cotangent.grads), channel_id=1, source_target_pairs={{0,2},{1,3},{2,0},{3,1},{4,6},{5,7},{6,4},{7,5},{8,10},{9,11},{10,... | collective-permute-start | bytes 6291464 | tf_op jit(solution)/shard_map/ppermute | solution.py:1011
  14.1 10.2 %collective-permute-start.4 = (bf16[1,320,256]{2,1,0:T(8,128)(2,1)S(1)}, bf16[1,320,256]{2,1,0:T(8,128)(2,1)S(1)}, u32[]{:S(2)}, u32[]{:S(2)}) collective-permute-start(bf16[1,320,256]{2,1,0:T(8,128)(2,1)S(1)} %bitcast.153), channel_id=1, source_target_pairs={{0,16},{1,17},{2,18},{3,19},{4,20},{5,21},{6,22},{7,23},{8,24},{9,... | collective-permute-start | bytes 491528 | tf_op jit(solution)/shard_map/ppermute | solution.py:1011
  14.1 3.5 collective-permute-start.6
  26.9 2.7 collective-permute-start.8
  28.2 6.9 %collective-permute-start.9 = (bf16[2,320,256]{2,1,0:T(8,128)(2,1)S(1)}, bf16[2,320,256]{2,1,0:T(8,128)(2,1)S(1)}, u32[]{:S(2)}, u32[]{:S(2)}) collective-permute-start(bf16[2,320,256]{2,1,0:T(8,128)(2,1)S(1)} %pad_maximum_fusion.11), channel_id=1, source_target_pairs={{0,8},{1,9},{2,10},{3,11},{4,12},{5,13},{6,14},{7,15},{8,0},{9,1},... | collective-permute-start | bytes 983048 | tf_op jit(solution)/shard_map/ppermute | solution.py:1011
  35.2 11.2 %collective-permute-start.10 = (bf16[4,320,256]{2,1,0:T(8,128)(2,1)S(1)}, bf16[4,320,256]{2,1,0:T(8,128)(2,1)S(1)}, u32[]{:S(2)}, u32[]{:S(2)}) collective-permute-start(bf16[4,320,256]{2,1,0:T(8,128)(2,1)S(1)} %pad_maximum_fusion.6), channel_id=1, source_target_pairs={{0,1},{1,0},{2,6},{3,7},{4,5},{5,4},{6,2},{7,3},{8,9},{9,8},{10,14... | collective-permute-start | bytes 1966088 | tf_op jit(solution)/shard_map/ppermute | solution.py:1011
  46.5 18.4 %collective-permute-start.13 = (bf16[8,320,256]{2,1,0:T(8,128)(2,1)S(1)}, bf16[8,320,256]{2,1,0:T(8,128)(2,1)S(1)}, u32[]{:S(2)}, u32[]{:S(2)}) collective-permute-start(bf16[8,320,256]{2,1,0:T(8,128)(2,1)S(1)} %pad_maximum_fusion.2.refs_0_.refs_2_.refs_4_.refs_6_), channel_id=1, source_target_pairs={{0,4},{1,5},{2,3},{3,2},{4,0},{5,1},{6,7},{7,6},{8,12},{9,13},{10,... | collective-permute-start | bytes 3932168 | tf_op jit(solution)/shard_map/ppermute | solution.py:1011
  49.3 15.7 %collective-permute-start.12 = (bf16[1,128,1024]{2,1,0:T(8,128)(2,1)S(1)}, bf16[1,128,1024]{2,1,0:T(8,128)(2,1)S(1)}, u32[]{:S(2)}, u32[]{:S(2)}) collective-permute-start(bf16[1,128,1024]{2,1,0:T(8,128)(2,1)S(1)} %maximum_bitcast_fusion), channel_id=1, source_target_pairs={{0,16},{1,17},{2,18},{3,19},{4,20},{5,21},{6,22},{7,23},{8,24},{9,... | collective-permute-start | bytes 786440 | tf_op jit(solution)/shard_map/ppermute | solution.py:1011
  65.9 13.9 %collective-permute-start.14 = (bf16[2,128,1024]{2,1,0:T(8,128)(2,1)}, bf16[2,128,1024]{2,1,0:T(8,128)(2,1)}, u32[]{:S(2)}, u32[]{:S(2)}) collective-permute-start(bf16[2,128,1024]{2,1,0:T(8,128)(2,1)} %pad_maximum_fusion.7), channel_id=1, source_target_pairs={{0,8},{1,9},{2,10},{3,11},{4,12},{5,13},{6,14},{7,15},{8,0},{9,1},... | collective-permute-start | bytes 1572872 | tf_op jit(solution)/shard_map/ppermute | solution.py:1011
  81.3 20.1 %collective-permute-start.16 = (bf16[1,128,1024]{2,1,0:T(8,128)(2,1)S(1)}, bf16[1,128,1024]{2,1,0:T(8,128)(2,1)S(1)}, u32[]{:S(2)}, u32[]{:S(2)}) collective-permute-start(bf16[1,128,1024]{2,1,0:T(8,128)(2,1)S(1)} %maximum_bitcast_fusion.1), channel_id=1, source_target_pairs={{0,16},{1,17},{2,18},{3,19},{4,20},{5,21},{6,22},{7,23},{8,24},{9,... | collective-permute-start | bytes 786440 | tf_op jit(solution)/shard_map/ppermute | solution.py:1011
  81.8 19.5 %collective-permute-start.15 = (bf16[4,128,1024]{2,1,0:T(8,128)(2,1)S(1)}, bf16[4,128,1024]{2,1,0:T(8,128)(2,1)S(1)}, u32[]{:S(2)}, u32[]{:S(2)}) collective-permute-start(bf16[4,128,1024]{2,1,0:T(8,128)(2,1)S(1)} %pad_maximum_fusion.3), channel_id=1, source_target_pairs={{0,1},{1,0},{2,6},{3,7},{4,5},{5,4},{6,2},{7,3},{8,9},{9,8},{10,14... | collective-permute-start | bytes 3145736 | tf_op jit(solution)/shard_map/ppermute | solution.py:1011
  102.9 19.4 %collective-permute-start.17 = (bf16[2,128,1024]{2,1,0:T(8,128)(2,1)S(1)}, bf16[2,128,1024]{2,1,0:T(8,128)(2,1)S(1)}, u32[]{:S(2)}, u32[]{:S(2)}) collective-permute-start(bf16[2,128,1024]{2,1,0:T(8,128)(2,1)S(1)} %pad_maximum_fusion.8), channel_id=1, source_target_pairs={{0,8},{1,9},{2,10},{3,11},{4,12},{5,13},{6,14},{7,15},{8,0},{9,1},... | collective-permute-start | bytes 1572872 | tf_op jit(solution)/shard_map/ppermute | solution.py:1011
  104.1 46.7 %collective-permute-start.22 = (bf16[8,128,1024]{2,1,0:T(8,128)(2,1)}, bf16[8,128,1024]{2,1,0:T(8,128)(2,1)}, u32[]{:S(2)}, u32[]{:S(2)}) collective-permute-start(bf16[8,128,1024]{2,1,0:T(8,128)(2,1)} %pad_maximum_fusion.near), channel_id=1, source_target_pairs={{0,4},{1,5},{2,3},{3,2},{4,0},{5,1},{6,7},{7,6},{8,12},{9,13},{10,... | collective-permute-start | bytes 6291464 | tf_op jit(solution)/shard_map/ppermute | solution.py:1011
  123.3 7.6 %collective-permute-start.18 = (bf16[1,192,256]{2,1,0:T(8,128)(2,1)S(1)}, bf16[1,192,256]{2,1,0:T(8,128)(2,1)S(1)}, u32[]{:S(2)}, u32[]{:S(2)}) collective-permute-start(bf16[1,192,256]{2,1,0:T(8,128)(2,1)S(1)} %bitcast.156), channel_id=1, source_target_pairs={{0,16},{1,17},{2,18},{3,19},{4,20},{5,21},{6,22},{7,23},{8,24},{9,... | collective-permute-start | bytes 294920 | tf_op jit(solution)/shard_map/ppermute | solution.py:1011
  124.4 26.4 %collective-permute-start.19 = (bf16[4,128,1024]{2,1,0:T(8,128)(2,1)}, bf16[4,128,1024]{2,1,0:T(8,128)(2,1)}, u32[]{:S(2)}, u32[]{:S(2)}) collective-permute-start(bf16[4,128,1024]{2,1,0:T(8,128)(2,1)} %pad_maximum_fusion.4), channel_id=1, source_target_pairs={{0,1},{1,0},{2,6},{3,7},{4,5},{5,4},{6,2},{7,3},{8,9},{9,8},{10,14... | collective-permute-start | bytes 3145736 | tf_op jit(solution)/shard_map/ppermute | solution.py:1011
  130.9 19.8 %collective-permute-start.20 = (bf16[8,192,256]{2,1,0:T(8,128)(2,1)S(1)}, bf16[8,192,256]{2,1,0:T(8,128)(2,1)S(1)}, u32[]{:S(2)}, u32[]{:S(2)}) collective-permute-start(bf16[8,192,256]{2,1,0:T(8,128)(2,1)S(1)} %get-tuple-element.360), channel_id=1, source_target_pairs={{0,4},{1,5},{2,3},{3,2},{4,0},{5,1},{6,7},{7,6},{8,12},{9,13},{10,... | collective-permute-start | bytes 2359304 | tf_op jit(solution)/shard_map/ppermute | solution.py:1011
  131.4 13.3 %collective-permute-start.21 = (bf16[2,192,256]{2,1,0:T(8,128)(2,1)S(1)}, bf16[2,192,256]{2,1,0:T(8,128)(2,1)S(1)}, u32[]{:S(2)}, u32[]{:S(2)}) collective-permute-start(bf16[2,192,256]{2,1,0:T(8,128)(2,1)S(1)} %pad_maximum_fusion.13), channel_id=1, source_target_pairs={{0,8},{1,9},{2,10},{3,11},{4,12},{5,13},{6,14},{7,15},{8,0},{9,1},... | collective-permute-start | bytes 589832 | tf_op jit(solution)/shard_map/ppermute | solution.py:1011
  152.7 38.7 %collective-permute-start.23 = (bf16[4,192,256]{2,1,0:T(8,128)(2,1)S(1)}, bf16[4,192,256]{2,1,0:T(8,128)(2,1)S(1)}, u32[]{:S(2)}, u32[]{:S(2)}) collective-permute-start(bf16[4,192,256]{2,1,0:T(8,128)(2,1)S(1)} %get-tuple-element.382), channel_id=1, source_target_pairs={{0,1},{1,0},{2,6},{3,7},{4,5},{5,4},{6,2},{7,3},{8,9},{9,8},{10,14... | collective-permute-start | bytes 1179656 | tf_op jit(solution)/shard_map/ppermute | solution.py:1011
  153.6 37.9 %collective-permute-start.24 = (bf16[4,192,256]{2,1,0:T(8,128)(2,1)S(1)}, bf16[4,192,256]{2,1,0:T(8,128)(2,1)S(1)}, u32[]{:S(2)}, u32[]{:S(2)}) collective-permute-start(bf16[4,192,256]{2,1,0:T(8,128)(2,1)S(1)} %pad_maximum_fusion.10), channel_id=1, source_target_pairs={{0,1},{1,0},{2,6},{3,7},{4,5},{5,4},{6,2},{7,3},{8,9},{9,8},{10,14... | collective-permute-start | bytes 1179656 | tf_op jit(solution)/shard_map/ppermute | solution.py:1011
  154.3 37.2 %collective-permute-start.25 = (bf16[8,128,1024]{2,1,0:T(8,128)(2,1)S(1)}, bf16[8,128,1024]{2,1,0:T(8,128)(2,1)S(1)}, u32[]{:S(2)}, u32[]{:S(2)}) collective-permute-start(bf16[8,128,1024]{2,1,0:T(8,128)(2,1)S(1)} %pad_maximum_fusion.1.near), channel_id=1, source_target_pairs={{0,4},{1,5},{2,3},{3,2},{4,0},{5,1},{6,7},{7,6},{8,12},{9,13},{10,... | collective-permute-start | bytes 6291464 | tf_op jit(solution)/shard_map/ppermute | solution.py:1011
  191.7 40.5 %collective-permute-start.26 = (bf16[2,192,256]{2,1,0:T(8,128)(2,1)S(1)}, bf16[2,192,256]{2,1,0:T(8,128)(2,1)S(1)}, u32[]{:S(2)}, u32[]{:S(2)}) collective-permute-start(bf16[2,192,256]{2,1,0:T(8,128)(2,1)S(1)} %get-tuple-element.408), channel_id=1, source_target_pairs={{0,8},{1,9},{2,10},{3,11},{4,12},{5,13},{6,14},{7,15},{8,0},{9,1},... | collective-permute-start | bytes 589832 | tf_op jit(solution)/shard_map/ppermute | solution.py:1011
  192.8 39.4 %collective-permute-start.28 = (bf16[8,192,256]{2,1,0:T(8,128)(2,1)S(1)}, bf16[8,192,256]{2,1,0:T(8,128)(2,1)S(1)}, u32[]{:S(2)}, u32[]{:S(2)}) collective-permute-start(bf16[8,192,256]{2,1,0:T(8,128)(2,1)S(1)} %pad_maximum_fusion.5.refs_0_.refs_2_.refs_4_), channel_id=1, source_target_pairs={{0,4},{1,5},{2,3},{3,2},{4,0},{5,1},{6,7},{7,6},{8,12},{9,13},{10,... | collective-permute-start | bytes 2359304 | tf_op jit(solution)/shard_map/ppermute | solution.py:1011
  194.2 38.0 %collective-permute-start.27 = (bf16[8,128,1024]{2,1,0:T(8,128)(2,1)S(1)}, bf16[8,128,1024]{2,1,0:T(8,128)(2,1)S(1)}, u32[]{:S(2)}, u32[]{:S(2)}) collective-permute-start(bf16[8,128,1024]{2,1,0:T(8,128)(2,1)S(1)} %get-tuple-element.410), channel_id=1, source_target_pairs={{0,4},{1,5},{2,3},{3,2},{4,0},{5,1},{6,7},{7,6},{8,12},{9,13},{10,... | collective-permute-start | bytes 6291464 | tf_op jit(solution)/shard_map/ppermute | solution.py:1011
  235.2 14.3 %collective-permute-start.29 = (bf16[4,128,1024]{2,1,0:T(8,128)(2,1)}, bf16[4,128,1024]{2,1,0:T(8,128)(2,1)}, u32[]{:S(2)}, u32[]{:S(2)}) collective-permute-start(bf16[4,128,1024]{2,1,0:T(8,128)(2,1)} %get-tuple-element.423), channel_id=1, source_target_pairs={{0,1},{1,0},{2,6},{3,7},{4,5},{5,4},{6,2},{7,3},{8,9},{9,8},{10,14... | collective-permute-start | bytes 3145736 | tf_op jit(solution)/shard_map/ppermute | solution.py:1011
  236.0 12.2 %collective-permute-start.30 = (bf16[1,192,256]{2,1,0:T(8,128)(2,1)S(1)}, bf16[1,192,256]{2,1,0:T(8,128)(2,1)S(1)}, u32[]{:S(2)}, u32[]{:S(2)}) collective-permute-start(bf16[1,192,256]{2,1,0:T(8,128)(2,1)S(1)} %get-tuple-element.428), channel_id=1, source_target_pairs={{0,16},{1,17},{2,18},{3,19},{4,20},{5,21},{6,22},{7,23},{8,24},{9,... | collective-permute-start | bytes 294920 | tf_op jit(solution)/shard_map/ppermute | solution.py:1011
  251.1 26.5 %collective-permute-start.32 = (bf16[1024,1024]{1,0:T(8,128)(2,1)}, bf16[1024,1024]{1,0:T(8,128)(2,1)S(1)}, u32[]{:S(2)}, u32[]{:S(2)}) collective-permute-start(bf16[1024,1024]{1,0:T(8,128)(2,1)} %get-tuple-element.440), channel_id=1, source_target_pairs={{0,2},{1,3},{2,0},{3,1},{4,6},{5,7},{6,4},{7,5},{8,10},{9,11},{10,... | collective-permute-start | bytes 6291464 | tf_op jit(solution)/shard_map/ppermute | solution.py:1011
  257.2 20.3 %collective-permute-start.31 = (bf16[2,128,1024]{2,1,0:T(8,128)(2,1)S(1)}, bf16[2,128,1024]{2,1,0:T(8,128)(2,1)S(1)}, u32[]{:S(2)}, u32[]{:S(2)}) collective-permute-start(bf16[2,128,1024]{2,1,0:T(8,128)(2,1)S(1)} %get-tuple-element.439), channel_id=1, source_target_pairs={{0,8},{1,9},{2,10},{3,11},{4,12},{5,13},{6,14},{7,15},{8,0},{9,1},... | collective-permute-start | bytes 1572872 | tf_op jit(solution)/shard_map/ppermute | solution.py:1011
  258.0 38.8 %collective-permute-start.33 = (bf16[8,128,1024]{2,1,0:T(8,128)(2,1)}, bf16[8,128,1024]{2,1,0:T(8,128)(2,1)S(1)}, u32[]{:S(2)}, u32[]{:S(2)}) collective-permute-start(bf16[8,128,1024]{2,1,0:T(8,128)(2,1)} %get-tuple-element.451), channel_id=1, source_target_pairs={{0,4},{1,5},{2,3},{3,2},{4,0},{5,1},{6,7},{7,6},{8,12},{9,13},{10,... | collective-permute-start | bytes 6291464 | tf_op jit(solution)/shard_map/ppermute | solution.py:1011
  278.9 17.9 %collective-permute-start.34 = (bf16[1,128,1024]{2,1,0:T(8,128)(2,1)S(1)}, bf16[1,128,1024]{2,1,0:T(8,128)(2,1)S(1)}, u32[]{:S(2)}, u32[]{:S(2)}) collective-permute-start(bf16[1,128,1024]{2,1,0:T(8,128)(2,1)S(1)} %get-tuple-element.453), channel_id=1, source_target_pairs={{0,16},{1,17},{2,18},{3,19},{4,20},{5,21},{6,22},{7,23},{8,24},{9,... | collective-permute-start | bytes 786440 | tf_op jit(solution)/shard_map/ppermute | solution.py:1011
  299.5 14.4 %collective-permute-start.35 = (bf16[4,128,1024]{2,1,0:T(8,128)(2,1)}, bf16[4,128,1024]{2,1,0:T(8,128)(2,1)S(1)}, u32[]{:S(2)}, u32[]{:S(2)}) collective-permute-start(bf16[4,128,1024]{2,1,0:T(8,128)(2,1)} %get-tuple-element.467), channel_id=1, source_target_pairs={{0,1},{1,0},{2,6},{3,7},{4,5},{5,4},{6,2},{7,3},{8,9},{9,8},{10,14... | collective-permute-start | bytes 3145736 | tf_op jit(solution)/shard_map/ppermute | solution.py:1011
  314.3 15.3 %collective-permute-start.37 = (bf16[1024,1024]{1,0:T(8,128)(2,1)}, bf16[1024,1024]{1,0:T(8,128)(2,1)}, u32[]{:S(2)}, u32[]{:S(2)}) collective-permute-start(bf16[1024,1024]{1,0:T(8,128)(2,1)} %get-tuple-element.484), channel_id=1, source_target_pairs={{0,2},{1,3},{2,0},{3,1},{4,6},{5,7},{6,4},{7,5},{8,10},{9,11},{10,... | collective-permute-start | bytes 6291464 | tf_op jit(solution)/shard_map/ppermute | solution.py:1011
  315.5 14.1 %collective-permute-start.38 = (bf16[1024,1024]{1,0:T(8,128)(2,1)}, bf16[1024,1024]{1,0:T(8,128)(2,1)}, u32[]{:S(2)}, u32[]{:S(2)}) collective-permute-start(bf16[1024,1024]{1,0:T(8,128)(2,1)} %get-tuple-element.485), channel_id=1, source_target_pairs={{0,2},{1,3},{2,0},{3,1},{4,6},{5,7},{6,4},{7,5},{8,10},{9,11},{10,... | collective-permute-start | bytes 6291464 | tf_op jit(solution)/shard_map/ppermute | solution.py:1011
  315.5 14.0 %collective-permute-start.36 = (bf16[2,128,1024]{2,1,0:T(8,128)(2,1)S(1)}, bf16[2,128,1024]{2,1,0:T(8,128)(2,1)S(1)}, u32[]{:S(2)}, u32[]{:S(2)}) collective-permute-start(bf16[2,128,1024]{2,1,0:T(8,128)(2,1)S(1)} %get-tuple-element.483), channel_id=1, source_target_pairs={{0,8},{1,9},{2,10},{3,11},{4,12},{5,13},{6,14},{7,15},{8,0},{9,1},... | collective-permute-start | bytes 1572872 | tf_op jit(solution)/shard_map/ppermute | solution.py:1011
  329.8 17.1 %collective-permute-start.39 = (bf16[8,320,256]{2,1,0:T(8,128)(2,1)}, bf16[8,320,256]{2,1,0:T(8,128)(2,1)}, u32[]{:S(2)}, u32[]{:S(2)}) collective-permute-start(bf16[8,320,256]{2,1,0:T(8,128)(2,1)} %get-tuple-element.504), channel_id=1, source_target_pairs={{0,4},{1,5},{2,3},{3,2},{4,0},{5,1},{6,7},{7,6},{8,12},{9,13},{10,... | collective-permute-start | bytes 3932168 | tf_op jit(solution)/shard_map/ppermute | solution.py:1011
  330.5 15.1 %collective-permute-start.40 = (bf16[1,128,1024]{2,1,0:T(8,128)(2,1)S(1)}, bf16[1,128,1024]{2,1,0:T(8,128)(2,1)S(1)}, u32[]{:S(2)}, u32[]{:S(2)}) collective-permute-start(bf16[1,128,1024]{2,1,0:T(8,128)(2,1)S(1)} %get-tuple-element.506), channel_id=1, source_target_pairs={{0,16},{1,17},{2,18},{3,19},{4,20},{5,21},{6,22},{7,23},{8,24},{9,... | collective-permute-start | bytes 786440 | tf_op jit(solution)/shard_map/ppermute | solution.py:1011
  351.6 10.0 %collective-permute-start.42 = (bf16[4,320,256]{2,1,0:T(8,128)(2,1)}, bf16[4,320,256]{2,1,0:T(8,128)(2,1)S(1)}, u32[]{:S(2)}, u32[]{:S(2)}) collective-permute-start(bf16[4,320,256]{2,1,0:T(8,128)(2,1)} %get-tuple-element.521), channel_id=1, source_target_pairs={{0,1},{1,0},{2,6},{3,7},{4,5},{5,4},{6,2},{7,3},{8,9},{9,8},{10,14... | collective-permute-start | bytes 1966088 | tf_op jit(solution)/shard_map/ppermute | solution.py:1011
  352.6 3.6 collective-permute-start.41
  362.6 8.0 %collective-permute-start.45 = (bf16[2,320,256]{2,1,0:T(8,128)(2,1)S(1)}, bf16[2,320,256]{2,1,0:T(8,128)(2,1)S(1)}, u32[]{:S(2)}, u32[]{:S(2)}) collective-permute-start(bf16[2,320,256]{2,1,0:T(8,128)(2,1)S(1)} %get-tuple-element.530), channel_id=1, source_target_pairs={{0,8},{1,9},{2,10},{3,11},{4,12},{5,13},{6,14},{7,15},{8,0},{9,1},... | collective-permute-start | bytes 983048 | tf_op jit(solution)/shard_map/ppermute | solution.py:1011
  364.4 6.1 %collective-permute-start.44 = (f32[4,384]{1,0:T(4,128)S(1)}, f32[4,384]{1,0:T(4,128)S(1)}, u32[]{:S(2)}, u32[]{:S(2)}) collective-permute-start(f32[4,384]{1,0:T(4,128)S(1)} %slice_select_fusion.2), channel_id=1, source_target_pairs={{0,4},{1,5},{2,6},{3,7},{4,0},{5,1},{6,2},{7,3},{8,12},{9,13},{10,... | collective-permute-start | bytes 18440 | tf_op jit(solution)/shard_map/ppermute | solution.py:1011
  370.7 18.3 %collective-permute-start.48 = (f32[3,32,256]{2,1,0:T(8,128)S(1)}, f32[3,32,256]{2,1,0:T(8,128)S(1)}, u32[]{:S(2)}, u32[]{:S(2)}) collective-permute-start(f32[3,32,256]{2,1,0:T(8,128)S(1)} %get-tuple-element.599), channel_id=1, source_target_pairs={{0,2},{1,3},{2,0},{3,1},{4,6},{5,7},{6,4},{7,5},{8,10},{9,11},{10,... | collective-permute-start | bytes 294920 | tf_op jit(solution)/shard_map/ppermute | solution.py:1011
  375.5 10.5 %collective-permute-start.49 = (bf16[1,320,256]{2,1,0:T(8,128)(2,1)S(1)}, bf16[1,320,256]{2,1,0:T(8,128)(2,1)S(1)}, u32[]{:S(2)}, u32[]{:S(2)}) collective-permute-start(bf16[1,320,256]{2,1,0:T(8,128)(2,1)S(1)} %get-tuple-element.547), channel_id=1, source_target_pairs={{0,16},{1,17},{2,18},{3,19},{4,20},{5,21},{6,22},{7,23},{8,24},{9,... | collective-permute-start | bytes 491528 | tf_op jit(solution)/shard_map/ppermute | solution.py:1011
  376.8 10.5 %collective-permute-start.51 = (f32[1,32,1024]{2,1,0:T(8,128)S(1)}, f32[1,32,1024]{2,1,0:T(8,128)S(1)}, u32[]{:S(2)}, u32[]{:S(2)}) collective-permute-start(f32[1,32,1024]{2,1,0:T(8,128)S(1)} %get-tuple-element.591), channel_id=1, source_target_pairs={{0,2},{1,3},{2,0},{3,1},{4,6},{5,7},{6,4},{7,5},{8,10},{9,11},{10,... | collective-permute-start | bytes 393224 | tf_op jit(solution)/shard_map/ppermute | solution.py:1011
  377.8 9.5 %collective-permute-start.52 = (f32[1,32,1024]{2,1,0:T(8,128)S(1)}, f32[1,32,1024]{2,1,0:T(8,128)S(1)}, u32[]{:S(2)}, u32[]{:S(2)}) collective-permute-start(f32[1,32,1024]{2,1,0:T(8,128)S(1)} %get-tuple-element.589), channel_id=1, source_target_pairs={{0,2},{1,3},{2,0},{3,1},{4,6},{5,7},{6,4},{7,5},{8,10},{9,11},{10,... | collective-permute-start | bytes 393224 | tf_op jit(solution)/shard_map/ppermute | solution.py:1011
  386.1 2.9 collective-permute-start.50
  (58 other events, 497.4 us)
